TPU v7x, 32 devices: a whole 2x2x4 slice. The times are simulated.
32 devices in a mesh: seq: 8 (over z, core), tp: 4 (over y, x).
Axes of the slice: x: 2, y: 2, z: 4, core: 2. Of those that a mesh axis runs over, the one named last changes fastest.
Arguments:
- layer_input: bfloat16 [6144, 2048], P(('seq', 'tp')), may hold values from -6 to 6
- cotangent: bfloat16 [6144, 2048], P(('seq', 'tp')), may hold values from -6 to 6
- query_key_value_weight: bfloat16 [3, 2048, 2048], P(None, 'seq', 'tp'), may hold values from -0.125 to 0.125
- output_weight: bfloat16 [2048, 2048], P('tp', 'seq'), may hold values from -0.125 to 0.125
- gate_up_weight: bfloat16 [2, 2048, 8192], P(None, 'seq', 'tp'), may hold values from -0.125 to 0.125
- down_weight: bfloat16 [8192, 2048], P('tp', 'seq'), may hold values from -0.0625 to 0.0625
- input_first_factor: bfloat16 [5, 2048, 128], P(None, 'seq'), may hold values from -0.125 to 0.125
- output_first_factor: bfloat16 [2048, 128], P('tp', 'seq'), may hold values from -0.125 to 0.125
- down_first_factor: bfloat16 [8192, 128], P('tp', 'seq'), may hold values from -0.0625 to 0.0625
- query_key_value_second: bfloat16 [3, 128, 2048], P(None, 'seq', 'tp'), may hold values from -0.375 to 0.375
- gate_up_second_factor: bfloat16 [2, 128, 8192], P(None, 'seq', 'tp'), may hold values from -0.375 to 0.375
- output_down_second_factor: bfloat16 [2, 128, 2048], P(None, 'seq'), may hold values from -0.375 to 0.375
- norm_gain_table: float32 [4, 2048], replicated, may hold values from 0.5 to 2
- sequence_adapter: int32 [3], replicated, may hold values from 0 to 7
- block_sequence: int32 [48], replicated, may hold values from 0 to 2, as said below
- block_position: int32 [48], replicated, may hold values from 0 to 15
Outputs:
- output: float32 [6144, 2048], P(('seq', 'tp'))
- input_grad: float32 [6144, 2048], P(('seq', 'tp'))
- grad_a_in: float32 [5, 2048, 128], P(None, 'seq')
- grad_a_o: float32 [2048, 128], P('tp', 'seq')
- grad_a_down: float32 [8192, 128], P('tp', 'seq')
- grad_b_qkv: float32 [3, 128, 2048], P(None, 'seq', 'tp')
- grad_b_gu: float32 [2, 128, 8192], P(None, 'seq', 'tp')
- grad_b_out: float32 [2, 128, 2048], P(None, 'seq')
Inputs may be any that keep to these rules, and one draw needn't show every extreme that they name: block_sequence and block_position together name each of the 3 sequences' 8 + 8 places exactly once; places below 8 are the prompt's blocks in order, the others its continuations.
All inputs are finite; a program needn't handle non-finite values.
Results may differ from a plain program's by a relative error of at most 0.028.
Values may be sent and summed in bfloat16 or wider, within the bound.
No kernel may reach another device: no remote copies, remote signals or barrier semaphores. Data moves between devices by JAX's collectives and lax.ppermute only.
A program may use at most 256 MiB of HBM per device.

v0:
```python
import jax
import jax.numpy as jnp
from jax import lax
from jax.sharding import PartitionSpec as P

HEAD_DIM = 128
ADAPTER_RANK = 16
BLK = 128
PROMPT_BLOCKS = 8


EPS = 1e-06
THETA = 500000.0
adapter_scale = 2.0
NEG = -1e30
HIGH = lax.Precision.HIGHEST


def lowrank_product(left, right):
    return jnp.dot(left, right, preferred_element_type=jnp.float32)


def full_product(left, right):
    return jnp.dot(
        left.astype(jnp.float32),
        right.astype(jnp.float32),
        precision=HIGH,
        preferred_element_type=jnp.float32,
    )


def rms_norm(values_in, gain_row):
    return (
        values_in
        * lax.rsqrt(jnp.mean(values_in * values_in, axis=-1, keepdims=True) + EPS)
        * gain_row
    )


def rms_back(values_in, grad_in, gain_row):
    inv_root = lax.rsqrt(jnp.mean(values_in * values_in, axis=-1, keepdims=True) + EPS)
    scaled = grad_in * gain_row
    return inv_root * scaled - values_in * inv_root**3 * jnp.mean(
        scaled * values_in, axis=-1, keepdims=True
    )


def rotary(vals_in, cosine, sine_table):
    half_dim = vals_in.shape[-1] // 2
    first_half = vals_in[..., :half_dim]
    second_half = vals_in[..., half_dim:]
    return jnp.concatenate(
        [
            first_half * cosine - second_half * sine_table,
            second_half * cosine + first_half * sine_table,
        ],
        axis=-1,
    )


def unrotary(grads_in, cosine, sine_table):
    half_dim = grads_in.shape[-1] // 2
    first_half = grads_in[..., :half_dim]
    second_half = grads_in[..., half_dim:]
    return jnp.concatenate(
        [
            first_half * cosine + second_half * sine_table,
            second_half * cosine - first_half * sine_table,
        ],
        axis=-1,
    )


def round_trip(tensor):
    return lax.optimization_barrier(tensor.astype(jnp.bfloat16)).astype(jnp.float32)


def row_layout(block_sequence, block_position, first_block, count_blocks):
    seq_ids = lax.dynamic_slice_in_dim(block_sequence, first_block, count_blocks)
    places = lax.dynamic_slice_in_dim(block_position, first_block, count_blocks)
    block_ids = first_block + jnp.arange(count_blocks, dtype=jnp.int32)
    offsets = jnp.tile(jnp.arange(BLK, dtype=jnp.int32), count_blocks)
    return (jnp.repeat(seq_ids, BLK), jnp.repeat(places, BLK), jnp.repeat(block_ids, BLK), offsets)


def visible_mask(query_info, key_info):
    same_seq = query_info[0][:, None] == key_info[0][None, :]
    prompt_seen = (key_info[1][None, :] < PROMPT_BLOCKS) & (
        key_info[1][None, :] < query_info[1][:, None]
    )
    own_block = (key_info[2][None, :] == query_info[2][:, None]) & (
        key_info[3][None, :] <= query_info[3][:, None]
    )
    return same_seq & (prompt_seen | own_block)


def tile_scores(query_tile, key_tile, key_mask, scale):
    scores = (
        jnp.einsum("qhd,khd->hqk", query_tile, key_tile, preferred_element_type=jnp.float32) * scale
    )
    return jnp.where(key_mask[None], scores, NEG)


def score_grads(
    query_tile, key_tile, value_tile, grad_tile, total_tile, delta_tile, key_mask, scale
):
    scores = tile_scores(query_tile, key_tile, key_mask, scale)
    probs_tile = jnp.where(key_mask[None], jnp.exp(scores - total_tile[:, :, None]), 0.0)
    d_probs = jnp.einsum("qhd,khd->hqk", grad_tile, value_tile, preferred_element_type=jnp.float32)
    d_scores = (probs_tile * (d_probs - delta_tile[:, :, None])).astype(jnp.bfloat16)
    return (probs_tile.astype(jnp.bfloat16), d_scores)


def column_pullback(
    source_rows,
    output_gradient,
    frozen_weight,
    adapter_first,
    adapter_second,
    latent_rows,
    adapter_selector,
):
    latent_gradient = (
        adapter_scale * lowrank_product(output_gradient, adapter_second.T) * adapter_selector
    )
    source_gradient = lowrank_product(output_gradient, frozen_weight.T) + full_product(
        latent_gradient, adapter_first.T
    )
    return (
        source_gradient,
        full_product(source_rows.T, latent_gradient),
        adapter_scale * full_product(latent_rows.T, output_gradient),
    )


def local(
    layer_input,
    cotangent,
    query_key_value_weight,
    output_weight,
    gate_up_weight,
    down_weight,
    input_first_factor,
    output_first_factor,
    down_first_factor,
    query_key_value_second,
    gate_up_second_factor,
    output_down_second_factor,
    norm_gain_table,
    sequence_adapter,
    block_sequence,
    block_position,
):
    (
        query_key_value_weight,
        output_weight,
        gate_up_weight,
        down_weight,
        input_first_factor,
        output_first_factor,
        down_first_factor,
        query_key_value_second,
        gate_up_second_factor,
        output_down_second_factor,
    ) = (
        lax.all_gather(query_key_value_weight, "seq", axis=1, tiled=True),
        lax.all_gather(output_weight, "seq", axis=1, tiled=True),
        lax.all_gather(gate_up_weight, "seq", axis=1, tiled=True),
        lax.all_gather(down_weight, "seq", axis=1, tiled=True),
        lax.all_gather(input_first_factor, "seq", axis=1, tiled=True),
        lax.all_gather(output_first_factor, "seq", axis=1, tiled=True),
        lax.all_gather(down_first_factor, "seq", axis=1, tiled=True),
        lax.all_gather(query_key_value_second, "seq", axis=1, tiled=True),
        lax.all_gather(gate_up_second_factor, "seq", axis=1, tiled=True),
        lax.all_gather(output_down_second_factor, "seq", axis=1, tiled=True),
    )
    tp_count = lax.axis_size("tp")
    tp_rank = lax.axis_index("tp")
    seq_count = lax.axis_size("seq")
    seq_rank = lax.axis_index("seq")
    input_rows, upstream = (
        lax.all_gather(layer_input, "tp", axis=0, tiled=True),
        lax.all_gather(cotangent, "tp", axis=0, tiled=True),
    )
    group_rows = input_rows.shape[0]
    model_width = input_rows.shape[1]
    my_blocks = group_rows // BLK
    share_rows = group_rows // tp_count
    my_start = tp_rank * share_rows
    query_info = row_layout(block_sequence, block_position, seq_rank * my_blocks, my_blocks)
    seq_match = (
        query_info[0][:, None] == jnp.arange(sequence_adapter.shape[0], dtype=jnp.int32)[None, :]
    )
    row_adapter = jnp.sum(jnp.where(seq_match, sequence_adapter[None, :], 0), axis=1)
    adapter_slots = input_first_factor.shape[2]
    adapter_selector = (
        jnp.arange(adapter_slots, dtype=jnp.int32)[None, :] // ADAPTER_RANK == row_adapter[:, None]
    ).astype(jnp.float32)
    position = (
        jnp.where(query_info[1] < PROMPT_BLOCKS, query_info[1] * BLK, PROMPT_BLOCKS * BLK)
        + query_info[3]
    )
    frequency = THETA ** (-(jnp.arange(HEAD_DIM // 2, dtype=jnp.float32) * 2.0) / HEAD_DIM)
    angles = position.astype(jnp.float32)[:, None] * frequency[None, :]
    cosine = jnp.cos(angles)[:, None, :]
    sine_table = jnp.sin(angles)[:, None, :]
    col_width = query_key_value_weight.shape[2]
    local_heads = col_width // HEAD_DIM
    head_shape = (group_rows, local_heads, HEAD_DIM)
    scale = HEAD_DIM ** (-0.5)
    latent_stack = []
    projected = []
    for projection_index in range(3):
        latent_rows = (
            lowrank_product(input_rows, input_first_factor[projection_index]) * adapter_selector
        )
        latent_stack.append(latent_rows)
        projected.append(
            lowrank_product(input_rows, query_key_value_weight[projection_index])
            + adapter_scale * full_product(latent_rows, query_key_value_second[projection_index])
        )
    normed_query, normed_key, projected_value = projected
    gain_q = lax.dynamic_slice_in_dim(norm_gain_table[0], tp_rank * col_width, col_width)
    gain_k = lax.dynamic_slice_in_dim(norm_gain_table[1], tp_rank * col_width, col_width)
    sum_q, sum_k = lax.psum(
        (jnp.sum(normed_query * normed_query, axis=1), jnp.sum(normed_key * normed_key, axis=1)),
        "tp",
    )
    inv_q = lax.rsqrt(sum_q / model_width + EPS)[:, None]
    inv_k = lax.rsqrt(sum_k / model_width + EPS)[:, None]
    queries = rotary(
        (normed_query * inv_q * gain_q).reshape(head_shape), cosine, sine_table
    ).astype(jnp.bfloat16)
    key_rows = rotary((normed_key * inv_k * gain_k).reshape(head_shape), cosine, sine_table).astype(
        jnp.bfloat16
    )
    value_rows = projected_value.astype(jnp.bfloat16).reshape(head_shape)
    all_keys, all_values = (
        lax.all_gather(key_rows, "seq", axis=0, tiled=True),
        lax.all_gather(value_rows, "seq", axis=0, tiled=True),
    )
    tile_shape = (seq_count, group_rows, local_heads, HEAD_DIM)
    key_tiles = all_keys.reshape(tile_shape)
    value_tiles = all_values.reshape(tile_shape)
    tile_ids = jnp.arange(seq_count, dtype=jnp.int32)

    def tile_info(tile_index):
        return row_layout(block_sequence, block_position, tile_index * my_blocks, my_blocks)

    def stats_step(running, packed):
        tile_index, keys_tile = packed
        scores = tile_scores(
            queries, keys_tile, visible_mask(query_info, tile_info(tile_index)), scale
        )
        top_old, total_old = running
        top_new = jnp.maximum(top_old, jnp.max(scores, axis=2))
        total_new = total_old * jnp.exp(top_old - top_new) + jnp.sum(
            jnp.exp(scores - top_new[:, :, None]), axis=2
        )
        return ((top_new, total_new), None)

    start_stats = (
        jnp.full((local_heads, group_rows), NEG, jnp.float32),
        jnp.zeros((local_heads, group_rows), jnp.float32),
    )
    (top_rows, total_rows), unused_out = lax.scan(stats_step, start_stats, (tile_ids, key_tiles))
    log_total = top_rows + jnp.log(total_rows)

    def value_step(running, packed):
        tile_index, keys_tile, values_tile = packed
        key_mask = visible_mask(query_info, tile_info(tile_index))
        scores = tile_scores(queries, keys_tile, key_mask, scale)
        probs_low = jnp.where(key_mask[None], jnp.exp(scores - log_total[:, :, None]), 0.0).astype(
            jnp.bfloat16
        )
        return (
            running
            + jnp.einsum(
                "hqk,khd->qhd", probs_low, values_tile, preferred_element_type=jnp.float32
            ),
            None,
        )

    attended, unused_out = lax.scan(
        value_step, jnp.zeros(head_shape, jnp.float32), (tile_ids, key_tiles, value_tiles)
    )
    head_outputs = attended.reshape(group_rows, col_width).astype(jnp.bfloat16)
    output_latent = lowrank_product(head_outputs, output_first_factor) * adapter_selector
    attention_addend = lowrank_product(head_outputs, output_weight) + adapter_scale * full_product(
        output_latent, output_down_second_factor[0]
    )
    attention_output = lax.psum(attention_addend.astype(jnp.bfloat16), "tp").astype(jnp.float32)
    hidden = input_rows.astype(jnp.float32) + rms_norm(attention_output, norm_gain_table[2])
    hidden_lowrank = hidden.astype(jnp.bfloat16)
    gate_latent = lowrank_product(hidden_lowrank, input_first_factor[3]) * adapter_selector
    up_latent = lowrank_product(hidden_lowrank, input_first_factor[4]) * adapter_selector
    gate_activation = lowrank_product(
        hidden_lowrank, gate_up_weight[0]
    ) + adapter_scale * full_product(gate_latent, gate_up_second_factor[0])
    up_activation = lowrank_product(
        hidden_lowrank, gate_up_weight[1]
    ) + adapter_scale * full_product(up_latent, gate_up_second_factor[1])
    sigmoid_gate = jax.nn.sigmoid(gate_activation)
    silu_gate = gate_activation * sigmoid_gate
    gated_activation = (silu_gate * up_activation).astype(jnp.bfloat16)
    down_latent = lowrank_product(gated_activation, down_first_factor) * adapter_selector
    feedforward_addend = lowrank_product(
        gated_activation, down_weight
    ) + adapter_scale * full_product(down_latent, output_down_second_factor[1])
    feedforward_output = lax.psum(feedforward_addend.astype(jnp.bfloat16), "tp").astype(jnp.float32)
    result_full = hidden + rms_norm(feedforward_output, norm_gain_table[3])
    output = lax.dynamic_slice_in_dim(result_full, my_start, share_rows, 0)
    upstream_f = upstream.astype(jnp.float32)
    feedforward_gradient = rms_back(feedforward_output, upstream_f, norm_gain_table[3]).astype(
        jnp.bfloat16
    )
    down_latent_gradient = (
        adapter_scale
        * lowrank_product(feedforward_gradient, output_down_second_factor[1].T)
        * adapter_selector
    )
    activation_gradient = lowrank_product(feedforward_gradient, down_weight.T) + full_product(
        down_latent_gradient, down_first_factor.T
    )
    grad_a_down = full_product(gated_activation.T, down_latent_gradient)
    down_second_gradient = adapter_scale * full_product(down_latent.T, feedforward_gradient)
    d_silu = sigmoid_gate * (1.0 + gate_activation * (1.0 - sigmoid_gate))
    gate_gradient = (activation_gradient * up_activation * d_silu).astype(jnp.bfloat16)
    up_gradient = (activation_gradient * silu_gate).astype(jnp.bfloat16)
    dh_gate, grad_a_gate, grad_b_gate = column_pullback(
        hidden_lowrank,
        gate_gradient,
        gate_up_weight[0],
        input_first_factor[3],
        gate_up_second_factor[0],
        gate_latent,
        adapter_selector,
    )
    dh_up, grad_a_up, grad_b_up = column_pullback(
        hidden_lowrank,
        up_gradient,
        gate_up_weight[1],
        input_first_factor[4],
        gate_up_second_factor[1],
        up_latent,
        adapter_selector,
    )
    d_hidden = upstream_f + lax.psum((dh_gate + dh_up).astype(jnp.bfloat16), "tp").astype(
        jnp.float32
    )
    attention_gradient = rms_back(attention_output, d_hidden, norm_gain_table[2]).astype(
        jnp.bfloat16
    )
    d_hidden_own = lax.dynamic_slice_in_dim(d_hidden, my_start, share_rows, 0)
    output_latent_gradient = (
        adapter_scale
        * lowrank_product(attention_gradient, output_down_second_factor[0].T)
        * adapter_selector
    )
    head_gradient = (
        lowrank_product(attention_gradient, output_weight.T)
        + full_product(output_latent_gradient, output_first_factor.T)
    ).astype(jnp.bfloat16)
    grad_a_o = full_product(head_outputs.T, output_latent_gradient)
    output_second_gradient = adapter_scale * full_product(output_latent.T, attention_gradient)
    d_heads3 = head_gradient.reshape(head_shape)
    delta_rows = jnp.sum(d_heads3.astype(jnp.float32) * attended, axis=2).T
    zero_heads = jnp.zeros(head_shape, jnp.float32)

    def send_step(running, packed):
        tile_index, keys_tile, values_tile = packed
        key_mask = visible_mask(query_info, tile_info(tile_index))
        probs_low, d_scores = score_grads(
            queries, keys_tile, values_tile, d_heads3, log_total, delta_rows, key_mask, scale
        )
        d_query_new = (
            running
            + jnp.einsum("hqk,khd->qhd", d_scores, keys_tile, preferred_element_type=jnp.float32)
            * scale
        )
        key_grad = (
            jnp.einsum("hqk,qhd->khd", d_scores, queries, preferred_element_type=jnp.float32)
            * scale
        )
        value_grad = jnp.einsum(
            "hqk,qhd->khd", probs_low, d_heads3, preferred_element_type=jnp.float32
        )
        return (d_query_new, (key_grad, value_grad))

    d_query, (key_grads, value_grads) = lax.scan(
        send_step, zero_heads, (tile_ids, key_tiles, value_tiles)
    )
    flat_shape = (seq_count * group_rows, local_heads, HEAD_DIM)
    d_key, d_value = (
        lax.psum_scatter(
            key_grads.reshape(flat_shape).astype(jnp.bfloat16),
            "seq",
            scatter_dimension=0,
            tiled=True,
        ).astype(jnp.float32),
        lax.psum_scatter(
            value_grads.reshape(flat_shape).astype(jnp.bfloat16),
            "seq",
            scatter_dimension=0,
            tiled=True,
        ).astype(jnp.float32),
    )
    d_qn = unrotary(round_trip(d_query), cosine, sine_table).reshape(group_rows, col_width)
    d_kn = unrotary(round_trip(d_key), cosine, sine_table).reshape(group_rows, col_width)
    value_lowrank_gradient = d_value.astype(jnp.bfloat16).reshape(group_rows, col_width)
    scaled_q = d_qn * gain_q
    scaled_k = d_kn * gain_k
    part_q, part_k = lax.psum(
        (jnp.sum(scaled_q * normed_query, axis=1), jnp.sum(scaled_k * normed_key, axis=1)), "tp"
    )
    normed_query_gradient = (
        inv_q * scaled_q - normed_query * inv_q**3 * (part_q / model_width)[:, None]
    ).astype(jnp.bfloat16)
    normed_key_gradient = (
        inv_k * scaled_k - normed_key * inv_k**3 * (part_k / model_width)[:, None]
    ).astype(jnp.bfloat16)
    dx_query, grad_a_query, grad_b_query = column_pullback(
        input_rows,
        normed_query_gradient,
        query_key_value_weight[0],
        input_first_factor[0],
        query_key_value_second[0],
        latent_stack[0],
        adapter_selector,
    )
    dx_key, grad_a_key, grad_b_key = column_pullback(
        input_rows,
        normed_key_gradient,
        query_key_value_weight[1],
        input_first_factor[1],
        query_key_value_second[1],
        latent_stack[1],
        adapter_selector,
    )
    dx_value, grad_a_value, grad_b_value = column_pullback(
        input_rows,
        value_lowrank_gradient,
        query_key_value_weight[2],
        input_first_factor[2],
        query_key_value_second[2],
        latent_stack[2],
        adapter_selector,
    )
    dx_part = lax.psum_scatter(
        (dx_query + dx_key + dx_value).astype(jnp.bfloat16), "tp", scatter_dimension=0, tiled=True
    ).astype(jnp.float32)
    input_grad = d_hidden_own + dx_part
    grad_a_in = jnp.stack([grad_a_query, grad_a_key, grad_a_value, grad_a_gate, grad_a_up])
    grad_b_qkv = jnp.stack([grad_b_query, grad_b_key, grad_b_value])
    grad_b_gu = jnp.stack([grad_b_gate, grad_b_up])
    grad_b_out = jnp.stack([output_second_gradient, down_second_gradient])
    grad_a_in, grad_a_o, grad_a_down, grad_b_qkv, grad_b_gu, grad_b_out = (
        lax.psum_scatter(
            grad_a_in.astype(jnp.bfloat16), "seq", scatter_dimension=1, tiled=True
        ).astype(jnp.float32),
        lax.psum_scatter(
            grad_a_o.astype(jnp.bfloat16), "seq", scatter_dimension=1, tiled=True
        ).astype(jnp.float32),
        lax.psum_scatter(
            grad_a_down.astype(jnp.bfloat16), "seq", scatter_dimension=1, tiled=True
        ).astype(jnp.float32),
        lax.psum_scatter(
            grad_b_qkv.astype(jnp.bfloat16), "seq", scatter_dimension=1, tiled=True
        ).astype(jnp.float32),
        lax.psum_scatter(
            grad_b_gu.astype(jnp.bfloat16), "seq", scatter_dimension=1, tiled=True
        ).astype(jnp.float32),
        lax.psum_scatter(
            grad_b_out.astype(jnp.bfloat16), "seq", scatter_dimension=1, tiled=True
        ).astype(jnp.float32),
    )
    grad_a_in, grad_b_out = (
        lax.psum(grad_a_in.astype(jnp.bfloat16), "tp").astype(jnp.float32),
        lax.psum(grad_b_out.astype(jnp.bfloat16), "tp").astype(jnp.float32),
    )
    return (output, input_grad, grad_a_in, grad_a_o, grad_a_down, grad_b_qkv, grad_b_gu, grad_b_out)


def solution(mesh):
    return jax.shard_map(
        local,
        mesh=mesh,
        in_specs=(
            P(("seq", "tp"), None),
            P(("seq", "tp"), None),
            P(None, "seq", "tp"),
            P("tp", "seq"),
            P(None, "seq", "tp"),
            P("tp", "seq"),
            P(None, "seq", None),
            P("tp", "seq"),
            P("tp", "seq"),
            P(None, "seq", "tp"),
            P(None, "seq", "tp"),
            P(None, "seq", None),
            P(),
            P(),
            P(),
            P(),
        ),
        out_specs=(
            P(("seq", "tp"), None),
            P(("seq", "tp"), None),
            P(None, "seq", None),
            P("tp", "seq"),
            P("tp", "seq"),
            P(None, "seq", "tp"),
            P(None, "seq", "tp"),
            P(None, "seq", None),
        ),
        check_vma=False,
    )
```

profile of v0, /device:TPU:0, one launch (start us, length us, event | category | flops | bytes accessed | tf_op | source)
XLA Modules:
  0.0 1730.8 jit_solution(6933294453101621257)
XLA Ops:
  15.0 18.8 %all_gather.45 = bf16[3,128,512]{2,1,0:T(8,128)(2,1)} all-gather(bf16[3,16,512]{2,1,0:T(8,128)(2,1)} %param.31), channel_id=1, replica_groups=mesh['seq'=8,'tp'=4] {'seq'}, dimensions={1}, use_global_device_ids=true | all-gather | bytes 442368 | tf_op jit(solution)/shard_map/all_gather | solution.py:173
  36.3 11.8 all-gather.16.cloned.1.call-done
  48.1 45.4 %all-gather.12.cloned.1.call-done = bf16[768,2048]{1,0:T(8,128)(2,1)} async-done(((bf16[192,2048]{1,0:T(8,128)(2,1)}), bf16[768,2048]{1,0:T(8,128)(2,1)}) %all-gather.12.cloned.1.call-update) | async-done | bytes 3145744 | tf_op jit(solution)/shard_map/all_gather | solution.py:182
  100.2 59.6 %all-gather.14.cloned.1.call-done = bf16[3,2048,512]{2,1,0:T(8,128)(2,1)} async-done(((bf16[3,256,512]{2,1,0:T(8,128)(2,1)}), bf16[3,2048,512]{2,1,0:T(8,128)(2,1)}) %all-gather.14.cloned.1.call-update) | async-done | bytes 6291472 | tf_op jit(solution)/shard_map/all_gather | solution.py:166
  172.2 11.1 all-reduce.1
  218.2 16.0 all_gather.49
  235.7 34.8 %all-gather.20.cloned.1.call-done = bf16[6144,4,128]{2,0,1:T(8,128)(2,1)} async-done(((bf16[768,4,128]{2,0,1:T(8,128)(2,1)}), bf16[6144,4,128]{2,0,1:T(8,128)(2,1)}) %all-gather.20.cloned.1.call-update) | async-done | bytes 6291472 | tf_op jit(solution)/shard_map/all_gather | solution.py:239
  276.5 124.7 %while.39 = (s32[]{:T(128)}, f32[4,768]{1,0:T(4,128)S(1)}, f32[4,768]{1,0:T(4,128)S(1)}, s32[8]{0:T(128)S(1)}, s32[48]{0:T(128)S(1)}, /*index=5*/s32[48]{0:T(128...) while((s32[]{:T(128)}, f32[4,768]{1,0:T(4,128)S(1)}, ...), condition=%wide.region_8.9_spmd.clone, body=%wide.region_5.8_spmd.clone.sunk | while | flops 625229568 | bytes 22422012 | solution.py:266
  401.3 64.6 %while.40 = (s32[]{:T(128)}, f32[768,4,128]{0,2,1:T(8,128)S(1)}, bf16[8,768,4,128]{3,1,0,2:T(8,128)(2,1)}, s32[8]{0:T(128)S(1)}, s32[48]{0:T(128)S(1)}, /*index=...) while((s32[]{:T(128)}, f32[768,4,128]{0,2,1:T(8,128)S(1)}, ...), condition=%wide.region_10.11_spmd.clone, body=%wide.region_9.10_spmd.clone.sunk | while | flops 1225261824 | bytes 6743045 | solution.py:284
  484.9 15.8 all_gather.54
  500.7 67.2 %all-reduce.8.cloned.1.call-done = bf16[768,2048]{1,0:T(8,128)(2,1)} async-done(((bf16[768,2048]{1,0:T(8,128)(2,1)}), bf16[768,2048]{1,0:T(8,128)(2,1)}) %all-reduce.8.cloned.1.call-update) | async-done | bytes 3145744 | tf_op jit(solution)/shard_map/psum | solution.py:292
  580.8 139.9 %all-gather.26.cloned.1.call-done = bf16[2,2048,2048]{2,1,0:T(8,128)(2,1)} async-done(((bf16[2,256,2048]{2,1,0:T(8,128)(2,1)}), bf16[2,2048,2048]{2,1,0:T(8,128)(2,1)}) %all-gather.26.cloned.1.call-update) | async-done | bytes 16777232 | tf_op jit(solution)/shard_map/all_gather | solution.py:168
  720.6 12.2 fusion.78
  754.9 71.3 %all-gather.30.cloned.1.call-done = bf16[2048,2048]{1,0:T(8,128)(2,1)} async-done(((bf16[2048,256]{1,0:T(8,128)(2,1)}), bf16[2048,2048]{1,0:T(8,128)(2,1)}) %all-gather.30.cloned.1.call-update) | async-done | bytes 8388624 | tf_op jit(solution)/shard_map/all_gather | solution.py:169
  826.2 9.1 fusion.132
  840.0 30.0 %all-gather.32.cloned.1.call-done = bf16[768,2048]{1,0:T(8,128)(2,1)} async-done(((bf16[192,2048]{1,0:T(8,128)(2,1)}), bf16[768,2048]{1,0:T(8,128)(2,1)}) %all-gather.32.cloned.1.call-update) | async-done | bytes 3145744 | tf_op jit(solution)/shard_map/all_gather | solution.py:183
  870.0 90.1 %all-reduce.10.cloned.1.call-done = bf16[768,2048]{1,0:T(8,128)(2,1)} async-done(((bf16[768,2048]{1,0:T(8,128)(2,1)}), bf16[768,2048]{1,0:T(8,128)(2,1)}) %all-reduce.10.cloned.1.call-update) | async-done | bytes 3145744 | tf_op jit(solution)/shard_map/psum | solution.py:310
  967.1 12.9 fusion.133
  989.9 10.4 fusion.77
  1000.3 9.3 fusion.79
  1020.1 87.0 %all-reduce.12.cloned.1.call-done = bf16[768,2048]{1,0:T(8,128)(2,1)} async-done(((bf16[768,2048]{1,0:T(8,128)(2,1)}), bf16[768,2048]{1,0:T(8,128)(2,1)}) %all-reduce.12.cloned.1.call-update) | async-done | bytes 3145744 | tf_op jit(solution)/shard_map/psum | solution.py:348
  1123.5 162.8 %while.41 = (s32[]{:T(128)}, f32[768,4,128]{0,2,1:T(8,128)S(1)}, bf16[8,768,4,128]{3,1,0,2:T(8,128)(2,1)}, bf16[8,768,4,128]{3,1,0,2:T(8,128)(2,1)}, bf16[8,768,...) while((s32[]{:T(128)}, f32[768,4,128]{0,2,1:T(8,128)S(1)}, ...), condition=%wide.region_20.21_spmd.clone, body=%wide.region_19.20_spmd.clone.sunk | while | flops 3054502656 | bytes 78137944 | solution.py:390
  1296.7 59.5 %reduce-scatter.10.cloned.1.call-done = bf16[768,4,128]{2,0,1:T(8,128)(2,1)} async-done(((bf16[6144,4,128]{2,0,1:T(8,128)(2,1)}), bf16[768,4,128]{2,0,1:T(8,128)(2,1)}) %reduce-scatter.10.cloned.1.call-update) | async-done | bytes 786448 | tf_op jit(solution)/shard_map/reduce_scatter | solution.py:395
  1373.3 10.1 all-reduce
  1387.0 39.6 %reduce-scatter.12.cloned.1.call-done = bf16[768,4,128]{2,0,1:T(8,128)(2,1)} async-done(((bf16[6144,4,128]{2,0,1:T(8,128)(2,1)}), bf16[768,4,128]{2,0,1:T(8,128)(2,1)}) %reduce-scatter.12.cloned.1.call-update) | async-done | bytes 786448 | tf_op jit(solution)/shard_map/reduce_scatter | solution.py:401
  1498.1 13.5 add_convert_fusion
  1517.2 14.0 reduce-scatter.20.cloned.1.call-done
  1532.7 32.2 %reduce-scatter.24.cloned.1.call-done = bf16[2,16,2048]{2,1,0:T(8,128)(2,1)} async-done(((bf16[2,128,2048]{2,1,0:T(8,128)(2,1)}), bf16[2,16,2048]{2,1,0:T(8,128)(2,1)}) %reduce-scatter.24.cloned.1.call-update) | async-done | bytes 131088 | tf_op jit(solution)/shard_map/reduce_scatter | solution.py:470
  1566.5 30.0 %reduce-scatter.18.cloned.1.call-done = bf16[512,16]{0,1:T(8,128)(2,1)} async-done(((bf16[512,128]{0,1:T(8,128)(2,1)}), bf16[512,16]{0,1:T(8,128)(2,1)}) %reduce-scatter.18.cloned.1.call-update) | async-done | bytes 16400 | tf_op jit(solution)/shard_map/reduce_scatter | solution.py:461
  1597.9 30.1 %reduce-scatter.22.cloned.1.call-done = bf16[3,16,512]{2,1,0:T(8,128)(2,1)} async-done(((bf16[3,128,512]{2,1,0:T(8,128)(2,1)}), bf16[3,16,512]{2,1,0:T(8,128)(2,1)}) %reduce-scatter.22.cloned.1.call-update) | async-done | bytes 49168 | tf_op jit(solution)/shard_map/reduce_scatter | solution.py:467
  1629.4 44.5 %all-reduce.14.cloned.1.call-done = (bf16[5,256,128]{1,2,0:T(8,128)(2,1)}, bf16[2,16,2048]{2,1,0:T(8,128)(2,1)}) async-done(((bf16[5,256,128]{1,2,0:T(8,128)(2,1)}, bf16[2,16,2048]{2,1,0:T(8,128)(2,1)}), (bf16[5,256,128]{1,2,0:T(8,128)(2,1)}, bf16[2,16,2048]{2,1,0:T(8,128)(2,1)})) %all-reduce.14.cloned.1.call-update) | async-done | bytes 458768 | tf_op jit(solution)/shard_map/psum | solution.py:478
  1677.5 43.2 %reduce-scatter.14.cloned.1.call-done = bf16[192,2048]{1,0:T(8,128)(2,1)} async-done(((bf16[768,2048]{1,0:T(8,128)(2,1)}), bf16[192,2048]{1,0:T(8,128)(2,1)}) %reduce-scatter.14.cloned.1.call-update) | async-done | bytes 786448 | tf_op jit(solution)/shard_map/reduce_scatter | solution.py:449
  (766 shorter events, 628.5 us)
Async XLA Ops:
  7.2 41.0 %all-gather.16.cloned.1.call-start = ((), (), s32[]{:S(2)}) async-start(), calls=%async_computation.11 | async-start | bytes 2949120 | tf_op jit(solution)/shard_map/all_gather | solution.py:170
  7.9 85.6 %all-gather.12.cloned.1.call-start = ((), (), s32[]{:S(2)}) async-start(), calls=%async_computation.9 | async-start | bytes 3932160 | tf_op jit(solution)/shard_map/all_gather | solution.py:182
  8.6 151.2 %all-gather.14.cloned.1.call-start = ((), (), s32[]{:S(2)}) async-start(), calls=%async_computation.10 | async-start | bytes 7077888 | tf_op jit(solution)/shard_map/all_gather | solution.py:166
  9.4 261.1 %all-gather.20.cloned.1.call-start = ((), (), s32[]{:S(2)}) async-start(), calls=%async_computation.13 | async-start | bytes 7077888 | tf_op jit(solution)/shard_map/all_gather | solution.py:239
  36.3 165.3 %copy-start.35 = (f32[768,64]{1,0:T(8,128)}, f32[768,64]{1,0:T(8,128)S(1)}, u32[]{:S(2)}) copy-start(f32[768,64]{1,0:T(8,128)S(1)} %get-tuple-element.714) | copy-start | bytes 589828
  207.8 193.5 %all-gather.18.cloned.1.call-start = ((), (), s32[]{:S(2)}) async-start(), calls=%async_computation.12 | async-start | bytes 7077888 | tf_op jit(solution)/shard_map/all_gather | solution.py:240
  216.7 252.9 %all-gather.22.cloned.1.call-start = ((), (), s32[]{:S(2)}) async-start(), calls=%async_computation.14 | async-start | bytes 2359296 | tf_op jit(solution)/shard_map/all_gather | solution.py:167
  217.3 258.6 %all-gather.24.cloned.1.call-start = ((), (), s32[]{:S(2)}) async-start(), calls=%async_computation.15 | async-start | bytes 1179648 | tf_op jit(solution)/shard_map/all_gather | solution.py:175
  218.1 349.8 %all-reduce.8.cloned.1.call-start = ((), (), s32[]{:S(2)}) async-start(), calls=%async_computation.16 | async-start | bytes 6291456 | tf_op jit(solution)/shard_map/psum | solution.py:292
  482.2 238.4 %all-gather.26.cloned.1.call-start = ((), (), s32[]{:S(2)}) async-start(), calls=%async_computation.17 | async-start | bytes 18874368 | tf_op jit(solution)/shard_map/all_gather | solution.py:168
  482.3 88.4 %copy-start.8 = (bf16[768,2048]{1,0:T(8,128)(2,1)S(1)}, bf16[768,2048]{1,0:T(8,128)(2,1)}, u32[]{:S(2)}) copy-start(bf16[768,2048]{1,0:T(8,128)(2,1)} %all-gather.12.cloned.1.call-done) | copy-start | bytes 9437188
  483.0 259.6 %all-gather.28.cloned.1.call-start = ((), (), s32[]{:S(2)}) async-start(), calls=%async_computation.18 | async-start | bytes 1179648 | tf_op jit(solution)/shard_map/all_gather | solution.py:174
  483.5 342.6 %all-gather.30.cloned.1.call-start = ((), (), s32[]{:S(2)}) async-start(), calls=%async_computation.19 | async-start | bytes 9437184 | tf_op jit(solution)/shard_map/all_gather | solution.py:169
  484.3 385.7 %all-gather.32.cloned.1.call-start = ((), (), s32[]{:S(2)}) async-start(), calls=%async_computation.21 | async-start | bytes 3932160 | tf_op jit(solution)/shard_map/all_gather | solution.py:183
  484.9 475.2 %all-reduce.10.cloned.1.call-start = ((), (), s32[]{:S(2)}) async-start(), calls=%async_computation.20 | async-start | bytes 6291456 | tf_op jit(solution)/shard_map/psum | solution.py:310
  577.7 164.8 %copy-start.52 = (f32[768,128]{1,0:T(8,128)}, f32[768,128]{1,0:T(8,128)S(1)}, u32[]{:S(2)}) copy-start(f32[768,128]{1,0:T(8,128)S(1)} %compare_select_fusion.9) | copy-start | bytes 1179652
  580.7 152.1 %copy-start.13 = (bf16[768,2048]{1,0:T(8,128)(2,1)S(1)}, bf16[768,2048]{1,0:T(8,128)(2,1)}, u32[]{:S(2)}) copy-start(bf16[768,2048]{1,0:T(8,128)(2,1)} %copy-done.12) | copy-start | bytes 9437188
  753.9 81.4 %copy-start.41 = (bf16[768,2048]{1,0:T(8,128)(2,1)}, bf16[768,2048]{1,0:T(8,128)(2,1)S(1)}, u32[]{:S(2)}) copy-start(bf16[768,2048]{1,0:T(8,128)(2,1)S(1)} %get-tuple-element.728) | copy-start | bytes 9437188
  754.9 80.4 %copy-start.54 = (f32[768,128]{1,0:T(8,128)}, f32[768,128]{1,0:T(8,128)S(1)}, u32[]{:S(2)}) copy-start(f32[768,128]{1,0:T(8,128)S(1)} %compare_select_fusion.7) | copy-start | bytes 1179652
  839.9 120.1 %copy-start.77 = (f32[1,2048]{1,0:T(1,128)S(1)}, f32[1,2048]{1,0:T(1,128)}, u32[]{:S(2)}) copy-start(f32[1,2048]{1,0:T(1,128)} %get-tuple-element.710) | copy-start | bytes 24580
  839.9 267.2 %all-reduce.12.cloned.1.call-start = ((), (), s32[]{:S(2)}) async-start(), calls=%async_computation.22 | async-start | bytes 6291456 | tf_op jit(solution)/shard_map/psum | solution.py:348
  1020.0 336.2 %reduce-scatter.10.cloned.1.call-start = ((), (), s32[]{:S(2)}) async-start(), calls=%async_computation.23 | async-start | bytes 7077888 | tf_op jit(solution)/shard_map/reduce_scatter | solution.py:395
  1286.3 140.3 %reduce-scatter.12.cloned.1.call-start = ((), (), s32[]{:S(2)}) async-start(), calls=%async_computation.24 | async-start | bytes 7077888 | tf_op jit(solution)/shard_map/reduce_scatter | solution.py:401
  1286.9 207.7 %reduce-scatter.26.cloned.1.call-start = ((), (), s32[]{:S(2)}) async-start(), calls=%async_computation.31 | async-start | bytes 1179648 | tf_op jit(solution)/shard_map/reduce_scatter | solution.py:473
  1295.5 61.9 %copy-start.36 = (f32[768,64]{1,0:T(8,128)S(1)}, f32[768,64]{1,0:T(8,128)}, u32[]{:S(2)}) copy-start(f32[768,64]{1,0:T(8,128)} %copy-done.35) | copy-start | bytes 589828
  1296.6 201.4 %reduce-scatter.16.cloned.1.call-start = ((), (), s32[]{:S(2)}) async-start(), calls=%async_computation.26 | async-start | bytes 2949120 | tf_op jit(solution)/shard_map/reduce_scatter | solution.py:458
  1443.9 87.3 %reduce-scatter.20.cloned.1.call-start = ((), (), s32[]{:S(2)}) async-start(), calls=%async_computation.28 | async-start | bytes 589824 | tf_op jit(solution)/shard_map/reduce_scatter | solution.py:464
  1447.3 117.6 %reduce-scatter.24.cloned.1.call-start = ((), (), s32[]{:S(2)}) async-start(), calls=%async_computation.30 | async-start | bytes 1179648 | tf_op jit(solution)/shard_map/reduce_scatter | solution.py:470
  1455.7 140.8 %reduce-scatter.18.cloned.1.call-start = ((), (), s32[]{:S(2)}) async-start(), calls=%async_computation.27 | async-start | bytes 147456 | tf_op jit(solution)/shard_map/reduce_scatter | solution.py:461
  1458.3 169.6 %reduce-scatter.22.cloned.1.call-start = ((), (), s32[]{:S(2)}) async-start(), calls=%async_computation.29 | async-start | bytes 442368 | tf_op jit(solution)/shard_map/reduce_scatter | solution.py:467
  1465.1 208.8 %all-reduce.14.cloned.1.call-start = ((), (), s32[]{:S(2)}) async-start(), calls=%async_computation.32 | async-start | bytes 917504 | tf_op jit(solution)/shard_map/psum | solution.py:478
  1498.1 222.6 %reduce-scatter.14.cloned.1.call-start = ((), (), s32[]{:S(2)}) async-start(), calls=%async_computation.25 | async-start | bytes 3932160 | tf_op jit(solution)/shard_map/reduce_scatter | solution.py:449
  (120 other events, 762.2 us)
Sparse Core Ops, SparseCore 0:
  9.6 38.5 all-gather.15
  50.0 43.4 all-gather.11
  95.1 64.6 all-gather.13
  208.0 62.4 all-gather.19
  271.9 63.3 all-gather.17
  336.7 29.2 all-gather.21
  367.6 21.2 all-gather.23
  482.3 85.5 all-reduce.7
  569.5 151.0 all-gather.25
  722.1 20.4 all-gather.27
  744.1 82.0 all-gather.29
  827.9 42.0 all-gather.31
  873.0 86.9 all-reduce.9
  1020.1 86.9 all-reduce.11
  1286.5 69.7 reduce-scatter.9
  1358.4 68.1 reduce-scatter.11
  1428.7 31.0 reduce-scatter.25
  1462.0 36.0 reduce-scatter.15
  1500.9 30.2 reduce-scatter.19
  1533.9 30.9 reduce-scatter.23
  1567.7 28.7 reduce-scatter.17
  1598.8 29.1 reduce-scatter.21
  1631.0 42.8 all-reduce.13
  1676.8 43.8 reduce-scatter.13
where the time goes:
time: 1740 us; the launch traced here: 1730 us
  waiting for transfers between devices  941 us (54%)
  matrix products  464 us (27%)
  other arithmetic  150 us (9%)
  blocking collectives  71.8 us (4%)
  local copies, waits for them, and re-layouts  69.6 us (4%)
    all_gather x1, waiting for transfers between devices, local(): lax.all_gather(gate_up_weight, 'seq', axis=1, tiled=True)  140 us
    dot_general x28, matrix products, lowrank_product(): return jnp.dot(left, right, preferred_element_type=jnp.float32)  125 us
    dot_general x28, matrix products, full_product(): jnp.dot(left.astype(jnp.float32), right.astype(jnp.float32), precision=HI...  109 us
    psum x1, waiting for transfers between devices, local(): lax.psum(feedforward_addend.astype(jnp.bfloat16), 'tp').astype(jnp.float32)  90.1 us
    psum x1, waiting for transfers between devices, local(): lax.psum((dh_gate + dh_up).astype(jnp.bfloat16), 'tp').astype(jnp.float32)  87 us
    dot_general x16, matrix products, tile_scores(): jnp.einsum('qhd,khd->hqk', query_tile, key_tile, preferred_element_type=j...  73.5 us
    all_gather x1, waiting for transfers between devices, local(): lax.all_gather(down_weight, 'seq', axis=1, tiled=True)  71.3 us
    psum x1, waiting for transfers between devices, local(): lax.psum(attention_addend.astype(jnp.bfloat16), 'tp').astype(jnp.float32)  67.2 us
  transfers between devices with their start and end apart: 24, of which 20 were waited for; matrix products, arithmetic and copies ran while one was open for 23% of the time, Pallas kernels for 0%

commit v1 on v0

v1 whole, which is shorter than its diff:
```python
import functools

import jax
import jax.numpy as jnp
from jax import lax
from jax.experimental import pallas as pl
from jax.experimental.pallas import tpu as pltpu
from jax.sharding import PartitionSpec as P

HEAD_DIM = 128
ADAPTER_RANK = 16
BLK = 128
PROMPT_BLOCKS = 8
EPS = 1e-06
THETA = 500000.0
NEG = -1e30
LOG2E = 1.4426950408889634
F32 = jnp.float32
BF16 = jnp.bfloat16


def mm(a, b):
    return jnp.dot(a, b, preferred_element_type=F32)


def mm_nt(a, b):
    return lax.dot_general(a, b, (((1,), (1,)), ((), ())), preferred_element_type=F32)


def mm_tn(a, b):
    return lax.dot_general(a, b, (((0,), (0,)), ((), ())), preferred_element_type=F32)


def bits_of(count):
    n = count.bit_length() - 1
    assert 1 << n == count
    return n


def flip(value, axis, count, bit):
    return lax.ppermute(value, axis, [(i, i ^ (1 << bit)) for i in range(count)])


def gather_order(value, axis, count, order):
    rank = lax.axis_index(axis)
    have = []
    current = value
    for bit in order:
        other = flip(current, axis, count, bit)
        mine_low = ((rank >> bit) & 1) == 0
        at = len([b for b in have if b > bit])
        low = jnp.where(mine_low, current, other)
        high = jnp.where(mine_low, other, current)
        current = jnp.stack([low, high], axis=at)
        have = sorted(have + [bit], reverse=True)
    return current.reshape((count,) + value.shape)


def gather_rows(value, axis, count):
    order = list(range(bits_of(count)))
    half = value.shape[0] // 2
    first = gather_order(value[:half], axis, count, order)
    second = gather_order(value[half:], axis, count, order[::-1])
    return jnp.concatenate([first, second], axis=1).reshape(-1, value.shape[1])


def scatter_order(value, axis, count, order):
    n = bits_of(count)
    rank = lax.axis_index(axis)
    current = value.reshape((2,) * n + value.shape[1:])
    have = list(range(n - 1, -1, -1))
    for bit in order:
        at = have.index(bit)
        mine = (rank >> bit) & 1
        keep = lax.dynamic_index_in_dim(current, mine, at, keepdims=False)
        give = lax.dynamic_index_in_dim(current, 1 - mine, at, keepdims=False)
        got = flip(give.astype(BF16), axis, count, bit)
        current = keep.astype(F32) + got.astype(F32)
        have.remove(bit)
    return current


def scatter_rows(value, axis, count):
    order = list(range(bits_of(count)))
    rows, width = value.shape
    blocks = value.reshape(count, rows // count, width)
    half = rows // count // 2
    first = scatter_order(blocks[:, :half], axis, count, order[::-1])
    second = scatter_order(blocks[:, half:], axis, count, order)
    return jnp.concatenate([first, second], axis=0)


def sum_all(value, axis, count):
    for bit in range(bits_of(count)):
        value = value + flip(value, axis, count, bit)
    return value


def fill(sources, sem):
    copies = [pltpu.make_async_copy(src, dst, sem.at[i]) for i, (src, dst) in enumerate(sources)]
    for copy in copies:
        copy.start()
    for copy in copies:
        copy.wait()


def gather_prompt(prompt_at, source, target, count):
    def step(i, carry):
        start = pl.multiple_of(prompt_at[i] * BLK, BLK)
        target[pl.ds(pl.multiple_of(i * BLK, BLK), BLK), :] = source[pl.ds(start, BLK), :]
        return carry

    lax.fori_loop(0, count, step, 0)


def masked_scores(keys, own_keys, queries, place, scale):
    prompt = mm_nt(keys, queries) * scale
    block = lax.broadcasted_iota(jnp.int32, prompt.shape, 0) // BLK
    prompt = jnp.where(block < place, prompt, NEG)
    own = mm_nt(own_keys, queries) * scale
    causal = lax.broadcasted_iota(jnp.int32, own.shape, 0) <= lax.broadcasted_iota(
        jnp.int32, own.shape, 1
    )
    own = jnp.where(causal, own, NEG)
    top = jnp.maximum(jnp.max(prompt, axis=0, keepdims=True), jnp.max(own, axis=0, keepdims=True))
    prompt = jnp.exp2(prompt - top)
    own = jnp.exp2(own - top)
    total = jnp.sum(prompt, axis=0, keepdims=True) + jnp.sum(own, axis=0, keepdims=True)
    return prompt, own, 1.0 / total


def attend_kernel(
    slots, group, rows, prompt_count, q_seq, q_place, prompt_at, *refs
):
    near = refs[:slots]
    far = refs[slots : slots * group]
    out = refs[slots * group]
    q_buf, k_buf, v_buf, kp, vp, sem = refs[slots * group + 1 :]
    plan = []
    for i, ref in enumerate(near):
        at = pl.ds(i * rows, rows)
        plan += [(ref.at[0], q_buf.at[at]), (ref.at[1], k_buf.at[at]), (ref.at[2], v_buf.at[at])]
    for i, ref in enumerate(far):
        at = pl.ds((slots + i) * rows, rows)
        plan += [(ref.at[0], k_buf.at[at]), (ref.at[1], v_buf.at[at])]
    fill(plan, sem)
    gather_prompt(prompt_at, k_buf, kp, prompt_count)
    gather_prompt(prompt_at, v_buf, vp, prompt_count)
    scale = HEAD_DIM ** (-0.5) * LOG2E
    span = PROMPT_BLOCKS * BLK

    def step(i, carry):
        at = pl.ds(pl.multiple_of(i * BLK, BLK), BLK)
        of_seq = pl.ds(pl.multiple_of(q_seq[i] * span, span), span)
        prompt, own, inverse = masked_scores(
            kp[of_seq, :], k_buf[at, :], q_buf[at, :], q_place[i], scale
        )
        result = mm_tn(vp[of_seq, :], prompt.astype(BF16)) + mm_tn(v_buf[at, :], own.astype(BF16))
        out[at, :] = (result * inverse).T.astype(BF16)
        return carry

    lax.fori_loop(0, slots * rows // BLK, step, 0)


def attend_back_kernel(
    slots, group, rows, prompt_count, q_seq, q_place, prompt_at, *refs
):
    near = refs[:slots]
    far = refs[slots : slots * group]
    grads = refs[slots * group : slots * group + slots]
    dq_out, dk_out, dv_out = refs[slots * group + slots : slots * group + slots + 3]
    q_buf, k_buf, v_buf, do_buf, kp, vp, dkp, dvp, sem = refs[slots * group + slots + 3 :]
    plan = []
    for i, ref in enumerate(near):
        at = pl.ds(i * rows, rows)
        plan += [(ref.at[0], q_buf.at[at]), (ref.at[1], k_buf.at[at]), (ref.at[2], v_buf.at[at])]
    for i, ref in enumerate(far):
        at = pl.ds((slots + i) * rows, rows)
        plan += [(ref.at[0], k_buf.at[at]), (ref.at[1], v_buf.at[at])]
    for i, ref in enumerate(grads):
        plan += [(ref, do_buf.at[pl.ds(i * rows, rows)])]
    fill(plan, sem)
    gather_prompt(prompt_at, k_buf, kp, prompt_count)
    gather_prompt(prompt_at, v_buf, vp, prompt_count)
    dkp[...] = jnp.zeros_like(dkp)
    dvp[...] = jnp.zeros_like(dvp)
    scale = HEAD_DIM ** (-0.5)
    span = PROMPT_BLOCKS * BLK
    own_rows = slots * rows
    zeros = jnp.zeros((BLK, HEAD_DIM), BF16)

    def clear(i, carry):
        at = pl.ds(pl.multiple_of(own_rows + i * BLK, BLK), BLK)
        dk_out[at, :] = zeros
        dv_out[at, :] = zeros
        return carry

    lax.fori_loop(0, (group - 1) * own_rows // BLK, clear, 0)

    def step(i, carry):
        at = pl.ds(pl.multiple_of(i * BLK, BLK), BLK)
        seq, place = q_seq[i], q_place[i]
        of_seq = pl.ds(pl.multiple_of(seq * span, span), span)
        queries, grad = q_buf[at, :], do_buf[at, :]
        prompt, own, inverse = masked_scores(
            kp[of_seq, :], k_buf[at, :], queries, place, scale * LOG2E
        )
        prompt, own = prompt * inverse, own * inverse
        d_prompt = mm_nt(vp[of_seq, :], grad)
        d_own = mm_nt(v_buf[at, :], grad)
        delta = jnp.sum(prompt * d_prompt, axis=0, keepdims=True) + jnp.sum(
            own * d_own, axis=0, keepdims=True
        )
        ds_prompt = (prompt * (d_prompt - delta)).astype(BF16)
        ds_own = (own * (d_own - delta)).astype(BF16)
        dq = mm_tn(ds_prompt, kp[of_seq, :]) + mm_tn(ds_own, k_buf[at, :])
        dq_out[at, :] = (dq * scale).astype(BF16)
        dvp[of_seq, :] += mm(prompt.astype(BF16), grad)
        dkp[of_seq, :] += mm(ds_prompt, queries) * scale
        dk_out[at, :] = (mm(ds_own, queries) * scale).astype(BF16)
        dv_out[at, :] = mm(own.astype(BF16), grad).astype(BF16)
        return carry

    lax.fori_loop(0, own_rows // BLK, step, 0)

    def spread(i, carry):
        to = pl.ds(pl.multiple_of(prompt_at[i] * BLK, BLK), BLK)
        at = pl.ds(pl.multiple_of(i * BLK, BLK), BLK)
        dk_out[to, :] = (dk_out[to, :].astype(F32) + dkp[at, :]).astype(BF16)
        dv_out[to, :] = (dv_out[to, :].astype(F32) + dvp[at, :]).astype(BF16)
        return carry

    lax.fori_loop(0, prompt_count, spread, 0)


ANY = pl.BlockSpec(memory_space=pl.ANY)
WHOLE = pl.BlockSpec(memory_space=pltpu.VMEM)


def attend(tables, near, far, rows, prompt_count):
    slots = len(near)
    group = 1 + len(far) // slots
    own, every = slots * rows, slots * group * rows
    pairs = own * (PROMPT_BLOCKS + 1) * BLK
    return pl.pallas_call(
        functools.partial(attend_kernel, slots, group, rows, prompt_count),
        out_shape=jax.ShapeDtypeStruct((own, HEAD_DIM), BF16),
        grid_spec=pltpu.PrefetchScalarGridSpec(
            num_scalar_prefetch=3,
            in_specs=[ANY] * (slots * group),
            out_specs=WHOLE,
            scratch_shapes=[
                pltpu.VMEM((own, HEAD_DIM), BF16),
                pltpu.VMEM((every, HEAD_DIM), BF16),
                pltpu.VMEM((every, HEAD_DIM), BF16),
                pltpu.VMEM((prompt_count * BLK, HEAD_DIM), BF16),
                pltpu.VMEM((prompt_count * BLK, HEAD_DIM), BF16),
                pltpu.SemaphoreType.DMA((3 * slots + 2 * slots * (group - 1),)),
            ],
        ),
        cost_estimate=pl.CostEstimate(
            flops=4 * pairs * HEAD_DIM, bytes_accessed=6 * every * HEAD_DIM, transcendentals=pairs
        ),
        name="attend",
    )(*tables, *near, *far)


def attend_back(tables, near, far, grads, rows, prompt_count):
    slots = len(near)
    group = 1 + len(far) // slots
    own, every = slots * rows, slots * group * rows
    pairs = own * (PROMPT_BLOCKS + 1) * BLK
    return pl.pallas_call(
        functools.partial(attend_back_kernel, slots, group, rows, prompt_count),
        out_shape=[
            jax.ShapeDtypeStruct((own, HEAD_DIM), BF16),
            jax.ShapeDtypeStruct((every, HEAD_DIM), BF16),
            jax.ShapeDtypeStruct((every, HEAD_DIM), BF16),
        ],
        grid_spec=pltpu.PrefetchScalarGridSpec(
            num_scalar_prefetch=3,
            in_specs=[ANY] * (slots * group + slots),
            out_specs=[WHOLE] * 3,
            scratch_shapes=[
                pltpu.VMEM((own, HEAD_DIM), BF16),
                pltpu.VMEM((every, HEAD_DIM), BF16),
                pltpu.VMEM((every, HEAD_DIM), BF16),
                pltpu.VMEM((own, HEAD_DIM), BF16),
                pltpu.VMEM((prompt_count * BLK, HEAD_DIM), BF16),
                pltpu.VMEM((prompt_count * BLK, HEAD_DIM), BF16),
                pltpu.VMEM((prompt_count * BLK, HEAD_DIM), F32),
                pltpu.VMEM((prompt_count * BLK, HEAD_DIM), F32),
                pltpu.SemaphoreType.DMA((4 * slots + 2 * slots * (group - 1),)),
            ],
        ),
        cost_estimate=pl.CostEstimate(
            flops=10 * pairs * HEAD_DIM, bytes_accessed=12 * every * HEAD_DIM, transcendentals=pairs
        ),
        name="attend_back",
    )(*tables, *near, *far, *grads)


def rotate(values, cosine, sine):
    half = HEAD_DIM // 2
    first, second = values[..., :half], values[..., half:]
    return jnp.concatenate(
        [first * cosine - second * sine, second * cosine + first * sine], axis=-1
    )


def local(
    layer_input,
    cotangent,
    query_key_value_weight,
    output_weight,
    gate_up_weight,
    down_weight,
    input_first_factor,
    output_first_factor,
    down_first_factor,
    query_key_value_second,
    gate_up_second_factor,
    output_down_second_factor,
    norm_gain_table,
    sequence_adapter,
    block_sequence,
    block_position,
):
    tp, tp_rank = lax.axis_size("tp"), lax.axis_index("tp")
    seqs, seq_rank = lax.axis_size("seq"), lax.axis_index("seq")
    own_rows, width = layer_input.shape
    rows = own_rows * tp
    my_blocks = rows // BLK
    cols = query_key_value_weight.shape[2]
    heads = cols // HEAD_DIM
    hidden_cols = gate_up_weight.shape[2]
    k_rows = query_key_value_weight.shape[1]
    slots_a = input_first_factor.shape[2]
    rank_cols = output_first_factor.shape[1]
    group = seqs // heads
    head_rank, group_rank = seq_rank // group, seq_rank % group
    n_seq = sequence_adapter.shape[0]

    gather = lambda value: lax.all_gather(value, "seq", axis=0, tiled=True)
    w_qkv = gather(query_key_value_weight.transpose(1, 0, 2).reshape(k_rows, 3 * cols))
    a_part = k_rows // tp
    b_part = width // tp
    a_mine = lax.dynamic_slice_in_dim(input_first_factor, tp_rank * a_part, a_part, 1)
    b_mine = lax.dynamic_slice_in_dim(output_down_second_factor, tp_rank * b_part, b_part, 2)
    pieces = [
        a_mine,
        b_mine,
        query_key_value_second,
        output_first_factor,
        down_first_factor,
        gate_up_second_factor,
    ]
    packed = jnp.concatenate([piece.reshape(-1, 128) for piece in pieces], axis=0)
    packed = lax.all_gather(packed, "seq", axis=0)
    split, at = [], 0
    for piece in pieces:
        size = piece.size // 128
        split.append(packed[:, at : at + size])
        at += size
    w_o = gather(output_weight.T)
    w_gu = gather(gate_up_weight.transpose(1, 0, 2).reshape(k_rows, 2 * hidden_cols))
    w_down = gather(down_weight.T)

    shared = jnp.concatenate(split[:2], axis=1)
    shared = gather_order(shared, "tp", tp, list(range(bits_of(tp))))
    a_size = a_mine.size // 128
    a_in = (
        shared[:, :, :a_size]
        .reshape(tp, seqs, 5, a_part, slots_a)
        .transpose(2, 1, 0, 3, 4)
        .reshape(5, width, slots_a)
    )
    b_od = (
        shared[:, :, a_size:]
        .reshape(tp, seqs, 2, rank_cols, b_part)
        .transpose(2, 1, 3, 0, 4)
        .reshape(2, slots_a, width)
    )
    b_qkv = split[2].reshape(seqs, 3, rank_cols, cols).transpose(1, 0, 2, 3).reshape(3, slots_a, cols)
    a_o = split[3].reshape(seqs, cols, rank_cols).transpose(1, 0, 2).reshape(cols, slots_a)
    a_down = (
        split[4].reshape(seqs, hidden_cols, rank_cols).transpose(1, 0, 2).reshape(hidden_cols, slots_a)
    )
    b_gu = (
        split[5]
        .reshape(seqs, 2, rank_cols, hidden_cols)
        .transpose(1, 0, 2, 3)
        .reshape(2, slots_a, hidden_cols)
    )

    block_ids = seq_rank * my_blocks + jnp.arange(my_blocks, dtype=jnp.int32)
    block_of_row = jnp.arange(rows, dtype=jnp.int32) // BLK
    offset = jnp.arange(rows, dtype=jnp.int32) % BLK
    seq_blocks = block_sequence[block_ids]
    place_blocks = block_position[block_ids]
    adapter_blocks = sequence_adapter[seq_blocks]
    pick = lambda per_block: jnp.repeat(per_block, BLK)
    adapter_rows = pick(adapter_blocks)
    place_rows = pick(place_blocks)
    select = (
        jnp.arange(slots_a, dtype=jnp.int32)[None, :] // ADAPTER_RANK == adapter_rows[:, None]
    ).astype(F32) * 2.0
    position = (
        jnp.where(place_rows < PROMPT_BLOCKS, place_rows * BLK, PROMPT_BLOCKS * BLK) + offset
    )
    frequency = THETA ** (-(jnp.arange(HEAD_DIM // 2, dtype=F32) * 2.0) / HEAD_DIM)
    angles = position.astype(F32)[:, None] * frequency[None, :]
    cosine = jnp.cos(angles)[:, None, :]
    sine = jnp.sin(angles)[:, None, :]

    owner = (
        ((head_rank - jnp.arange(heads)) % heads)[None, :] * group
        + ((group_rank + jnp.arange(group)) % group)[:, None]
    ).reshape(-1)
    held = (owner[:, None] * my_blocks + jnp.arange(my_blocks)[None, :]).reshape(-1)
    held_seq = block_sequence[held].astype(jnp.int32)
    held_place = block_position[held].astype(jnp.int32)
    prompt_count = n_seq * PROMPT_BLOCKS
    wanted = jnp.arange(prompt_count, dtype=jnp.int32)
    code = jnp.where(held_place < PROMPT_BLOCKS, held_seq * PROMPT_BLOCKS + held_place, -1)
    prompt_at = jnp.sum(
        jnp.where(
            code[None, :] == wanted[:, None], jnp.arange(held.shape[0], dtype=jnp.int32)[None, :], 0
        ),
        axis=1,
    ).astype(jnp.int32)
    own_blocks = heads * my_blocks
    tables = (held_seq[:own_blocks], held_place[:own_blocks], prompt_at)

    def head_shift(value, by):
        return lax.ppermute(
            value,
            "seq",
            [
                (h * group + j, ((h + by) % heads) * group + j)
                for h in range(heads)
                for j in range(group)
            ],
        )

    def group_shift(value, by):
        return lax.ppermute(
            value,
            "seq",
            [
                (h * group + j, h * group + (j + by) % group)
                for h in range(heads)
                for j in range(group)
            ],
        )

    def to_heads(value):
        out = []
        for k in range(heads):
            piece = lax.dynamic_index_in_dim(value, (head_rank + k) % heads, 0, keepdims=False)
            out.append(piece if k == 0 else head_shift(piece, k))
        return out

    def from_heads(parts):
        back = [part if k == 0 else head_shift(part, -k) for k, part in enumerate(parts)]
        twice = jnp.stack(back + back)
        return lax.dynamic_slice_in_dim(twice, (-head_rank) % heads, heads, 0)

    x = gather_rows(layer_input, "tp", tp)
    latents = []
    projected = mm(x, w_qkv)
    for i in range(3):
        latents.append((mm(x, a_in[i]) * select).astype(BF16))
    z_q, z_k, z_v = [
        projected[:, i * cols : (i + 1) * cols] + mm(latents[i], b_qkv[i]) for i in range(3)
    ]
    gain_q = lax.dynamic_slice_in_dim(norm_gain_table[0], tp_rank * cols, cols)
    gain_k = lax.dynamic_slice_in_dim(norm_gain_table[1], tp_rank * cols, cols)
    squares = jnp.stack([jnp.sum(z_q * z_q, axis=1), jnp.sum(z_k * z_k, axis=1)])
    squares = sum_all(squares, "tp", tp)
    inv_q, inv_k = lax.rsqrt(squares / width + EPS)[:, :, None]
    shape3 = (rows, heads, HEAD_DIM)
    queries = rotate((z_q * inv_q * gain_q).reshape(shape3), cosine, sine).astype(BF16)
    keys = rotate((z_k * inv_k * gain_k).reshape(shape3), cosine, sine).astype(BF16)
    values = z_v.astype(BF16).reshape(shape3)
    qkv = jnp.stack([queries, keys, values]).transpose(2, 0, 1, 3)
    near = to_heads(qkv)
    far = []
    for j in range(1, group):
        far += [group_shift(part[1:], -j) for part in near]
    attended = attend(tables, near, far, rows, prompt_count)
    heads_out = (
        from_heads([attended[k * rows : (k + 1) * rows] for k in range(heads)])
        .transpose(1, 0, 2)
        .reshape(rows, cols)
    )

    o_latent = (mm(heads_out, a_o) * select).astype(BF16)
    partial = mm_nt(heads_out, w_o) + mm(o_latent, b_od[0])
    attn_out = scatter_rows(partial.astype(BF16), "tp", tp)
    x_own = layer_input.astype(F32)
    d_y = cotangent.astype(F32)
    scale_o = lax.rsqrt(jnp.mean(attn_out * attn_out, axis=1, keepdims=True) + EPS)
    hidden = x_own + attn_out * scale_o * norm_gain_table[2]
    h_low = gather_rows(hidden.astype(BF16), "tp", tp)

    g_latent = (mm(h_low, a_in[3]) * select).astype(BF16)
    u_latent = (mm(h_low, a_in[4]) * select).astype(BF16)
    gate = mm(h_low, w_gu[:, :hidden_cols]) + mm(g_latent, b_gu[0])
    up = mm(h_low, w_gu[:, hidden_cols:]) + mm(u_latent, b_gu[1])
    sigmoid = jax.nn.sigmoid(gate)
    silu = gate * sigmoid
    act = (silu * up).astype(BF16)
    d_latent = (mm(act, a_down) * select).astype(BF16)
    partial = mm_nt(act, w_down) + mm(d_latent, b_od[1])
    ff_out = scatter_rows(partial.astype(BF16), "tp", tp)
    scale_f = lax.rsqrt(jnp.mean(ff_out * ff_out, axis=1, keepdims=True) + EPS)
    output = hidden + ff_out * scale_f * norm_gain_table[3]

    def norm_back(values_in, inv, scaled):
        return inv * scaled - values_in * inv**3 * jnp.mean(scaled * values_in, axis=1, keepdims=True)

    d_ff = norm_back(ff_out, scale_f, d_y * norm_gain_table[3]).astype(BF16)
    d_ff = gather_rows(d_ff, "tp", tp)
    u_down = (mm_nt(d_ff, b_od[1]) * select).astype(BF16)
    d_act = mm(d_ff, w_down) + mm_nt(u_down, a_down)
    grad_a_down = mm_tn(act, u_down)
    grad_b_down = mm_tn(d_latent, d_ff)
    d_silu = sigmoid * (1.0 + gate * (1.0 - sigmoid))
    d_gate = (d_act * up * d_silu).astype(BF16)
    d_up = (d_act * silu).astype(BF16)
    u_gate = (mm_nt(d_gate, b_gu[0]) * select).astype(BF16)
    u_up = (mm_nt(d_up, b_gu[1]) * select).astype(BF16)
    partial = (
        mm_nt(d_gate, w_gu[:, :hidden_cols])
        + mm_nt(d_up, w_gu[:, hidden_cols:])
        + mm_nt(u_gate, a_in[3])
        + mm_nt(u_up, a_in[4])
    )
    d_hidden = d_y + scatter_rows(partial.astype(BF16), "tp", tp)
    grad_a_gate = mm_tn(h_low, u_gate)
    grad_a_up = mm_tn(h_low, u_up)
    grad_b_gate = mm_tn(g_latent, d_gate)
    grad_b_up = mm_tn(u_latent, d_up)

    d_attn = norm_back(attn_out, scale_o, d_hidden * norm_gain_table[2]).astype(BF16)
    d_attn = gather_rows(d_attn, "tp", tp)
    u_o = (mm_nt(d_attn, b_od[0]) * select).astype(BF16)
    d_heads = (mm(d_attn, w_o) + mm_nt(u_o, a_o)).astype(BF16)
    grad_a_o = mm_tn(heads_out, u_o)
    grad_b_o = mm_tn(o_latent, d_attn)
    grads = to_heads(d_heads.reshape(shape3).transpose(1, 0, 2))
    dq, dk, dv = attend_back(tables, near, far, grads, rows, prompt_count)
    kv_rows = heads * rows
    d_kv = jnp.stack([dk, dv]).reshape(2, group, kv_rows, HEAD_DIM)
    total = d_kv[:, 0].astype(F32)
    for j in range(1, group):
        total = total + group_shift(d_kv[:, j], j).astype(F32)
    d_qkv = jnp.concatenate([dq[None], total.astype(BF16)], axis=0)
    d_qkv = from_heads([d_qkv[:, k * rows : (k + 1) * rows] for k in range(heads)])
    d_qkv = d_qkv.transpose(1, 2, 0, 3)
    d_query, d_key = d_qkv[0].astype(F32), d_qkv[1].astype(F32)
    dz_v = d_qkv[2].reshape(rows, cols)
    scaled_q = rotate(d_query, cosine, -sine).reshape(rows, cols) * gain_q
    scaled_k = rotate(d_key, cosine, -sine).reshape(rows, cols) * gain_k
    parts = jnp.stack([jnp.sum(scaled_q * z_q, axis=1), jnp.sum(scaled_k * z_k, axis=1)])
    parts = sum_all(parts, "tp", tp) / width
    dz_q = (inv_q * scaled_q - z_q * inv_q**3 * parts[0][:, None]).astype(BF16)
    dz_k = (inv_k * scaled_k - z_k * inv_k**3 * parts[1][:, None]).astype(BF16)
    dz = [dz_q, dz_k, dz_v]
    us = [(mm_nt(dz[i], b_qkv[i]) * select).astype(BF16) for i in range(3)]
    partial = sum(mm_nt(dz[i], w_qkv[:, i * cols : (i + 1) * cols]) + mm_nt(us[i], a_in[i]) for i in range(3))
    input_grad = d_hidden + scatter_rows(partial.astype(BF16), "tp", tp)

    grad_a_in = jnp.stack([mm_tn(x, u) for u in us] + [grad_a_gate, grad_a_up])
    grad_b_qkv = jnp.stack([mm_tn(latents[i], dz[i]) for i in range(3)])
    grad_b_gu = jnp.stack([grad_b_gate, grad_b_up])
    grad_b_out = jnp.stack([grad_b_o, grad_b_down])

    def reduce_seq(value, dim):
        return lax.psum_scatter(
            value.astype(BF16), "seq", scatter_dimension=dim, tiled=True
        ).astype(F32)

    grad_a_in = reduce_seq(grad_a_in, 1)
    grad_a_o = reduce_seq(grad_a_o, 1)
    grad_a_down = reduce_seq(grad_a_down, 1)
    grad_b_qkv = reduce_seq(grad_b_qkv, 1)
    grad_b_gu = reduce_seq(grad_b_gu, 1)
    grad_b_out = reduce_seq(grad_b_out, 1)
    grad_a_in, grad_b_out = (
        lax.psum(grad_a_in.astype(BF16), "tp").astype(F32),
        lax.psum(grad_b_out.astype(BF16), "tp").astype(F32),
    )
    return (output, input_grad, grad_a_in, grad_a_o, grad_a_down, grad_b_qkv, grad_b_gu, grad_b_out)


def solution(mesh):
    return jax.shard_map(
        local,
        mesh=mesh,
        in_specs=(
            P(("seq", "tp"), None),
            P(("seq", "tp"), None),
            P(None, "seq", "tp"),
            P("tp", "seq"),
            P(None, "seq", "tp"),
            P("tp", "seq"),
            P(None, "seq", None),
            P("tp", "seq"),
            P("tp", "seq"),
            P(None, "seq", "tp"),
            P(None, "seq", "tp"),
            P(None, "seq", None),
            P(),
            P(),
            P(),
            P(),
        ),
        out_specs=(
            P(("seq", "tp"), None),
            P(("seq", "tp"), None),
            P(None, "seq", None),
            P("tp", "seq"),
            P("tp", "seq"),
            P(None, "seq", "tp"),
            P(None, "seq", "tp"),
            P(None, "seq", None),
        ),
        check_vma=False,
    )
```

time: 1740 us -> 985 us (0.57)
  waiting for transfers between devices: 941 us -> 458 us
  matrix products: 464 us -> 158 us
  starting transfers between devices: 1.31 us -> 115 us
  other arithmetic: 150 us -> 68 us
  blocking collectives: 71.8 us -> 0 us
  Pallas kernels: 0 us -> 54.3 us
  local copies, waits for them, and re-layouts: 69.6 us -> 106 us
    all_gather x11 -> x5, waiting for transfers between devices: 394 us -> 24.9 us  [the longest x1 24.8 us: local(): packed = lax.all_gather(packed, 'seq', axis=0)]
    ppermute x0 -> x55, waiting for transfers between devices: none -> 344 us  [the longest x38 188 us: flip(): return lax.ppermute(value, axis, [(i, i ^ 1 << bit) for i in range(count)])]
    dot_general x112 -> x54, matrix products: 464 us -> 158 us  [the longest x21 79.7 us: mm_nt(): lax.dot_general(a, b, (((1,), (1,)), ((), ())), preferred_element_type=F32)]
    psum x4 -> x1, waiting for transfers between devices: 289 us -> 44.1 us  [local(): lax.psum(grad_a_in.astype(BF16), 'tp').astype(F32)]
    reduce_scatter x9 -> x6, waiting for transfers between devices: 252 us -> 44.1 us  [reduce_seq(): lax.psum_scatter(value.astype(BF16), 'seq', scatter_dimension=dim, tiled=...]
    ppermute x0 -> x55, starting transfers between devices: none -> 115 us  [the longest x12 62.7 us: head_shift(): lax.ppermute(value, 'seq', [(h * group + j, (h + by) % heads * group + j)...]
    reduce_sum x14 -> x6, other arithmetic: 62.1 us -> 3.53 us  [the longest x1 1.73 us: local(): jnp.sum(scaled_k * z_k, axis=1)]
    pallas_call x0 -> x2, Pallas kernels: none -> 54.3 us  [the longest x1 32.7 us: attend_back(): pl.pallas_call(functools.partial(attend_back_kernel, slots, group, rows,...]
  transfers between devices with their start and end apart: 24 -> 67, of which waited for: 20 -> 41; matrix products, arithmetic and copies ran while one was open for 23% -> 24% of each run, Pallas kernels for 0% -> 2%
where the time goes in v1:
time: 985 us; the launch traced here: 976 us
  waiting for transfers between devices  458 us (46%)
  matrix products  158 us (16%)
  starting transfers between devices  115 us (12%)
  local copies, waits for them, and re-layouts  106 us (11%)
  other arithmetic  68 us (7%)
  Pallas kernels  54.3 us (6%)
  between operations  17.3 us (2%)
    ppermute x38, waiting for transfers between devices, flip(): return lax.ppermute(value, axis, [(i, i ^ 1 << bit) for i in range(count)])  188 us
    ppermute x12, waiting for transfers between devices, head_shift(): lax.ppermute(value, 'seq', [(h * group + j, (h + by) % heads * group + j)...  156 us
    dot_general x21, matrix products, mm_nt(): lax.dot_general(a, b, (((1,), (1,)), ((), ())), preferred_element_type=F32)  79.7 us
    ppermute x12, starting transfers between devices, head_shift(): lax.ppermute(value, 'seq', [(h * group + j, (h + by) % heads * group + j)...  62.7 us
    dot_general x19, matrix products, mm(): return jnp.dot(a, b, preferred_element_type=F32)  56.7 us
    ppermute x38, starting transfers between devices, flip(): return lax.ppermute(value, axis, [(i, i ^ 1 << bit) for i in range(count)])  51.3 us
    reduce_scatter x6, waiting for transfers between devices, reduce_seq(): lax.psum_scatter(value.astype(BF16), 'seq', scatter_dimension=dim, tiled=...  44.1 us
    psum x1, waiting for transfers between devices, local(): lax.psum(grad_a_in.astype(BF16), 'tp').astype(F32)  44.1 us
  transfers between devices with their start and end apart: 67, of which 41 were waited for; matrix products, arithmetic and copies ran while one was open for 24% of the time, Pallas kernels for 2%

profile of v1, /device:TPU:0, one launch (start us, length us, event | category | flops | bytes accessed | tf_op | source)
XLA Modules:
  0.0 976.4 jit_solution(17793938157635983736)
XLA Ops:
  30.5 24.8 %all-gather.15.cloned.1.call-done = bf16[11776,128]{1,0:T(8,128)(2,1)} async-done(((bf16[1472,128]{1,0:T(8,128)(2,1)}), bf16[11776,128]{1,0:T(8,128)(2,1)}) %all-gather.15.cloned.1.call-update) | async-done | bytes 3014672 | tf_op jit(solution)/shard_map/all_gather | solution.py:359
  60.6 19.3 %collective-permute-done.4 = bf16[8,448,128]{2,1,0:T(8,128)(2,1)S(1)} collective-permute-done((bf16[8,448,128]{2,1,0:T(8,128)(2,1)S(1)}, bf16[8,448,128]{2,1,0:T(8,128)(2,1)S(1)}, u32[]{:S(2)}, u32[]{:S(2)}) %collective-permute-start.4) | collective-permute-done | bytes 917536 | tf_op jit(solution)/shard_map/ppermute | solution.py:41
  84.3 11.7 %collective-permute-done.3 = bf16[2,96,2048]{2,1,0:T(8,128)(2,1)S(1)} collective-permute-done((bf16[2,96,2048]{2,1,0:T(8,128)(2,1)S(1)}, bf16[2,96,2048]{2,1,0:T(8,128)(2,1)S(1)}, u32[]{:S(2)}, u32[]{:S(2)}) %collective-permute-start.3) | collective-permute-done | bytes 786464 | tf_op jit(solution)/shard_map/ppermute | solution.py:41
  100.3 23.2 %collective-permute-done.5 = bf16[2,8,448,128]{3,2,1,0:T(8,128)(2,1)} collective-permute-done((bf16[2,8,448,128]{3,2,1,0:T(8,128)(2,1)}, bf16[2,8,448,128]{3,2,1,0:T(8,128)(2,1)}, u32[]{:S(2)}, u32[]{:S(2)}) %collective-permute-start.5) | collective-permute-done | bytes 1835040 | tf_op jit(solution)/shard_map/ppermute | solution.py:41
  134.8 7.8 fusion.107
  170.1 23.3 %collective-permute-done.8.refs_1_ = bf16[3,768,128]{2,1,0:T(8,128)(2,1)} collective-permute-done((bf16[3,768,128]{2,1,0:T(8,128)(2,1)}, bf16[3,768,128]{2,1,0:T(8,128)(2,1)}, u32[]{:S(2)}, u32[]{:S(2)}) %collective-permute-start.8) | collective-permute-done | bytes 589856 | tf_op jit(solution)/shard_map/ppermute | solution.py:436
  195.2 42.0 %collective-permute-done.9.refs_2_ = bf16[3,768,128]{2,1,0:T(8,128)(2,1)} collective-permute-done((bf16[3,768,128]{2,1,0:T(8,128)(2,1)}, bf16[3,768,128]{2,1,0:T(8,128)(2,1)}, u32[]{:S(2)}, u32[]{:S(2)}) %collective-permute-start.9) | collective-permute-done | bytes 589856 | tf_op jit(solution)/shard_map/ppermute | solution.py:436
  246.4 21.6 %attend.1 = bf16[3072,128]{1,0:T(8,128)(2,1)} custom-call(s32[24]{0:T(128)} %bitcast.595, s32[24]{0:T(128)} %bitcast.597, s32[24]{0:T(128)} %select_reduce_fusion.prompt_at, bf16[3,768,128]{2,1,0:T(8,128)(2,1)} %bitcast.557, bf16[3,768,128]{2,1,0:T(8,128)(2,1)} %collective-permute-done.8.refs_1_, bf16[3,768,128]{2,1,0:T(8,128)(2,1)} %collective-permute-done.9.refs_2_, ...), custom_call_target="tpu_custom_call" | custom-call | flops 1811939328 | bytes 4718592 | tf_op jit(solution)/shard_map/attend/pallas_call | solution.py:245
  269.2 48.2 %collective-permute-start.15 = (bf16[768,128]{1,0:T(8,128)(2,1)S(1)}, bf16[768,128]{1,0:T(8,128)(2,1)S(1)}, u32[]{:S(2)}, u32[]{:S(2)}) collective-permute-start(bf16[768,128]{1,0:T(8,128)(2,1)S(1)} %get-tuple-element.115), channel_id=1, source_target_pairs={{0,24},{4,28},{8,0},{12,4},{16,8},{20,12},{24,16},{28,20},{1,25},{... | collective-permute-start | bytes 589832 | tf_op jit(solution)/shard_map/ppermute | solution.py:436
  319.2 7.8 collective-permute-done.15
  326.9 25.6 %collective-permute-done.16 = bf16[768,128]{1,0:T(8,128)(2,1)S(1)} collective-permute-done((bf16[768,128]{1,0:T(8,128)(2,1)S(1)}, bf16[768,128]{1,0:T(8,128)(2,1)S(1)}, u32[]{:S(2)}, u32[]{:S(2)}) %collective-permute-start.16) | collective-permute-done | bytes 196640 | tf_op jit(solution)/shard_map/ppermute | solution.py:436
  363.8 16.5 %collective-permute-done.18 = bf16[2,96,2048]{2,1,0:T(8,128)(2,1)} collective-permute-done((bf16[2,96,2048]{2,1,0:T(8,128)(2,1)}, bf16[2,96,2048]{2,1,0:T(8,128)(2,1)}, u32[]{:S(2)}, u32[]{:S(2)}) %collective-permute-start.18) | collective-permute-done | bytes 786464 | tf_op jit(solution)/shard_map/ppermute | solution.py:41
  398.1 7.7 collective-permute-done.22
  438.5 9.2 fusion.6
  448.8 11.4 %fusion.2 = f32[768,2048]{1,0:T(8,128)S(1)} fusion(bf16[768,2048]{1,0:T(8,128)(2,1)S(1)} %bitcast.533, bf16[2048,4096]{0,1:T(8,128)(2,1)} %all-gather.11.cloned.1.call-done), kind=kOutput, calls=%fused_computation.7 | convolution fusion | flops 6442450944 | bytes 17825792 | tf_op jit(solution)/shard_map/dot_general | solution.py:23
  466.1 9.1 fusion.109
  478.2 15.0 %collective-permute-done.26 = bf16[2,96,2048]{2,1,0:T(8,128)(2,1)S(1)} collective-permute-done((bf16[2,96,2048]{2,1,0:T(8,128)(2,1)S(1)}, bf16[2,96,2048]{2,1,0:T(8,128)(2,1)S(1)}, u32[]{:S(2)}, u32[]{:S(2)}) %collective-permute-start.26) | collective-permute-done | bytes 786464 | tf_op jit(solution)/shard_map/ppermute | solution.py:41
  507.1 7.7 collective-permute-done.30
  519.9 9.5 collective-permute-done.33
  534.6 8.8 fusion.110
  553.9 9.2 fusion
  563.2 9.3 fusion.4
  577.9 12.3 %collective-permute-done.34 = bf16[2,96,2048]{2,1,0:T(8,128)(2,1)S(1)} collective-permute-done((bf16[2,96,2048]{2,1,0:T(8,128)(2,1)S(1)}, bf16[2,96,2048]{2,1,0:T(8,128)(2,1)S(1)}, u32[]{:S(2)}, u32[]{:S(2)}) %collective-permute-start.34) | collective-permute-done | bytes 786464 | tf_op jit(solution)/shard_map/ppermute | solution.py:41
  609.2 10.0 %collective-permute-done.38 = bf16[96,2048]{1,0:T(8,128)(2,1)S(1)} collective-permute-done((bf16[96,2048]{1,0:T(8,128)(2,1)S(1)}, bf16[96,2048]{1,0:T(8,128)(2,1)S(1)}, u32[]{:S(2)}, u32[]{:S(2)}) %collective-permute-start.38) | collective-permute-done | bytes 393248 | tf_op jit(solution)/shard_map/ppermute | solution.py:41
  622.7 10.8 %collective-permute-done.41 = bf16[2,96,2048]{2,1,0:T(8,128)(2,1)S(1)} collective-permute-done((bf16[2,96,2048]{2,1,0:T(8,128)(2,1)S(1)}, bf16[2,96,2048]{2,1,0:T(8,128)(2,1)S(1)}, u32[]{:S(2)}, u32[]{:S(2)}) %collective-permute-start.41) | collective-permute-done | bytes 786464 | tf_op jit(solution)/shard_map/ppermute | solution.py:41
  651.6 32.7 %attend_back.1 = (bf16[3072,128]{1,0:T(8,128)(2,1)}, bf16[6144,128]{1,0:T(8,128)(2,1)}, bf16[6144,128]{1,0:T(8,128)(2,1)}) custom-call(s32[24]{0:T(128)} %bitcast.596, s32[24]{0:T(128)} %bitcast.598, s32[24]{0:T(128)} %select_reduce_fusion.prompt_at, bf16[3,768,128]{2,1,0:T(8,128)(2,1)} %bitcast.558, bf16[3,768,128]{2,1,0:T(8,128)(2,1)} %collective-permute-done.8.refs_1_, ...), custom_call_target="tpu_custom_call" | custom-call | flops 4529848320 | bytes 9437184 | tf_op jit(solution)/shard_map/attend_back/pallas_call | solution.py:273
  707.3 13.0 %collective-permute-done.46 = bf16[3,768,128]{1,2,0:T(8,128)(2,1)S(1)} collective-permute-done((bf16[3,768,128]{1,2,0:T(8,128)(2,1)}, bf16[3,768,128]{1,2,0:T(8,128)(2,1)S(1)}, u32[]{:S(2)}, u32[]{:S(2)}) %collective-permute-start.46) | collective-permute-done | bytes 589856 | tf_op jit(solution)/shard_map/ppermute | solution.py:436
  720.4 38.6 %collective-permute-done.47 = bf16[3,768,128]{1,2,0:T(8,128)(2,1)} collective-permute-done((bf16[3,768,128]{1,2,0:T(8,128)(2,1)}, bf16[3,768,128]{1,2,0:T(8,128)(2,1)}, u32[]{:S(2)}, u32[]{:S(2)}) %collective-permute-start.47) | collective-permute-done | bytes 589856 | tf_op jit(solution)/shard_map/ppermute | solution.py:436
  829.9 9.2 add_convert_fusion
  849.7 9.3 collective-permute-done.51
  880.6 38.5 %reduce-scatter.7.cloned.1.call-done = bf16[5,256,128]{2,1,0:T(8,128)(2,1)} async-done(((bf16[5,2048,128]{2,1,0:T(8,128)(2,1)}), bf16[5,256,128]{2,1,0:T(8,128)(2,1)}) %reduce-scatter.7.cloned.1.call-update) | async-done | bytes 327696 | tf_op jit(solution)/shard_map/reduce_scatter | solution.py:581
  921.8 44.1 %all-reduce.3.cloned.1.call-done = (bf16[5,256,128]{2,1,0:T(8,128)(2,1)}, bf16[2,16,2048]{2,1,0:T(8,128)(2,1)}) async-done(((bf16[5,256,128]{2,1,0:T(8,128)(2,1)}, bf16[2,16,2048]{2,1,0:T(8,128)(2,1)}), (bf16[5,256,128]{2,1,0:T(8,128)(2,1)}, bf16[2,16,2048]{2,1,0:T(8,128)(2,1)})) %all-reduce.3.cloned.1.call-update) | async-done | bytes 458768 | tf_op jit(solution)/shard_map/psum | solution.py:592
  (720 shorter events, 372.3 us)
Async XLA Ops:
  7.2 48.1 %all-gather.15.cloned.1.call-start = ((), (), s32[]{:S(2)}) async-start(), calls=%async_computation.16 | async-start | bytes 3391488 | tf_op jit(solution)/shard_map/all_gather | solution.py:359
  15.4 119.4 %all-gather.7.cloned.1.call-start = ((), (), s32[]{:S(2)}) async-start(), calls=%async_computation.6 | async-start | bytes 7077888 | tf_op jit(solution)/shard_map/all_gather | solution.py:344
  16.6 337.9 %all-gather.9.cloned.1.call-start = ((), (), s32[]{:S(2)}) async-start(), calls=%async_computation.7 | async-start | bytes 2359296 | tf_op jit(solution)/shard_map/all_gather | solution.py:344
  17.4 421.2 %all-gather.11.cloned.1.call-start = ((), (), s32[]{:S(2)}) async-start(), calls=%async_computation.8 | async-start | bytes 18874368 | tf_op jit(solution)/shard_map/all_gather | solution.py:344
  20.0 445.5 %all-gather.13.cloned.1.call-start = ((), (), s32[]{:S(2)}) async-start(), calls=%async_computation.9 | async-start | bytes 9437184 | tf_op jit(solution)/shard_map/all_gather | solution.py:344
  21.1 37.0 %collective-permute-start = (bf16[96,2048]{1,0:T(8,128)(2,1)S(1)}, bf16[96,2048]{1,0:T(8,128)(2,1)S(1)}, u32[]{:S(2)}, u32[]{:S(2)}) collective-permute-start(bf16[96,2048]{1,0:T(8,128)(2,1)S(1)} %get-tuple-element.118), channel_id=1, source_target_pairs={{0,1},{1,0},{2,3},{3,2},{4,5},{5,4},{6,7},{7,6},{8,9},{9,8},{10,11... | collective-permute-start | bytes 1179656 | tf_op jit(solution)/shard_map/ppermute | solution.py:41
  24.2 34.0 %collective-permute-start.2 = (bf16[96,2048]{1,0:T(8,128)(2,1)S(1)}, bf16[96,2048]{1,0:T(8,128)(2,1)S(1)}, u32[]{:S(2)}, u32[]{:S(2)}) collective-permute-start(bf16[96,2048]{1,0:T(8,128)(2,1)S(1)} %get-tuple-element.119), channel_id=1, source_target_pairs={{0,2},{1,3},{2,0},{3,1},{4,6},{5,7},{6,4},{7,5},{8,10},{9,11},{10,... | collective-permute-start | bytes 1179656 | tf_op jit(solution)/shard_map/ppermute | solution.py:41
  56.6 23.3 %collective-permute-start.4 = (bf16[8,448,128]{2,1,0:T(8,128)(2,1)S(1)}, bf16[8,448,128]{2,1,0:T(8,128)(2,1)S(1)}, u32[]{:S(2)}, u32[]{:S(2)}) collective-permute-start(bf16[8,448,128]{2,1,0:T(8,128)(2,1)S(1)} %concatenate.89), channel_id=1, source_target_pairs={{0,1},{1,0},{2,3},{3,2},{4,5},{5,4},{6,7},{7,6},{8,9},{9,8},{10,11... | collective-permute-start | bytes 2752520 | tf_op jit(solution)/shard_map/ppermute | solution.py:41
  58.3 25.7 %collective-permute-start.1 = (bf16[2,96,2048]{2,1,0:T(8,128)(2,1)S(1)}, bf16[2,96,2048]{2,1,0:T(8,128)(2,1)S(1)}, u32[]{:S(2)}, u32[]{:S(2)}) collective-permute-start(bf16[2,96,2048]{2,1,0:T(8,128)(2,1)S(1)} %pad_maximum_fusion.22), channel_id=1, source_target_pairs={{0,2},{1,3},{2,0},{3,1},{4,6},{5,7},{6,4},{7,5},{8,10},{9,11},{10,... | collective-permute-start | bytes 2359304 | tf_op jit(solution)/shard_map/ppermute | solution.py:41
  59.9 36.0 %collective-permute-start.3 = (bf16[2,96,2048]{2,1,0:T(8,128)(2,1)S(1)}, bf16[2,96,2048]{2,1,0:T(8,128)(2,1)S(1)}, u32[]{:S(2)}, u32[]{:S(2)}) collective-permute-start(bf16[2,96,2048]{2,1,0:T(8,128)(2,1)S(1)} %pad_maximum_fusion.23), channel_id=1, source_target_pairs={{0,1},{1,0},{2,3},{3,2},{4,5},{5,4},{6,7},{7,6},{8,9},{9,8},{10,11... | collective-permute-start | bytes 2359304 | tf_op jit(solution)/shard_map/ppermute | solution.py:41
  82.6 41.0 %collective-permute-start.5 = (bf16[2,8,448,128]{3,2,1,0:T(8,128)(2,1)}, bf16[2,8,448,128]{3,2,1,0:T(8,128)(2,1)}, u32[]{:S(2)}, u32[]{:S(2)}) collective-permute-start(bf16[2,8,448,128]{3,2,1,0:T(8,128)(2,1)} %pad_maximum_fusion.6), channel_id=1, source_target_pairs={{0,2},{1,3},{2,0},{3,1},{4,6},{5,7},{6,4},{7,5},{8,10},{9,11},{10,... | collective-permute-start | bytes 5505032 | tf_op jit(solution)/shard_map/ppermute | solution.py:41
  162.5 31.0 %collective-permute-start.8 = (bf16[3,768,128]{2,1,0:T(8,128)(2,1)}, bf16[3,768,128]{2,1,0:T(8,128)(2,1)}, u32[]{:S(2)}, u32[]{:S(2)}) collective-permute-start(bf16[3,768,128]{2,1,0:T(8,128)(2,1)} %bitcast.45), channel_id=1, source_target_pairs={{0,8},{4,12},{8,16},{12,20},{16,24},{20,28},{24,0},{28,4},{1,9},{5... | collective-permute-start | bytes 1769480 | tf_op jit(solution)/shard_map/ppermute | solution.py:436
  164.2 73.0 %collective-permute-start.9 = (bf16[3,768,128]{2,1,0:T(8,128)(2,1)}, bf16[3,768,128]{2,1,0:T(8,128)(2,1)}, u32[]{:S(2)}, u32[]{:S(2)}) collective-permute-start(bf16[3,768,128]{2,1,0:T(8,128)(2,1)} %bitcast.46), channel_id=1, source_target_pairs={{0,16},{4,20},{8,24},{12,28},{16,0},{20,4},{24,8},{28,12},{1,17},{... | collective-permute-start | bytes 1769480 | tf_op jit(solution)/shard_map/ppermute | solution.py:436
  165.7 73.3 %collective-permute-start.10 = (bf16[3,768,128]{2,1,0:T(8,128)(2,1)S(1)}, bf16[3,768,128]{2,1,0:T(8,128)(2,1)S(1)}, u32[]{:S(2)}, u32[]{:S(2)}) collective-permute-start(bf16[3,768,128]{2,1,0:T(8,128)(2,1)S(1)} %bitcast.564), channel_id=1, source_target_pairs={{0,24},{4,28},{8,0},{12,4},{16,8},{20,12},{24,16},{28,20},{1,25},{... | collective-permute-start | bytes 1769480 | tf_op jit(solution)/shard_map/ppermute | solution.py:436
  170.0 76.3 %collective-permute-start.11 = (bf16[2,768,128]{2,1,0:T(8,128)(2,1)S(1)}, bf16[2,768,128]{2,1,0:T(8,128)(2,1)}, u32[]{:S(2)}, u32[]{:S(2)}) collective-permute-start(bf16[2,768,128]{2,1,0:T(8,128)(2,1)S(1)} %slice_bitcast_fusion.2), channel_id=1, source_target_pairs={{0,4},{4,0},{8,12},{12,8},{16,20},{20,16},{24,28},{28,24},{1,5},{5... | collective-permute-start | bytes 1179656 | tf_op jit(solution)/shard_map/ppermute | solution.py:447
  195.2 51.2 %collective-permute-start.12 = (bf16[2,768,128]{2,1,0:T(8,128)(2,1)}, bf16[2,768,128]{2,1,0:T(8,128)(2,1)}, u32[]{:S(2)}, u32[]{:S(2)}) collective-permute-start(bf16[2,768,128]{2,1,0:T(8,128)(2,1)} %slice.363), channel_id=1, source_target_pairs={{0,4},{4,0},{8,12},{12,8},{16,20},{20,16},{24,28},{28,24},{1,5},{5... | collective-permute-start | bytes 1179656 | tf_op jit(solution)/shard_map/ppermute | solution.py:447
  269.2 57.7 %collective-permute-start.15 = (bf16[768,128]{1,0:T(8,128)(2,1)S(1)}, bf16[768,128]{1,0:T(8,128)(2,1)S(1)}, u32[]{:S(2)}, u32[]{:S(2)}) collective-permute-start(bf16[768,128]{1,0:T(8,128)(2,1)S(1)} %get-tuple-element.115), channel_id=1, source_target_pairs={{0,24},{4,28},{8,0},{12,4},{16,8},{20,12},{24,16},{28,20},{1,25},{... | collective-permute-start | bytes 589832 | tf_op jit(solution)/shard_map/ppermute | solution.py:436
  317.4 35.1 %collective-permute-start.16 = (bf16[768,128]{1,0:T(8,128)(2,1)S(1)}, bf16[768,128]{1,0:T(8,128)(2,1)S(1)}, u32[]{:S(2)}, u32[]{:S(2)}) collective-permute-start(bf16[768,128]{1,0:T(8,128)(2,1)S(1)} %get-tuple-element.114), channel_id=1, source_target_pairs={{0,16},{4,20},{8,24},{12,28},{16,0},{20,4},{24,8},{28,12},{1,17},{... | collective-permute-start | bytes 589832 | tf_op jit(solution)/shard_map/ppermute | solution.py:436
  317.4 35.1 %collective-permute-start.17 = (bf16[768,128]{1,0:T(8,128)(2,1)S(1)}, bf16[768,128]{1,0:T(8,128)(2,1)S(1)}, u32[]{:S(2)}, u32[]{:S(2)}) collective-permute-start(bf16[768,128]{1,0:T(8,128)(2,1)S(1)} %get-tuple-element.113), channel_id=1, source_target_pairs={{0,8},{4,12},{8,16},{12,20},{16,24},{20,28},{24,0},{28,4},{1,9},{5... | collective-permute-start | bytes 589832 | tf_op jit(solution)/shard_map/ppermute | solution.py:436
  360.3 20.0 %collective-permute-start.18 = (bf16[2,96,2048]{2,1,0:T(8,128)(2,1)}, bf16[2,96,2048]{2,1,0:T(8,128)(2,1)}, u32[]{:S(2)}, u32[]{:S(2)}) collective-permute-start(bf16[2,96,2048]{2,1,0:T(8,128)(2,1)} %dynamic-slice_bitcast_fusion.8), channel_id=1, source_target_pairs={{0,2},{1,3},{2,0},{3,1},{4,6},{5,7},{6,4},{7,5},{8,10},{9,11},{10,... | collective-permute-start | bytes 2359304 | tf_op jit(solution)/shard_map/ppermute | solution.py:41
  361.4 483.8 %reduce-scatter.11.cloned.1.call-start = ((), (), s32[]{:S(2)}) async-start(), calls=%async_computation.12 | async-start | bytes 589824 | tf_op jit(solution)/shard_map/reduce_scatter | solution.py:581
  362.4 20.9 %collective-permute-start.20 = (bf16[2,96,2048]{2,1,0:T(8,128)(2,1)}, bf16[2,96,2048]{2,1,0:T(8,128)(2,1)}, u32[]{:S(2)}, u32[]{:S(2)}) collective-permute-start(bf16[2,96,2048]{2,1,0:T(8,128)(2,1)} %dynamic-slice_bitcast_fusion.7), channel_id=1, source_target_pairs={{0,1},{1,0},{2,3},{3,2},{4,5},{5,4},{6,7},{7,6},{8,9},{9,8},{10,11... | collective-permute-start | bytes 2359304 | tf_op jit(solution)/shard_map/ppermute | solution.py:41
  408.9 22.5 %collective-permute-start.25 = (bf16[2,96,2048]{2,1,0:T(8,128)(2,1)}, bf16[2,96,2048]{2,1,0:T(8,128)(2,1)}, u32[]{:S(2)}, u32[]{:S(2)}) collective-permute-start(bf16[2,96,2048]{2,1,0:T(8,128)(2,1)} %pad_maximum_fusion.25), channel_id=1, source_target_pairs={{0,1},{1,0},{2,3},{3,2},{4,5},{5,4},{6,7},{7,6},{8,9},{9,8},{10,11... | collective-permute-start | bytes 2359304 | tf_op jit(solution)/shard_map/ppermute | solution.py:41
  692.2 154.5 %reduce-scatter.15.cloned.1.call-start = ((), (), s32[]{:S(2)}) async-start(), calls=%async_computation.14 | async-start | bytes 1179648 | tf_op jit(solution)/shard_map/reduce_scatter | solution.py:581
  700.4 19.9 %collective-permute-start.46 = (bf16[3,768,128]{1,2,0:T(8,128)(2,1)}, bf16[3,768,128]{1,2,0:T(8,128)(2,1)S(1)}, u32[]{:S(2)}, u32[]{:S(2)}) collective-permute-start(bf16[3,768,128]{1,2,0:T(8,128)(2,1)} %get-tuple-element.45), channel_id=1, source_target_pairs={{0,24},{4,28},{8,0},{12,4},{16,8},{20,12},{24,16},{28,20},{1,25},{... | collective-permute-start | bytes 1769480 | tf_op jit(solution)/shard_map/ppermute | solution.py:436
  704.2 54.8 %collective-permute-start.47 = (bf16[3,768,128]{1,2,0:T(8,128)(2,1)}, bf16[3,768,128]{1,2,0:T(8,128)(2,1)}, u32[]{:S(2)}, u32[]{:S(2)}) collective-permute-start(bf16[3,768,128]{1,2,0:T(8,128)(2,1)} %get-tuple-element.46), channel_id=1, source_target_pairs={{0,16},{4,20},{8,24},{12,28},{16,0},{20,4},{24,8},{28,12},{1,17},{... | collective-permute-start | bytes 1769480 | tf_op jit(solution)/shard_map/ppermute | solution.py:436
  706.3 142.1 %reduce-scatter.9.cloned.1.call-start = ((), (), s32[]{:S(2)}) async-start(), calls=%async_computation.11 | async-start | bytes 147456 | tf_op jit(solution)/shard_map/reduce_scatter | solution.py:581
  706.3 53.7 %collective-permute-start.48 = (bf16[3,768,128]{1,2,0:T(8,128)(2,1)}, bf16[3,768,128]{1,2,0:T(8,128)(2,1)S(1)}, u32[]{:S(2)}, u32[]{:S(2)}) collective-permute-start(bf16[3,768,128]{1,2,0:T(8,128)(2,1)} %get-tuple-element.44), channel_id=1, source_target_pairs={{0,8},{4,12},{8,16},{12,20},{16,24},{20,28},{24,0},{28,4},{1,9},{5... | collective-permute-start | bytes 1769480 | tf_op jit(solution)/shard_map/ppermute | solution.py:436
  778.6 87.0 %reduce-scatter.13.cloned.1.call-start = ((), (), s32[]{:S(2)}) async-start(), calls=%async_computation.13 | async-start | bytes 442368 | tf_op jit(solution)/shard_map/reduce_scatter | solution.py:581
  788.2 92.4 %reduce-scatter.17.cloned.1.call-start = ((), (), s32[]{:S(2)}) async-start(), calls=%async_computation.15 | async-start | bytes 1179648 | tf_op jit(solution)/shard_map/reduce_scatter | solution.py:581
  792.8 126.3 %reduce-scatter.7.cloned.1.call-start = ((), (), s32[]{:S(2)}) async-start(), calls=%async_computation.10 | async-start | bytes 2949120 | tf_op jit(solution)/shard_map/reduce_scatter | solution.py:581
  817.3 148.6 %all-reduce.3.cloned.1.call-start = ((), (), s32[]{:S(2)}) async-start(), calls=%async_computation.17 | async-start | bytes 917504 | tf_op jit(solution)/shard_map/psum | solution.py:592
  (188 other events, 2377.7 us)
Sparse Core Ops, SparseCore 0:
  15.5 39.7 all-gather.14
  57.5 64.0 all-gather.6
  123.2 28.7 all-gather.8
  153.5 215.8 all-gather.10
  370.8 81.6 all-gather.12
  692.3 39.6 reduce-scatter.10
  734.3 50.2 reduce-scatter.14
  787.4 28.6 reduce-scatter.8
  818.4 29.2 reduce-scatter.12
  849.8 30.7 reduce-scatter.16
  882.9 36.1 reduce-scatter.6
  922.0 43.8 all-reduce.2

commit v2 on v1

v2 whole, which is shorter than its diff:
```python
import functools

import jax
import jax.numpy as jnp
from jax import lax
from jax.experimental import pallas as pl
from jax.experimental.pallas import tpu as pltpu
from jax.sharding import PartitionSpec as P

HEAD_DIM = 128
ADAPTER_RANK = 16
BLK = 128
PROMPT_BLOCKS = 8
EPS = 1e-06
THETA = 500000.0
NEG = -1e30
LOG2E = 1.4426950408889634
F32 = jnp.float32
BF16 = jnp.bfloat16


def mm(a, b):
    return jnp.dot(a, b, preferred_element_type=F32)


def mm_nt(a, b):
    return lax.dot_general(a, b, (((1,), (1,)), ((), ())), preferred_element_type=F32)


def mm_tn(a, b):
    return lax.dot_general(a, b, (((0,), (0,)), ((), ())), preferred_element_type=F32)


def bits_of(count):
    n = count.bit_length() - 1
    assert 1 << n == count
    return n


def flip(value, axis, count, bit):
    return lax.ppermute(value, axis, [(i, i ^ (1 << bit)) for i in range(count)])


def gather_order(value, axis, count, order):
    rank = lax.axis_index(axis)
    have = []
    current = value
    for bit in order:
        other = flip(current, axis, count, bit)
        mine_low = ((rank >> bit) & 1) == 0
        at = len([b for b in have if b > bit])
        low = jnp.where(mine_low, current, other)
        high = jnp.where(mine_low, other, current)
        current = jnp.stack([low, high], axis=at)
        have = sorted(have + [bit], reverse=True)
    return current.reshape((count,) + value.shape)


def scatter_order(value, axis, count, order):
    n = bits_of(count)
    rank = lax.axis_index(axis)
    current = value.reshape((2,) * n + value.shape[1:])
    have = list(range(n - 1, -1, -1))
    for bit in order:
        at = have.index(bit)
        mine = (rank >> bit) & 1
        keep = lax.dynamic_index_in_dim(current, mine, at, keepdims=False)
        give = lax.dynamic_index_in_dim(current, 1 - mine, at, keepdims=False)
        got = flip(give.astype(BF16), axis, count, bit)
        current = keep.astype(F32) + got.astype(F32)
        have.remove(bit)
    return current


def part_orders(count):
    order = list(range(bits_of(count)))
    return (order, order[::-1])


def group_masks(count):
    groups = ([], [])
    for part, order in enumerate(part_orders(count)):
        for j in range(count):
            mask = sum(1 << bit for i, bit in enumerate(order) if (j >> i) & 1)
            groups[j >= count // 2].append((mask, part))
    return groups


def row_runs(count):
    return [run for masks in group_masks(count) for run in masks]


def gather_groups(parts, count, beside=None):
    near, far = [], []
    for value, order in zip(parts, part_orders(count)):
        for bit in order[:-1]:
            value = jnp.concatenate([value, flip(value, "tp", count, bit)], axis=0)
        near.append(value)
    if beside is not None:
        near[1], beside = lax.optimization_barrier((near[1], beside))
    for value, order in zip(near, part_orders(count)):
        far.append(flip(value, "tp", count, order[-1]))
    if beside is not None:
        return jnp.concatenate(near, axis=0), jnp.concatenate(far, axis=0), beside
    return jnp.concatenate(near, axis=0), jnp.concatenate(far, axis=0)


def scatter_groups(near, far, count):
    out = []
    size = near.shape[0] // 2
    for i, order in enumerate(part_orders(count)):
        got = flip(far[i], "tp", count, order[-1])
        total = near[i * size : (i + 1) * size].astype(F32) + got.astype(F32)
        for bit in order[-2::-1]:
            half = total.shape[0] // 2
            got = flip(total[half:].astype(BF16), "tp", count, bit)
            total = total[:half] + got.astype(F32)
        out.append(total)
    return out


def sum_rows(value, count):
    runs = row_runs(count)
    value = value.reshape(value.shape[0], len(runs), -1)
    total = value
    for mask in range(1, count):
        got = lax.ppermute(value, "tp", [(i, i ^ mask) for i in range(count)])
        order = [runs.index((other ^ mask, which)) for other, which in runs]
        total = total + jnp.concatenate([got[:, j : j + 1] for j in order], axis=1)
    return total.reshape(value.shape[0], -1)


def sum_all(value, axis, count):
    for bit in range(bits_of(count)):
        value = value + flip(value, axis, count, bit)
    return value


def copy_all(pairs, sem):
    copies = [pltpu.make_async_copy(src, dst, sem.at[i]) for i, (src, dst) in enumerate(pairs)]
    for copy in copies:
        copy.start()
    for copy in copies:
        copy.wait()


def gather_prompt(prompt_at, source, target, count):
    def step(i, carry):
        start = pl.multiple_of(prompt_at[i] * BLK, BLK)
        target[pl.ds(pl.multiple_of(i * BLK, BLK), BLK), :] = source[pl.ds(start, BLK), :]
        return carry

    lax.fori_loop(0, count, step, 0)


def masked_scores(keys, own_keys, queries, place, scale):
    prompt = mm_nt(keys, queries) * scale
    block = lax.broadcasted_iota(jnp.int32, prompt.shape, 0) // BLK
    prompt = jnp.where(block < place, prompt, NEG)
    own = mm_nt(own_keys, queries) * scale
    causal = lax.broadcasted_iota(jnp.int32, own.shape, 0) <= lax.broadcasted_iota(
        jnp.int32, own.shape, 1
    )
    own = jnp.where(causal, own, NEG)
    top = jnp.maximum(jnp.max(prompt, axis=0, keepdims=True), jnp.max(own, axis=0, keepdims=True))
    prompt = jnp.exp2(prompt - top)
    own = jnp.exp2(own - top)
    total = jnp.sum(prompt, axis=0, keepdims=True) + jnp.sum(own, axis=0, keepdims=True)
    return prompt, own, 1.0 / total


def load_plan(slots, group, rows, refs, q_buf, k_buf, v_buf):
    plan = []
    for i in range(slots):
        plan.append((refs[i], q_buf.at[pl.ds(i * rows, rows)]))
    for i in range(slots * group):
        at = pl.ds(i * rows, rows)
        ref = refs[slots + i]
        plan += [(ref.at[0], k_buf.at[at]), (ref.at[1], v_buf.at[at])]
    return plan


def attend_kernel(slots, group, rows, prompt_count, q_seq, q_place, prompt_at, *refs):
    n_in = slots + slots * group
    outs = refs[n_in : n_in + slots]
    q_buf, k_buf, v_buf, kp, vp, o_buf, sem = refs[n_in + slots :]
    copy_all(load_plan(slots, group, rows, refs, q_buf, k_buf, v_buf), sem)
    gather_prompt(prompt_at, k_buf, kp, prompt_count)
    gather_prompt(prompt_at, v_buf, vp, prompt_count)
    scale = HEAD_DIM ** (-0.5) * LOG2E
    span = PROMPT_BLOCKS * BLK

    def step(i, carry):
        at = pl.ds(pl.multiple_of(i * BLK, BLK), BLK)
        of_seq = pl.ds(pl.multiple_of(q_seq[i] * span, span), span)
        prompt, own, inverse = masked_scores(
            kp[of_seq, :], k_buf[at, :], q_buf[at, :], q_place[i], scale
        )
        result = mm_tn(vp[of_seq, :], prompt.astype(BF16)) + mm_tn(v_buf[at, :], own.astype(BF16))
        o_buf[at, :] = (result * inverse).T.astype(BF16)
        return carry

    lax.fori_loop(0, slots * rows // BLK, step, 0)
    copy_all([(o_buf.at[pl.ds(i * rows, rows)], outs[i]) for i in range(slots)], sem)


def attend_back_kernel(
    slots, group, rows, pieces, prompt_count, q_seq, q_place, prompt_at, piece_at, *refs
):
    n_in = slots + slots * group
    n_grad = slots * 2
    grads = refs[n_in : n_in + n_grad]
    outs = refs[n_in + n_grad : n_in + n_grad + slots]
    near_out = refs[n_in + n_grad + slots]
    rest = refs[n_in + n_grad + slots + 1 :]
    far_outs, rest = rest[: group - 1], rest[group - 1 :]
    q_buf, k_buf, v_buf, do_buf, kp, vp, dkp, dvp, dq_buf, dkv_buf, sem = rest
    plan = load_plan(slots, group, rows, refs, q_buf, k_buf, v_buf)
    size = rows // pieces
    for i in range(slots):
        for p in range(pieces):
            half, at = divmod(p, pieces // 2)
            to = pl.multiple_of(i * rows + piece_at[p] * size, 16)
            plan.append(
                (grads[i * 2 + half].at[pl.ds(at * size, size)], do_buf.at[pl.ds(to, size)])
            )
    copy_all(plan, sem)
    gather_prompt(prompt_at, k_buf, kp, prompt_count)
    gather_prompt(prompt_at, v_buf, vp, prompt_count)
    dkp[...] = jnp.zeros_like(dkp)
    dvp[...] = jnp.zeros_like(dvp)
    scale = HEAD_DIM ** (-0.5)
    span = PROMPT_BLOCKS * BLK
    own_rows = slots * rows
    zeros = jnp.zeros((BLK, HEAD_DIM), BF16)

    def rows_of(i):
        return pl.ds(pl.multiple_of(i * BLK, BLK), BLK)

    def clear(i, carry):
        for j in range(1, group):
            dkv_buf[j, 0, rows_of(i), :] = zeros
            dkv_buf[j, 1, rows_of(i), :] = zeros
        return carry

    lax.fori_loop(0, own_rows // BLK, clear, 0)

    def step(i, carry):
        at = rows_of(i)
        seq, place = q_seq[i], q_place[i]
        of_seq = pl.ds(pl.multiple_of(seq * span, span), span)
        queries, grad = q_buf[at, :], do_buf[at, :]
        prompt, own, inverse = masked_scores(
            kp[of_seq, :], k_buf[at, :], queries, place, scale * LOG2E
        )
        prompt, own = prompt * inverse, own * inverse
        d_prompt = mm_nt(vp[of_seq, :], grad)
        d_own = mm_nt(v_buf[at, :], grad)
        delta = jnp.sum(prompt * d_prompt, axis=0, keepdims=True) + jnp.sum(
            own * d_own, axis=0, keepdims=True
        )
        ds_prompt = (prompt * (d_prompt - delta)).astype(BF16)
        ds_own = (own * (d_own - delta)).astype(BF16)
        dq = mm_tn(ds_prompt, kp[of_seq, :]) + mm_tn(ds_own, k_buf[at, :])
        dq_buf[at, :] = (dq * scale).astype(BF16)
        dvp[of_seq, :] += mm(prompt.astype(BF16), grad)
        dkp[of_seq, :] += mm(ds_prompt, queries) * scale
        dkv_buf[0, 0, at, :] = (mm(ds_own, queries) * scale).astype(BF16)
        dkv_buf[0, 1, at, :] = mm(own.astype(BF16), grad).astype(BF16)
        return carry

    lax.fori_loop(0, own_rows // BLK, step, 0)
    blocks = own_rows // BLK

    def spread(i, carry):
        place = prompt_at[i]
        j, to = place // blocks, rows_of(place % blocks)
        dkv_buf[j, 0, to, :] = (dkv_buf[j, 0, to, :].astype(F32) + dkp[rows_of(i), :]).astype(BF16)
        dkv_buf[j, 1, to, :] = (dkv_buf[j, 1, to, :].astype(F32) + dvp[rows_of(i), :]).astype(BF16)
        return carry

    lax.fori_loop(0, prompt_count, spread, 0)
    plan = [(dq_buf.at[pl.ds(i * rows, rows)], outs[i]) for i in range(slots)]
    plan.append((dkv_buf.at[0], near_out))
    plan += [(dkv_buf.at[j], far_outs[j - 1]) for j in range(1, group)]
    copy_all(plan, sem)


ANY = pl.BlockSpec(memory_space=pl.ANY)


def attend(tables, queries, near, far, prompt_count):
    slots = len(near)
    rows = queries[0].shape[0]
    group = 1 + len(far) // slots
    own, every = slots * rows, slots * group * rows
    pairs = own * (PROMPT_BLOCKS + 1) * BLK
    wide = lambda count, kind=BF16: pltpu.VMEM((count, HEAD_DIM), kind)
    return pl.pallas_call(
        functools.partial(attend_kernel, slots, group, rows, prompt_count),
        out_shape=[jax.ShapeDtypeStruct((rows, HEAD_DIM), BF16)] * slots,
        grid_spec=pltpu.PrefetchScalarGridSpec(
            num_scalar_prefetch=3,
            in_specs=[ANY] * (slots + slots * group),
            out_specs=[ANY] * slots,
            scratch_shapes=[
                wide(own),
                wide(every),
                wide(every),
                wide(prompt_count * BLK),
                wide(prompt_count * BLK),
                wide(own),
                pltpu.SemaphoreType.DMA((slots + 2 * slots * group,)),
            ],
        ),
        cost_estimate=pl.CostEstimate(
            flops=4 * pairs * HEAD_DIM, bytes_accessed=6 * every * HEAD_DIM, transcendentals=pairs
        ),
        name="attend",
    )(*tables, *queries, *near, *far)


def attend_back(tables, piece_at, queries, near, far, grads, prompt_count):
    pieces = piece_at.shape[0]
    slots = len(near)
    rows = queries[0].shape[0]
    group = 1 + len(far) // slots
    own, every = slots * rows, slots * group * rows
    pairs = own * (PROMPT_BLOCKS + 1) * BLK
    wide = lambda count, kind=BF16: pltpu.VMEM((count, HEAD_DIM), kind)
    return pl.pallas_call(
        functools.partial(attend_back_kernel, slots, group, rows, pieces, prompt_count),
        out_shape=[jax.ShapeDtypeStruct((rows, HEAD_DIM), BF16)] * slots
        + [jax.ShapeDtypeStruct((2, own, HEAD_DIM), BF16)] * group,
        grid_spec=pltpu.PrefetchScalarGridSpec(
            num_scalar_prefetch=4,
            in_specs=[ANY] * (slots + slots * group + 2 * slots),
            out_specs=[ANY] * (slots + group),
            scratch_shapes=[
                wide(own),
                wide(every),
                wide(every),
                wide(own),
                wide(prompt_count * BLK),
                wide(prompt_count * BLK),
                wide(prompt_count * BLK, F32),
                wide(prompt_count * BLK, F32),
                wide(own),
                pltpu.VMEM((group, 2, own, HEAD_DIM), BF16),
                pltpu.SemaphoreType.DMA((slots + 2 * slots * group + slots * pieces,)),
            ],
        ),
        cost_estimate=pl.CostEstimate(
            flops=10 * pairs * HEAD_DIM, bytes_accessed=12 * every * HEAD_DIM, transcendentals=pairs
        ),
        name="attend_back",
    )(*tables, piece_at, *queries, *near, *far, *grads)


def turn(values, cosine, sine):
    return values * cosine + pltpu.roll(values, HEAD_DIM // 2, 1) * sine


def lanes(head, base=0):
    return pl.ds(pl.multiple_of(base + head * HEAD_DIM, HEAD_DIM), HEAD_DIM)


def piece_rows(index, size):
    return pl.ds(pl.multiple_of(index * size, 16), size)


def spread_kernel(slots, pieces, order, piece_at, z, inv, cs, gain, *outs):
    cols = slots * HEAD_DIM
    size = z.shape[0] // pieces

    def step(p, carry):
        at, to = piece_rows(p, size), piece_rows(piece_at[p], size)
        cosine, sine = cs[at, :HEAD_DIM], cs[at, HEAD_DIM:]
        for which in range(2):
            factor = inv[at, which : which + 1]
            for k in range(slots):
                head = order[k]
                scaled = z[at, lanes(head, which * cols)] * factor
                scaled = scaled * gain[which : which + 1, lanes(head)]
                turned = turn(scaled, cosine, sine).astype(BF16)
                if which == 0:
                    outs[k][to, :] = turned
                else:
                    outs[slots + k][0, to, :] = turned
        for k in range(slots):
            outs[slots + k][1, to, :] = z[at, lanes(order[k], 2 * cols)].astype(BF16)
        return carry

    lax.fori_loop(0, pieces, step, 0)


WHOLE = pl.BlockSpec(memory_space=pltpu.VMEM)
BIG = pltpu.CompilerParams(vmem_limit_bytes=56 * 1024 * 1024)


def spread_heads(order, piece_at, z, inv, cs, gain, slots):
    rows = z.shape[0]
    return pl.pallas_call(
        functools.partial(spread_kernel, slots, piece_at.shape[0]),
        out_shape=[jax.ShapeDtypeStruct((rows, HEAD_DIM), BF16)] * slots
        + [jax.ShapeDtypeStruct((2, rows, HEAD_DIM), BF16)] * slots,
        grid_spec=pltpu.PrefetchScalarGridSpec(
            num_scalar_prefetch=2, in_specs=[WHOLE] * 4, out_specs=[WHOLE] * (2 * slots)
        ),
        compiler_params=BIG,
        name="spread_heads",
    )(order, piece_at, z, inv, cs, gain)


def collect_kernel(slots, pieces, order, piece_at, *refs):
    outs = refs[slots:]
    size = refs[0].shape[0] // pieces
    for p in range(pieces):
        half, at = divmod(p, pieces // 2)
        for k in range(slots):
            outs[half][pl.ds(at * size, size), lanes(order[k])] = refs[k][
                piece_rows(piece_at[p], size), :
            ]


def collect_heads(order, piece_at, parts):
    slots = len(parts)
    rows = parts[0].shape[0]
    return pl.pallas_call(
        functools.partial(collect_kernel, slots, piece_at.shape[0]),
        out_shape=[jax.ShapeDtypeStruct((rows // 2, slots * HEAD_DIM), BF16)] * 2,
        grid_spec=pltpu.PrefetchScalarGridSpec(
            num_scalar_prefetch=2, in_specs=[WHOLE] * slots, out_specs=[WHOLE] * 2
        ),
        name="collect_heads",
    )(order, piece_at, *parts)


def unturn_kernel(slots, pieces, order, piece_at, *refs):
    dqs, dkvs, rest = refs[:slots], refs[slots : 2 * slots], refs[2 * slots :]
    z, cs, gain, scaled_out, part_out = rest
    cols = slots * HEAD_DIM
    size = z.shape[0] // pieces

    def step(p, carry):
        at, source = piece_rows(p, size), piece_rows(piece_at[p], size)
        cosine, sine = cs[at, :HEAD_DIM], cs[at, HEAD_DIM:]
        for which in range(2):
            total = jnp.zeros((size, HEAD_DIM), F32)
            for k in range(slots):
                head = order[k]
                grad = dqs[k][source, :] if which == 0 else dkvs[k][0, source, :]
                grad = turn(grad.astype(F32), cosine, -sine) * gain[which : which + 1, lanes(head)]
                scaled_out[at, lanes(head, which * cols)] = grad
                total = total + grad * z[at, lanes(head, which * cols)]
            part_out[at, which : which + 1] = jnp.sum(total, axis=1, keepdims=True)
        return carry

    lax.fori_loop(0, pieces, step, 0)


def unturn_heads(order, piece_at, dqs, dkvs, z, cs, gain):
    slots = len(dqs)
    rows = z.shape[0]
    cols = slots * HEAD_DIM
    return pl.pallas_call(
        functools.partial(unturn_kernel, slots, piece_at.shape[0]),
        out_shape=[
            jax.ShapeDtypeStruct((rows, 2 * cols), F32),
            jax.ShapeDtypeStruct((rows, 2), F32),
        ],
        grid_spec=pltpu.PrefetchScalarGridSpec(
            num_scalar_prefetch=2, in_specs=[WHOLE] * (2 * slots + 3), out_specs=[WHOLE] * 2
        ),
        compiler_params=BIG,
        name="unturn_heads",
    )(order, piece_at, *dqs, *dkvs, z, cs, gain)


def norm_back_kernel(slots, pieces, order, piece_at, *refs):
    dkvs, (scaled, z, coef, out) = refs[:slots], refs[slots:]
    cols = slots * HEAD_DIM
    size = z.shape[0] // pieces

    def step(p, carry):
        at, source = piece_rows(p, size), piece_rows(piece_at[p], size)
        for which in range(2):
            to = slice(which * cols, (which + 1) * cols)
            out[at, to] = (
                scaled[at, to] * coef[at, which : which + 1]
                - z[at, to] * coef[at, 2 + which : 3 + which]
            ).astype(BF16)
        for k in range(slots):
            out[at, lanes(order[k], 2 * cols)] = dkvs[k][1, source, :]
        return carry

    lax.fori_loop(0, pieces, step, 0)


def norm_back_heads(order, piece_at, dkvs, scaled, z, coef):
    slots = len(dkvs)
    return pl.pallas_call(
        functools.partial(norm_back_kernel, slots, piece_at.shape[0]),
        out_shape=jax.ShapeDtypeStruct(z.shape, BF16),
        grid_spec=pltpu.PrefetchScalarGridSpec(
            num_scalar_prefetch=2, in_specs=[WHOLE] * (slots + 3), out_specs=WHOLE
        ),
        compiler_params=BIG,
        name="norm_back_heads",
    )(order, piece_at, *dkvs, scaled, z, coef)


def fixed(*shape, at=None):
    place = at or (0,) * len(shape)
    return pl.BlockSpec(shape, lambda i: place)


def flat(value):
    return value.reshape(-1, value.shape[-1])


def qkv_kernel(x, latent, weight, second, z, squares):
    i = pl.program_id(0)
    result = mm(x[...], flat(weight[...])) + mm(latent[...], flat(second[...]))
    z[...] = result
    squares[0, :, :] = jnp.sum(result * result, axis=1, keepdims=True)


def qkv_product(x, latents, first, second, k_rows, cols):
    rows, width = x.shape
    shards, _, total = first.shape
    low = latents.shape[1] // 3
    return pl.pallas_call(
        qkv_kernel,
        grid=(3,),
        out_shape=[
            jax.ShapeDtypeStruct((rows, total), F32),
            jax.ShapeDtypeStruct((3, rows, 1), F32),
        ],
        in_specs=[
            fixed(rows, width),
            pl.BlockSpec((rows, low), lambda i: (0, i)),
            pl.BlockSpec((shards, k_rows, cols), lambda i: (0, 0, i)),
            pl.BlockSpec((low, cols), lambda i: (0, i)),
        ],
        out_specs=[
            pl.BlockSpec((rows, cols), lambda i: (0, i)),
            pl.BlockSpec((1, rows, 1), lambda i: (i, 0, 0)),
        ],
        compiler_params=BIG,
        cost_estimate=pl.CostEstimate(
            flops=2 * rows * width * total, bytes_accessed=2 * first.size, transcendentals=0
        ),
        name="qkv_product",
    )(x, latents, first, second)


def add_kernel(parts, a, weight, first, second, pick, *refs):
    outs, (latent_out, latent) = refs[:parts], refs[parts:]

    @pl.when(pl.program_id(0) == 0)
    def _():
        latent[...] = (mm(a[...], first[...]) * pick[...]).astype(BF16)
        latent_out[...] = latent[...]

    result = mm_nt(a[...], weight[...]) + mm(latent[...], second[...])
    size = result.shape[0] // parts
    for i in range(parts):
        outs[i][...] = result[i * size : (i + 1) * size].astype(BF16)


def add_product(a, weight, first, second, pick, parts, tile=512):
    rows, depth = a.shape
    width, low = weight.shape[0], first.shape[1]
    size = rows // parts
    return pl.pallas_call(
        functools.partial(add_kernel, parts),
        grid=(width // tile,),
        out_shape=[jax.ShapeDtypeStruct((size, width), BF16)] * parts
        + [jax.ShapeDtypeStruct((rows, low), BF16)],
        in_specs=[
            fixed(rows, depth),
            pl.BlockSpec((tile, depth), lambda i: (i, 0)),
            fixed(depth, low),
            pl.BlockSpec((low, tile), lambda i: (0, i)),
            fixed(rows, low),
        ],
        out_specs=[pl.BlockSpec((size, tile), lambda i: (0, i))] * parts + [fixed(rows, low)],
        scratch_shapes=[pltpu.VMEM((rows, low), BF16)],
        compiler_params=BIG,
        cost_estimate=pl.CostEstimate(
            flops=2 * rows * width * depth, bytes_accessed=2 * weight.size, transcendentals=0
        ),
        name="add_product",
    )(a, weight, first, second, pick)


def back_kernel(parts, a, weight, u, first, *outs):
    result = mm_nt(a[...], flat(weight[...])) + mm_nt(u[...], first[...])
    size = result.shape[0] // parts
    for i in range(parts):
        outs[i][...] = result[i * size : (i + 1) * size].astype(BF16)


def back_product(a, group, weight, k_rows, u, first, parts):
    rows, depth = a.shape
    rows //= 2
    shards = weight.shape[0]
    width, low = first.shape
    per = max(1, 512 // k_rows)
    size = rows // parts
    return pl.pallas_call(
        functools.partial(back_kernel, parts),
        grid=(shards // per,),
        out_shape=[jax.ShapeDtypeStruct((size, width), BF16)] * parts,
        in_specs=[
            fixed(rows, depth, at=(group, 0)),
            pl.BlockSpec((per, k_rows, depth), lambda i: (i, 0, 0)),
            fixed(rows, low, at=(group, 0)),
            pl.BlockSpec((per * k_rows, low), lambda i: (i, 0)),
        ],
        out_specs=[pl.BlockSpec((size, per * k_rows), lambda i: (0, i))] * parts,
        compiler_params=BIG,
        cost_estimate=pl.CostEstimate(
            flops=2 * rows * width * depth, bytes_accessed=2 * width * depth, transcendentals=0
        ),
        name="back_product",
    )(a, weight, u, first)


def gate_up_kernel(h, first, pick, w_g, w_u, b_g, b_u, gate_out, up_out, act, latent_out, latent):
    low = pick.shape[1]

    @pl.when(pl.program_id(0) == 0)
    def _():
        both = mm(h[...], first[...])
        latent[:, :low] = (both[:, :low] * pick[...]).astype(BF16)
        latent[:, low:] = (both[:, low:] * pick[...]).astype(BF16)
        latent_out[...] = latent[...]

    gate = mm(h[...], w_g[...]) + mm(latent[:, :low], b_g[...])
    up = mm(h[...], w_u[...]) + mm(latent[:, low:], b_u[...])
    gate_out[...] = gate
    up_out[...] = up
    act[...] = (gate / (1.0 + jnp.exp(-gate)) * up).astype(BF16)


def gate_up_product(h, w_gu, a_gu, b_gu, pick, tile=512):
    rows, width = h.shape
    units, low = w_gu.shape[1] // 2, pick.shape[1]
    n = units // tile
    left = lambda depth: pl.BlockSpec((depth, tile), lambda i: (0, i))
    out = pl.BlockSpec((rows, tile), lambda i: (0, i))
    return pl.pallas_call(
        gate_up_kernel,
        grid=(n,),
        out_shape=[jax.ShapeDtypeStruct((rows, units), F32)] * 2
        + [
            jax.ShapeDtypeStruct((rows, units), BF16),
            jax.ShapeDtypeStruct((rows, 2 * low), BF16),
        ],
        in_specs=[
            fixed(rows, width),
            fixed(width, 2 * low),
            fixed(rows, low),
            left(width),
            pl.BlockSpec((width, tile), lambda i: (0, i + n)),
            left(low),
            pl.BlockSpec((low, tile), lambda i: (1, i)),
        ],
        out_specs=[out, out, out, fixed(rows, 2 * low)],
        scratch_shapes=[pltpu.VMEM((rows, 2 * low), BF16)],
        compiler_params=BIG,
        cost_estimate=pl.CostEstimate(
            flops=4 * rows * width * units, bytes_accessed=4 * width * units, transcendentals=0
        ),
        name="gate_up_product",
    )(h, a_gu, pick, w_gu, w_gu, b_gu, b_gu)


def ff_back_kernel(
    parts, steps, d_ff, b_down, pick, w_down, a_down, gate, up, w_g, w_u, b_g, b_u, a_gu, *refs
):
    outs, (d_gate_out, d_up_out, u_out, u_down_out, acc, u_g, u_u, u_down) = refs[:parts], refs[parts:]
    i = pl.program_id(0)

    @pl.when(i == 0)
    def _():
        u_down[...] = (mm_nt(d_ff[...], b_down[...]) * pick[...]).astype(BF16)
        u_down_out[...] = u_down[...]

    d_act = mm(d_ff[...], w_down[...]) + mm_nt(u_down[...], a_down[...])
    g = gate[...]
    sigmoid = 1.0 / (1.0 + jnp.exp(-g))
    silu = g * sigmoid
    d_gate = (d_act * up[...] * (sigmoid + silu * (1.0 - sigmoid))).astype(BF16)
    d_up = (d_act * silu).astype(BF16)
    d_gate_out[...] = d_gate
    d_up_out[...] = d_up
    part = mm_nt(d_gate, w_g[...]) + mm_nt(d_up, w_u[...])
    part_g, part_u = mm_nt(d_gate, b_g[...]), mm_nt(d_up, b_u[...])

    @pl.when(i == 0)
    def _():
        acc[...] = part
        u_g[...] = part_g
        u_u[...] = part_u

    @pl.when(i > 0)
    def _():
        acc[...] += part
        u_g[...] += part_g
        u_u[...] += part_u

    @pl.when(i == steps - 1)
    def _():
        low = pick.shape[1]
        last_g = (u_g[...] * pick[...]).astype(BF16)
        last_u = (u_u[...] * pick[...]).astype(BF16)
        u_out[:, :low] = last_g
        u_out[:, low:] = last_u
        size = acc.shape[0] // parts
        for p in range(parts):
            at = slice(p * size, (p + 1) * size)
            outs[p][...] = (
                acc[at, :]
                + mm_nt(last_g[at], a_gu[:, :low])
                + mm_nt(last_u[at], a_gu[:, low:])
            ).astype(BF16)


def ff_back(d_ff, b_down, pick, w_down, a_down, gate, up, w_gu, b_gu, a_gu, parts, tile=512):
    rows, width = d_ff.shape
    units, low = gate.shape[1], pick.shape[1]
    n = units // tile
    size = rows // parts
    column = lambda depth: pl.BlockSpec((depth, tile), lambda i: (0, i))
    return pl.pallas_call(
        functools.partial(ff_back_kernel, parts, n),
        grid=(n,),
        out_shape=[jax.ShapeDtypeStruct((size, width), BF16)] * parts
        + [jax.ShapeDtypeStruct((rows, units), BF16)] * 2
        + [
            jax.ShapeDtypeStruct((rows, 2 * low), BF16),
            jax.ShapeDtypeStruct((rows, low), BF16),
        ],
        in_specs=[
            fixed(rows, width),
            fixed(low, width),
            fixed(rows, low),
            column(width),
            pl.BlockSpec((tile, low), lambda i: (i, 0)),
            column(rows),
            column(rows),
            column(width),
            pl.BlockSpec((width, tile), lambda i: (0, i + n)),
            column(low),
            pl.BlockSpec((low, tile), lambda i: (1, i)),
            fixed(width, 2 * low),
        ],
        out_specs=[fixed(size, width)] * parts
        + [column(rows), column(rows), fixed(rows, 2 * low), fixed(rows, low)],
        scratch_shapes=[
            pltpu.VMEM((rows, width), F32),
            pltpu.VMEM((rows, low), F32),
            pltpu.VMEM((rows, low), F32),
            pltpu.VMEM((rows, low), BF16),
        ],
        compiler_params=BIG,
        cost_estimate=pl.CostEstimate(
            flops=6 * rows * width * units, bytes_accessed=6 * width * units, transcendentals=0
        ),
        name="ff_back",
    )(d_ff, b_down, pick, w_down, a_down, gate, up, w_gu, w_gu, b_gu, b_gu, a_gu)


def blocked(parts):
    zeros = lambda a, b: jnp.zeros((a.shape[0], b.shape[1]), a.dtype)
    return jnp.concatenate(
        [
            jnp.concatenate([a if a is b else zeros(a, b) for b in parts], axis=1)
            for a in parts
        ],
        axis=0,
    )


def local(
    layer_input,
    cotangent,
    query_key_value_weight,
    output_weight,
    gate_up_weight,
    down_weight,
    input_first_factor,
    output_first_factor,
    down_first_factor,
    query_key_value_second,
    gate_up_second_factor,
    output_down_second_factor,
    norm_gain_table,
    sequence_adapter,
    block_sequence,
    block_position,
):
    tp, tp_rank = lax.axis_size("tp"), lax.axis_index("tp")
    seqs, seq_rank = lax.axis_size("seq"), lax.axis_index("seq")
    own_rows, width = layer_input.shape
    rows = own_rows * tp
    part = own_rows // 2
    my_blocks = rows // BLK
    cols = query_key_value_weight.shape[2]
    heads = cols // HEAD_DIM
    hidden_cols = gate_up_weight.shape[2]
    k_rows = query_key_value_weight.shape[1]
    slots_a = input_first_factor.shape[2]
    rank_cols = output_first_factor.shape[1]
    group = seqs // heads
    head_rank, group_rank = seq_rank // group, seq_rank % group
    n_seq = sequence_adapter.shape[0]
    groups = (0, 1)

    a_part = k_rows // tp
    b_part = width // tp
    a_mine = lax.dynamic_slice_in_dim(input_first_factor, tp_rank * a_part, a_part, 1)
    b_mine = lax.dynamic_slice_in_dim(output_down_second_factor, tp_rank * b_part, b_part, 2)
    first = jnp.concatenate(
        [
            query_key_value_weight.transpose(1, 0, 2).reshape(k_rows, 3 * cols),
            query_key_value_second.transpose(1, 0, 2).reshape(rank_cols, 3 * cols),
            a_mine[:3].reshape(-1, 3 * cols),
        ],
        axis=0,
    )
    x_parts = [layer_input] + [
        lax.ppermute(layer_input, "tp", [(i, i ^ mask) for i in range(tp)]) for mask in range(1, tp)
    ]
    first = lax.all_gather(first, "seq", axis=0)
    pieces = [
        output_weight.T,
        output_first_factor.T,
        b_mine.reshape(-1, cols),
        a_mine[3:].reshape(-1, cols),
        down_first_factor.T.reshape(-1, cols),
        gate_up_second_factor.reshape(-1, cols),
    ]
    packed = jnp.concatenate(pieces, axis=0)
    x_parts, packed, w_gu, w_down = lax.optimization_barrier(
        (
            x_parts,
            packed,
            gate_up_weight.transpose(1, 0, 2).reshape(k_rows, 2 * hidden_cols),
            down_weight.T,
        )
    )
    packed = lax.all_gather(packed, "seq", axis=0)
    split, at = [], 0
    for piece in pieces:
        split.append(packed[:, at : at + piece.shape[0]])
        at += piece.shape[0]
    w_gu = lax.all_gather(w_gu, "seq", axis=0, tiled=True)
    w_down = lax.all_gather(w_down, "seq", axis=0, tiled=True)

    tp_order, seq_order = list(range(bits_of(tp))), list(range(bits_of(seqs)))
    a_qkv = first[:, k_rows + rank_cols :].reshape(seqs, 3, a_part, slots_a)
    a_qkv = a_qkv.transpose(0, 2, 1, 3).reshape(seqs, a_part, 3 * slots_a)
    a_parts = [a_qkv] + [
        lax.ppermute(a_qkv, "tp", [(i, i ^ mask) for i in range(tp)]) for mask in range(1, tp)
    ]
    a_qkv = jnp.zeros((seqs, tp, a_part, 3 * slots_a), BF16)
    for mask, value in enumerate(a_parts):
        a_qkv = lax.dynamic_update_slice(a_qkv, value[:, None], (0, tp_rank ^ mask, 0, 0))
    a_qkv = a_qkv.reshape(width, 3 * slots_a)
    b_qkv = first[:, k_rows : k_rows + rank_cols].reshape(slots_a, 3 * cols)
    b_qkv = blocked([b_qkv[:, i * cols : (i + 1) * cols] for i in range(3)])
    w_o = split[0].reshape(width, cols)
    a_o = split[1].reshape(slots_a, cols).T
    shared = gather_order(jnp.concatenate(split[2:4], axis=1), "tp", tp, tp_order)
    b_size = split[2].shape[1]
    b_od = (
        shared[:, :, :b_size]
        .reshape(tp, seqs, 2, rank_cols, b_part)
        .transpose(2, 1, 3, 0, 4)
        .reshape(2, slots_a, width)
    )
    a_gu = (
        shared[:, :, b_size:]
        .reshape(tp, seqs, 2, a_part, slots_a)
        .transpose(1, 0, 3, 2, 4)
        .reshape(width, 2 * slots_a)
    )
    a_down = split[4].reshape(slots_a, hidden_cols).T
    b_gu = (
        split[5]
        .reshape(seqs, 2, rank_cols, hidden_cols)
        .transpose(1, 0, 2, 3)
        .reshape(2 * slots_a, hidden_cols)
    )

    runs = row_runs(tp)
    piece_at = jnp.stack([2 * (tp_rank ^ mask) + which for mask, which in runs]).astype(jnp.int32)
    token = (piece_at[:, None] * part + jnp.arange(part, dtype=jnp.int32)[None, :]).reshape(-1)
    token_block, offset = token // BLK, token % BLK
    block_ids = seq_rank * my_blocks + jnp.arange(my_blocks, dtype=jnp.int32)
    place_blocks = block_position[block_ids]
    adapter_blocks = sequence_adapter[block_sequence[block_ids]]
    in_block = token_block[:, None] == jnp.arange(my_blocks, dtype=jnp.int32)[None, :]
    pick = lambda per_block: jnp.sum(jnp.where(in_block, per_block[None, :], 0), axis=1)
    select = (
        jnp.arange(slots_a, dtype=jnp.int32)[None, :] // ADAPTER_RANK
        == pick(adapter_blocks)[:, None]
    ).astype(F32) * 2.0
    half = rows // 2
    selects = [select[:half], select[half:]]
    start = jnp.where(place_blocks < PROMPT_BLOCKS, place_blocks, PROMPT_BLOCKS) * BLK
    position = pick(start) + offset
    frequency = THETA ** (-(jnp.arange(HEAD_DIM // 2, dtype=F32) * 2.0) / HEAD_DIM)
    angles = position.astype(F32)[:, None] * frequency[None, :]
    cosine, sine = jnp.cos(angles), jnp.sin(angles)
    cs = jnp.concatenate([cosine, cosine, -sine, sine], axis=1)

    owner = (
        ((head_rank - jnp.arange(heads)) % heads)[None, :] * group
        + ((group_rank + jnp.arange(group)) % group)[:, None]
    ).reshape(-1)
    held = (owner[:, None] * my_blocks + jnp.arange(my_blocks)[None, :]).reshape(-1)
    held_seq = block_sequence[held].astype(jnp.int32)
    held_place = block_position[held].astype(jnp.int32)
    prompt_count = n_seq * PROMPT_BLOCKS
    wanted = jnp.arange(prompt_count, dtype=jnp.int32)
    code = jnp.where(held_place < PROMPT_BLOCKS, held_seq * PROMPT_BLOCKS + held_place, -1)
    prompt_at = jnp.sum(
        jnp.where(
            code[None, :] == wanted[:, None], jnp.arange(held.shape[0], dtype=jnp.int32)[None, :], 0
        ),
        axis=1,
    ).astype(jnp.int32)
    own_blocks = heads * my_blocks
    tables = (held_seq[:own_blocks], held_place[:own_blocks], prompt_at)
    head_order = ((head_rank + jnp.arange(heads)) % heads).astype(jnp.int32)

    def head_shift(value, by):
        if by == 0:
            return value
        return lax.ppermute(
            value,
            "seq",
            [
                (h * group + j, ((h + by) % heads) * group + j)
                for h in range(heads)
                for j in range(group)
            ],
        )

    def group_shift(value, by):
        return lax.ppermute(
            value,
            "seq",
            [
                (h * group + j, h * group + (j + by) % group)
                for h in range(heads)
                for j in range(group)
            ],
        )

    own = lambda value, i: value[i * part : (i + 1) * part].astype(F32)
    x = jnp.concatenate(
        [x_parts[mask][which * part : (which + 1) * part] for mask, which in runs], axis=0
    )
    gain = lax.dynamic_slice_in_dim(norm_gain_table[:2], tp_rank * cols, cols, 1)
    pick3 = jnp.tile(select, (1, 3))
    latents = (mm(x, a_qkv) * pick3).astype(BF16)
    z, squares = qkv_product(
        x, latents, first, first[:, k_rows : k_rows + rank_cols].reshape(slots_a, 3 * cols), k_rows, cols
    )
    squares = sum_rows(squares[:2].reshape(2, rows), tp)
    inv = lax.rsqrt(squares / width + EPS)
    spread = spread_heads(head_order, piece_at, z, inv.T, cs, gain, heads)
    near = [head_shift(spread[heads + k], k) for k in range(heads)]
    queries = [head_shift(spread[k], k) for k in range(heads)]
    far = [group_shift(near[k], -j) for j in range(1, group) for k in range(heads)]
    attended = attend(tables, queries, near, far, prompt_count)
    heads_out = collect_heads(
        head_order, piece_at, [head_shift(attended[k], -k) for k in range(heads)]
    )

    def norm_back(values_in, inv, scaled):
        return inv * scaled - values_in * inv**3 * jnp.mean(scaled * values_in, axis=1, keepdims=True)

    def inverse_norm(values_in):
        return lax.rsqrt(jnp.mean(values_in * values_in, axis=1, keepdims=True) + EPS)

    *far_part, o_latent1 = add_product(heads_out[1], w_o, a_o, b_od[0], selects[1], 2)
    near_part, o_latent0 = add_product(heads_out[0], w_o, a_o, b_od[0], selects[0], 1)
    attn_out = scatter_groups(near_part, far_part, tp)
    scale_o = [inverse_norm(value) for value in attn_out]
    hidden = [
        own(layer_input, i) + attn_out[i] * scale_o[i] * norm_gain_table[2] for i in groups
    ]
    h_low = gather_groups([value.astype(BF16) for value in hidden], tp)

    gates, ups, acts, gu_latents = zip(
        *[gate_up_product(h_low[g], w_gu, a_gu, b_gu, selects[g]) for g in groups]
    )
    *far_part, d_latent1 = add_product(acts[1], w_down, a_down, b_od[1], selects[1], 2)
    near_part, d_latent0 = add_product(acts[0], w_down, a_down, b_od[1], selects[0], 1)
    ff_out = scatter_groups(near_part, far_part, tp)
    scale_f = [inverse_norm(value) for value in ff_out]
    output = jnp.concatenate(
        [hidden[i] + ff_out[i] * scale_f[i] * norm_gain_table[3] for i in groups], axis=0
    )

    d_ffs = gather_groups(
        [
            norm_back(ff_out[i], scale_f[i], own(cotangent, i) * norm_gain_table[3]).astype(BF16)
            for i in groups
        ],
        tp,
    )
    backs = [
        ff_back(
            d_ffs[g], b_od[1], selects[g], w_down, a_down, gates[g], ups[g], w_gu, b_gu, a_gu, 1 + g
        )
        for g in groups
    ]
    summed = scatter_groups(backs[0][0], backs[1][:2], tp)
    d_gates, d_ups, u_gus, u_downs = zip(*[back[-4:] for back in backs])
    d_hidden = [own(cotangent, i) + summed[i] for i in groups]
    d_attn = [
        norm_back(attn_out[i], scale_o[i], d_hidden[i] * norm_gain_table[2]).astype(BF16)
        for i in groups
    ]
    d_latents = (d_latent0, d_latent1)
    both_groups = lambda f: f(0) + f(1)
    grad_a_down = both_groups(lambda g: mm_tn(u_downs[g], acts[g]))
    grad_b_down = both_groups(lambda g: mm_tn(d_latents[g], d_ffs[g]))
    grad_a_gu = both_groups(lambda g: mm_tn(h_low[g], u_gus[g]))
    grad_b_gate = both_groups(lambda g: mm_tn(gu_latents[g][:, :slots_a], d_gates[g]))
    grad_b_up = both_groups(lambda g: mm_tn(gu_latents[g][:, slots_a:], d_ups[g]))
    lane = 2 * slots_a
    shards = lambda value: value.astype(BF16).reshape(seqs, -1, lane)
    early = jnp.concatenate(
        [
            shards(grad_a_gu),
            shards(grad_b_down),
            shards(grad_a_down),
            shards(grad_b_gate),
            shards(grad_b_up),
        ],
        axis=1,
    )

    *d_rows, early = gather_groups(d_attn, tp, early)
    early = lax.psum_scatter(early, "seq", scatter_dimension=0, tiled=False)
    o_latents = (o_latent0, o_latent1)
    u_os, grads = [], []
    for g in groups:
        u_os.append((mm_nt(d_rows[g], b_od[0]) * selects[g]).astype(BF16))
        d_heads = (mm(d_rows[g], w_o) + mm_nt(u_os[g], a_o)).astype(BF16)
        grads.append(
            [
                head_shift(
                    lax.dynamic_slice_in_dim(d_heads, head_order[k] * HEAD_DIM, HEAD_DIM, 1), k
                )
                for k in range(heads)
            ]
        )
    grad_a_o = both_groups(lambda g: mm_tn(u_os[g], heads_out[g]))
    grad_b_o = both_groups(lambda g: mm_tn(o_latents[g], d_rows[g]))
    late_o = jnp.concatenate(
        [
            grad_b_o.astype(BF16).reshape(seqs, -1, cols),
            grad_a_o.astype(BF16).reshape(seqs, -1, cols),
        ],
        axis=1,
    )
    late_o = scatter_order(late_o, "seq", seqs, seq_order)
    grads = [grads[g][k] for k in range(heads) for g in groups]
    grads[-1], early = lax.optimization_barrier((grads[-1], early))
    results = list(attend_back(tables, piece_at, queries, near, far, grads, prompt_count))
    dqs = [head_shift(results[k], -k) for k in range(heads)]
    d_kv = results[heads].reshape(2, heads, rows, HEAD_DIM)
    others = [
        group_shift(results[heads + j], j).reshape(2, heads, rows, HEAD_DIM) for j in range(1, group)
    ]
    dkvs = []
    for k in range(heads):
        total = d_kv[:, k].astype(F32)
        for other in others:
            total = total + other[:, k].astype(F32)
        dkvs.append(head_shift(total.astype(BF16), -k))
    scaled, parts = unturn_heads(head_order, piece_at, dqs, dkvs, z, cs, gain)
    parts = sum_rows(parts.T, tp) / width
    coef = jnp.concatenate([inv, inv**3 * parts], axis=0)
    dz = norm_back_heads(head_order, piece_at, dkvs, scaled, z, coef.T)
    us = (mm_nt(dz, b_qkv) * pick3).astype(BF16)
    far_part = list(back_product(dz, 1, first, k_rows, us, a_qkv, 2))
    far_part[0], us = lax.optimization_barrier((far_part[0], us))
    grad_a_qkv = mm_tn(x, us)
    grad_b_qkv = mm_tn(latents, dz)
    lane3 = 3 * slots_a
    grad_b_qkv = jnp.concatenate(
        [
            grad_b_qkv[i * slots_a : (i + 1) * slots_a, i * cols : (i + 1) * cols]
            for i in range(3)
        ],
        axis=1,
    )
    late = jnp.concatenate(
        [
            grad_a_qkv.astype(BF16).reshape(seqs, k_rows, lane3),
            grad_b_qkv.astype(BF16).reshape(seqs, -1, lane3),
        ],
        axis=1,
    )
    dz, late = lax.optimization_barrier((dz, late))
    (near_part,) = back_product(dz, 0, first, k_rows, us, a_qkv, 1)
    summed = scatter_groups(near_part, far_part, tp)
    input_grad = jnp.concatenate([d_hidden[i] + summed[i] for i in groups], axis=0)

    late = scatter_order(late, "seq", seqs, seq_order)
    sum_tp = lambda value: sum_all(value.astype(BF16), "tp", tp).astype(F32)
    grad_a_qkv = sum_tp(late[:k_rows])
    grad_b_qkv = late[k_rows:].reshape(rank_cols, 3, cols).transpose(1, 0, 2)
    down_size = rank_cols * width // lane
    both = sum_tp(early[: k_rows + down_size])
    grad_a_gu, grad_b_down = both[:k_rows], both[k_rows:].reshape(rank_cols, width)
    a_size = rank_cols * hidden_cols // lane
    rest = early[k_rows + down_size :].astype(F32)
    grad_a_down = rest[:a_size].reshape(rank_cols, hidden_cols).T
    grad_b_gu = rest[a_size:].reshape(2, rank_cols, hidden_cols)
    o_size = rank_cols * width // cols
    grad_b_o = sum_tp(late_o[:o_size]).reshape(rank_cols, width)
    grad_a_o = late_o[o_size:].T
    grad_a_in = jnp.stack(
        [grad_a_qkv[:, i * slots_a : (i + 1) * slots_a] for i in range(3)]
        + [grad_a_gu[:, i * slots_a : (i + 1) * slots_a] for i in range(2)]
    )
    grad_b_out = jnp.stack([grad_b_o, grad_b_down])
    return (output, input_grad, grad_a_in, grad_a_o, grad_a_down, grad_b_qkv, grad_b_gu, grad_b_out)


def solution(mesh):
    return jax.shard_map(
        local,
        mesh=mesh,
        in_specs=(
            P(("seq", "tp"), None),
            P(("seq", "tp"), None),
            P(None, "seq", "tp"),
            P("tp", "seq"),
            P(None, "seq", "tp"),
            P("tp", "seq"),
            P(None, "seq", None),
            P("tp", "seq"),
            P("tp", "seq"),
            P(None, "seq", "tp"),
            P(None, "seq", "tp"),
            P(None, "seq", None),
            P(),
            P(),
            P(),
            P(),
        ),
        out_specs=(
            P(("seq", "tp"), None),
            P(("seq", "tp"), None),
            P(None, "seq", None),
            P("tp", "seq"),
            P("tp", "seq"),
            P(None, "seq", "tp"),
            P(None, "seq", "tp"),
            P(None, "seq", None),
        ),
        check_vma=False,
    )
```

time: 985 us -> 950 us (0.964)
  Pallas kernels: 54.3 us -> 208 us
  matrix products: 158 us -> 36.1 us
  waiting for transfers between devices: 458 us -> 421 us
  other arithmetic: 68 us -> 47.1 us
    pallas_call x0 -> x15, Pallas kernels: none -> 154 us  [the longest x2 45.6 us: ff_back(): pl.pallas_call(functools.partial(ff_back_kernel, parts, n), grid=(n,), ou...]
    ppermute x38 -> x42, waiting for transfers between devices: 188 us -> 85.6 us  [flip(): return lax.ppermute(value, axis, [(i, i ^ 1 << bit) for i in range(count)])]
    dot_general x21 -> x5, matrix products: 79.7 us -> 5.09 us  [mm_nt(): lax.dot_general(a, b, (((1,), (1,)), ((), ())), preferred_element_type=F32)]
    all_gather x4 -> x3, waiting for transfers between devices: 0.06 us -> 67.9 us  [the longest x1 67.8 us: local(): first = lax.all_gather(first, 'seq', axis=0)]
    ppermute x0 -> x12, waiting for transfers between devices: none -> 66 us  [the longest x3 25.9 us: local(): lax.ppermute(layer_input, 'tp', [(i, i ^ mask) for i in range(tp)])]
    dot_general x19 -> x3, matrix products: 56.7 us -> 8.06 us  [mm(): return jnp.dot(a, b, preferred_element_type=F32)]
    psum x1 -> x0, waiting for transfers between devices: 44.1 us -> none  [local(): lax.psum(grad_a_in.astype(BF16), 'tp').astype(F32)]
    reduce_scatter x6 -> x1, waiting for transfers between devices: 44.1 us -> 8.68 us  [local(): early = lax.psum_scatter(early, 'seq', scatter_dimension=0, tiled=False)]
  transfers between devices with their start and end apart: 67 -> 85, of which waited for: 41 -> 40; matrix products, arithmetic and copies ran while one was open for 24% -> 17% of each run, Pallas kernels for 2% -> 14%
where the time goes in v2:
time: 950 us; the launch traced here: 943 us
  waiting for transfers between devices  421 us (44%)
  Pallas kernels  208 us (22%)
  starting transfers between devices  109 us (11%)
  local copies, waits for them, and re-layouts  103 us (11%)
  other arithmetic  47.1 us (5%)
  matrix products  36.1 us (4%)
  between operations  18.8 us (2%)
    ppermute x21, waiting for transfers between devices, head_shift(): lax.ppermute(value, 'seq', [(h * group + j, (h + by) % heads * group + j)...  168 us
    ppermute x42, waiting for transfers between devices, flip(): return lax.ppermute(value, axis, [(i, i ^ 1 << bit) for i in range(count)])  85.6 us
    all_gather x1, waiting for transfers between devices, local(): first = lax.all_gather(first, 'seq', axis=0)  67.8 us
    ppermute x42, starting transfers between devices, flip(): return lax.ppermute(value, axis, [(i, i ^ 1 << bit) for i in range(count)])  49.3 us
    pallas_call x2, Pallas kernels, ff_back(): pl.pallas_call(functools.partial(ff_back_kernel, parts, n), grid=(n,), ou...  45.6 us
    ppermute x21, starting transfers between devices, head_shift(): lax.ppermute(value, 'seq', [(h * group + j, (h + by) % heads * group + j)...  42.9 us
    unnamed x309, local copies, waits for them, and re-layouts  36.6 us
    pallas_call x1, Pallas kernels, attend_back(): pl.pallas_call(functools.partial(attend_back_kernel, slots, group, rows,...  32.8 us
  transfers between devices with their start and end apart: 85, of which 40 were waited for; matrix products, arithmetic and copies ran while one was open for 17% of the time, Pallas kernels for 14%

profile of v2, /device:TPU:0, one launch (start us, length us, event | category | flops | bytes accessed | tf_op | source)
XLA Modules:
  0.0 942.5 jit_solution(1353422659053489277)
XLA Ops:
  20.5 8.5 collective-permute-done
  29.0 17.5 %collective-permute-done.1 = bf16[192,2048]{1,0:T(8,128)(2,1)} collective-permute-done((bf16[192,2048]{1,0:T(8,128)(2,1)}, bf16[192,2048]{1,0:T(8,128)(2,1)}, u32[]{:S(2)}, u32[]{:S(2)}) %collective-permute-start.1) | collective-permute-done | bytes 786464 | tf_op jit(solution)/shard_map/ppermute | solution.py:836
  71.5 23.4 %all-gather.13.cloned.1.call-done = bf16[4224,512]{1,0:T(8,128)(2,1)} async-done(((bf16[528,512]{1,0:T(8,128)(2,1)}), bf16[4224,512]{1,0:T(8,128)(2,1)}) %all-gather.13.cloned.1.call-update) | async-done | bytes 4325392 | tf_op jit(solution)/shard_map/all_gather | solution.py:856
  99.3 67.8 %all-gather.11.cloned.1.call-done = bf16[2304,1536]{1,0:T(8,128)(2,1)} async-done(((bf16[288,1536]{1,0:T(8,128)(2,1)}), bf16[2304,1536]{1,0:T(8,128)(2,1)}) %all-gather.11.cloned.1.call-update) | async-done | bytes 7077904 | tf_op jit(solution)/shard_map/all_gather | solution.py:838
  184.3 10.2 %collective-permute-done.4 = bf16[8,64,384]{2,1,0:T(8,128)(2,1)S(1)} collective-permute-done((bf16[8,64,384]{2,1,0:T(8,128)(2,1)}, bf16[8,64,384]{2,1,0:T(8,128)(2,1)S(1)}, u32[]{:S(2)}, u32[]{:S(2)}) %collective-permute-start.4) | collective-permute-done | bytes 393248 | tf_op jit(solution)/shard_map/ppermute | solution.py:868
  199.8 10.4 %qkv_product.1 = (f32[768,1536]{1,0:T(8,128)}, f32[3,768,1]{2,1,0:T(8,128)}) custom-call(bf16[768,2048]{1,0:T(8,128)(2,1)} %slice_dynamic-update-slice_fusion.x, bf16[768,384]{1,0:T(8,128)(2,1)} %fusion.7.latent, bf16[8,288,1536]{2,1,0:T(8,128)(2,1)} %bitcast.282, bf16[128,1536]{1,0:T(8,128)(2,1)} %bitcast.330), custom_call_target="tpu_custom_call" | custom-call | flops 4831838208 | bytes 7077888 | tf_op jit(solution)/shard_map/qkv_product/pallas_call | solution.py:533
  222.3 20.2 %collective-permute-done.7 = f32[2,8,96]{2,1,0:T(8,128)S(1)} collective-permute-done((f32[2,8,96]{2,1,0:T(8,128)S(1)}, f32[2,8,96]{2,1,0:T(8,128)S(1)}, u32[]{:S(2)}, u32[]{:S(2)}) %collective-permute-start.7) | collective-permute-done | bytes 6176 | tf_op jit(solution)/shard_map/ppermute | solution.py:127
  246.0 7.2 spread_heads.1
  264.3 84.2 %collective-permute-done.10.refs_2_ = bf16[768,128]{1,0:T(8,128)(2,1)S(1)} collective-permute-done((bf16[768,128]{1,0:T(8,128)(2,1)S(1)}, bf16[768,128]{1,0:T(8,128)(2,1)S(1)}, u32[]{:S(2)}, u32[]{:S(2)}) %collective-permute-start.10) | collective-permute-done | bytes 196640 | tf_op jit(solution)/shard_map/ppermute | solution.py:945
  350.5 6.3 collective-permute-start.9
  363.0 21.6 %attend.1 = (bf16[768,128]{1,0:T(8,128)(2,1)}, bf16[768,128]{1,0:T(8,128)(2,1)}, bf16[768,128]{1,0:T(8,128)(2,1)}, bf16[768,128]{1,0:T(8,128)(2,1)}) custom-call(s32[24]{0:T(128)} %bitcast.362, s32[24]{0:T(128)} %bitcast.364, s32[24]{0:T(128)} %select_reduce_fusion.2.prompt_at, bf16[768,128]{1,0:T(8,128)(2,1)} %get-tuple-element.84.refs_0_, ...), custom_call_target="tpu_custom_call" | custom-call | flops 1811939328 | bytes 4718592 | tf_op jit(solution)/shard_map/attend/pallas_call | solution.py:299
  384.7 6.6 collective-permute-start.19
  394.7 8.8 collective-permute-done.19.refs_1_
  403.5 27.5 %collective-permute-done.20.refs_2_ = bf16[768,128]{1,0:T(8,128)(2,1)S(1)} collective-permute-done((bf16[768,128]{1,0:T(8,128)(2,1)}, bf16[768,128]{1,0:T(8,128)(2,1)S(1)}, u32[]{:S(2)}, u32[]{:S(2)}) %collective-permute-start.20) | collective-permute-done | bytes 196640 | tf_op jit(solution)/shard_map/ppermute | solution.py:945
  448.3 6.7 collective-permute-done.24
  461.6 7.7 collective-permute-done.25
  473.4 11.1 %collective-permute-done.26 = bf16[96,2048]{1,0:T(8,128)(2,1)S(1)} collective-permute-done((bf16[96,2048]{1,0:T(8,128)(2,1)S(1)}, bf16[96,2048]{1,0:T(8,128)(2,1)S(1)}, u32[]{:S(2)}, u32[]{:S(2)}) %collective-permute-start.26) | collective-permute-done | bytes 393248 | tf_op jit(solution)/shard_map/ppermute | solution.py:41
  501.6 14.5 %gate_up_product.3 = (f32[384,2048]{1,0:T(8,128)}, f32[384,2048]{1,0:T(8,128)}, bf16[384,2048]{1,0:T(8,128)(2,1)}, bf16[384,256]{1,0:T(8,128)(2,1)}) custom-call(bf16[384,2048]{1,0:T(8,128)(2,1)} %copy-done.8, bf16[2048,256]{1,0:T(8,128)(2,1)} %bitcast.285, f32[384,128]{1,0:T(8,128)} %get-tuple-element.249.pick, ...), custom_call_target="tpu_custom_call" | custom-call | flops 6442450944 | bytes 16777216 | tf_op jit(solution)/shard_map/gate_up_product/pallas_call | solution.py:654
  516.1 8.7 add_product.7
  527.5 14.5 %gate_up_product.2 = (f32[384,2048]{1,0:T(8,128)}, f32[384,2048]{1,0:T(8,128)}, bf16[384,2048]{1,0:T(8,128)(2,1)}, bf16[384,256]{1,0:T(8,128)(2,1)}) custom-call(bf16[384,2048]{1,0:T(8,128)(2,1)} %pad_maximum_fusion.2.h, bf16[2048,256]{1,0:T(8,128)(2,1)} %bitcast.286, f32[384,128]{1,0:T(8,128)} %get-tuple-element.248.pick, ...), custom_call_target="tpu_custom_call" | custom-call | flops 6442450944 | bytes 16777216 | tf_op jit(solution)/shard_map/gate_up_product/pallas_call | solution.py:654
  542.0 9.3 add_product.6
  554.9 9.6 %collective-permute-done.33 = bf16[96,2048]{1,0:T(8,128)(2,1)S(1)} collective-permute-done((bf16[96,2048]{1,0:T(8,128)(2,1)S(1)}, bf16[96,2048]{1,0:T(8,128)(2,1)S(1)}, u32[]{:S(2)}, u32[]{:S(2)}) %collective-permute-start.33) | collective-permute-done | bytes 393248 | tf_op jit(solution)/shard_map/ppermute | solution.py:41
  568.0 7.9 collective-permute-done.37
  581.6 22.7 %ff_back.2 = (bf16[384,2048]{1,0:T(8,128)(2,1)}, bf16[384,2048]{1,0:T(8,128)(2,1)}, bf16[384,2048]{1,0:T(8,128)(2,1)}, bf16[384,256]{1,0:T(8,128)(2,1)}, bf16[384,128]{1,0:T(8,128)(2,1)}) custom-call(bf16[384,2048]{1,0:T(8,128)(2,1)} %pad_maximum_fusion.4.d_ff, bf16[128,2048]{1,0:T(8,128)(2,1)} %bitcast.318, f32[384,128]{1,0:T(8,128)} %get-tuple-element.248.pick, ...), custom_call_target="tpu_custom_call" | custom-call | flops 9663676416 | bytes 25165824 | tf_op jit(solution)/shard_map/ff_back/pallas_call | solution.py:738
  605.6 22.8 %ff_back.3 = (bf16[192,2048]{1,0:T(8,128)(2,1)}, bf16[192,2048]{1,0:T(8,128)(2,1)}, bf16[384,2048]{1,0:T(8,128)(2,1)}, bf16[384,2048]{1,0:T(8,128)(2,1)}, bf16[3...) custom-call(bf16[384,2048]{1,0:T(8,128)(2,1)} %copy-done.22, bf16[128,2048]{1,0:T(8,128)(2,1)} %bitcast.319, ...), custom_call_target="tpu_custom_call" | custom-call | flops 9663676416 | bytes 25165824 | tf_op jit(solution)/shard_map/ff_back/pallas_call | solution.py:738
  719.2 8.7 reduce-scatter.2.cloned.1.call-done
  732.4 32.8 %attend_back.1 = (bf16[768,128]{1,0:T(8,128)(2,1)}, bf16[768,128]{1,0:T(8,128)(2,1)}, bf16[768,128]{1,0:T(8,128)(2,1)}, bf16[768,128]{1,0:T(8,128)(2,1)}, bf16[2...) custom-call(s32[24]{0:T(128)} %bitcast.363, s32[24]{0:T(128)} %bitcast.365, s32[24]{0:T(128)} %select_reduce_fusion.2.prompt_at, ...), custom_call_target="tpu_custom_call" | custom-call | flops 4529848320 | bytes 9437184 | tf_op jit(solution)/shard_map/attend_back/pallas_call | solution.py:331
  786.9 41.4 %collective-permute-done.59.refs_2_ = bf16[768,128]{1,0:T(8,128)(2,1)S(1)} collective-permute-done((bf16[768,128]{1,0:T(8,128)(2,1)S(1)}, bf16[768,128]{1,0:T(8,128)(2,1)S(1)}, u32[]{:S(2)}, u32[]{:S(2)}) %collective-permute-start.59) | collective-permute-done | bytes 196640 | tf_op jit(solution)/shard_map/ppermute | solution.py:945
  829.4 7.8 unturn_heads.1
  853.7 7.1 norm_back_heads.1.a
  866.1 7.5 back_product.2
  899.0 7.6 back_product.3
  (696 shorter events, 355.0 us)
Async XLA Ops:
  7.2 87.7 %all-gather.13.cloned.1.call-start = ((), (), s32[]{:S(2)}) async-start(), calls=%async_computation.5 | async-start | bytes 4866048 | tf_op jit(solution)/shard_map/all_gather | solution.py:856
  7.2 21.7 %collective-permute-start = (bf16[192,2048]{1,0:T(8,128)(2,1)}, bf16[192,2048]{1,0:T(8,128)(2,1)}, u32[]{:S(2)}, u32[]{:S(2)}) collective-permute-start(bf16[192,2048]{1,0:T(8,128)(2,1)} %param.16), channel_id=1, source_target_pairs={{0,1},{1,0},{2,3},{3,2},{4,5},{5,4},{6,7},{7,6},{8,9},{9,8},{10,11... | collective-permute-start | bytes 2359304 | tf_op jit(solution)/shard_map/ppermute | solution.py:836
  10.3 36.2 %collective-permute-start.1 = (bf16[192,2048]{1,0:T(8,128)(2,1)}, bf16[192,2048]{1,0:T(8,128)(2,1)}, u32[]{:S(2)}, u32[]{:S(2)}) collective-permute-start(bf16[192,2048]{1,0:T(8,128)(2,1)} %param.16), channel_id=1, source_target_pairs={{0,2},{1,3},{2,0},{3,1},{4,6},{5,7},{6,4},{7,5},{8,10},{9,11},{10,... | collective-permute-start | bytes 2359304 | tf_op jit(solution)/shard_map/ppermute | solution.py:836
  11.8 34.7 %collective-permute-start.2 = (bf16[192,2048]{1,0:T(8,128)(2,1)}, bf16[192,2048]{1,0:T(8,128)(2,1)}, u32[]{:S(2)}, u32[]{:S(2)}) collective-permute-start(bf16[192,2048]{1,0:T(8,128)(2,1)} %param.16), channel_id=1, source_target_pairs={{0,3},{1,2},{2,1},{3,0},{4,7},{5,6},{6,5},{7,4},{8,11},{9,10},{10,... | collective-permute-start | bytes 2359304 | tf_op jit(solution)/shard_map/ppermute | solution.py:836
  46.5 120.7 %all-gather.11.cloned.1.call-start = ((), (), s32[]{:S(2)}) async-start(), calls=%async_computation.4 | async-start | bytes 7962624 | tf_op jit(solution)/shard_map/all_gather | solution.py:838
  49.0 451.5 %all-gather.7.cloned.1.call-start = ((), (), s32[]{:S(2)}) async-start(), calls=%async_computation.1 | async-start | bytes 18874368 | tf_op jit(solution)/shard_map/all_gather | solution.py:861
  49.8 466.3 %all-gather.9.cloned.1.call-start = ((), (), s32[]{:S(2)}) async-start(), calls=%async_computation.2 | async-start | bytes 9437184 | tf_op jit(solution)/shard_map/all_gather | solution.py:862
  60.9 667.0 %reduce-scatter.2.cloned.1.call-start = ((), (), s32[]{:S(2)}) async-start(), calls=%async_computation.3 | async-start | bytes 3538944 | tf_op jit(solution)/shard_map/reduce_scatter | solution.py:1054
  96.0 76.4 %collective-permute-start.22 = (bf16[8,64,512]{2,1,0:T(8,128)(2,1)S(1)}, bf16[8,64,512]{2,1,0:T(8,128)(2,1)S(1)}, u32[]{:S(2)}, u32[]{:S(2)}) collective-permute-start(bf16[8,64,512]{2,1,0:T(8,128)(2,1)S(1)} %concatenate.174), channel_id=1, source_target_pairs={{0,1},{1,0},{2,3},{3,2},{4,5},{5,4},{6,7},{7,6},{8,9},{9,8},{10,11... | collective-permute-start | bytes 1572872 | tf_op jit(solution)/shard_map/ppermute | solution.py:41
  174.9 19.7 %collective-permute-start.4 = (bf16[8,64,384]{2,1,0:T(8,128)(2,1)}, bf16[8,64,384]{2,1,0:T(8,128)(2,1)S(1)}, u32[]{:S(2)}, u32[]{:S(2)}) collective-permute-start(bf16[8,64,384]{2,1,0:T(8,128)(2,1)} %reshape.567), channel_id=1, source_target_pairs={{0,2},{1,3},{2,0},{3,1},{4,6},{5,7},{6,4},{7,5},{8,10},{9,11},{10,... | collective-permute-start | bytes 1179656 | tf_op jit(solution)/shard_map/ppermute | solution.py:868
  218.0 43.9 %collective-permute-start.23 = (bf16[2,8,64,512]{3,2,1,0:T(8,128)(2,1)}, bf16[2,8,64,512]{3,2,1,0:T(8,128)(2,1)}, u32[]{:S(2)}, u32[]{:S(2)}) collective-permute-start(bf16[2,8,64,512]{3,2,1,0:T(8,128)(2,1)} %pad_maximum_fusion.8), channel_id=1, source_target_pairs={{0,2},{1,3},{2,0},{3,1},{4,6},{5,7},{6,4},{7,5},{8,10},{9,11},{10,... | collective-permute-start | bytes 3145736 | tf_op jit(solution)/shard_map/ppermute | solution.py:41
  219.5 23.0 %collective-permute-start.7 = (f32[2,8,96]{2,1,0:T(8,128)S(1)}, f32[2,8,96]{2,1,0:T(8,128)S(1)}, u32[]{:S(2)}, u32[]{:S(2)}) collective-permute-start(f32[2,8,96]{2,1,0:T(8,128)S(1)} %copy.219), channel_id=1, source_target_pairs={{0,2},{1,3},{2,0},{3,1},{4,6},{5,7},{6,4},{7,5},{8,10},{9,11},{10,... | collective-permute-start | bytes 18440 | tf_op jit(solution)/shard_map/ppermute | solution.py:127
  220.0 22.9 %collective-permute-start.8 = (f32[2,8,96]{2,1,0:T(8,128)S(1)}, f32[2,8,96]{2,1,0:T(8,128)S(1)}, u32[]{:S(2)}, u32[]{:S(2)}) collective-permute-start(f32[2,8,96]{2,1,0:T(8,128)S(1)} %copy.219), channel_id=1, source_target_pairs={{0,3},{1,2},{2,1},{3,0},{4,7},{5,6},{6,5},{7,4},{8,11},{9,10},{10,... | collective-permute-start | bytes 18440 | tf_op jit(solution)/shard_map/ppermute | solution.py:127
  253.2 95.3 %collective-permute-start.12 = (bf16[2,768,128]{2,1,0:T(8,128)(2,1)}, bf16[2,768,128]{2,1,0:T(8,128)(2,1)S(1)}, u32[]{:S(2)}, u32[]{:S(2)}) collective-permute-start(bf16[2,768,128]{2,1,0:T(8,128)(2,1)} %get-tuple-element.89), channel_id=1, source_target_pairs={{0,8},{4,12},{8,16},{12,20},{16,24},{20,28},{24,0},{28,4},{1,9},{5... | collective-permute-start | bytes 1179656 | tf_op jit(solution)/shard_map/ppermute | solution.py:945
  253.2 95.9 %collective-permute-start.13 = (bf16[2,768,128]{2,1,0:T(8,128)(2,1)}, bf16[2,768,128]{2,1,0:T(8,128)(2,1)}, u32[]{:S(2)}, u32[]{:S(2)}) collective-permute-start(bf16[2,768,128]{2,1,0:T(8,128)(2,1)} %get-tuple-element.90), channel_id=1, source_target_pairs={{0,16},{4,20},{8,24},{12,28},{16,0},{20,4},{24,8},{28,12},{1,17},{... | collective-permute-start | bytes 1179656 | tf_op jit(solution)/shard_map/ppermute | solution.py:945
  254.5 94.6 %collective-permute-start.14 = (bf16[2,768,128]{2,1,0:T(8,128)(2,1)}, bf16[2,768,128]{2,1,0:T(8,128)(2,1)}, u32[]{:S(2)}, u32[]{:S(2)}) collective-permute-start(bf16[2,768,128]{2,1,0:T(8,128)(2,1)} %get-tuple-element.91), channel_id=1, source_target_pairs={{0,24},{4,28},{8,0},{12,4},{16,8},{20,12},{24,16},{28,20},{1,25},{... | collective-permute-start | bytes 1179656 | tf_op jit(solution)/shard_map/ppermute | solution.py:945
  260.1 88.4 %collective-permute-start.10 = (bf16[768,128]{1,0:T(8,128)(2,1)S(1)}, bf16[768,128]{1,0:T(8,128)(2,1)S(1)}, u32[]{:S(2)}, u32[]{:S(2)}) collective-permute-start(bf16[768,128]{1,0:T(8,128)(2,1)S(1)} %copy-done.128), channel_id=1, source_target_pairs={{0,16},{4,20},{8,24},{12,28},{16,0},{20,4},{24,8},{28,12},{1,17},{... | collective-permute-start | bytes 589832 | tf_op jit(solution)/shard_map/ppermute | solution.py:945
  261.9 87.8 %collective-permute-start.11 = (bf16[768,128]{1,0:T(8,128)(2,1)S(1)}, bf16[768,128]{1,0:T(8,128)(2,1)S(1)}, u32[]{:S(2)}, u32[]{:S(2)}) collective-permute-start(bf16[768,128]{1,0:T(8,128)(2,1)S(1)} %copy-done.127), channel_id=1, source_target_pairs={{0,24},{4,28},{8,0},{12,4},{16,8},{20,12},{24,16},{28,20},{1,25},{... | collective-permute-start | bytes 589832 | tf_op jit(solution)/shard_map/ppermute | solution.py:945
  391.3 39.6 %collective-permute-start.20 = (bf16[768,128]{1,0:T(8,128)(2,1)}, bf16[768,128]{1,0:T(8,128)(2,1)S(1)}, u32[]{:S(2)}, u32[]{:S(2)}) collective-permute-start(bf16[768,128]{1,0:T(8,128)(2,1)} %get-tuple-element.94), channel_id=1, source_target_pairs={{0,16},{4,20},{8,24},{12,28},{16,0},{20,4},{24,8},{28,12},{1,17},{... | collective-permute-start | bytes 589832 | tf_op jit(solution)/shard_map/ppermute | solution.py:945
  391.3 39.6 %collective-permute-start.21 = (bf16[768,128]{1,0:T(8,128)(2,1)}, bf16[768,128]{1,0:T(8,128)(2,1)S(1)}, u32[]{:S(2)}, u32[]{:S(2)}) collective-permute-start(bf16[768,128]{1,0:T(8,128)(2,1)} %get-tuple-element.95), channel_id=1, source_target_pairs={{0,8},{4,12},{8,16},{12,20},{16,24},{20,28},{24,0},{28,4},{1,9},{5... | collective-permute-start | bytes 589832 | tf_op jit(solution)/shard_map/ppermute | solution.py:945
  524.8 26.5 %collective-permute-start.32 = (bf16[192,2048]{1,0:T(8,128)(2,1)}, bf16[192,2048]{1,0:T(8,128)(2,1)S(1)}, u32[]{:S(2)}, u32[]{:S(2)}) collective-permute-start(bf16[192,2048]{1,0:T(8,128)(2,1)} %get-tuple-element.107), channel_id=1, source_target_pairs={{0,2},{1,3},{2,0},{3,1},{4,6},{5,7},{6,4},{7,5},{8,10},{9,11},{10,... | collective-permute-start | bytes 2359304 | tf_op jit(solution)/shard_map/ppermute | solution.py:41
  526.5 24.8 %collective-permute-start.34 = (bf16[192,2048]{1,0:T(8,128)(2,1)}, bf16[192,2048]{1,0:T(8,128)(2,1)S(1)}, u32[]{:S(2)}, u32[]{:S(2)}) collective-permute-start(bf16[192,2048]{1,0:T(8,128)(2,1)} %get-tuple-element.108), channel_id=1, source_target_pairs={{0,1},{1,0},{2,3},{3,2},{4,5},{5,4},{6,7},{7,6},{8,9},{9,8},{10,11... | collective-permute-start | bytes 2359304 | tf_op jit(solution)/shard_map/ppermute | solution.py:41
  576.0 28.4 %collective-permute-start.39 = (bf16[192,2048]{1,0:T(8,128)(2,1)S(1)}, bf16[192,2048]{1,0:T(8,128)(2,1)S(1)}, u32[]{:S(2)}, u32[]{:S(2)}) collective-permute-start(bf16[192,2048]{1,0:T(8,128)(2,1)S(1)} %pad_maximum_fusion.13), channel_id=1, source_target_pairs={{0,1},{1,0},{2,3},{3,2},{4,5},{5,4},{6,7},{7,6},{8,9},{9,8},{10,11... | collective-permute-start | bytes 2359304 | tf_op jit(solution)/shard_map/ppermute | solution.py:41
  578.5 25.8 %collective-permute-start.38 = (bf16[192,2048]{1,0:T(8,128)(2,1)S(1)}, bf16[192,2048]{1,0:T(8,128)(2,1)S(1)}, u32[]{:S(2)}, u32[]{:S(2)}) collective-permute-start(bf16[192,2048]{1,0:T(8,128)(2,1)S(1)} %pad_maximum_fusion.12), channel_id=1, source_target_pairs={{0,2},{1,3},{2,0},{3,1},{4,6},{5,7},{6,4},{7,5},{8,10},{9,11},{10,... | collective-permute-start | bytes 2359304 | tf_op jit(solution)/shard_map/ppermute | solution.py:41
  704.8 23.0 %collective-permute-start.48 = (bf16[384,128]{1,0:T(8,128)(2,1)S(1)}, bf16[384,128]{1,0:T(8,128)(2,1)S(1)}, u32[]{:S(2)}, u32[]{:S(2)}) collective-permute-start(bf16[384,128]{1,0:T(8,128)(2,1)S(1)} %get-tuple-element.246), channel_id=1, source_target_pairs={{0,8},{4,12},{8,16},{12,20},{16,24},{20,28},{24,0},{28,4},{1,9},{5... | collective-permute-start | bytes 294920 | tf_op jit(solution)/shard_map/ppermute | solution.py:945
  708.6 19.3 %collective-permute-start.50 = (bf16[384,128]{1,0:T(8,128)(2,1)S(1)}, bf16[384,128]{1,0:T(8,128)(2,1)S(1)}, u32[]{:S(2)}, u32[]{:S(2)}) collective-permute-start(bf16[384,128]{1,0:T(8,128)(2,1)S(1)} %get-tuple-element.245), channel_id=1, source_target_pairs={{0,16},{4,20},{8,24},{12,28},{16,0},{20,4},{24,8},{28,12},{1,17},{... | collective-permute-start | bytes 294920 | tf_op jit(solution)/shard_map/ppermute | solution.py:945
  779.7 48.6 %collective-permute-start.55 = (bf16[2,768,128]{2,1,0:T(8,128)(2,1)S(1)}, bf16[2,768,128]{2,1,0:T(8,128)(2,1)S(1)}, u32[]{:S(2)}, u32[]{:S(2)}) collective-permute-start(bf16[2,768,128]{2,1,0:T(8,128)(2,1)S(1)} %get-tuple-element.205), channel_id=1, source_target_pairs={{0,24},{4,28},{8,0},{12,4},{16,8},{20,12},{24,16},{28,20},{1,25},{... | collective-permute-start | bytes 1179656 | tf_op jit(solution)/shard_map/ppermute | solution.py:945
  779.7 48.5 %collective-permute-start.56 = (bf16[2,768,128]{2,1,0:T(8,128)(2,1)S(1)}, bf16[2,768,128]{2,1,0:T(8,128)(2,1)S(1)}, u32[]{:S(2)}, u32[]{:S(2)}) collective-permute-start(bf16[2,768,128]{2,1,0:T(8,128)(2,1)S(1)} %get-tuple-element.204), channel_id=1, source_target_pairs={{0,16},{4,20},{8,24},{12,28},{16,0},{20,4},{24,8},{28,12},{1,17},{... | collective-permute-start | bytes 1179656 | tf_op jit(solution)/shard_map/ppermute | solution.py:945
  781.5 46.8 %collective-permute-start.57 = (bf16[2,768,128]{2,1,0:T(8,128)(2,1)S(1)}, bf16[2,768,128]{2,1,0:T(8,128)(2,1)S(1)}, u32[]{:S(2)}, u32[]{:S(2)}) collective-permute-start(bf16[2,768,128]{2,1,0:T(8,128)(2,1)S(1)} %get-tuple-element.203), channel_id=1, source_target_pairs={{0,8},{4,12},{8,16},{12,20},{16,24},{20,28},{24,0},{28,4},{1,9},{5... | collective-permute-start | bytes 1179656 | tf_op jit(solution)/shard_map/ppermute | solution.py:945
  782.4 45.8 %collective-permute-start.59 = (bf16[768,128]{1,0:T(8,128)(2,1)S(1)}, bf16[768,128]{1,0:T(8,128)(2,1)S(1)}, u32[]{:S(2)}, u32[]{:S(2)}) collective-permute-start(bf16[768,128]{1,0:T(8,128)(2,1)S(1)} %copy-done.123), channel_id=1, source_target_pairs={{0,16},{4,20},{8,24},{12,28},{16,0},{20,4},{24,8},{28,12},{1,17},{... | collective-permute-start | bytes 589832 | tf_op jit(solution)/shard_map/ppermute | solution.py:945
  785.3 42.9 %collective-permute-start.60 = (bf16[768,128]{1,0:T(8,128)(2,1)S(1)}, bf16[768,128]{1,0:T(8,128)(2,1)S(1)}, u32[]{:S(2)}, u32[]{:S(2)}) collective-permute-start(bf16[768,128]{1,0:T(8,128)(2,1)S(1)} %copy-done.122), channel_id=1, source_target_pairs={{0,8},{4,12},{8,16},{12,20},{16,24},{20,28},{24,0},{28,4},{1,9},{5... | collective-permute-start | bytes 589832 | tf_op jit(solution)/shard_map/ppermute | solution.py:945
  840.0 40.5 %collective-permute-start.77 = (bf16[80,512]{1,0:T(8,128)(2,1)S(1)}, bf16[80,512]{1,0:T(8,128)(2,1)}, u32[]{:S(2)}, u32[]{:S(2)}) collective-permute-start(bf16[80,512]{1,0:T(8,128)(2,1)S(1)} %fusion.66), channel_id=1, source_target_pairs={{0,16},{4,20},{8,24},{12,28},{16,0},{20,4},{24,8},{28,12},{1,17},{... | collective-permute-start | bytes 245768 | tf_op jit(solution)/shard_map/ppermute | solution.py:41
  (193 other events, 1562.3 us)
Sparse Core Ops, SparseCore 0:
  46.6 48.2 all-gather.12
  97.1 69.9 all-gather.10
  168.7 200.0 all-gather.6
  370.3 96.7 all-gather.8
  674.7 53.1 reduce-scatter.1

commit v3 on v2

--- a/solution.py
+++ b/solution.py
@@ -845,8 +845,9 @@
         gate_up_second_factor.reshape(-1, cols),
     ]
     packed = jnp.concatenate(pieces, axis=0)
-    x_parts, packed, w_gu, w_down = lax.optimization_barrier(
+    first, x_parts, packed, w_gu, w_down = lax.optimization_barrier(
         (
+            first,
             x_parts,
             packed,
             gate_up_weight.transpose(1, 0, 2).reshape(k_rows, 2 * hidden_cols),
@@ -854,10 +855,6 @@
         )
     )
     packed = lax.all_gather(packed, "seq", axis=0)
-    split, at = [], 0
-    for piece in pieces:
-        split.append(packed[:, at : at + piece.shape[0]])
-        at += piece.shape[0]
     w_gu = lax.all_gather(w_gu, "seq", axis=0, tiled=True)
     w_down = lax.all_gather(w_down, "seq", axis=0, tiled=True)
 
@@ -873,30 +870,6 @@
     a_qkv = a_qkv.reshape(width, 3 * slots_a)
     b_qkv = first[:, k_rows : k_rows + rank_cols].reshape(slots_a, 3 * cols)
     b_qkv = blocked([b_qkv[:, i * cols : (i + 1) * cols] for i in range(3)])
-    w_o = split[0].reshape(width, cols)
-    a_o = split[1].reshape(slots_a, cols).T
-    shared = gather_order(jnp.concatenate(split[2:4], axis=1), "tp", tp, tp_order)
-    b_size = split[2].shape[1]
-    b_od = (
-        shared[:, :, :b_size]
-        .reshape(tp, seqs, 2, rank_cols, b_part)
-        .transpose(2, 1, 3, 0, 4)
-        .reshape(2, slots_a, width)
-    )
-    a_gu = (
-        shared[:, :, b_size:]
-        .reshape(tp, seqs, 2, a_part, slots_a)
-        .transpose(1, 0, 3, 2, 4)
-        .reshape(width, 2 * slots_a)
-    )
-    a_down = split[4].reshape(slots_a, hidden_cols).T
-    b_gu = (
-        split[5]
-        .reshape(seqs, 2, rank_cols, hidden_cols)
-        .transpose(1, 0, 2, 3)
-        .reshape(2 * slots_a, hidden_cols)
-    )
-
     runs = row_runs(tp)
     piece_at = jnp.stack([2 * (tp_rank ^ mask) + which for mask, which in runs]).astype(jnp.int32)
     token = (piece_at[:, None] * part + jnp.arange(part, dtype=jnp.int32)[None, :]).reshape(-1)
@@ -975,6 +948,34 @@
     )
     squares = sum_rows(squares[:2].reshape(2, rows), tp)
     inv = lax.rsqrt(squares / width + EPS)
+    inv, packed = lax.optimization_barrier((inv, packed))
+    split, at = [], 0
+    for piece in pieces:
+        split.append(packed[:, at : at + piece.shape[0]])
+        at += piece.shape[0]
+    w_o = split[0].reshape(width, cols)
+    a_o = split[1].reshape(slots_a, cols).T
+    shared = gather_order(jnp.concatenate(split[2:4], axis=1), "tp", tp, tp_order)
+    b_size = split[2].shape[1]
+    b_od = (
+        shared[:, :, :b_size]
+        .reshape(tp, seqs, 2, rank_cols, b_part)
+        .transpose(2, 1, 3, 0, 4)
+        .reshape(2, slots_a, width)
+    )
+    a_gu = (
+        shared[:, :, b_size:]
+        .reshape(tp, seqs, 2, a_part, slots_a)
+        .transpose(1, 0, 3, 2, 4)
+        .reshape(width, 2 * slots_a)
+    )
+    a_down = split[4].reshape(slots_a, hidden_cols).T
+    b_gu = (
+        split[5]
+        .reshape(seqs, 2, rank_cols, hidden_cols)
+        .transpose(1, 0, 2, 3)
+        .reshape(2 * slots_a, hidden_cols)
+    )
     spread = spread_heads(head_order, piece_at, z, inv.T, cs, gain, heads)
     near = [head_shift(spread[heads + k], k) for k in range(heads)]
     queries = [head_shift(spread[k], k) for k in range(heads)]
@@ -1031,6 +1032,36 @@
         for i in groups
     ]
     d_latents = (d_latent0, d_latent1)
+    d_rows = gather_groups(d_attn, tp)
+    o_latents = (o_latent0, o_latent1)
+    u_os, grads = [], []
+    for g in groups:
+        u_os.append((mm_nt(d_rows[g], b_od[0]) * selects[g]).astype(BF16))
+        d_heads = (mm(d_rows[g], w_o) + mm_nt(u_os[g], a_o)).astype(BF16)
+        grads.append(
+            [
+                head_shift(
+                    lax.dynamic_slice_in_dim(d_heads, head_order[k] * HEAD_DIM, HEAD_DIM, 1), k
+                )
+                for k in range(heads)
+            ]
+        )
+    grads = [grads[g][k] for k in range(heads) for g in groups]
+    results = list(attend_back(tables, piece_at, queries, near, far, grads, prompt_count))
+    dqs = [head_shift(results[k], -k) for k in range(heads)]
+    d_kv = results[heads].reshape(2, heads, rows, HEAD_DIM)
+    others = [
+        group_shift(results[heads + j], j).reshape(2, heads, rows, HEAD_DIM) for j in range(1, group)
+    ]
+    dkvs = []
+    for k in range(heads):
+        total = d_kv[:, k].astype(F32)
+        for other in others:
+            total = total + other[:, k].astype(F32)
+        dkvs.append(head_shift(total.astype(BF16), -k))
+    dkvs[1], u_os, o_latents, u_downs, d_latents, u_gus, gu_latents = lax.optimization_barrier(
+        (dkvs[1], u_os, o_latents, u_downs, d_latents, u_gus, gu_latents)
+    )
     both_groups = lambda f: f(0) + f(1)
     grad_a_down = both_groups(lambda g: mm_tn(u_downs[g], acts[g]))
     grad_b_down = both_groups(lambda g: mm_tn(d_latents[g], d_ffs[g]))
@@ -1049,22 +1080,6 @@
         ],
         axis=1,
     )
-
-    *d_rows, early = gather_groups(d_attn, tp, early)
-    early = lax.psum_scatter(early, "seq", scatter_dimension=0, tiled=False)
-    o_latents = (o_latent0, o_latent1)
-    u_os, grads = [], []
-    for g in groups:
-        u_os.append((mm_nt(d_rows[g], b_od[0]) * selects[g]).astype(BF16))
-        d_heads = (mm(d_rows[g], w_o) + mm_nt(u_os[g], a_o)).astype(BF16)
-        grads.append(
-            [
-                head_shift(
-                    lax.dynamic_slice_in_dim(d_heads, head_order[k] * HEAD_DIM, HEAD_DIM, 1), k
-                )
-                for k in range(heads)
-            ]
-        )
     grad_a_o = both_groups(lambda g: mm_tn(u_os[g], heads_out[g]))
     grad_b_o = both_groups(lambda g: mm_tn(o_latents[g], d_rows[g]))
     late_o = jnp.concatenate(
@@ -1074,28 +1089,14 @@
         ],
         axis=1,
     )
+    dqs, dkvs, early, late_o = lax.optimization_barrier((dqs, dkvs, early, late_o))
+    early = lax.psum_scatter(early, "seq", scatter_dimension=0, tiled=False)
     late_o = scatter_order(late_o, "seq", seqs, seq_order)
-    grads = [grads[g][k] for k in range(heads) for g in groups]
-    grads[-1], early = lax.optimization_barrier((grads[-1], early))
-    results = list(attend_back(tables, piece_at, queries, near, far, grads, prompt_count))
-    dqs = [head_shift(results[k], -k) for k in range(heads)]
-    d_kv = results[heads].reshape(2, heads, rows, HEAD_DIM)
-    others = [
-        group_shift(results[heads + j], j).reshape(2, heads, rows, HEAD_DIM) for j in range(1, group)
-    ]
-    dkvs = []
-    for k in range(heads):
-        total = d_kv[:, k].astype(F32)
-        for other in others:
-            total = total + other[:, k].astype(F32)
-        dkvs.append(head_shift(total.astype(BF16), -k))
     scaled, parts = unturn_heads(head_order, piece_at, dqs, dkvs, z, cs, gain)
     parts = sum_rows(parts.T, tp) / width
     coef = jnp.concatenate([inv, inv**3 * parts], axis=0)
     dz = norm_back_heads(head_order, piece_at, dkvs, scaled, z, coef.T)
     us = (mm_nt(dz, b_qkv) * pick3).astype(BF16)
-    far_part = list(back_product(dz, 1, first, k_rows, us, a_qkv, 2))
-    far_part[0], us = lax.optimization_barrier((far_part[0], us))
     grad_a_qkv = mm_tn(x, us)
     grad_b_qkv = mm_tn(latents, dz)
     lane3 = 3 * slots_a
@@ -1114,24 +1115,32 @@
         axis=1,
     )
     dz, late = lax.optimization_barrier((dz, late))
+    far_part = list(back_product(dz, 1, first, k_rows, us, a_qkv, 2))
+    far_part[0], dz = lax.optimization_barrier((far_part[0], dz))
     (near_part,) = back_product(dz, 0, first, k_rows, us, a_qkv, 1)
+    near_part, early, late_o = lax.optimization_barrier((near_part, early, late_o))
     summed = scatter_groups(near_part, far_part, tp)
     input_grad = jnp.concatenate([d_hidden[i] + summed[i] for i in groups], axis=0)
 
     late = scatter_order(late, "seq", seqs, seq_order)
     sum_tp = lambda value: sum_all(value.astype(BF16), "tp", tp).astype(F32)
-    grad_a_qkv = sum_tp(late[:k_rows])
-    grad_b_qkv = late[k_rows:].reshape(rank_cols, 3, cols).transpose(1, 0, 2)
     down_size = rank_cols * width // lane
-    both = sum_tp(early[: k_rows + down_size])
-    grad_a_gu, grad_b_down = both[:k_rows], both[k_rows:].reshape(rank_cols, width)
+    o_size = rank_cols * width // cols
+    both = sum_tp(
+        jnp.concatenate(
+            [early[: k_rows + down_size], late_o[:o_size].astype(BF16).reshape(-1, lane)], axis=0
+        )
+    )
+    grad_a_gu = both[:k_rows]
+    grad_b_down = both[k_rows : k_rows + down_size].reshape(rank_cols, width)
+    grad_b_o = both[k_rows + down_size :].reshape(rank_cols, width)
     a_size = rank_cols * hidden_cols // lane
     rest = early[k_rows + down_size :].astype(F32)
     grad_a_down = rest[:a_size].reshape(rank_cols, hidden_cols).T
     grad_b_gu = rest[a_size:].reshape(2, rank_cols, hidden_cols)
-    o_size = rank_cols * width // cols
-    grad_b_o = sum_tp(late_o[:o_size]).reshape(rank_cols, width)
     grad_a_o = late_o[o_size:].T
+    grad_a_qkv = sum_tp(late[:k_rows])
+    grad_b_qkv = late[k_rows:].reshape(rank_cols, 3, cols).transpose(1, 0, 2)
     grad_a_in = jnp.stack(
         [grad_a_qkv[:, i * slots_a : (i + 1) * slots_a] for i in range(3)]
         + [grad_a_gu[:, i * slots_a : (i + 1) * slots_a] for i in range(2)]

time: 950 us -> 839 us (0.88)
  waiting for transfers between devices: 421 us -> 327 us
  starting transfers between devices: 109 us -> 94.6 us
    all_gather x1, waiting for transfers between devices: 67.8 us -> 35 us  [local(): first = lax.all_gather(first, 'seq', axis=0)]
    ppermute x21, waiting for transfers between devices: 168 us -> 144 us  [head_shift(): lax.ppermute(value, 'seq', [(h * group + j, (h + by) % heads * group + j)...]
    all_gather x1, waiting for transfers between devices: 23.4 us -> 0.01 us  [local(): packed = lax.all_gather(packed, 'seq', axis=0)]
    ppermute x6, waiting for transfers between devices: 23.9 us -> 5.18 us  [sum_rows(): got = lax.ppermute(value, 'tp', [(i, i ^ mask) for i in range(count)])]
    ppermute x42 -> x40, waiting for transfers between devices: 85.6 us -> 102 us  [flip(): return lax.ppermute(value, axis, [(i, i ^ 1 << bit) for i in range(count)])]
    ppermute x3, waiting for transfers between devices: 16.2 us -> 5.38 us  [local(): lax.ppermute(a_qkv, 'tp', [(i, i ^ mask) for i in range(tp)])]
    ppermute x42 -> x40, starting transfers between devices: 49.3 us -> 42.7 us  [flip(): return lax.ppermute(value, axis, [(i, i ^ 1 << bit) for i in range(count)])]
    unnamed x309 -> x276, local copies, waits for them, and re-layouts: 36.6 us -> 32 us
  transfers between devices with their start and end apart: 85 -> 83, of which waited for: 40 -> 45; matrix products, arithmetic and copies ran while one was open for 17% -> 19% of each run, Pallas kernels for 14% -> 16%
where the time goes in v3:
time: 839 us; the launch traced here: 832 us
  waiting for transfers between devices  327 us (39%)
  Pallas kernels  209 us (25%)
  local copies, waits for them, and re-layouts  101 us (12%)
  starting transfers between devices  94.6 us (11%)
  other arithmetic  49.8 us (6%)
  matrix products  33.3 us (4%)
  between operations  18.5 us (2%)
    ppermute x21, waiting for transfers between devices, head_shift(): lax.ppermute(value, 'seq', [(h * group + j, (h + by) % heads * group + j)...  144 us
    ppermute x40, waiting for transfers between devices, flip(): return lax.ppermute(value, axis, [(i, i ^ 1 << bit) for i in range(count)])  102 us
    pallas_call x2, Pallas kernels, ff_back(): pl.pallas_call(functools.partial(ff_back_kernel, parts, n), grid=(n,), ou...  45.7 us
    ppermute x40, starting transfers between devices, flip(): return lax.ppermute(value, axis, [(i, i ^ 1 << bit) for i in range(count)])  42.7 us
    ppermute x21, starting transfers between devices, head_shift(): lax.ppermute(value, 'seq', [(h * group + j, (h + by) % heads * group + j)...  35.4 us
    all_gather x1, waiting for transfers between devices, local(): first = lax.all_gather(first, 'seq', axis=0)  35 us
    pallas_call x1, Pallas kernels, attend_back(): pl.pallas_call(functools.partial(attend_back_kernel, slots, group, rows,...  32.8 us
    unnamed x276, local copies, waits for them, and re-layouts  32 us
  transfers between devices with their start and end apart: 83, of which 45 were waited for; matrix products, arithmetic and copies ran while one was open for 19% of the time, Pallas kernels for 16%

profile of v3, /device:TPU:0, one launch (start us, length us, event | category | flops | bytes accessed | tf_op | source)
XLA Modules:
  0.0 832.5 jit_solution(16259976255422002690)
XLA Ops:
  22.4 10.9 %collective-permute-done = bf16[192,2048]{1,0:T(8,128)(2,1)S(1)} collective-permute-done((bf16[192,2048]{1,0:T(8,128)(2,1)S(1)}, bf16[192,2048]{1,0:T(8,128)(2,1)S(1)}, u32[]{:S(2)}, u32[]{:S(2)}) %collective-permute-start) | collective-permute-done | bytes 786464 | tf_op jit(solution)/shard_map/ppermute | solution.py:836
  33.3 17.6 %collective-permute-done.1 = bf16[192,2048]{1,0:T(8,128)(2,1)} collective-permute-done((bf16[192,2048]{1,0:T(8,128)(2,1)S(1)}, bf16[192,2048]{1,0:T(8,128)(2,1)}, u32[]{:S(2)}, u32[]{:S(2)}) %collective-permute-start.1) | collective-permute-done | bytes 786464 | tf_op jit(solution)/shard_map/ppermute | solution.py:836
  50.8 35.0 %all-gather.11.cloned.1.call-done = bf16[2304,1536]{1,0:T(8,128)(2,1)} async-done(((bf16[288,1536]{1,0:T(8,128)(2,1)}), bf16[2304,1536]{1,0:T(8,128)(2,1)}) %all-gather.11.cloned.1.call-update) | async-done | bytes 7077904 | tf_op jit(solution)/shard_map/all_gather | solution.py:838
  124.0 10.4 %qkv_product.1 = (f32[768,1536]{1,0:T(8,128)}, f32[3,768,1]{2,1,0:T(8,128)}) custom-call(bf16[768,2048]{1,0:T(8,128)(2,1)} %slice_dynamic-update-slice_fusion.x, bf16[768,384]{1,0:T(8,128)(2,1)} %fusion.7.latent, bf16[8,288,1536]{2,1,0:T(8,128)(2,1)} %bitcast.277, bf16[128,1536]{1,0:T(8,128)(2,1)} %bitcast.323), custom_call_target="tpu_custom_call" | custom-call | flops 4831838208 | bytes 7077888 | tf_op jit(solution)/shard_map/qkv_product/pallas_call | solution.py:533
  134.4 5.8 copy.210
  154.2 7.2 spread_heads.1
  171.5 86.1 %collective-permute-done.10.refs_2_ = bf16[768,128]{1,0:T(8,128)(2,1)S(1)} collective-permute-done((bf16[768,128]{1,0:T(8,128)(2,1)}, bf16[768,128]{1,0:T(8,128)(2,1)S(1)}, u32[]{:S(2)}, u32[]{:S(2)}) %collective-permute-start.10) | collective-permute-done | bytes 196640 | tf_op jit(solution)/shard_map/ppermute | solution.py:918
  264.5 10.4 %collective-permute-done.9.refs_1_ = bf16[768,128]{1,0:T(8,128)(2,1)S(1)} collective-permute-done((bf16[768,128]{1,0:T(8,128)(2,1)S(1)}, bf16[768,128]{1,0:T(8,128)(2,1)S(1)}, u32[]{:S(2)}, u32[]{:S(2)}) %collective-permute-start.9) | collective-permute-done | bytes 196640 | tf_op jit(solution)/shard_map/ppermute | solution.py:918
  278.5 21.6 %attend.1 = (bf16[768,128]{1,0:T(8,128)(2,1)}, bf16[768,128]{1,0:T(8,128)(2,1)}, bf16[768,128]{1,0:T(8,128)(2,1)}, bf16[768,128]{1,0:T(8,128)(2,1)}) custom-call(s32[24]{0:T(128)} %bitcast.356, s32[24]{0:T(128)} %bitcast.358, s32[24]{0:T(128)} %select_reduce_fusion.2.prompt_at, bf16[768,128]{1,0:T(8,128)(2,1)} %get-tuple-element.112.refs_0_, ...), custom_call_target="tpu_custom_call" | custom-call | flops 1811939328 | bytes 4718592 | tf_op jit(solution)/shard_map/attend/pallas_call | solution.py:299
  300.2 6.5 collective-permute-start.19
  316.6 20.7 %collective-permute-done.20.refs_2_ = bf16[768,128]{1,0:T(8,128)(2,1)S(1)} collective-permute-done((bf16[768,128]{1,0:T(8,128)(2,1)}, bf16[768,128]{1,0:T(8,128)(2,1)S(1)}, u32[]{:S(2)}, u32[]{:S(2)}) %collective-permute-start.20) | collective-permute-done | bytes 196640 | tf_op jit(solution)/shard_map/ppermute | solution.py:918
  359.7 11.4 %collective-permute-done.24 = bf16[192,2048]{1,0:T(8,128)(2,1)S(1)} collective-permute-done((bf16[192,2048]{1,0:T(8,128)(2,1)}, bf16[192,2048]{1,0:T(8,128)(2,1)S(1)}, u32[]{:S(2)}, u32[]{:S(2)}) %collective-permute-start.24) | collective-permute-done | bytes 786464 | tf_op jit(solution)/shard_map/ppermute | solution.py:41
  376.8 7.7 collective-permute-done.25
  387.8 7.6 collective-permute-done.26
  416.9 14.8 %gate_up_product.3 = (f32[384,2048]{1,0:T(8,128)}, f32[384,2048]{1,0:T(8,128)}, bf16[384,2048]{1,0:T(8,128)(2,1)}, bf16[384,256]{1,0:T(8,128)(2,1)}) custom-call(bf16[384,2048]{1,0:T(8,128)(2,1)} %copy-done.8, bf16[2048,256]{1,0:T(8,128)(2,1)} %bitcast.280, f32[384,128]{1,0:T(8,128)} %get-tuple-element.299.pick, ...), custom_call_target="tpu_custom_call" | custom-call | flops 6442450944 | bytes 16777216 | tf_op jit(solution)/shard_map/gate_up_product/pallas_call | solution.py:654
  434.9 8.7 %add_product.7 = (bf16[192,2048]{1,0:T(8,128)(2,1)}, bf16[192,2048]{1,0:T(8,128)(2,1)}, bf16[384,128]{1,0:T(8,128)(2,1)}) custom-call(bf16[384,2048]{1,0:T(8,128)(2,1)} %get-tuple-element.134.a, bf16[2048,2048]{1,0:T(8,128)(2,1)} %all-gather.9.cloned.1.call-done.weight.w_down, bf16[2048,128]{1,0:T(8,128)(2,1)} %bitcast.305, bf16[128,2048]{1,0:T(8,128)(2,1)} %bitcast.309, ...), custom_call_target="tpu_custom_call" | custom-call | flops 3221225472 | bytes 8388608 | tf_op jit(solution)/shard_map/add_product/pallas_call | solution.py:576
  446.6 14.6 %gate_up_product.2 = (f32[384,2048]{1,0:T(8,128)}, f32[384,2048]{1,0:T(8,128)}, bf16[384,2048]{1,0:T(8,128)(2,1)}, bf16[384,256]{1,0:T(8,128)(2,1)}) custom-call(bf16[384,2048]{1,0:T(8,128)(2,1)} %pad_maximum_fusion.2.h, bf16[2048,256]{1,0:T(8,128)(2,1)} %bitcast.281, f32[384,128]{1,0:T(8,128)} %get-tuple-element.298.pick, ...), custom_call_target="tpu_custom_call" | custom-call | flops 6442450944 | bytes 16777216 | tf_op jit(solution)/shard_map/gate_up_product/pallas_call | solution.py:654
  461.1 9.2 %add_product.6 = (bf16[384,2048]{1,0:T(8,128)(2,1)}, bf16[384,128]{1,0:T(8,128)(2,1)}) custom-call(bf16[384,2048]{1,0:T(8,128)(2,1)} %get-tuple-element.131.a, bf16[2048,2048]{1,0:T(8,128)(2,1)} %all-gather.9.cloned.1.call-done.weight.w_down, bf16[2048,128]{1,0:T(8,128)(2,1)} %bitcast.306, bf16[128,2048]{1,0:T(8,128)(2,1)} %bitcast.310, ...), custom_call_target="tpu_custom_call" | custom-call | flops 3221225472 | bytes 8388608 | tf_op jit(solution)/shard_map/add_product/pallas_call | solution.py:576
  473.7 9.5 %collective-permute-done.33 = bf16[96,2048]{1,0:T(8,128)(2,1)S(1)} collective-permute-done((bf16[96,2048]{1,0:T(8,128)(2,1)S(1)}, bf16[96,2048]{1,0:T(8,128)(2,1)S(1)}, u32[]{:S(2)}, u32[]{:S(2)}) %collective-permute-start.33) | collective-permute-done | bytes 393248 | tf_op jit(solution)/shard_map/ppermute | solution.py:41
  486.7 7.5 collective-permute-done.36
  497.8 14.5 %collective-permute-done.38 = bf16[192,2048]{1,0:T(8,128)(2,1)S(1)} collective-permute-done((bf16[192,2048]{1,0:T(8,128)(2,1)S(1)}, bf16[192,2048]{1,0:T(8,128)(2,1)S(1)}, u32[]{:S(2)}, u32[]{:S(2)}) %collective-permute-start.38) | collective-permute-done | bytes 786464 | tf_op jit(solution)/shard_map/ppermute | solution.py:41
  513.7 22.8 %ff_back.3 = (bf16[192,2048]{1,0:T(8,128)(2,1)}, bf16[192,2048]{1,0:T(8,128)(2,1)}, bf16[384,2048]{1,0:T(8,128)(2,1)}, bf16[384,2048]{1,0:T(8,128)(2,1)}, bf16[3...) custom-call(bf16[384,2048]{1,0:T(8,128)(2,1)} %copy-done.18, bf16[128,2048]{1,0:T(8,128)(2,1)} %bitcast.311, ...), custom_call_target="tpu_custom_call" | custom-call | flops 9663676416 | bytes 25165824 | tf_op jit(solution)/shard_map/ff_back/pallas_call | solution.py:738
  539.0 22.9 %ff_back.2 = (bf16[384,2048]{1,0:T(8,128)(2,1)}, bf16[384,2048]{1,0:T(8,128)(2,1)}, bf16[384,2048]{1,0:T(8,128)(2,1)}, bf16[384,256]{1,0:T(8,128)(2,1)}, bf16[384,128]{1,0:T(8,128)(2,1)}) custom-call(bf16[384,2048]{1,0:T(8,128)(2,1)} %pad_maximum_fusion.4.d_ff, bf16[128,2048]{1,0:T(8,128)(2,1)} %bitcast.312, f32[384,128]{1,0:T(8,128)} %get-tuple-element.298.pick, ...), custom_call_target="tpu_custom_call" | custom-call | flops 9663676416 | bytes 25165824 | tf_op jit(solution)/shard_map/ff_back/pallas_call | solution.py:738
  565.9 6.1 collective-permute-done.41
  613.0 32.8 %attend_back.1 = (bf16[768,128]{1,0:T(8,128)(2,1)}, bf16[768,128]{1,0:T(8,128)(2,1)}, bf16[768,128]{1,0:T(8,128)(2,1)}, bf16[768,128]{1,0:T(8,128)(2,1)}, bf16[2...) custom-call(s32[24]{0:T(128)} %bitcast.357, s32[24]{0:T(128)} %bitcast.359, s32[24]{0:T(128)} %select_reduce_fusion.2.prompt_at, ...), custom_call_target="tpu_custom_call" | custom-call | flops 4529848320 | bytes 9437184 | tf_op jit(solution)/shard_map/attend_back/pallas_call | solution.py:331
  692.1 7.6 collective-permute-done.55.refs_2_
  699.7 7.6 collective-permute-done.59.refs_6_.refs_2_
  707.3 8.2 unturn_heads.1
  725.1 7.2 norm_back_heads.1.a
  752.0 7.5 back_product.2
  761.5 7.6 back_product.3
  773.3 9.8 %collective-permute-done.73 = bf16[320,384]{1,0:T(8,128)(2,1)S(1)} collective-permute-done((bf16[320,384]{1,0:T(8,128)(2,1)S(1)}, bf16[320,384]{1,0:T(8,128)(2,1)S(1)}, u32[]{:S(2)}, u32[]{:S(2)}) %collective-permute-start.73) | collective-permute-done | bytes 245792 | tf_op jit(solution)/shard_map/ppermute | solution.py:41
  (666 shorter events, 336.4 us)
Async XLA Ops:
  7.2 78.7 %all-gather.11.cloned.1.call-start = ((), (), s32[]{:S(2)}) async-start(), calls=%async_computation.4 | async-start | bytes 7962624 | tf_op jit(solution)/shard_map/all_gather | solution.py:838
  11.8 136.4 %all-gather.13.cloned.1.call-start = ((), (), s32[]{:S(2)}) async-start(), calls=%async_computation.5 | async-start | bytes 4866048 | tf_op jit(solution)/shard_map/all_gather | solution.py:857
  11.8 21.4 %collective-permute-start = (bf16[192,2048]{1,0:T(8,128)(2,1)S(1)}, bf16[192,2048]{1,0:T(8,128)(2,1)S(1)}, u32[]{:S(2)}, u32[]{:S(2)}) collective-permute-start(bf16[192,2048]{1,0:T(8,128)(2,1)S(1)} %copy-done.21), channel_id=1, source_target_pairs={{0,1},{1,0},{2,3},{3,2},{4,5},{5,4},{6,7},{7,6},{8,9},{9,8},{10,11... | collective-permute-start | bytes 2359304 | tf_op jit(solution)/shard_map/ppermute | solution.py:836
  14.9 36.0 %collective-permute-start.1 = (bf16[192,2048]{1,0:T(8,128)(2,1)S(1)}, bf16[192,2048]{1,0:T(8,128)(2,1)}, u32[]{:S(2)}, u32[]{:S(2)}) collective-permute-start(bf16[192,2048]{1,0:T(8,128)(2,1)S(1)} %copy-done.21), channel_id=1, source_target_pairs={{0,2},{1,3},{2,0},{3,1},{4,6},{5,7},{6,4},{7,5},{8,10},{9,11},{10,... | collective-permute-start | bytes 2359304 | tf_op jit(solution)/shard_map/ppermute | solution.py:836
  16.4 34.4 %collective-permute-start.2 = (bf16[192,2048]{1,0:T(8,128)(2,1)S(1)}, bf16[192,2048]{1,0:T(8,128)(2,1)}, u32[]{:S(2)}, u32[]{:S(2)}) collective-permute-start(bf16[192,2048]{1,0:T(8,128)(2,1)S(1)} %copy-done.21), channel_id=1, source_target_pairs={{0,3},{1,2},{2,1},{3,0},{4,7},{5,6},{6,5},{7,4},{8,11},{9,10},{10,... | collective-permute-start | bytes 2359304 | tf_op jit(solution)/shard_map/ppermute | solution.py:836
  85.9 329.9 %all-gather.7.cloned.1.call-start = ((), (), s32[]{:S(2)}) async-start(), calls=%async_computation.1 | async-start | bytes 18874368 | tf_op jit(solution)/shard_map/all_gather | solution.py:858
  86.6 348.3 %all-gather.9.cloned.1.call-start = ((), (), s32[]{:S(2)}) async-start(), calls=%async_computation.2 | async-start | bytes 9437184 | tf_op jit(solution)/shard_map/all_gather | solution.py:859
  97.0 19.7 %collective-permute-start.4 = (bf16[8,64,384]{2,1,0:T(8,128)(2,1)}, bf16[8,64,384]{2,1,0:T(8,128)(2,1)}, u32[]{:S(2)}, u32[]{:S(2)}) collective-permute-start(bf16[8,64,384]{2,1,0:T(8,128)(2,1)} %reshape.572), channel_id=1, source_target_pairs={{0,2},{1,3},{2,0},{3,1},{4,6},{5,7},{6,4},{7,5},{8,10},{9,11},{10,... | collective-permute-start | bytes 1179656 | tf_op jit(solution)/shard_map/ppermute | solution.py:865
  98.4 19.3 %collective-permute-start.5 = (bf16[8,64,384]{2,1,0:T(8,128)(2,1)}, bf16[8,64,384]{2,1,0:T(8,128)(2,1)}, u32[]{:S(2)}, u32[]{:S(2)}) collective-permute-start(bf16[8,64,384]{2,1,0:T(8,128)(2,1)} %reshape.572), channel_id=1, source_target_pairs={{0,3},{1,2},{2,1},{3,0},{4,7},{5,6},{6,5},{7,4},{8,11},{9,10},{10,... | collective-permute-start | bytes 1179656 | tf_op jit(solution)/shard_map/ppermute | solution.py:865
  101.4 697.7 %reduce-scatter.2.cloned.1.call-start = ((), (), s32[]{:S(2)}) async-start(), calls=%async_computation.3 | async-start | bytes 3538944 | tf_op jit(solution)/shard_map/reduce_scatter | solution.py:1093
  161.4 113.5 %collective-permute-start.12 = (bf16[2,768,128]{2,1,0:T(8,128)(2,1)}, bf16[2,768,128]{2,1,0:T(8,128)(2,1)}, u32[]{:S(2)}, u32[]{:S(2)}) collective-permute-start(bf16[2,768,128]{2,1,0:T(8,128)(2,1)} %get-tuple-element.117), channel_id=1, source_target_pairs={{0,8},{4,12},{8,16},{12,20},{16,24},{20,28},{24,0},{28,4},{1,9},{5... | collective-permute-start | bytes 1179656 | tf_op jit(solution)/shard_map/ppermute | solution.py:918
  161.4 114.0 %collective-permute-start.13 = (bf16[2,768,128]{2,1,0:T(8,128)(2,1)}, bf16[2,768,128]{2,1,0:T(8,128)(2,1)}, u32[]{:S(2)}, u32[]{:S(2)}) collective-permute-start(bf16[2,768,128]{2,1,0:T(8,128)(2,1)} %get-tuple-element.118), channel_id=1, source_target_pairs={{0,16},{4,20},{8,24},{12,28},{16,0},{20,4},{24,8},{28,12},{1,17},{... | collective-permute-start | bytes 1179656 | tf_op jit(solution)/shard_map/ppermute | solution.py:918
  162.8 112.7 %collective-permute-start.14 = (bf16[2,768,128]{2,1,0:T(8,128)(2,1)}, bf16[2,768,128]{2,1,0:T(8,128)(2,1)}, u32[]{:S(2)}, u32[]{:S(2)}) collective-permute-start(bf16[2,768,128]{2,1,0:T(8,128)(2,1)} %get-tuple-element.119), channel_id=1, source_target_pairs={{0,24},{4,28},{8,0},{12,4},{16,8},{20,12},{24,16},{28,20},{1,25},{... | collective-permute-start | bytes 1179656 | tf_op jit(solution)/shard_map/ppermute | solution.py:918
  165.5 92.1 %collective-permute-start.10 = (bf16[768,128]{1,0:T(8,128)(2,1)}, bf16[768,128]{1,0:T(8,128)(2,1)S(1)}, u32[]{:S(2)}, u32[]{:S(2)}) collective-permute-start(bf16[768,128]{1,0:T(8,128)(2,1)} %get-tuple-element.114), channel_id=1, source_target_pairs={{0,16},{4,20},{8,24},{12,28},{16,0},{20,4},{24,8},{28,12},{1,17},{... | collective-permute-start | bytes 589832 | tf_op jit(solution)/shard_map/ppermute | solution.py:918
  167.3 94.9 %collective-permute-start.11 = (bf16[768,128]{1,0:T(8,128)(2,1)}, bf16[768,128]{1,0:T(8,128)(2,1)S(1)}, u32[]{:S(2)}, u32[]{:S(2)}) collective-permute-start(bf16[768,128]{1,0:T(8,128)(2,1)} %get-tuple-element.115), channel_id=1, source_target_pairs={{0,24},{4,28},{8,0},{12,4},{16,8},{20,12},{24,16},{28,20},{1,25},{... | collective-permute-start | bytes 589832 | tf_op jit(solution)/shard_map/ppermute | solution.py:918
  262.2 78.7 %collective-permute-start.23 = (bf16[2,8,64,512]{3,2,1,0:T(8,128)(2,1)}, bf16[2,8,64,512]{3,2,1,0:T(8,128)(2,1)}, u32[]{:S(2)}, u32[]{:S(2)}) collective-permute-start(bf16[2,8,64,512]{3,2,1,0:T(8,128)(2,1)} %pad_maximum_fusion.8), channel_id=1, source_target_pairs={{0,2},{1,3},{2,0},{3,1},{4,6},{5,7},{6,4},{7,5},{8,10},{9,11},{10,... | collective-permute-start | bytes 3145736 | tf_op jit(solution)/shard_map/ppermute | solution.py:41
  306.7 30.5 %collective-permute-start.20 = (bf16[768,128]{1,0:T(8,128)(2,1)}, bf16[768,128]{1,0:T(8,128)(2,1)S(1)}, u32[]{:S(2)}, u32[]{:S(2)}) collective-permute-start(bf16[768,128]{1,0:T(8,128)(2,1)} %get-tuple-element.122), channel_id=1, source_target_pairs={{0,16},{4,20},{8,24},{12,28},{16,0},{20,4},{24,8},{28,12},{1,17},{... | collective-permute-start | bytes 589832 | tf_op jit(solution)/shard_map/ppermute | solution.py:918
  306.7 30.5 %collective-permute-start.21 = (bf16[768,128]{1,0:T(8,128)(2,1)}, bf16[768,128]{1,0:T(8,128)(2,1)S(1)}, u32[]{:S(2)}, u32[]{:S(2)}) collective-permute-start(bf16[768,128]{1,0:T(8,128)(2,1)} %get-tuple-element.123), channel_id=1, source_target_pairs={{0,8},{4,12},{8,16},{12,20},{16,24},{20,28},{24,0},{28,4},{1,9},{5... | collective-permute-start | bytes 589832 | tf_op jit(solution)/shard_map/ppermute | solution.py:918
  351.4 19.7 %collective-permute-start.24 = (bf16[192,2048]{1,0:T(8,128)(2,1)}, bf16[192,2048]{1,0:T(8,128)(2,1)S(1)}, u32[]{:S(2)}, u32[]{:S(2)}) collective-permute-start(bf16[192,2048]{1,0:T(8,128)(2,1)} %get-tuple-element.128), channel_id=1, source_target_pairs={{0,2},{1,3},{2,0},{3,1},{4,6},{5,7},{6,4},{7,5},{8,10},{9,11},{10,... | collective-permute-start | bytes 2359304 | tf_op jit(solution)/shard_map/ppermute | solution.py:41
  353.4 19.2 %collective-permute-start.27 = (bf16[192,2048]{1,0:T(8,128)(2,1)}, bf16[192,2048]{1,0:T(8,128)(2,1)S(1)}, u32[]{:S(2)}, u32[]{:S(2)}) collective-permute-start(bf16[192,2048]{1,0:T(8,128)(2,1)} %get-tuple-element.129), channel_id=1, source_target_pairs={{0,1},{1,0},{2,3},{3,2},{4,5},{5,4},{6,7},{7,6},{8,9},{9,8},{10,11... | collective-permute-start | bytes 2359304 | tf_op jit(solution)/shard_map/ppermute | solution.py:41
  443.6 26.7 %collective-permute-start.32 = (bf16[192,2048]{1,0:T(8,128)(2,1)}, bf16[192,2048]{1,0:T(8,128)(2,1)S(1)}, u32[]{:S(2)}, u32[]{:S(2)}) collective-permute-start(bf16[192,2048]{1,0:T(8,128)(2,1)} %get-tuple-element.135), channel_id=1, source_target_pairs={{0,2},{1,3},{2,0},{3,1},{4,6},{5,7},{6,4},{7,5},{8,10},{9,11},{10,... | collective-permute-start | bytes 2359304 | tf_op jit(solution)/shard_map/ppermute | solution.py:41
  445.1 25.2 %collective-permute-start.34 = (bf16[192,2048]{1,0:T(8,128)(2,1)}, bf16[192,2048]{1,0:T(8,128)(2,1)S(1)}, u32[]{:S(2)}, u32[]{:S(2)}) collective-permute-start(bf16[192,2048]{1,0:T(8,128)(2,1)} %get-tuple-element.136), channel_id=1, source_target_pairs={{0,1},{1,0},{2,3},{3,2},{4,5},{5,4},{6,7},{7,6},{8,9},{9,8},{10,11... | collective-permute-start | bytes 2359304 | tf_op jit(solution)/shard_map/ppermute | solution.py:41
  536.5 25.4 %collective-permute-start.40 = (bf16[192,2048]{1,0:T(8,128)(2,1)}, bf16[192,2048]{1,0:T(8,128)(2,1)S(1)}, u32[]{:S(2)}, u32[]{:S(2)}) collective-permute-start(bf16[192,2048]{1,0:T(8,128)(2,1)} %get-tuple-element.142), channel_id=1, source_target_pairs={{0,2},{1,3},{2,0},{3,1},{4,6},{5,7},{6,4},{7,5},{8,10},{9,11},{10,... | collective-permute-start | bytes 2359304 | tf_op jit(solution)/shard_map/ppermute | solution.py:41
  537.5 24.4 %collective-permute-start.43 = (bf16[192,2048]{1,0:T(8,128)(2,1)}, bf16[192,2048]{1,0:T(8,128)(2,1)S(1)}, u32[]{:S(2)}, u32[]{:S(2)}) collective-permute-start(bf16[192,2048]{1,0:T(8,128)(2,1)} %get-tuple-element.143), channel_id=1, source_target_pairs={{0,1},{1,0},{2,3},{3,2},{4,5},{5,4},{6,7},{7,6},{8,9},{9,8},{10,11... | collective-permute-start | bytes 2359304 | tf_op jit(solution)/shard_map/ppermute | solution.py:41
  656.5 35.6 %collective-permute-start.54 = (bf16[768,128]{1,0:T(8,128)(2,1)}, bf16[768,128]{1,0:T(8,128)(2,1)}, u32[]{:S(2)}, u32[]{:S(2)}) collective-permute-start(bf16[768,128]{1,0:T(8,128)(2,1)} %get-tuple-element.145), channel_id=1, source_target_pairs={{0,24},{4,28},{8,0},{12,4},{16,8},{20,12},{24,16},{28,20},{1,25},{... | collective-permute-start | bytes 589832 | tf_op jit(solution)/shard_map/ppermute | solution.py:918
  656.7 43.0 %collective-permute-start.55 = (bf16[768,128]{1,0:T(8,128)(2,1)}, bf16[768,128]{1,0:T(8,128)(2,1)}, u32[]{:S(2)}, u32[]{:S(2)}) collective-permute-start(bf16[768,128]{1,0:T(8,128)(2,1)} %get-tuple-element.146), channel_id=1, source_target_pairs={{0,16},{4,20},{8,24},{12,28},{16,0},{20,4},{24,8},{28,12},{1,17},{... | collective-permute-start | bytes 589832 | tf_op jit(solution)/shard_map/ppermute | solution.py:918
  657.2 42.5 %collective-permute-start.56 = (bf16[768,128]{1,0:T(8,128)(2,1)}, bf16[768,128]{1,0:T(8,128)(2,1)}, u32[]{:S(2)}, u32[]{:S(2)}) collective-permute-start(bf16[768,128]{1,0:T(8,128)(2,1)} %get-tuple-element.147), channel_id=1, source_target_pairs={{0,8},{4,12},{8,16},{12,20},{16,24},{20,28},{24,0},{28,4},{1,9},{5... | collective-permute-start | bytes 589832 | tf_op jit(solution)/shard_map/ppermute | solution.py:918
  658.8 48.5 %collective-permute-start.59 = (bf16[2,768,128]{2,1,0:T(8,128)(2,1)}, bf16[2,768,128]{2,1,0:T(8,128)(2,1)}, u32[]{:S(2)}, u32[]{:S(2)}) collective-permute-start(bf16[2,768,128]{2,1,0:T(8,128)(2,1)} %get-tuple-element.254), channel_id=1, source_target_pairs={{0,16},{4,20},{8,24},{12,28},{16,0},{20,4},{24,8},{28,12},{1,17},{... | collective-permute-start | bytes 1179656 | tf_op jit(solution)/shard_map/ppermute | solution.py:918
  665.2 42.1 %collective-permute-start.60 = (bf16[2,768,128]{2,1,0:T(8,128)(2,1)}, bf16[2,768,128]{2,1,0:T(8,128)(2,1)}, u32[]{:S(2)}, u32[]{:S(2)}) collective-permute-start(bf16[2,768,128]{2,1,0:T(8,128)(2,1)} %get-tuple-element.253), channel_id=1, source_target_pairs={{0,8},{4,12},{8,16},{12,20},{16,24},{20,28},{24,0},{28,4},{1,9},{5... | collective-permute-start | bytes 1179656 | tf_op jit(solution)/shard_map/ppermute | solution.py:918
  751.9 19.5 %collective-permute-start.64 = (bf16[2,2,80,512]{3,2,1,0:T(8,128)(2,1)S(1)}, bf16[2,2,80,512]{3,2,1,0:T(8,128)(2,1)S(1)}, u32[]{:S(2)}, u32[]{:S(2)}) collective-permute-start(bf16[2,2,80,512]{3,2,1,0:T(8,128)(2,1)S(1)} %dynamic-slice_bitcast_fusion.1), channel_id=1, source_target_pairs={{0,4},{4,0},{8,12},{12,8},{16,20},{20,16},{24,28},{28,24},{1,5},{5... | collective-permute-start | bytes 983048 | tf_op jit(solution)/shard_map/ppermute | solution.py:41
  759.5 44.0 %collective-permute-start.67 = (bf16[192,2048]{1,0:T(8,128)(2,1)}, bf16[192,2048]{1,0:T(8,128)(2,1)S(1)}, u32[]{:S(2)}, u32[]{:S(2)}) collective-permute-start(bf16[192,2048]{1,0:T(8,128)(2,1)} %get-tuple-element.193), channel_id=1, source_target_pairs={{0,2},{1,3},{2,0},{3,1},{4,6},{5,7},{6,4},{7,5},{8,10},{9,11},{10,... | collective-permute-start | bytes 2359304 | tf_op jit(solution)/shard_map/ppermute | solution.py:41
  760.5 43.0 %collective-permute-start.69 = (bf16[192,2048]{1,0:T(8,128)(2,1)}, bf16[192,2048]{1,0:T(8,128)(2,1)}, u32[]{:S(2)}, u32[]{:S(2)}) collective-permute-start(bf16[192,2048]{1,0:T(8,128)(2,1)} %get-tuple-element.194), channel_id=1, source_target_pairs={{0,1},{1,0},{2,3},{3,2},{4,5},{5,4},{6,7},{7,6},{8,9},{9,8},{10,11... | collective-permute-start | bytes 2359304 | tf_op jit(solution)/shard_map/ppermute | solution.py:41
  (175 other events, 1670.6 us)
Sparse Core Ops, SparseCore 0:
  11.9 73.9 all-gather.10
  88.1 46.5 all-gather.12
  136.2 216.9 all-gather.6
  354.7 80.1 all-gather.8
  720.7 43.2 reduce-scatter.1

commit v4 on v3

--- a/solution.py
+++ b/solution.py
@@ -106,11 +106,21 @@
 
 
 def scatter_groups(near, far, count):
+    return scatter_rest(scatter_first(near, far, count), count)
+
+
+def scatter_first(near, far, count):
     out = []
     size = near.shape[0] // 2
     for i, order in enumerate(part_orders(count)):
         got = flip(far[i], "tp", count, order[-1])
-        total = near[i * size : (i + 1) * size].astype(F32) + got.astype(F32)
+        out.append(near[i * size : (i + 1) * size].astype(F32) + got.astype(F32))
+    return out
+
+
+def scatter_rest(totals, count):
+    out = []
+    for total, order in zip(totals, part_orders(count)):
         for bit in order[-2::-1]:
             half = total.shape[0] // 2
             got = flip(total[half:].astype(BF16), "tp", count, bit)
@@ -172,16 +182,16 @@
 def load_plan(slots, group, rows, refs, q_buf, k_buf, v_buf):
     plan = []
     for i in range(slots):
-        plan.append((refs[i], q_buf.at[pl.ds(i * rows, rows)]))
+        plan.append((refs[i].at[0], q_buf.at[pl.ds(i * rows, rows)]))
     for i in range(slots * group):
         at = pl.ds(i * rows, rows)
-        ref = refs[slots + i]
-        plan += [(ref.at[0], k_buf.at[at]), (ref.at[1], v_buf.at[at])]
+        skip = int(i < slots)
+        plan += [(refs[i].at[skip], k_buf.at[at]), (refs[i].at[skip + 1], v_buf.at[at])]
     return plan
 
 
 def attend_kernel(slots, group, rows, prompt_count, q_seq, q_place, prompt_at, *refs):
-    n_in = slots + slots * group
+    n_in = slots * group
     outs = refs[n_in : n_in + slots]
     q_buf, k_buf, v_buf, kp, vp, o_buf, sem = refs[n_in + slots :]
     copy_all(load_plan(slots, group, rows, refs, q_buf, k_buf, v_buf), sem)
@@ -190,24 +200,31 @@
     scale = HEAD_DIM ** (-0.5) * LOG2E
     span = PROMPT_BLOCKS * BLK
 
-    def step(i, carry):
+    def block(i):
         at = pl.ds(pl.multiple_of(i * BLK, BLK), BLK)
         of_seq = pl.ds(pl.multiple_of(q_seq[i] * span, span), span)
         prompt, own, inverse = masked_scores(
             kp[of_seq, :], k_buf[at, :], q_buf[at, :], q_place[i], scale
         )
         result = mm_tn(vp[of_seq, :], prompt.astype(BF16)) + mm_tn(v_buf[at, :], own.astype(BF16))
-        o_buf[at, :] = (result * inverse).T.astype(BF16)
+        return at, (result * inverse).T.astype(BF16)
+
+    blocks = slots * rows // BLK
+    pair = 2 if blocks % 2 == 0 else 1
+
+    def step(i, carry):
+        for at, result in [block(i * pair + j) for j in range(pair)]:
+            o_buf[at, :] = result
         return carry
 
-    lax.fori_loop(0, slots * rows // BLK, step, 0)
+    lax.fori_loop(0, blocks // pair, step, 0)
     copy_all([(o_buf.at[pl.ds(i * rows, rows)], outs[i]) for i in range(slots)], sem)
 
 
 def attend_back_kernel(
     slots, group, rows, pieces, prompt_count, q_seq, q_place, prompt_at, piece_at, *refs
 ):
-    n_in = slots + slots * group
+    n_in = slots * group
     n_grad = slots * 2
     grads = refs[n_in : n_in + n_grad]
     outs = refs[n_in + n_grad : n_in + n_grad + slots]
@@ -245,7 +262,7 @@
 
     lax.fori_loop(0, own_rows // BLK, clear, 0)
 
-    def step(i, carry):
+    def block(i):
         at = rows_of(i)
         seq, place = q_seq[i], q_place[i]
         of_seq = pl.ds(pl.multiple_of(seq * span, span), span)
@@ -262,15 +279,31 @@
         ds_prompt = (prompt * (d_prompt - delta)).astype(BF16)
         ds_own = (own * (d_own - delta)).astype(BF16)
         dq = mm_tn(ds_prompt, kp[of_seq, :]) + mm_tn(ds_own, k_buf[at, :])
-        dq_buf[at, :] = (dq * scale).astype(BF16)
-        dvp[of_seq, :] += mm(prompt.astype(BF16), grad)
-        dkp[of_seq, :] += mm(ds_prompt, queries) * scale
-        dkv_buf[0, 0, at, :] = (mm(ds_own, queries) * scale).astype(BF16)
-        dkv_buf[0, 1, at, :] = mm(own.astype(BF16), grad).astype(BF16)
+        return (
+            at,
+            of_seq,
+            (dq * scale).astype(BF16),
+            mm(prompt.astype(BF16), grad),
+            mm(ds_prompt, queries) * scale,
+            (mm(ds_own, queries) * scale).astype(BF16),
+            mm(own.astype(BF16), grad).astype(BF16),
+        )
+
+    blocks = own_rows // BLK
+    pair = 2 if blocks % 2 == 0 else 1
+
+    def step(i, carry):
+        for at, of_seq, dq, dv_prompt, dk_prompt, dk_own, dv_own in [
+            block(i * pair + j) for j in range(pair)
+        ]:
+            dq_buf[at, :] = dq
+            dvp[of_seq, :] += dv_prompt
+            dkp[of_seq, :] += dk_prompt
+            dkv_buf[0, 0, at, :] = dk_own
+            dkv_buf[0, 1, at, :] = dv_own
         return carry
 
-    lax.fori_loop(0, own_rows // BLK, step, 0)
-    blocks = own_rows // BLK
+    lax.fori_loop(0, blocks // pair, step, 0)
 
     def spread(i, carry):
         place = prompt_at[i]
@@ -289,9 +322,9 @@
 ANY = pl.BlockSpec(memory_space=pl.ANY)
 
 
-def attend(tables, queries, near, far, prompt_count):
+def attend(tables, near, far, prompt_count):
     slots = len(near)
-    rows = queries[0].shape[0]
+    rows = near[0].shape[1]
     group = 1 + len(far) // slots
     own, every = slots * rows, slots * group * rows
     pairs = own * (PROMPT_BLOCKS + 1) * BLK
@@ -301,7 +334,7 @@
         out_shape=[jax.ShapeDtypeStruct((rows, HEAD_DIM), BF16)] * slots,
         grid_spec=pltpu.PrefetchScalarGridSpec(
             num_scalar_prefetch=3,
-            in_specs=[ANY] * (slots + slots * group),
+            in_specs=[ANY] * (slots * group),
             out_specs=[ANY] * slots,
             scratch_shapes=[
                 wide(own),
@@ -317,13 +350,13 @@
             flops=4 * pairs * HEAD_DIM, bytes_accessed=6 * every * HEAD_DIM, transcendentals=pairs
         ),
         name="attend",
-    )(*tables, *queries, *near, *far)
-
-
-def attend_back(tables, piece_at, queries, near, far, grads, prompt_count):
+    )(*tables, *near, *far)
+
+
+def attend_back(tables, piece_at, near, far, grads, prompt_count):
     pieces = piece_at.shape[0]
     slots = len(near)
-    rows = queries[0].shape[0]
+    rows = near[0].shape[1]
     group = 1 + len(far) // slots
     own, every = slots * rows, slots * group * rows
     pairs = own * (PROMPT_BLOCKS + 1) * BLK
@@ -334,7 +367,7 @@
         + [jax.ShapeDtypeStruct((2, own, HEAD_DIM), BF16)] * group,
         grid_spec=pltpu.PrefetchScalarGridSpec(
             num_scalar_prefetch=4,
-            in_specs=[ANY] * (slots + slots * group + 2 * slots),
+            in_specs=[ANY] * (slots * group + 2 * slots),
             out_specs=[ANY] * (slots + group),
             scratch_shapes=[
                 wide(own),
@@ -354,7 +387,7 @@
             flops=10 * pairs * HEAD_DIM, bytes_accessed=12 * every * HEAD_DIM, transcendentals=pairs
         ),
         name="attend_back",
-    )(*tables, piece_at, *queries, *near, *far, *grads)
+    )(*tables, piece_at, *near, *far, *grads)
 
 
 def turn(values, cosine, sine):
@@ -383,12 +416,9 @@
                 scaled = z[at, lanes(head, which * cols)] * factor
                 scaled = scaled * gain[which : which + 1, lanes(head)]
                 turned = turn(scaled, cosine, sine).astype(BF16)
-                if which == 0:
-                    outs[k][to, :] = turned
-                else:
-                    outs[slots + k][0, to, :] = turned
+                outs[k][which, to, :] = turned
         for k in range(slots):
-            outs[slots + k][1, to, :] = z[at, lanes(order[k], 2 * cols)].astype(BF16)
+            outs[k][2, to, :] = z[at, lanes(order[k], 2 * cols)].astype(BF16)
         return carry
 
     lax.fori_loop(0, pieces, step, 0)
@@ -402,10 +432,9 @@
     rows = z.shape[0]
     return pl.pallas_call(
         functools.partial(spread_kernel, slots, piece_at.shape[0]),
-        out_shape=[jax.ShapeDtypeStruct((rows, HEAD_DIM), BF16)] * slots
-        + [jax.ShapeDtypeStruct((2, rows, HEAD_DIM), BF16)] * slots,
+        out_shape=[jax.ShapeDtypeStruct((3, rows, HEAD_DIM), BF16)] * slots,
         grid_spec=pltpu.PrefetchScalarGridSpec(
-            num_scalar_prefetch=2, in_specs=[WHOLE] * 4, out_specs=[WHOLE] * (2 * slots)
+            num_scalar_prefetch=2, in_specs=[WHOLE] * 4, out_specs=[WHOLE] * slots
         ),
         compiler_params=BIG,
         name="spread_heads",
@@ -977,10 +1006,9 @@
         .reshape(2 * slots_a, hidden_cols)
     )
     spread = spread_heads(head_order, piece_at, z, inv.T, cs, gain, heads)
-    near = [head_shift(spread[heads + k], k) for k in range(heads)]
-    queries = [head_shift(spread[k], k) for k in range(heads)]
-    far = [group_shift(near[k], -j) for j in range(1, group) for k in range(heads)]
-    attended = attend(tables, queries, near, far, prompt_count)
+    near = [head_shift(spread[k], k) for k in range(heads)]
+    far = [group_shift(near[k][1:], -j) for j in range(1, group) for k in range(heads)]
+    attended = attend(tables, near, far, prompt_count)
     heads_out = collect_heads(
         head_order, piece_at, [head_shift(attended[k], -k) for k in range(heads)]
     )
@@ -1003,6 +1031,7 @@
     gates, ups, acts, gu_latents = zip(
         *[gate_up_product(h_low[g], w_gu, a_gu, b_gu, selects[g]) for g in groups]
     )
+    acts, w_down = lax.optimization_barrier((acts, w_down))
     *far_part, d_latent1 = add_product(acts[1], w_down, a_down, b_od[1], selects[1], 2)
     near_part, d_latent0 = add_product(acts[0], w_down, a_down, b_od[1], selects[0], 1)
     ff_out = scatter_groups(near_part, far_part, tp)
@@ -1047,7 +1076,7 @@
             ]
         )
     grads = [grads[g][k] for k in range(heads) for g in groups]
-    results = list(attend_back(tables, piece_at, queries, near, far, grads, prompt_count))
+    results = list(attend_back(tables, piece_at, near, far, grads, prompt_count))
     dqs = [head_shift(results[k], -k) for k in range(heads)]
     d_kv = results[heads].reshape(2, heads, rows, HEAD_DIM)
     others = [
@@ -1119,18 +1148,22 @@
     far_part[0], dz = lax.optimization_barrier((far_part[0], dz))
     (near_part,) = back_product(dz, 0, first, k_rows, us, a_qkv, 1)
     near_part, early, late_o = lax.optimization_barrier((near_part, early, late_o))
-    summed = scatter_groups(near_part, far_part, tp)
-    input_grad = jnp.concatenate([d_hidden[i] + summed[i] for i in groups], axis=0)
-
-    late = scatter_order(late, "seq", seqs, seq_order)
-    sum_tp = lambda value: sum_all(value.astype(BF16), "tp", tp).astype(F32)
+
     down_size = rank_cols * width // lane
     o_size = rank_cols * width // cols
-    both = sum_tp(
-        jnp.concatenate(
-            [early[: k_rows + down_size], late_o[:o_size].astype(BF16).reshape(-1, lane)], axis=0
-        )
-    )
+    both = jnp.concatenate(
+        [early[: k_rows + down_size], late_o[:o_size].astype(BF16).reshape(-1, lane)], axis=0
+    )
+    both = both + flip(both, "tp", tp, 0)
+    totals = scatter_first(near_part, far_part, tp)
+    late = scatter_order(late, "seq", seqs, seq_order)
+    totals, both, late = lax.optimization_barrier((totals, both, late))
+    for bit in range(1, bits_of(tp)):
+        both = both + flip(both, "tp", tp, bit)
+    both = both.astype(F32)
+    summed = scatter_rest(totals, tp)
+    input_grad = jnp.concatenate([d_hidden[i] + summed[i] for i in groups], axis=0)
+    grad_a_qkv = sum_all(late[:k_rows].astype(BF16), "tp", tp).astype(F32)
     grad_a_gu = both[:k_rows]
     grad_b_down = both[k_rows : k_rows + down_size].reshape(rank_cols, width)
     grad_b_o = both[k_rows + down_size :].reshape(rank_cols, width)
@@ -1139,7 +1172,6 @@
     grad_a_down = rest[:a_size].reshape(rank_cols, hidden_cols).T
     grad_b_gu = rest[a_size:].reshape(2, rank_cols, hidden_cols)
     grad_a_o = late_o[o_size:].T
-    grad_a_qkv = sum_tp(late[:k_rows])
     grad_b_qkv = late[k_rows:].reshape(rank_cols, 3, cols).transpose(1, 0, 2)
     grad_a_in = jnp.stack(
         [grad_a_qkv[:, i * slots_a : (i + 1) * slots_a] for i in range(3)]

time: 839 us -> 851 us (1.014)
  starting transfers between devices: 94.6 us -> 125 us
  waiting for transfers between devices: 327 us -> 302 us
    ppermute x21 -> x18, waiting for transfers between devices: 144 us -> 114 us  [head_shift(): lax.ppermute(value, 'seq', [(h * group + j, (h + by) % heads * group + j)...]
    ppermute x21 -> x18, starting transfers between devices: 35.4 us -> 62.8 us  [head_shift(): lax.ppermute(value, 'seq', [(h * group + j, (h + by) % heads * group + j)...]
    ppermute x40, waiting for transfers between devices: 102 us -> 111 us  [flip(): return lax.ppermute(value, axis, [(i, i ^ 1 << bit) for i in range(count)])]
    unnamed x276 -> x294, local copies, waits for them, and re-layouts: 32 us -> 32 us
  transfers between devices with their start and end apart: 83 -> 80, of which waited for: 45 -> 43; matrix products, arithmetic and copies ran while one was open for 19% -> 19% of each run, Pallas kernels for 16% -> 16%
where the time goes in v4:
time: 851 us; the launch traced here: 844 us
  waiting for transfers between devices  302 us (35%)
  Pallas kernels  204 us (24%)
  starting transfers between devices  125 us (15%)
  local copies, waits for them, and re-layouts  109 us (13%)
  other arithmetic  49.3 us (6%)
  matrix products  35.7 us (4%)
  between operations  18.7 us (2%)
    ppermute x18, waiting for transfers between devices, head_shift(): lax.ppermute(value, 'seq', [(h * group + j, (h + by) % heads * group + j)...  114 us
    ppermute x40, waiting for transfers between devices, flip(): return lax.ppermute(value, axis, [(i, i ^ 1 << bit) for i in range(count)])  111 us
    ppermute x18, starting transfers between devices, head_shift(): lax.ppermute(value, 'seq', [(h * group + j, (h + by) % heads * group + j)...  62.8 us
    ppermute x40, starting transfers between devices, flip(): return lax.ppermute(value, axis, [(i, i ^ 1 << bit) for i in range(count)])  46.4 us
    pallas_call x2, Pallas kernels, ff_back(): pl.pallas_call(functools.partial(ff_back_kernel, parts, n), grid=(n,), ou...  45.6 us
    all_gather x1, waiting for transfers between devices, local(): first = lax.all_gather(first, 'seq', axis=0)  35 us
    unnamed x294, local copies, waits for them, and re-layouts  32 us
    pallas_call x1, Pallas kernels, attend_back(): pl.pallas_call(functools.partial(attend_back_kernel, slots, group, rows,...  30.9 us
  transfers between devices with their start and end apart: 80, of which 43 were waited for; matrix products, arithmetic and copies ran while one was open for 19% of the time, Pallas kernels for 16%

profile of v4, /device:TPU:0, one launch (start us, length us, event | category | flops | bytes accessed | tf_op | source)
XLA Modules:
  0.0 843.8 jit_solution(5334177198009134397)
XLA Ops:
  22.4 10.9 %collective-permute-done = bf16[192,2048]{1,0:T(8,128)(2,1)S(1)} collective-permute-done((bf16[192,2048]{1,0:T(8,128)(2,1)S(1)}, bf16[192,2048]{1,0:T(8,128)(2,1)S(1)}, u32[]{:S(2)}, u32[]{:S(2)}) %collective-permute-start) | collective-permute-done | bytes 786464 | tf_op jit(solution)/shard_map/ppermute | solution.py:865
  33.3 17.6 %collective-permute-done.1 = bf16[192,2048]{1,0:T(8,128)(2,1)} collective-permute-done((bf16[192,2048]{1,0:T(8,128)(2,1)S(1)}, bf16[192,2048]{1,0:T(8,128)(2,1)}, u32[]{:S(2)}, u32[]{:S(2)}) %collective-permute-start.1) | collective-permute-done | bytes 786464 | tf_op jit(solution)/shard_map/ppermute | solution.py:865
  50.8 35.0 %all-gather.11.cloned.1.call-done = bf16[2304,1536]{1,0:T(8,128)(2,1)} async-done(((bf16[288,1536]{1,0:T(8,128)(2,1)}), bf16[2304,1536]{1,0:T(8,128)(2,1)}) %all-gather.11.cloned.1.call-update) | async-done | bytes 7077904 | tf_op jit(solution)/shard_map/all_gather | solution.py:867
  124.0 10.4 %qkv_product.1 = (f32[768,1536]{1,0:T(8,128)}, f32[3,768,1]{2,1,0:T(8,128)}) custom-call(bf16[768,2048]{1,0:T(8,128)(2,1)} %slice_dynamic-update-slice_fusion.x, bf16[768,384]{1,0:T(8,128)(2,1)} %fusion.7.latent, bf16[8,288,1536]{2,1,0:T(8,128)(2,1)} %bitcast.277, bf16[128,1536]{1,0:T(8,128)(2,1)} %bitcast.323), custom_call_target="tpu_custom_call" | custom-call | flops 4831838208 | bytes 7077888 | tf_op jit(solution)/shard_map/qkv_product/pallas_call | solution.py:562
  134.4 5.8 copy.210
  154.2 7.3 spread_heads.1
  169.6 22.8 %collective-permute-done.9.refs_1_ = bf16[3,768,128]{2,1,0:T(8,128)(2,1)S(1)} collective-permute-done((bf16[3,768,128]{2,1,0:T(8,128)(2,1)}, bf16[3,768,128]{2,1,0:T(8,128)(2,1)S(1)}, u32[]{:S(2)}, u32[]{:S(2)}) %collective-permute-start.9) | collective-permute-done | bytes 589856 | tf_op jit(solution)/shard_map/ppermute | solution.py:947
  193.2 39.3 %collective-permute-done.10.refs_2_ = bf16[3,768,128]{2,1,0:T(8,128)(2,1)S(1)} collective-permute-done((bf16[3,768,128]{2,1,0:T(8,128)(2,1)}, bf16[3,768,128]{2,1,0:T(8,128)(2,1)S(1)}, u32[]{:S(2)}, u32[]{:S(2)}) %collective-permute-start.10) | collective-permute-done | bytes 589856 | tf_op jit(solution)/shard_map/ppermute | solution.py:947
  241.5 18.8 %attend.1 = (bf16[768,128]{1,0:T(8,128)(2,1)}, bf16[768,128]{1,0:T(8,128)(2,1)}, bf16[768,128]{1,0:T(8,128)(2,1)}, bf16[768,128]{1,0:T(8,128)(2,1)}) custom-call(s32[24]{0:T(128)} %bitcast.356, s32[24]{0:T(128)} %bitcast.358, s32[24]{0:T(128)} %select_reduce_fusion.2.prompt_at, bf16[3,768,128]{2,1,0:T(8,128)(2,1)} %get-tuple-element.115.refs_0_, ...), custom_call_target="tpu_custom_call" | custom-call | flops 1811939328 | bytes 4718592 | tf_op jit(solution)/shard_map/attend/pallas_call | solution.py:332
  260.3 41.2 %collective-permute-start.16 = (bf16[768,128]{1,0:T(8,128)(2,1)}, bf16[768,128]{1,0:T(8,128)(2,1)S(1)}, u32[]{:S(2)}, u32[]{:S(2)}) collective-permute-start(bf16[768,128]{1,0:T(8,128)(2,1)} %get-tuple-element.120), channel_id=1, source_target_pairs={{0,24},{4,28},{8,0},{12,4},{16,8},{20,12},{24,16},{28,20},{1,25},{... | collective-permute-start | bytes 589832 | tf_op jit(solution)/shard_map/ppermute | solution.py:947
  311.3 25.0 %collective-permute-done.17.refs_2_ = bf16[768,128]{1,0:T(8,128)(2,1)S(1)} collective-permute-done((bf16[768,128]{1,0:T(8,128)(2,1)}, bf16[768,128]{1,0:T(8,128)(2,1)S(1)}, u32[]{:S(2)}, u32[]{:S(2)}) %collective-permute-start.17) | collective-permute-done | bytes 196640 | tf_op jit(solution)/shard_map/ppermute | solution.py:947
  358.3 11.8 %collective-permute-done.21 = bf16[192,2048]{1,0:T(8,128)(2,1)S(1)} collective-permute-done((bf16[192,2048]{1,0:T(8,128)(2,1)}, bf16[192,2048]{1,0:T(8,128)(2,1)S(1)}, u32[]{:S(2)}, u32[]{:S(2)}) %collective-permute-start.21) | collective-permute-done | bytes 786464 | tf_op jit(solution)/shard_map/ppermute | solution.py:41
  375.7 8.1 collective-permute-done.25
  387.9 6.4 collective-permute-done.23
  417.0 14.7 %gate_up_product.3 = (f32[384,2048]{1,0:T(8,128)}, f32[384,2048]{1,0:T(8,128)}, bf16[384,2048]{1,0:T(8,128)(2,1)}, bf16[384,256]{1,0:T(8,128)(2,1)}) custom-call(bf16[384,2048]{1,0:T(8,128)(2,1)} %copy-done.8, bf16[2048,256]{1,0:T(8,128)(2,1)} %bitcast.280, f32[384,128]{1,0:T(8,128)} %get-tuple-element.305.pick, ...), custom_call_target="tpu_custom_call" | custom-call | flops 6442450944 | bytes 16777216 | tf_op jit(solution)/shard_map/gate_up_product/pallas_call | solution.py:683
  431.7 14.6 %gate_up_product.2 = (f32[384,2048]{1,0:T(8,128)}, f32[384,2048]{1,0:T(8,128)}, bf16[384,2048]{1,0:T(8,128)(2,1)}, bf16[384,256]{1,0:T(8,128)(2,1)}) custom-call(bf16[384,2048]{1,0:T(8,128)(2,1)} %pad_maximum_fusion.2.h, bf16[2048,256]{1,0:T(8,128)(2,1)} %bitcast.281, f32[384,128]{1,0:T(8,128)} %get-tuple-element.304.pick, ...), custom_call_target="tpu_custom_call" | custom-call | flops 6442450944 | bytes 16777216 | tf_op jit(solution)/shard_map/gate_up_product/pallas_call | solution.py:683
  446.3 8.7 %add_product.7 = (bf16[192,2048]{1,0:T(8,128)(2,1)}, bf16[192,2048]{1,0:T(8,128)(2,1)}, bf16[384,128]{1,0:T(8,128)(2,1)}) custom-call(bf16[384,2048]{1,0:T(8,128)(2,1)} %get-tuple-element.136.a, bf16[2048,2048]{1,0:T(8,128)(2,1)} %all-gather.9.cloned.1.call-done.weight.w_down, bf16[2048,128]{1,0:T(8,128)(2,1)} %bitcast.305, bf16[128,2048]{1,0:T(8,128)(2,1)} %bitcast.309, ...), custom_call_target="tpu_custom_call" | custom-call | flops 3221225472 | bytes 8388608 | tf_op jit(solution)/shard_map/add_product/pallas_call | solution.py:605
  457.1 9.2 %add_product.6 = (bf16[384,2048]{1,0:T(8,128)(2,1)}, bf16[384,128]{1,0:T(8,128)(2,1)}) custom-call(bf16[384,2048]{1,0:T(8,128)(2,1)} %get-tuple-element.133.a, bf16[2048,2048]{1,0:T(8,128)(2,1)} %all-gather.9.cloned.1.call-done.weight.w_down, bf16[2048,128]{1,0:T(8,128)(2,1)} %bitcast.306, bf16[128,2048]{1,0:T(8,128)(2,1)} %bitcast.310, ...), custom_call_target="tpu_custom_call" | custom-call | flops 3221225472 | bytes 8388608 | tf_op jit(solution)/shard_map/add_product/pallas_call | solution.py:605
  476.4 5.8 collective-permute-done.30
  488.1 10.1 %collective-permute-done.33 = bf16[96,2048]{1,0:T(8,128)(2,1)S(1)} collective-permute-done((bf16[96,2048]{1,0:T(8,128)(2,1)S(1)}, bf16[96,2048]{1,0:T(8,128)(2,1)S(1)}, u32[]{:S(2)}, u32[]{:S(2)}) %collective-permute-start.33) | collective-permute-done | bytes 393248 | tf_op jit(solution)/shard_map/ppermute | solution.py:41
  501.7 8.6 %collective-permute-done.35 = bf16[192,2048]{1,0:T(8,128)(2,1)S(1)} collective-permute-done((bf16[192,2048]{1,0:T(8,128)(2,1)S(1)}, bf16[192,2048]{1,0:T(8,128)(2,1)S(1)}, u32[]{:S(2)}, u32[]{:S(2)}) %collective-permute-start.35) | collective-permute-done | bytes 786464 | tf_op jit(solution)/shard_map/ppermute | solution.py:41
  513.5 22.7 %ff_back.3 = (bf16[192,2048]{1,0:T(8,128)(2,1)}, bf16[192,2048]{1,0:T(8,128)(2,1)}, bf16[384,2048]{1,0:T(8,128)(2,1)}, bf16[384,2048]{1,0:T(8,128)(2,1)}, bf16[3...) custom-call(bf16[384,2048]{1,0:T(8,128)(2,1)} %copy-done.19, bf16[128,2048]{1,0:T(8,128)(2,1)} %bitcast.311, ...), custom_call_target="tpu_custom_call" | custom-call | flops 9663676416 | bytes 25165824 | tf_op jit(solution)/shard_map/ff_back/pallas_call | solution.py:767
  538.2 22.9 %ff_back.2 = (bf16[384,2048]{1,0:T(8,128)(2,1)}, bf16[384,2048]{1,0:T(8,128)(2,1)}, bf16[384,2048]{1,0:T(8,128)(2,1)}, bf16[384,256]{1,0:T(8,128)(2,1)}, bf16[384,128]{1,0:T(8,128)(2,1)}) custom-call(bf16[384,2048]{1,0:T(8,128)(2,1)} %pad_maximum_fusion.4.d_ff, bf16[128,2048]{1,0:T(8,128)(2,1)} %bitcast.312, f32[384,128]{1,0:T(8,128)} %get-tuple-element.304.pick, ...), custom_call_target="tpu_custom_call" | custom-call | flops 9663676416 | bytes 25165824 | tf_op jit(solution)/shard_map/ff_back/pallas_call | solution.py:767
  565.7 9.2 %collective-permute-done.38 = bf16[96,2048]{1,0:T(8,128)(2,1)S(1)} collective-permute-done((bf16[96,2048]{1,0:T(8,128)(2,1)S(1)}, bf16[96,2048]{1,0:T(8,128)(2,1)S(1)}, u32[]{:S(2)}, u32[]{:S(2)}) %collective-permute-start.38) | collective-permute-done | bytes 393248 | tf_op jit(solution)/shard_map/ppermute | solution.py:41
  613.7 30.9 %attend_back.1 = (bf16[768,128]{1,0:T(8,128)(2,1)}, bf16[768,128]{1,0:T(8,128)(2,1)}, bf16[768,128]{1,0:T(8,128)(2,1)}, bf16[768,128]{1,0:T(8,128)(2,1)}, bf16[2...) custom-call(s32[24]{0:T(128)} %bitcast.357, s32[24]{0:T(128)} %bitcast.359, s32[24]{0:T(128)} %select_reduce_fusion.2.prompt_at, ...), custom_call_target="tpu_custom_call" | custom-call | flops 4529848320 | bytes 9437184 | tf_op jit(solution)/shard_map/attend_back/pallas_call | solution.py:364
  698.4 7.6 collective-permute-done.56.refs_6_.refs_2_
  706.0 8.2 unturn_heads.1
  723.9 7.3 norm_back_heads.1.a
  752.3 7.4 back_product.2
  762.6 10.4 %collective-permute-done.68 = bf16[2,320,384]{2,1,0:T(8,128)(2,1)S(1)} collective-permute-done((bf16[2,320,384]{2,1,0:T(8,128)(2,1)S(1)}, bf16[2,320,384]{2,1,0:T(8,128)(2,1)S(1)}, u32[]{:S(2)}, u32[]{:S(2)}) %collective-permute-start.68) | collective-permute-done | bytes 491552 | tf_op jit(solution)/shard_map/ppermute | solution.py:41
  774.0 7.5 back_product.3
  790.1 10.8 %collective-permute-done.64 = bf16[192,2048]{1,0:T(8,128)(2,1)} collective-permute-done((bf16[192,2048]{1,0:T(8,128)(2,1)}, bf16[192,2048]{1,0:T(8,128)(2,1)}, u32[]{:S(2)}, u32[]{:S(2)}) %collective-permute-start.64) | collective-permute-done | bytes 786464 | tf_op jit(solution)/shard_map/ppermute | solution.py:41
  (683 shorter events, 348.1 us)
Async XLA Ops:
  7.2 78.7 %all-gather.11.cloned.1.call-start = ((), (), s32[]{:S(2)}) async-start(), calls=%async_computation.4 | async-start | bytes 7962624 | tf_op jit(solution)/shard_map/all_gather | solution.py:867
  11.8 136.3 %all-gather.13.cloned.1.call-start = ((), (), s32[]{:S(2)}) async-start(), calls=%async_computation.5 | async-start | bytes 4866048 | tf_op jit(solution)/shard_map/all_gather | solution.py:886
  11.8 21.4 %collective-permute-start = (bf16[192,2048]{1,0:T(8,128)(2,1)S(1)}, bf16[192,2048]{1,0:T(8,128)(2,1)S(1)}, u32[]{:S(2)}, u32[]{:S(2)}) collective-permute-start(bf16[192,2048]{1,0:T(8,128)(2,1)S(1)} %copy-done.22), channel_id=1, source_target_pairs={{0,1},{1,0},{2,3},{3,2},{4,5},{5,4},{6,7},{7,6},{8,9},{9,8},{10,11... | collective-permute-start | bytes 2359304 | tf_op jit(solution)/shard_map/ppermute | solution.py:865
  14.9 36.0 %collective-permute-start.1 = (bf16[192,2048]{1,0:T(8,128)(2,1)S(1)}, bf16[192,2048]{1,0:T(8,128)(2,1)}, u32[]{:S(2)}, u32[]{:S(2)}) collective-permute-start(bf16[192,2048]{1,0:T(8,128)(2,1)S(1)} %copy-done.22), channel_id=1, source_target_pairs={{0,2},{1,3},{2,0},{3,1},{4,6},{5,7},{6,4},{7,5},{8,10},{9,11},{10,... | collective-permute-start | bytes 2359304 | tf_op jit(solution)/shard_map/ppermute | solution.py:865
  16.4 34.4 %collective-permute-start.2 = (bf16[192,2048]{1,0:T(8,128)(2,1)S(1)}, bf16[192,2048]{1,0:T(8,128)(2,1)}, u32[]{:S(2)}, u32[]{:S(2)}) collective-permute-start(bf16[192,2048]{1,0:T(8,128)(2,1)S(1)} %copy-done.22), channel_id=1, source_target_pairs={{0,3},{1,2},{2,1},{3,0},{4,7},{5,6},{6,5},{7,4},{8,11},{9,10},{10,... | collective-permute-start | bytes 2359304 | tf_op jit(solution)/shard_map/ppermute | solution.py:865
  85.9 330.0 %all-gather.7.cloned.1.call-start = ((), (), s32[]{:S(2)}) async-start(), calls=%async_computation.1 | async-start | bytes 18874368 | tf_op jit(solution)/shard_map/all_gather | solution.py:887
  86.6 359.6 %all-gather.9.cloned.1.call-start = ((), (), s32[]{:S(2)}) async-start(), calls=%async_computation.2 | async-start | bytes 9437184 | tf_op jit(solution)/shard_map/all_gather | solution.py:888
  97.0 19.7 %collective-permute-start.4 = (bf16[8,64,384]{2,1,0:T(8,128)(2,1)}, bf16[8,64,384]{2,1,0:T(8,128)(2,1)}, u32[]{:S(2)}, u32[]{:S(2)}) collective-permute-start(bf16[8,64,384]{2,1,0:T(8,128)(2,1)} %reshape.572), channel_id=1, source_target_pairs={{0,2},{1,3},{2,0},{3,1},{4,6},{5,7},{6,4},{7,5},{8,10},{9,11},{10,... | collective-permute-start | bytes 1179656 | tf_op jit(solution)/shard_map/ppermute | solution.py:894
  98.4 19.3 %collective-permute-start.5 = (bf16[8,64,384]{2,1,0:T(8,128)(2,1)}, bf16[8,64,384]{2,1,0:T(8,128)(2,1)}, u32[]{:S(2)}, u32[]{:S(2)}) collective-permute-start(bf16[8,64,384]{2,1,0:T(8,128)(2,1)} %reshape.572), channel_id=1, source_target_pairs={{0,3},{1,2},{2,1},{3,0},{4,7},{5,6},{6,5},{7,4},{8,11},{9,10},{10,... | collective-permute-start | bytes 1179656 | tf_op jit(solution)/shard_map/ppermute | solution.py:894
  103.1 684.2 %reduce-scatter.2.cloned.1.call-start = ((), (), s32[]{:S(2)}) async-start(), calls=%async_computation.3 | async-start | bytes 3538944 | tf_op jit(solution)/shard_map/reduce_scatter | solution.py:1122
  161.5 30.8 %collective-permute-start.9 = (bf16[3,768,128]{2,1,0:T(8,128)(2,1)}, bf16[3,768,128]{2,1,0:T(8,128)(2,1)S(1)}, u32[]{:S(2)}, u32[]{:S(2)}) collective-permute-start(bf16[3,768,128]{2,1,0:T(8,128)(2,1)} %get-tuple-element.116), channel_id=1, source_target_pairs={{0,8},{4,12},{8,16},{12,20},{16,24},{20,28},{24,0},{28,4},{1,9},{5... | collective-permute-start | bytes 1769480 | tf_op jit(solution)/shard_map/ppermute | solution.py:947
  161.5 71.0 %collective-permute-start.10 = (bf16[3,768,128]{2,1,0:T(8,128)(2,1)}, bf16[3,768,128]{2,1,0:T(8,128)(2,1)S(1)}, u32[]{:S(2)}, u32[]{:S(2)}) collective-permute-start(bf16[3,768,128]{2,1,0:T(8,128)(2,1)} %get-tuple-element.117), channel_id=1, source_target_pairs={{0,16},{4,20},{8,24},{12,28},{16,0},{20,4},{24,8},{28,12},{1,17},{... | collective-permute-start | bytes 1769480 | tf_op jit(solution)/shard_map/ppermute | solution.py:947
  162.9 74.7 %collective-permute-start.11 = (bf16[3,768,128]{2,1,0:T(8,128)(2,1)}, bf16[3,768,128]{2,1,0:T(8,128)(2,1)S(1)}, u32[]{:S(2)}, u32[]{:S(2)}) collective-permute-start(bf16[3,768,128]{2,1,0:T(8,128)(2,1)} %get-tuple-element.118), channel_id=1, source_target_pairs={{0,24},{4,28},{8,0},{12,4},{16,8},{20,12},{24,16},{28,20},{1,25},{... | collective-permute-start | bytes 1769480 | tf_op jit(solution)/shard_map/ppermute | solution.py:947
  169.0 171.1 %collective-permute-start.20 = (bf16[2,8,64,512]{3,2,1,0:T(8,128)(2,1)}, bf16[2,8,64,512]{3,2,1,0:T(8,128)(2,1)}, u32[]{:S(2)}, u32[]{:S(2)}) collective-permute-start(bf16[2,8,64,512]{3,2,1,0:T(8,128)(2,1)} %pad_maximum_fusion.8), channel_id=1, source_target_pairs={{0,2},{1,3},{2,0},{3,1},{4,6},{5,7},{6,4},{7,5},{8,10},{9,11},{10,... | collective-permute-start | bytes 3145736 | tf_op jit(solution)/shard_map/ppermute | solution.py:41
  169.5 72.0 %collective-permute-start.12 = (bf16[2,768,128]{2,1,0:T(8,128)(2,1)S(1)}, bf16[2,768,128]{2,1,0:T(8,128)(2,1)}, u32[]{:S(2)}, u32[]{:S(2)}) collective-permute-start(bf16[2,768,128]{2,1,0:T(8,128)(2,1)S(1)} %slice.503), channel_id=1, source_target_pairs={{0,4},{4,0},{8,12},{12,8},{16,20},{20,16},{24,28},{28,24},{1,5},{5... | collective-permute-start | bytes 1179656 | tf_op jit(solution)/shard_map/ppermute | solution.py:958
  192.4 49.1 %collective-permute-start.13 = (bf16[2,768,128]{2,1,0:T(8,128)(2,1)S(1)}, bf16[2,768,128]{2,1,0:T(8,128)(2,1)}, u32[]{:S(2)}, u32[]{:S(2)}) collective-permute-start(bf16[2,768,128]{2,1,0:T(8,128)(2,1)S(1)} %slice.633), channel_id=1, source_target_pairs={{0,4},{4,0},{8,12},{12,8},{16,20},{20,16},{24,28},{28,24},{1,5},{5... | collective-permute-start | bytes 1179656 | tf_op jit(solution)/shard_map/ppermute | solution.py:958
  260.3 51.1 %collective-permute-start.16 = (bf16[768,128]{1,0:T(8,128)(2,1)}, bf16[768,128]{1,0:T(8,128)(2,1)S(1)}, u32[]{:S(2)}, u32[]{:S(2)}) collective-permute-start(bf16[768,128]{1,0:T(8,128)(2,1)} %get-tuple-element.120), channel_id=1, source_target_pairs={{0,24},{4,28},{8,0},{12,4},{16,8},{20,12},{24,16},{28,20},{1,25},{... | collective-permute-start | bytes 589832 | tf_op jit(solution)/shard_map/ppermute | solution.py:947
  301.5 34.8 %collective-permute-start.17 = (bf16[768,128]{1,0:T(8,128)(2,1)}, bf16[768,128]{1,0:T(8,128)(2,1)S(1)}, u32[]{:S(2)}, u32[]{:S(2)}) collective-permute-start(bf16[768,128]{1,0:T(8,128)(2,1)} %get-tuple-element.121), channel_id=1, source_target_pairs={{0,16},{4,20},{8,24},{12,28},{16,0},{20,4},{24,8},{28,12},{1,17},{... | collective-permute-start | bytes 589832 | tf_op jit(solution)/shard_map/ppermute | solution.py:947
  301.5 34.8 %collective-permute-start.18 = (bf16[768,128]{1,0:T(8,128)(2,1)}, bf16[768,128]{1,0:T(8,128)(2,1)S(1)}, u32[]{:S(2)}, u32[]{:S(2)}) collective-permute-start(bf16[768,128]{1,0:T(8,128)(2,1)} %get-tuple-element.122), channel_id=1, source_target_pairs={{0,8},{4,12},{8,16},{12,20},{16,24},{20,28},{24,0},{28,4},{1,9},{5... | collective-permute-start | bytes 589832 | tf_op jit(solution)/shard_map/ppermute | solution.py:947
  350.3 19.9 %collective-permute-start.21 = (bf16[192,2048]{1,0:T(8,128)(2,1)}, bf16[192,2048]{1,0:T(8,128)(2,1)S(1)}, u32[]{:S(2)}, u32[]{:S(2)}) collective-permute-start(bf16[192,2048]{1,0:T(8,128)(2,1)} %get-tuple-element.127), channel_id=1, source_target_pairs={{0,2},{1,3},{2,0},{3,1},{4,6},{5,7},{6,4},{7,5},{8,10},{9,11},{10,... | collective-permute-start | bytes 2359304 | tf_op jit(solution)/shard_map/ppermute | solution.py:41
  351.8 19.6 %collective-permute-start.24 = (bf16[192,2048]{1,0:T(8,128)(2,1)}, bf16[192,2048]{1,0:T(8,128)(2,1)S(1)}, u32[]{:S(2)}, u32[]{:S(2)}) collective-permute-start(bf16[192,2048]{1,0:T(8,128)(2,1)} %get-tuple-element.128), channel_id=1, source_target_pairs={{0,1},{1,0},{2,3},{3,2},{4,5},{5,4},{6,7},{7,6},{8,9},{9,8},{10,11... | collective-permute-start | bytes 2359304 | tf_op jit(solution)/shard_map/ppermute | solution.py:41
  536.3 24.8 %collective-permute-start.37 = (bf16[192,2048]{1,0:T(8,128)(2,1)}, bf16[192,2048]{1,0:T(8,128)(2,1)S(1)}, u32[]{:S(2)}, u32[]{:S(2)}) collective-permute-start(bf16[192,2048]{1,0:T(8,128)(2,1)} %get-tuple-element.144), channel_id=1, source_target_pairs={{0,2},{1,3},{2,0},{3,1},{4,6},{5,7},{6,4},{7,5},{8,10},{9,11},{10,... | collective-permute-start | bytes 2359304 | tf_op jit(solution)/shard_map/ppermute | solution.py:41
  536.6 24.5 %collective-permute-start.40 = (bf16[192,2048]{1,0:T(8,128)(2,1)}, bf16[192,2048]{1,0:T(8,128)(2,1)S(1)}, u32[]{:S(2)}, u32[]{:S(2)}) collective-permute-start(bf16[192,2048]{1,0:T(8,128)(2,1)} %get-tuple-element.145), channel_id=1, source_target_pairs={{0,1},{1,0},{2,3},{3,2},{4,5},{5,4},{6,7},{7,6},{8,9},{9,8},{10,11... | collective-permute-start | bytes 2359304 | tf_op jit(solution)/shard_map/ppermute | solution.py:41
  655.2 38.9 %collective-permute-start.51 = (bf16[768,128]{1,0:T(8,128)(2,1)}, bf16[768,128]{1,0:T(8,128)(2,1)}, u32[]{:S(2)}, u32[]{:S(2)}) collective-permute-start(bf16[768,128]{1,0:T(8,128)(2,1)} %get-tuple-element.147), channel_id=1, source_target_pairs={{0,24},{4,28},{8,0},{12,4},{16,8},{20,12},{24,16},{28,20},{1,25},{... | collective-permute-start | bytes 589832 | tf_op jit(solution)/shard_map/ppermute | solution.py:947
  655.3 43.1 %collective-permute-start.52 = (bf16[768,128]{1,0:T(8,128)(2,1)}, bf16[768,128]{1,0:T(8,128)(2,1)}, u32[]{:S(2)}, u32[]{:S(2)}) collective-permute-start(bf16[768,128]{1,0:T(8,128)(2,1)} %get-tuple-element.148), channel_id=1, source_target_pairs={{0,16},{4,20},{8,24},{12,28},{16,0},{20,4},{24,8},{28,12},{1,17},{... | collective-permute-start | bytes 589832 | tf_op jit(solution)/shard_map/ppermute | solution.py:947
  655.9 42.5 %collective-permute-start.53 = (bf16[768,128]{1,0:T(8,128)(2,1)}, bf16[768,128]{1,0:T(8,128)(2,1)}, u32[]{:S(2)}, u32[]{:S(2)}) collective-permute-start(bf16[768,128]{1,0:T(8,128)(2,1)} %get-tuple-element.149), channel_id=1, source_target_pairs={{0,8},{4,12},{8,16},{12,20},{16,24},{20,28},{24,0},{28,4},{1,9},{5... | collective-permute-start | bytes 589832 | tf_op jit(solution)/shard_map/ppermute | solution.py:947
  657.5 48.5 %collective-permute-start.56 = (bf16[2,768,128]{2,1,0:T(8,128)(2,1)}, bf16[2,768,128]{2,1,0:T(8,128)(2,1)}, u32[]{:S(2)}, u32[]{:S(2)}) collective-permute-start(bf16[2,768,128]{2,1,0:T(8,128)(2,1)} %get-tuple-element.260), channel_id=1, source_target_pairs={{0,16},{4,20},{8,24},{12,28},{16,0},{20,4},{24,8},{28,12},{1,17},{... | collective-permute-start | bytes 1179656 | tf_op jit(solution)/shard_map/ppermute | solution.py:947
  664.0 42.0 %collective-permute-start.57 = (bf16[2,768,128]{2,1,0:T(8,128)(2,1)}, bf16[2,768,128]{2,1,0:T(8,128)(2,1)}, u32[]{:S(2)}, u32[]{:S(2)}) collective-permute-start(bf16[2,768,128]{2,1,0:T(8,128)(2,1)} %get-tuple-element.259), channel_id=1, source_target_pairs={{0,8},{4,12},{8,16},{12,20},{16,24},{20,28},{24,0},{28,4},{1,9},{5... | collective-permute-start | bytes 1179656 | tf_op jit(solution)/shard_map/ppermute | solution.py:947
  751.2 21.9 %collective-permute-start.68 = (bf16[2,320,384]{2,1,0:T(8,128)(2,1)S(1)}, bf16[2,320,384]{2,1,0:T(8,128)(2,1)S(1)}, u32[]{:S(2)}, u32[]{:S(2)}) collective-permute-start(bf16[2,320,384]{2,1,0:T(8,128)(2,1)S(1)} %fusion.36), channel_id=1, source_target_pairs={{0,8},{4,12},{8,0},{12,4},{16,24},{20,28},{24,16},{28,20},{1,9},{5... | collective-permute-start | bytes 1474568 | tf_op jit(solution)/shard_map/ppermute | solution.py:41
  759.8 24.7 %collective-permute-start.63 = (bf16[80,512]{1,0:T(8,128)(2,1)S(1)}, bf16[80,512]{1,0:T(8,128)(2,1)S(1)}, u32[]{:S(2)}, u32[]{:S(2)}) collective-permute-start(bf16[80,512]{1,0:T(8,128)(2,1)S(1)} %fusion.61), channel_id=1, source_target_pairs={{0,16},{4,20},{8,24},{12,28},{16,0},{20,4},{24,8},{28,12},{1,17},{... | collective-permute-start | bytes 245768 | tf_op jit(solution)/shard_map/ppermute | solution.py:41
  781.6 19.4 %collective-permute-start.64 = (bf16[192,2048]{1,0:T(8,128)(2,1)}, bf16[192,2048]{1,0:T(8,128)(2,1)}, u32[]{:S(2)}, u32[]{:S(2)}) collective-permute-start(bf16[192,2048]{1,0:T(8,128)(2,1)} %get-tuple-element.195), channel_id=1, source_target_pairs={{0,2},{1,3},{2,0},{3,1},{4,6},{5,7},{6,4},{7,5},{8,10},{9,11},{10,... | collective-permute-start | bytes 2359304 | tf_op jit(solution)/shard_map/ppermute | solution.py:41
  783.1 20.7 %collective-permute-start.65 = (bf16[192,2048]{1,0:T(8,128)(2,1)}, bf16[192,2048]{1,0:T(8,128)(2,1)}, u32[]{:S(2)}, u32[]{:S(2)}) collective-permute-start(bf16[192,2048]{1,0:T(8,128)(2,1)} %get-tuple-element.196), channel_id=1, source_target_pairs={{0,1},{1,0},{2,3},{3,2},{4,5},{5,4},{6,7},{7,6},{8,9},{9,8},{10,11... | collective-permute-start | bytes 2359304 | tf_op jit(solution)/shard_map/ppermute | solution.py:41
  (182 other events, 1616.1 us)
Sparse Core Ops, SparseCore 0:
  11.9 73.9 all-gather.10
  88.1 46.5 all-gather.12
  136.2 216.8 all-gather.6
  354.6 80.3 all-gather.8
  719.5 45.2 reduce-scatter.1

commit v5 on v4

--- a/solution.py
+++ b/solution.py
@@ -849,56 +849,6 @@
     n_seq = sequence_adapter.shape[0]
     groups = (0, 1)
 
-    a_part = k_rows // tp
-    b_part = width // tp
-    a_mine = lax.dynamic_slice_in_dim(input_first_factor, tp_rank * a_part, a_part, 1)
-    b_mine = lax.dynamic_slice_in_dim(output_down_second_factor, tp_rank * b_part, b_part, 2)
-    first = jnp.concatenate(
-        [
-            query_key_value_weight.transpose(1, 0, 2).reshape(k_rows, 3 * cols),
-            query_key_value_second.transpose(1, 0, 2).reshape(rank_cols, 3 * cols),
-            a_mine[:3].reshape(-1, 3 * cols),
-        ],
-        axis=0,
-    )
-    x_parts = [layer_input] + [
-        lax.ppermute(layer_input, "tp", [(i, i ^ mask) for i in range(tp)]) for mask in range(1, tp)
-    ]
-    first = lax.all_gather(first, "seq", axis=0)
-    pieces = [
-        output_weight.T,
-        output_first_factor.T,
-        b_mine.reshape(-1, cols),
-        a_mine[3:].reshape(-1, cols),
-        down_first_factor.T.reshape(-1, cols),
-        gate_up_second_factor.reshape(-1, cols),
-    ]
-    packed = jnp.concatenate(pieces, axis=0)
-    first, x_parts, packed, w_gu, w_down = lax.optimization_barrier(
-        (
-            first,
-            x_parts,
-            packed,
-            gate_up_weight.transpose(1, 0, 2).reshape(k_rows, 2 * hidden_cols),
-            down_weight.T,
-        )
-    )
-    packed = lax.all_gather(packed, "seq", axis=0)
-    w_gu = lax.all_gather(w_gu, "seq", axis=0, tiled=True)
-    w_down = lax.all_gather(w_down, "seq", axis=0, tiled=True)
-
-    tp_order, seq_order = list(range(bits_of(tp))), list(range(bits_of(seqs)))
-    a_qkv = first[:, k_rows + rank_cols :].reshape(seqs, 3, a_part, slots_a)
-    a_qkv = a_qkv.transpose(0, 2, 1, 3).reshape(seqs, a_part, 3 * slots_a)
-    a_parts = [a_qkv] + [
-        lax.ppermute(a_qkv, "tp", [(i, i ^ mask) for i in range(tp)]) for mask in range(1, tp)
-    ]
-    a_qkv = jnp.zeros((seqs, tp, a_part, 3 * slots_a), BF16)
-    for mask, value in enumerate(a_parts):
-        a_qkv = lax.dynamic_update_slice(a_qkv, value[:, None], (0, tp_rank ^ mask, 0, 0))
-    a_qkv = a_qkv.reshape(width, 3 * slots_a)
-    b_qkv = first[:, k_rows : k_rows + rank_cols].reshape(slots_a, 3 * cols)
-    b_qkv = blocked([b_qkv[:, i * cols : (i + 1) * cols] for i in range(3)])
     runs = row_runs(tp)
     piece_at = jnp.stack([2 * (tp_rank ^ mask) + which for mask, which in runs]).astype(jnp.int32)
     token = (piece_at[:, None] * part + jnp.arange(part, dtype=jnp.int32)[None, :]).reshape(-1)
@@ -921,6 +871,62 @@
     cosine, sine = jnp.cos(angles), jnp.sin(angles)
     cs = jnp.concatenate([cosine, cosine, -sine, sine], axis=1)
 
+    a_part = k_rows // tp
+    b_part = width // tp
+    a_mine = lax.dynamic_slice_in_dim(input_first_factor, tp_rank * a_part, a_part, 1)
+    b_mine = lax.dynamic_slice_in_dim(output_down_second_factor, tp_rank * b_part, b_part, 2)
+    first = jnp.concatenate(
+        [
+            query_key_value_weight.transpose(1, 0, 2).reshape(k_rows, 3 * cols),
+            query_key_value_second.transpose(1, 0, 2).reshape(rank_cols, 3 * cols),
+            a_mine[:3].reshape(-1, 3 * cols),
+        ],
+        axis=0,
+    )
+    x_parts = [layer_input] + [
+        lax.ppermute(layer_input, "tp", [(i, i ^ mask) for i in range(tp)]) for mask in range(1, tp)
+    ]
+    x = jnp.concatenate(
+        [x_parts[mask][which * part : (which + 1) * part] for mask, which in runs], axis=0
+    )
+    pick3 = jnp.tile(select, (1, 3))
+    first = lax.all_gather(first, "seq", axis=0)
+    pieces = [
+        output_weight.T,
+        output_first_factor.T,
+        b_mine.reshape(-1, cols),
+        a_mine[3:].reshape(-1, cols),
+        down_first_factor.T.reshape(-1, cols),
+        gate_up_second_factor.reshape(-1, cols),
+    ]
+    packed = jnp.concatenate(pieces, axis=0)
+    first, x, cs, pick3, packed, w_gu, w_down = lax.optimization_barrier(
+        (
+            first,
+            x,
+            cs,
+            pick3,
+            packed,
+            gate_up_weight.transpose(1, 0, 2).reshape(k_rows, 2 * hidden_cols),
+            down_weight.T,
+        )
+    )
+    packed = lax.all_gather(packed, "seq", axis=0)
+    w_gu = lax.all_gather(w_gu, "seq", axis=0, tiled=True)
+    w_down = lax.all_gather(w_down, "seq", axis=0, tiled=True)
+
+    tp_order, seq_order = list(range(bits_of(tp))), list(range(bits_of(seqs)))
+    a_qkv = first[:, k_rows + rank_cols :].reshape(seqs, 3, a_part, slots_a)
+    a_qkv = a_qkv.transpose(0, 2, 1, 3).reshape(seqs, a_part, 3 * slots_a)
+    a_parts = [a_qkv] + [
+        lax.ppermute(a_qkv, "tp", [(i, i ^ mask) for i in range(tp)]) for mask in range(1, tp)
+    ]
+    a_qkv = jnp.zeros((seqs, tp, a_part, 3 * slots_a), BF16)
+    for mask, value in enumerate(a_parts):
+        a_qkv = lax.dynamic_update_slice(a_qkv, value[:, None], (0, tp_rank ^ mask, 0, 0))
+    a_qkv = a_qkv.reshape(width, 3 * slots_a)
+    b_qkv = first[:, k_rows : k_rows + rank_cols].reshape(slots_a, 3 * cols)
+    b_qkv = blocked([b_qkv[:, i * cols : (i + 1) * cols] for i in range(3)])
     owner = (
         ((head_rank - jnp.arange(heads)) % heads)[None, :] * group
         + ((group_rank + jnp.arange(group)) % group)[:, None]
@@ -966,11 +972,7 @@
         )
 
     own = lambda value, i: value[i * part : (i + 1) * part].astype(F32)
-    x = jnp.concatenate(
-        [x_parts[mask][which * part : (which + 1) * part] for mask, which in runs], axis=0
-    )
     gain = lax.dynamic_slice_in_dim(norm_gain_table[:2], tp_rank * cols, cols, 1)
-    pick3 = jnp.tile(select, (1, 3))
     latents = (mm(x, a_qkv) * pick3).astype(BF16)
     z, squares = qkv_product(
         x, latents, first, first[:, k_rows : k_rows + rank_cols].reshape(slots_a, 3 * cols), k_rows, cols
@@ -1008,6 +1010,9 @@
     spread = spread_heads(head_order, piece_at, z, inv.T, cs, gain, heads)
     near = [head_shift(spread[k], k) for k in range(heads)]
     far = [group_shift(near[k][1:], -j) for j in range(1, group) for k in range(heads)]
+    far, w_o, a_o, b_od, a_gu, a_down, b_gu = lax.optimization_barrier(
+        (far, w_o, a_o, b_od, a_gu, a_down, b_gu)
+    )
     attended = attend(tables, near, far, prompt_count)
     heads_out = collect_heads(
         head_order, piece_at, [head_shift(attended[k], -k) for k in range(heads)]
@@ -1120,6 +1125,7 @@
     )
     dqs, dkvs, early, late_o = lax.optimization_barrier((dqs, dkvs, early, late_o))
     early = lax.psum_scatter(early, "seq", scatter_dimension=0, tiled=False)
+    dqs, dkvs, late_o = lax.optimization_barrier((dqs, dkvs, late_o))
     late_o = scatter_order(late_o, "seq", seqs, seq_order)
     scaled, parts = unturn_heads(head_order, piece_at, dqs, dkvs, z, cs, gain)
     parts = sum_rows(parts.T, tp) / width
@@ -1154,14 +1160,11 @@
     both = jnp.concatenate(
         [early[: k_rows + down_size], late_o[:o_size].astype(BF16).reshape(-1, lane)], axis=0
     )
-    both = both + flip(both, "tp", tp, 0)
-    totals = scatter_first(near_part, far_part, tp)
-    late = scatter_order(late, "seq", seqs, seq_order)
-    totals, both, late = lax.optimization_barrier((totals, both, late))
-    for bit in range(1, bits_of(tp)):
-        both = both + flip(both, "tp", tp, bit)
-    both = both.astype(F32)
-    summed = scatter_rest(totals, tp)
+    both = sum_all(both, "tp", tp).astype(F32)
+    late = lax.psum_scatter(late, "seq", scatter_dimension=0, tiled=False)
+    summed = scatter_groups(near_part, far_part, tp)
+    summed, late = lax.optimization_barrier((summed, late))
+    late = late.astype(F32)
     input_grad = jnp.concatenate([d_hidden[i] + summed[i] for i in groups], axis=0)
     grad_a_qkv = sum_all(late[:k_rows].astype(BF16), "tp", tp).astype(F32)
     grad_a_gu = both[:k_rows]

time: 851 us -> 826 us (0.971)
  waiting for transfers between devices: 302 us -> 273 us
    ppermute x18, waiting for transfers between devices: 114 us -> 94.6 us  [head_shift(): lax.ppermute(value, 'seq', [(h * group + j, (h + by) % heads * group + j)...]
    ppermute x3, waiting for transfers between devices: 28.4 us -> 18.7 us  [local(): lax.ppermute(layer_input, 'tp', [(i, i ^ mask) for i in range(tp)])]
    ppermute x3, waiting for transfers between devices: 5.39 us -> 14.9 us  [local(): lax.ppermute(a_qkv, 'tp', [(i, i ^ mask) for i in range(tp)])]
    ppermute x18, starting transfers between devices: 62.8 us -> 71.7 us  [head_shift(): lax.ppermute(value, 'seq', [(h * group + j, (h + by) % heads * group + j)...]
    all_gather x1, waiting for transfers between devices: 35 us -> 26.1 us  [local(): first = lax.all_gather(first, 'seq', axis=0)]
    ppermute x40 -> x37, starting transfers between devices: 46.4 us -> 39.6 us  [flip(): return lax.ppermute(value, axis, [(i, i ^ 1 << bit) for i in range(count)])]
    ppermute x40 -> x37, waiting for transfers between devices: 111 us -> 110 us  [flip(): return lax.ppermute(value, axis, [(i, i ^ 1 << bit) for i in range(count)])]
    unnamed x294 -> x272, local copies, waits for them, and re-layouts: 32 us -> 33.2 us
  transfers between devices with their start and end apart: 80 -> 78, of which waited for: 43 -> 47; matrix products, arithmetic and copies ran while one was open for 19% -> 21% of each run, Pallas kernels for 16% -> 17%
where the time goes in v5:
time: 826 us; the launch traced here: 819 us
  waiting for transfers between devices  273 us (33%)
  Pallas kernels  203 us (25%)
  starting transfers between devices  127 us (15%)
  local copies, waits for them, and re-layouts  111 us (13%)
  other arithmetic  51.1 us (6%)
  matrix products  34 us (4%)
  between operations  19.2 us (2%)
    ppermute x37, waiting for transfers between devices, flip(): return lax.ppermute(value, axis, [(i, i ^ 1 << bit) for i in range(count)])  110 us
    ppermute x18, waiting for transfers between devices, head_shift(): lax.ppermute(value, 'seq', [(h * group + j, (h + by) % heads * group + j)...  94.6 us
    ppermute x18, starting transfers between devices, head_shift(): lax.ppermute(value, 'seq', [(h * group + j, (h + by) % heads * group + j)...  71.7 us
    pallas_call x2, Pallas kernels, ff_back(): pl.pallas_call(functools.partial(ff_back_kernel, parts, n), grid=(n,), ou...  45.7 us
    ppermute x37, starting transfers between devices, flip(): return lax.ppermute(value, axis, [(i, i ^ 1 << bit) for i in range(count)])  39.6 us
    unnamed x272, local copies, waits for them, and re-layouts  33.2 us
    pallas_call x1, Pallas kernels, attend_back(): pl.pallas_call(functools.partial(attend_back_kernel, slots, group, rows,...  30.8 us
    pallas_call x2, Pallas kernels, gate_up_product(): pl.pallas_call(gate_up_kernel, grid=(n,), out_shape=[jax.ShapeDtypeStruct...  29.1 us
  transfers between devices with their start and end apart: 78, of which 47 were waited for; matrix products, arithmetic and copies ran while one was open for 21% of the time, Pallas kernels for 17%

profile of v5, /device:TPU:0, one launch (start us, length us, event | category | flops | bytes accessed | tf_op | source)
XLA Modules:
  0.0 819.2 jit_solution(3892508403739202925)
XLA Ops:
  36.0 14.9 %collective-permute-done.1 = bf16[192,2048]{1,0:T(8,128)(2,1)} collective-permute-done((bf16[192,2048]{1,0:T(8,128)(2,1)S(1)}, bf16[192,2048]{1,0:T(8,128)(2,1)}, u32[]{:S(2)}, u32[]{:S(2)}) %collective-permute-start.1) | collective-permute-done | bytes 786464 | tf_op jit(solution)/shard_map/ppermute | solution.py:887
  59.7 26.1 %all-gather.11.cloned.1.call-done = bf16[2304,1536]{1,0:T(8,128)(2,1)} async-done(((bf16[288,1536]{1,0:T(8,128)(2,1)}), bf16[2304,1536]{1,0:T(8,128)(2,1)}) %all-gather.11.cloned.1.call-update) | async-done | bytes 7077904 | tf_op jit(solution)/shard_map/all_gather | solution.py:893
  99.4 6.0 collective-permute-done.3
  106.5 8.9 %collective-permute-done.4 = bf16[8,64,384]{2,1,0:T(8,128)(2,1)} collective-permute-done((bf16[8,64,384]{2,1,0:T(8,128)(2,1)}, bf16[8,64,384]{2,1,0:T(8,128)(2,1)}, u32[]{:S(2)}, u32[]{:S(2)}) %collective-permute-start.4) | collective-permute-done | bytes 393248 | tf_op jit(solution)/shard_map/ppermute | solution.py:922
  122.6 10.4 %qkv_product.1 = (f32[768,1536]{1,0:T(8,128)}, f32[3,768,1]{2,1,0:T(8,128)}) custom-call(bf16[768,2048]{1,0:T(8,128)(2,1)} %slice_dynamic-update-slice_fusion.x, bf16[768,384]{1,0:T(8,128)(2,1)} %fusion.7.latent, bf16[8,288,1536]{2,1,0:T(8,128)(2,1)} %bitcast.262, bf16[128,1536]{1,0:T(8,128)(2,1)} %bitcast.302), custom_call_target="tpu_custom_call" | custom-call | flops 4831838208 | bytes 7077888 | tf_op jit(solution)/shard_map/qkv_product/pallas_call | solution.py:562
  150.2 9.1 %collective-permute-done.16 = bf16[8,64,512]{2,1,0:T(8,128)(2,1)S(1)} collective-permute-done((bf16[8,64,512]{2,1,0:T(8,128)(2,1)S(1)}, bf16[8,64,512]{2,1,0:T(8,128)(2,1)S(1)}, u32[]{:S(2)}, u32[]{:S(2)}) %collective-permute-start.16) | collective-permute-done | bytes 524320 | tf_op jit(solution)/shard_map/ppermute | solution.py:41
  163.5 7.3 spread_heads.1
  190.1 11.6 %collective-permute-done.9.refs_1_ = bf16[3,768,128]{2,1,0:T(8,128)(2,1)} collective-permute-done((bf16[3,768,128]{2,1,0:T(8,128)(2,1)}, bf16[3,768,128]{2,1,0:T(8,128)(2,1)}, u32[]{:S(2)}, u32[]{:S(2)}) %collective-permute-start.9) | collective-permute-done | bytes 589856 | tf_op jit(solution)/shard_map/ppermute | solution.py:953
  203.5 37.5 %collective-permute-done.10.refs_2_ = bf16[3,768,128]{2,1,0:T(8,128)(2,1)} collective-permute-done((bf16[3,768,128]{2,1,0:T(8,128)(2,1)}, bf16[3,768,128]{2,1,0:T(8,128)(2,1)}, u32[]{:S(2)}, u32[]{:S(2)}) %collective-permute-start.10) | collective-permute-done | bytes 589856 | tf_op jit(solution)/shard_map/ppermute | solution.py:953
  256.3 18.6 %attend.1 = (bf16[768,128]{1,0:T(8,128)(2,1)}, bf16[768,128]{1,0:T(8,128)(2,1)}, bf16[768,128]{1,0:T(8,128)(2,1)}, bf16[768,128]{1,0:T(8,128)(2,1)}) custom-call(s32[24]{0:T(128)} %bitcast.333, s32[24]{0:T(128)} %bitcast.335, s32[24]{0:T(128)} %select_reduce_fusion.2.prompt_at, bf16[3,768,128]{2,1,0:T(8,128)(2,1)} %get-tuple-element.131.refs_0_, ...), custom_call_target="tpu_custom_call" | custom-call | flops 1811939328 | bytes 4718592 | tf_op jit(solution)/shard_map/attend/pallas_call | solution.py:332
  274.9 44.0 %collective-permute-start.18 = (bf16[768,128]{1,0:T(8,128)(2,1)}, bf16[768,128]{1,0:T(8,128)(2,1)S(1)}, u32[]{:S(2)}, u32[]{:S(2)}) collective-permute-start(bf16[768,128]{1,0:T(8,128)(2,1)} %get-tuple-element.141), channel_id=1, source_target_pairs={{0,24},{4,28},{8,0},{12,4},{16,8},{20,12},{24,16},{28,20},{1,25},{... | collective-permute-start | bytes 589832 | tf_op jit(solution)/shard_map/ppermute | solution.py:953
  321.0 5.9 collective-permute-done.18.refs_1_
  326.9 17.4 %collective-permute-done.19.refs_2_ = bf16[768,128]{1,0:T(8,128)(2,1)S(1)} collective-permute-done((bf16[768,128]{1,0:T(8,128)(2,1)}, bf16[768,128]{1,0:T(8,128)(2,1)S(1)}, u32[]{:S(2)}, u32[]{:S(2)}) %collective-permute-start.19) | collective-permute-done | bytes 196640 | tf_op jit(solution)/shard_map/ppermute | solution.py:953
  361.4 10.8 %collective-permute-done.21 = bf16[192,2048]{1,0:T(8,128)(2,1)S(1)} collective-permute-done((bf16[192,2048]{1,0:T(8,128)(2,1)}, bf16[192,2048]{1,0:T(8,128)(2,1)S(1)}, u32[]{:S(2)}, u32[]{:S(2)}) %collective-permute-start.21) | collective-permute-done | bytes 786464 | tf_op jit(solution)/shard_map/ppermute | solution.py:41
  377.7 7.1 collective-permute-done.25
  399.4 13.1 %collective-permute-done.27 = bf16[192,2048]{1,0:T(8,128)(2,1)S(1)} collective-permute-done((bf16[192,2048]{1,0:T(8,128)(2,1)S(1)}, bf16[192,2048]{1,0:T(8,128)(2,1)S(1)}, u32[]{:S(2)}, u32[]{:S(2)}) %collective-permute-start.27) | collective-permute-done | bytes 786464 | tf_op jit(solution)/shard_map/ppermute | solution.py:41
  413.8 14.5 %gate_up_product.3 = (f32[384,2048]{1,0:T(8,128)}, f32[384,2048]{1,0:T(8,128)}, bf16[384,2048]{1,0:T(8,128)(2,1)}, bf16[384,256]{1,0:T(8,128)(2,1)}) custom-call(bf16[384,2048]{1,0:T(8,128)(2,1)} %copy-done.8, bf16[2048,256]{1,0:T(8,128)(2,1)} %bitcast.265, f32[384,128]{1,0:T(8,128)} %get-tuple-element.339.pick, ...), custom_call_target="tpu_custom_call" | custom-call | flops 6442450944 | bytes 16777216 | tf_op jit(solution)/shard_map/gate_up_product/pallas_call | solution.py:683
  428.3 14.6 %gate_up_product.2 = (f32[384,2048]{1,0:T(8,128)}, f32[384,2048]{1,0:T(8,128)}, bf16[384,2048]{1,0:T(8,128)(2,1)}, bf16[384,256]{1,0:T(8,128)(2,1)}) custom-call(bf16[384,2048]{1,0:T(8,128)(2,1)} %pad_maximum_fusion.2.h, bf16[2048,256]{1,0:T(8,128)(2,1)} %bitcast.266, f32[384,128]{1,0:T(8,128)} %get-tuple-element.338.pick, ...), custom_call_target="tpu_custom_call" | custom-call | flops 6442450944 | bytes 16777216 | tf_op jit(solution)/shard_map/gate_up_product/pallas_call | solution.py:683
  442.9 8.7 %add_product.7 = (bf16[192,2048]{1,0:T(8,128)(2,1)}, bf16[192,2048]{1,0:T(8,128)(2,1)}, bf16[384,128]{1,0:T(8,128)(2,1)}) custom-call(bf16[384,2048]{1,0:T(8,128)(2,1)} %get-tuple-element.162.a, bf16[2048,2048]{1,0:T(8,128)(2,1)} %all-gather.9.cloned.1.call-done.weight.w_down, bf16[2048,128]{1,0:T(8,128)(2,1)} %bitcast.284, ...), custom_call_target="tpu_custom_call" | custom-call | flops 3221225472 | bytes 8388608 | tf_op jit(solution)/shard_map/add_product/pallas_call | solution.py:605
  453.6 8.8 %add_product.6 = (bf16[384,2048]{1,0:T(8,128)(2,1)}, bf16[384,128]{1,0:T(8,128)(2,1)}) custom-call(bf16[384,2048]{1,0:T(8,128)(2,1)} %get-tuple-element.158.a, bf16[2048,2048]{1,0:T(8,128)(2,1)} %all-gather.9.cloned.1.call-done.weight.w_down, bf16[2048,128]{1,0:T(8,128)(2,1)} %bitcast.285, bf16[128,2048]{1,0:T(8,128)(2,1)} %get-tuple-element.316.second.b_down, ...), custom_call_target="tpu_custom_call" | custom-call | flops 3221225472 | bytes 8388608 | tf_op jit(solution)/shard_map/add_product/pallas_call | solution.py:605
  462.4 6.4 collective-permute-done.29
  473.8 6.5 collective-permute-done.30
  483.9 8.0 collective-permute-done.33
  497.4 10.5 %collective-permute-done.35 = bf16[192,2048]{1,0:T(8,128)(2,1)S(1)} collective-permute-done((bf16[192,2048]{1,0:T(8,128)(2,1)S(1)}, bf16[192,2048]{1,0:T(8,128)(2,1)S(1)}, u32[]{:S(2)}, u32[]{:S(2)}) %collective-permute-start.35) | collective-permute-done | bytes 786464 | tf_op jit(solution)/shard_map/ppermute | solution.py:41
  509.3 22.9 %ff_back.3 = (bf16[192,2048]{1,0:T(8,128)(2,1)}, bf16[192,2048]{1,0:T(8,128)(2,1)}, bf16[384,2048]{1,0:T(8,128)(2,1)}, bf16[384,2048]{1,0:T(8,128)(2,1)}, bf16[3...) custom-call(bf16[384,2048]{1,0:T(8,128)(2,1)} %copy-done.18, bf16[128,2048]{1,0:T(8,128)(2,1)} %get-tuple-element.316.second.b_down, ...), custom_call_target="tpu_custom_call" | custom-call | flops 9663676416 | bytes 25165824 | tf_op jit(solution)/shard_map/ff_back/pallas_call | solution.py:767
  533.6 22.9 %ff_back.2 = (bf16[384,2048]{1,0:T(8,128)(2,1)}, bf16[384,2048]{1,0:T(8,128)(2,1)}, bf16[384,2048]{1,0:T(8,128)(2,1)}, bf16[384,256]{1,0:T(8,128)(2,1)}, bf16[384,128]{1,0:T(8,128)(2,1)}) custom-call(bf16[384,2048]{1,0:T(8,128)(2,1)} %pad_maximum_fusion.4.d_ff, bf16[128,2048]{1,0:T(8,128)(2,1)} %get-tuple-element.316.second.b_down, ...), custom_call_target="tpu_custom_call" | custom-call | flops 9663676416 | bytes 25165824 | tf_op jit(solution)/shard_map/ff_back/pallas_call | solution.py:767
  610.7 30.8 %attend_back.1 = (bf16[768,128]{1,0:T(8,128)(2,1)}, bf16[768,128]{1,0:T(8,128)(2,1)}, bf16[768,128]{1,0:T(8,128)(2,1)}, bf16[768,128]{1,0:T(8,128)(2,1)}, bf16[2...) custom-call(s32[24]{0:T(128)} %bitcast.334, s32[24]{0:T(128)} %bitcast.336, s32[24]{0:T(128)} %select_reduce_fusion.2.prompt_at, ...), custom_call_target="tpu_custom_call" | custom-call | flops 4529848320 | bytes 9437184 | tf_op jit(solution)/shard_map/attend_back/pallas_call | solution.py:364
  694.8 7.6 collective-permute-done.56.refs_6_.refs_2_
  705.3 8.0 unturn_heads.1
  722.2 7.2 norm_back_heads.1.a
  749.6 7.6 back_product.2
  761.8 7.6 back_product.3
  (653 shorter events, 358.7 us)
Async XLA Ops:
  7.2 78.7 %all-gather.11.cloned.1.call-start = ((), (), s32[]{:S(2)}) async-start(), calls=%async_computation.6 | async-start | bytes 7962624 | tf_op jit(solution)/shard_map/all_gather | solution.py:893
  11.8 135.0 %all-gather.13.cloned.1.call-start = ((), (), s32[]{:S(2)}) async-start(), calls=%async_computation.7 | async-start | bytes 4866048 | tf_op jit(solution)/shard_map/all_gather | solution.py:914
  11.9 21.5 %collective-permute-start = (bf16[192,2048]{1,0:T(8,128)(2,1)S(1)}, bf16[192,2048]{1,0:T(8,128)(2,1)}, u32[]{:S(2)}, u32[]{:S(2)}) collective-permute-start(bf16[192,2048]{1,0:T(8,128)(2,1)S(1)} %copy-done.20), channel_id=1, source_target_pairs={{0,1},{1,0},{2,3},{3,2},{4,5},{5,4},{6,7},{7,6},{8,9},{9,8},{10,11... | collective-permute-start | bytes 2359304 | tf_op jit(solution)/shard_map/ppermute | solution.py:887
  14.9 36.0 %collective-permute-start.1 = (bf16[192,2048]{1,0:T(8,128)(2,1)S(1)}, bf16[192,2048]{1,0:T(8,128)(2,1)}, u32[]{:S(2)}, u32[]{:S(2)}) collective-permute-start(bf16[192,2048]{1,0:T(8,128)(2,1)S(1)} %copy-done.20), channel_id=1, source_target_pairs={{0,2},{1,3},{2,0},{3,1},{4,6},{5,7},{6,4},{7,5},{8,10},{9,11},{10,... | collective-permute-start | bytes 2359304 | tf_op jit(solution)/shard_map/ppermute | solution.py:887
  16.4 38.0 %collective-permute-start.2 = (bf16[192,2048]{1,0:T(8,128)(2,1)S(1)}, bf16[192,2048]{1,0:T(8,128)(2,1)}, u32[]{:S(2)}, u32[]{:S(2)}) collective-permute-start(bf16[192,2048]{1,0:T(8,128)(2,1)S(1)} %copy-done.20), channel_id=1, source_target_pairs={{0,3},{1,2},{2,1},{3,0},{4,7},{5,6},{6,5},{7,4},{8,11},{9,10},{10,... | collective-permute-start | bytes 2359304 | tf_op jit(solution)/shard_map/ppermute | solution.py:887
  86.0 326.7 %all-gather.7.cloned.1.call-start = ((), (), s32[]{:S(2)}) async-start(), calls=%async_computation.2 | async-start | bytes 18874368 | tf_op jit(solution)/shard_map/all_gather | solution.py:915
  86.7 356.2 %all-gather.9.cloned.1.call-start = ((), (), s32[]{:S(2)}) async-start(), calls=%async_computation.3 | async-start | bytes 9437184 | tf_op jit(solution)/shard_map/all_gather | solution.py:916
  87.3 682.8 %reduce-scatter.3.cloned.1.call-start = ((), (), s32[]{:S(2)}) async-start(), calls=%async_computation.4 | async-start | bytes 3538944 | tf_op jit(solution)/shard_map/reduce_scatter | solution.py:1127
  95.7 19.7 %collective-permute-start.4 = (bf16[8,64,384]{2,1,0:T(8,128)(2,1)}, bf16[8,64,384]{2,1,0:T(8,128)(2,1)}, u32[]{:S(2)}, u32[]{:S(2)}) collective-permute-start(bf16[8,64,384]{2,1,0:T(8,128)(2,1)} %reshape.564), channel_id=1, source_target_pairs={{0,2},{1,3},{2,0},{3,1},{4,6},{5,7},{6,4},{7,5},{8,10},{9,11},{10,... | collective-permute-start | bytes 1179656 | tf_op jit(solution)/shard_map/ppermute | solution.py:922
  97.1 19.3 %collective-permute-start.5 = (bf16[8,64,384]{2,1,0:T(8,128)(2,1)}, bf16[8,64,384]{2,1,0:T(8,128)(2,1)}, u32[]{:S(2)}, u32[]{:S(2)}) collective-permute-start(bf16[8,64,384]{2,1,0:T(8,128)(2,1)} %reshape.564), channel_id=1, source_target_pairs={{0,3},{1,2},{2,1},{3,0},{4,7},{5,6},{6,5},{7,4},{8,11},{9,10},{10,... | collective-permute-start | bytes 1179656 | tf_op jit(solution)/shard_map/ppermute | solution.py:922
  162.4 86.0 %collective-permute-start.17 = (bf16[2,8,64,512]{3,2,1,0:T(8,128)(2,1)}, bf16[2,8,64,512]{3,2,1,0:T(8,128)(2,1)}, u32[]{:S(2)}, u32[]{:S(2)}) collective-permute-start(bf16[2,8,64,512]{3,2,1,0:T(8,128)(2,1)} %pad_maximum_fusion.8), channel_id=1, source_target_pairs={{0,2},{1,3},{2,0},{3,1},{4,6},{5,7},{6,4},{7,5},{8,10},{9,11},{10,... | collective-permute-start | bytes 3145736 | tf_op jit(solution)/shard_map/ppermute | solution.py:41
  170.8 31.0 %collective-permute-start.9 = (bf16[3,768,128]{2,1,0:T(8,128)(2,1)}, bf16[3,768,128]{2,1,0:T(8,128)(2,1)}, u32[]{:S(2)}, u32[]{:S(2)}) collective-permute-start(bf16[3,768,128]{2,1,0:T(8,128)(2,1)} %get-tuple-element.132), channel_id=1, source_target_pairs={{0,8},{4,12},{8,16},{12,20},{16,24},{20,28},{24,0},{28,4},{1,9},{5... | collective-permute-start | bytes 1769480 | tf_op jit(solution)/shard_map/ppermute | solution.py:953
  170.8 70.2 %collective-permute-start.10 = (bf16[3,768,128]{2,1,0:T(8,128)(2,1)}, bf16[3,768,128]{2,1,0:T(8,128)(2,1)}, u32[]{:S(2)}, u32[]{:S(2)}) collective-permute-start(bf16[3,768,128]{2,1,0:T(8,128)(2,1)} %get-tuple-element.133), channel_id=1, source_target_pairs={{0,16},{4,20},{8,24},{12,28},{16,0},{20,4},{24,8},{28,12},{1,17},{... | collective-permute-start | bytes 1769480 | tf_op jit(solution)/shard_map/ppermute | solution.py:953
  172.1 74.5 %collective-permute-start.11 = (bf16[3,768,128]{2,1,0:T(8,128)(2,1)}, bf16[3,768,128]{2,1,0:T(8,128)(2,1)}, u32[]{:S(2)}, u32[]{:S(2)}) collective-permute-start(bf16[3,768,128]{2,1,0:T(8,128)(2,1)} %get-tuple-element.134), channel_id=1, source_target_pairs={{0,24},{4,28},{8,0},{12,4},{16,8},{20,12},{24,16},{28,20},{1,25},{... | collective-permute-start | bytes 1769480 | tf_op jit(solution)/shard_map/ppermute | solution.py:953
  184.2 72.0 %collective-permute-start.12 = (bf16[2,768,128]{2,1,0:T(8,128)(2,1)}, bf16[2,768,128]{2,1,0:T(8,128)(2,1)}, u32[]{:S(2)}, u32[]{:S(2)}) collective-permute-start(bf16[2,768,128]{2,1,0:T(8,128)(2,1)} %slice.497), channel_id=1, source_target_pairs={{0,4},{4,0},{8,12},{12,8},{16,20},{20,16},{24,28},{28,24},{1,5},{5... | collective-permute-start | bytes 1179656 | tf_op jit(solution)/shard_map/ppermute | solution.py:964
  203.5 52.7 %collective-permute-start.13 = (bf16[2,768,128]{2,1,0:T(8,128)(2,1)}, bf16[2,768,128]{2,1,0:T(8,128)(2,1)}, u32[]{:S(2)}, u32[]{:S(2)}) collective-permute-start(bf16[2,768,128]{2,1,0:T(8,128)(2,1)} %slice.632), channel_id=1, source_target_pairs={{0,4},{4,0},{8,12},{12,8},{16,20},{20,16},{24,28},{28,24},{1,5},{5... | collective-permute-start | bytes 1179656 | tf_op jit(solution)/shard_map/ppermute | solution.py:964
  274.9 52.0 %collective-permute-start.18 = (bf16[768,128]{1,0:T(8,128)(2,1)}, bf16[768,128]{1,0:T(8,128)(2,1)S(1)}, u32[]{:S(2)}, u32[]{:S(2)}) collective-permute-start(bf16[768,128]{1,0:T(8,128)(2,1)} %get-tuple-element.141), channel_id=1, source_target_pairs={{0,24},{4,28},{8,0},{12,4},{16,8},{20,12},{24,16},{28,20},{1,25},{... | collective-permute-start | bytes 589832 | tf_op jit(solution)/shard_map/ppermute | solution.py:953
  318.9 25.4 %collective-permute-start.19 = (bf16[768,128]{1,0:T(8,128)(2,1)}, bf16[768,128]{1,0:T(8,128)(2,1)S(1)}, u32[]{:S(2)}, u32[]{:S(2)}) collective-permute-start(bf16[768,128]{1,0:T(8,128)(2,1)} %get-tuple-element.142), channel_id=1, source_target_pairs={{0,16},{4,20},{8,24},{12,28},{16,0},{20,4},{24,8},{28,12},{1,17},{... | collective-permute-start | bytes 589832 | tf_op jit(solution)/shard_map/ppermute | solution.py:953
  318.9 25.4 %collective-permute-start.20 = (bf16[768,128]{1,0:T(8,128)(2,1)}, bf16[768,128]{1,0:T(8,128)(2,1)S(1)}, u32[]{:S(2)}, u32[]{:S(2)}) collective-permute-start(bf16[768,128]{1,0:T(8,128)(2,1)} %get-tuple-element.143), channel_id=1, source_target_pairs={{0,8},{4,12},{8,16},{12,20},{16,24},{20,28},{24,0},{28,4},{1,9},{5... | collective-permute-start | bytes 589832 | tf_op jit(solution)/shard_map/ppermute | solution.py:953
  353.1 19.2 %collective-permute-start.21 = (bf16[192,2048]{1,0:T(8,128)(2,1)}, bf16[192,2048]{1,0:T(8,128)(2,1)S(1)}, u32[]{:S(2)}, u32[]{:S(2)}) collective-permute-start(bf16[192,2048]{1,0:T(8,128)(2,1)} %get-tuple-element.150), channel_id=1, source_target_pairs={{0,2},{1,3},{2,0},{3,1},{4,6},{5,7},{6,4},{7,5},{8,10},{9,11},{10,... | collective-permute-start | bytes 2359304 | tf_op jit(solution)/shard_map/ppermute | solution.py:41
  354.8 18.7 %collective-permute-start.24 = (bf16[192,2048]{1,0:T(8,128)(2,1)}, bf16[192,2048]{1,0:T(8,128)(2,1)S(1)}, u32[]{:S(2)}, u32[]{:S(2)}) collective-permute-start(bf16[192,2048]{1,0:T(8,128)(2,1)} %get-tuple-element.151), channel_id=1, source_target_pairs={{0,1},{1,0},{2,3},{3,2},{4,5},{5,4},{6,7},{7,6},{8,9},{9,8},{10,11... | collective-permute-start | bytes 2359304 | tf_op jit(solution)/shard_map/ppermute | solution.py:41
  532.2 24.3 %collective-permute-start.37 = (bf16[192,2048]{1,0:T(8,128)(2,1)}, bf16[192,2048]{1,0:T(8,128)(2,1)S(1)}, u32[]{:S(2)}, u32[]{:S(2)}) collective-permute-start(bf16[192,2048]{1,0:T(8,128)(2,1)} %get-tuple-element.170), channel_id=1, source_target_pairs={{0,2},{1,3},{2,0},{3,1},{4,6},{5,7},{6,4},{7,5},{8,10},{9,11},{10,... | collective-permute-start | bytes 2359304 | tf_op jit(solution)/shard_map/ppermute | solution.py:41
  532.7 23.8 %collective-permute-start.40 = (bf16[192,2048]{1,0:T(8,128)(2,1)}, bf16[192,2048]{1,0:T(8,128)(2,1)S(1)}, u32[]{:S(2)}, u32[]{:S(2)}) collective-permute-start(bf16[192,2048]{1,0:T(8,128)(2,1)} %get-tuple-element.171), channel_id=1, source_target_pairs={{0,1},{1,0},{2,3},{3,2},{4,5},{5,4},{6,7},{7,6},{8,9},{9,8},{10,11... | collective-permute-start | bytes 2359304 | tf_op jit(solution)/shard_map/ppermute | solution.py:41
  652.1 38.8 %collective-permute-start.51 = (bf16[768,128]{1,0:T(8,128)(2,1)}, bf16[768,128]{1,0:T(8,128)(2,1)}, u32[]{:S(2)}, u32[]{:S(2)}) collective-permute-start(bf16[768,128]{1,0:T(8,128)(2,1)} %get-tuple-element.173), channel_id=1, source_target_pairs={{0,24},{4,28},{8,0},{12,4},{16,8},{20,12},{24,16},{28,20},{1,25},{... | collective-permute-start | bytes 589832 | tf_op jit(solution)/shard_map/ppermute | solution.py:953
  652.1 42.6 %collective-permute-start.52 = (bf16[768,128]{1,0:T(8,128)(2,1)}, bf16[768,128]{1,0:T(8,128)(2,1)}, u32[]{:S(2)}, u32[]{:S(2)}) collective-permute-start(bf16[768,128]{1,0:T(8,128)(2,1)} %get-tuple-element.174), channel_id=1, source_target_pairs={{0,16},{4,20},{8,24},{12,28},{16,0},{20,4},{24,8},{28,12},{1,17},{... | collective-permute-start | bytes 589832 | tf_op jit(solution)/shard_map/ppermute | solution.py:953
  652.2 42.6 %collective-permute-start.53 = (bf16[768,128]{1,0:T(8,128)(2,1)}, bf16[768,128]{1,0:T(8,128)(2,1)}, u32[]{:S(2)}, u32[]{:S(2)}) collective-permute-start(bf16[768,128]{1,0:T(8,128)(2,1)} %get-tuple-element.175), channel_id=1, source_target_pairs={{0,8},{4,12},{8,16},{12,20},{16,24},{20,28},{24,0},{28,4},{1,9},{5... | collective-permute-start | bytes 589832 | tf_op jit(solution)/shard_map/ppermute | solution.py:953
  654.2 48.2 %collective-permute-start.56 = (bf16[2,768,128]{2,1,0:T(8,128)(2,1)}, bf16[2,768,128]{2,1,0:T(8,128)(2,1)}, u32[]{:S(2)}, u32[]{:S(2)}) collective-permute-start(bf16[2,768,128]{2,1,0:T(8,128)(2,1)} %get-tuple-element.294), channel_id=1, source_target_pairs={{0,16},{4,20},{8,24},{12,28},{16,0},{20,4},{24,8},{28,12},{1,17},{... | collective-permute-start | bytes 1179656 | tf_op jit(solution)/shard_map/ppermute | solution.py:953
  661.7 40.7 %collective-permute-start.57 = (bf16[2,768,128]{2,1,0:T(8,128)(2,1)}, bf16[2,768,128]{2,1,0:T(8,128)(2,1)}, u32[]{:S(2)}, u32[]{:S(2)}) collective-permute-start(bf16[2,768,128]{2,1,0:T(8,128)(2,1)} %get-tuple-element.293), channel_id=1, source_target_pairs={{0,8},{4,12},{8,16},{12,20},{16,24},{20,28},{24,0},{28,4},{1,9},{5... | collective-permute-start | bytes 1179656 | tf_op jit(solution)/shard_map/ppermute | solution.py:953
  702.4 93.1 %reduce-scatter.5.cloned.1.call-start = ((), (), s32[]{:S(2)}) async-start(), calls=%async_computation.5 | async-start | bytes 2211840 | tf_op jit(solution)/shard_map/reduce_scatter | solution.py:1164
  718.7 27.6 %collective-permute-start.61 = (bf16[2,2,80,512]{3,2,1,0:T(8,128)(2,1)}, bf16[2,2,80,512]{3,2,1,0:T(8,128)(2,1)}, u32[]{:S(2)}, u32[]{:S(2)}) collective-permute-start(bf16[2,2,80,512]{3,2,1,0:T(8,128)(2,1)} %dynamic-slice_bitcast_fusion), channel_id=1, source_target_pairs={{0,4},{4,0},{8,12},{12,8},{16,20},{20,16},{24,28},{28,24},{1,5},{5... | collective-permute-start | bytes 983048 | tf_op jit(solution)/shard_map/ppermute | solution.py:41
  757.2 18.5 %collective-permute-start.64 = (bf16[192,2048]{1,0:T(8,128)(2,1)}, bf16[192,2048]{1,0:T(8,128)(2,1)S(1)}, u32[]{:S(2)}, u32[]{:S(2)}) collective-permute-start(bf16[192,2048]{1,0:T(8,128)(2,1)} %get-tuple-element.230), channel_id=1, source_target_pairs={{0,2},{1,3},{2,0},{3,1},{4,6},{5,7},{6,4},{7,5},{8,10},{9,11},{10,... | collective-permute-start | bytes 2359304 | tf_op jit(solution)/shard_map/ppermute | solution.py:41
  758.3 20.5 %collective-permute-start.66 = (bf16[192,2048]{1,0:T(8,128)(2,1)}, bf16[192,2048]{1,0:T(8,128)(2,1)}, u32[]{:S(2)}, u32[]{:S(2)}) collective-permute-start(bf16[192,2048]{1,0:T(8,128)(2,1)} %get-tuple-element.231), channel_id=1, source_target_pairs={{0,1},{1,0},{2,3},{3,2},{4,5},{5,4},{6,7},{7,6},{8,9},{9,8},{10,11... | collective-permute-start | bytes 2359304 | tf_op jit(solution)/shard_map/ppermute | solution.py:41
  (169 other events, 1245.7 us)
Sparse Core Ops, SparseCore 0:
  11.9 73.9 all-gather.10
  88.1 46.5 all-gather.12
  136.3 216.9 all-gather.6
  354.7 80.1 all-gather.8
  702.5 40.8 reduce-scatter.2
  745.7 36.7 reduce-scatter.4

commit v6 on v5

--- a/solution.py
+++ b/solution.py
@@ -398,30 +398,36 @@
     return pl.ds(pl.multiple_of(base + head * HEAD_DIM, HEAD_DIM), HEAD_DIM)
 
 
+def here(size, width):
+    return pl.BlockSpec((size, width), lambda p, order, piece_at: (p, 0))
+
+
+def there(size, at=None, count=1):
+    if at is None:
+        return pl.BlockSpec((size, HEAD_DIM), lambda p, order, piece_at: (piece_at[p], 0))
+    return pl.BlockSpec((count, size, HEAD_DIM), lambda p, order, piece_at: (at, piece_at[p], 0))
+
+
+def all_of(value):
+    return pl.BlockSpec(value.shape, lambda p, order, piece_at: (0, 0))
+
+
 def piece_rows(index, size):
     return pl.ds(pl.multiple_of(index * size, 16), size)
 
 
-def spread_kernel(slots, pieces, order, piece_at, z, inv, cs, gain, *outs):
+def spread_kernel(slots, order, piece_at, z, inv, cs, gain, *outs):
     cols = slots * HEAD_DIM
-    size = z.shape[0] // pieces
-
-    def step(p, carry):
-        at, to = piece_rows(p, size), piece_rows(piece_at[p], size)
-        cosine, sine = cs[at, :HEAD_DIM], cs[at, HEAD_DIM:]
-        for which in range(2):
-            factor = inv[at, which : which + 1]
-            for k in range(slots):
-                head = order[k]
-                scaled = z[at, lanes(head, which * cols)] * factor
-                scaled = scaled * gain[which : which + 1, lanes(head)]
-                turned = turn(scaled, cosine, sine).astype(BF16)
-                outs[k][which, to, :] = turned
+    cosine, sine = cs[:, :HEAD_DIM], cs[:, HEAD_DIM:]
+    for which in range(2):
+        factor = inv[:, which : which + 1]
         for k in range(slots):
-            outs[k][2, to, :] = z[at, lanes(order[k], 2 * cols)].astype(BF16)
-        return carry
-
-    lax.fori_loop(0, pieces, step, 0)
+            head = order[k]
+            scaled = z[:, lanes(head, which * cols)] * factor
+            scaled = scaled * gain[which : which + 1, lanes(head)]
+            outs[k][which, :, :] = turn(scaled, cosine, sine).astype(BF16)
+    for k in range(slots):
+        outs[k][2, :, :] = z[:, lanes(order[k], 2 * cols)].astype(BF16)
 
 
 WHOLE = pl.BlockSpec(memory_space=pltpu.VMEM)
@@ -430,11 +436,21 @@
 
 def spread_heads(order, piece_at, z, inv, cs, gain, slots):
     rows = z.shape[0]
+    pieces = piece_at.shape[0]
+    size = rows // pieces
     return pl.pallas_call(
-        functools.partial(spread_kernel, slots, piece_at.shape[0]),
+        functools.partial(spread_kernel, slots),
         out_shape=[jax.ShapeDtypeStruct((3, rows, HEAD_DIM), BF16)] * slots,
         grid_spec=pltpu.PrefetchScalarGridSpec(
-            num_scalar_prefetch=2, in_specs=[WHOLE] * 4, out_specs=[WHOLE] * slots
+            num_scalar_prefetch=2,
+            grid=(pieces,),
+            in_specs=[
+                here(size, z.shape[1]),
+                here(size, inv.shape[1]),
+                here(size, cs.shape[1]),
+                all_of(gain),
+            ],
+            out_specs=[there(size, 0, 3)] * slots,
         ),
         compiler_params=BIG,
         name="spread_heads",
@@ -465,78 +481,93 @@
     )(order, piece_at, *parts)
 
 
-def unturn_kernel(slots, pieces, order, piece_at, *refs):
+def unturn_kernel(slots, order, piece_at, *refs):
     dqs, dkvs, rest = refs[:slots], refs[slots : 2 * slots], refs[2 * slots :]
     z, cs, gain, scaled_out, part_out = rest
     cols = slots * HEAD_DIM
-    size = z.shape[0] // pieces
-
-    def step(p, carry):
-        at, source = piece_rows(p, size), piece_rows(piece_at[p], size)
-        cosine, sine = cs[at, :HEAD_DIM], cs[at, HEAD_DIM:]
-        for which in range(2):
-            total = jnp.zeros((size, HEAD_DIM), F32)
-            for k in range(slots):
-                head = order[k]
-                grad = dqs[k][source, :] if which == 0 else dkvs[k][0, source, :]
-                grad = turn(grad.astype(F32), cosine, -sine) * gain[which : which + 1, lanes(head)]
-                scaled_out[at, lanes(head, which * cols)] = grad
-                total = total + grad * z[at, lanes(head, which * cols)]
-            part_out[at, which : which + 1] = jnp.sum(total, axis=1, keepdims=True)
-        return carry
-
-    lax.fori_loop(0, pieces, step, 0)
+    cosine, sine = cs[:, :HEAD_DIM], cs[:, HEAD_DIM:]
+    for which in range(2):
+        total = jnp.zeros((z.shape[0], HEAD_DIM), F32)
+        for k in range(slots):
+            head = order[k]
+            grad = dqs[k][...] if which == 0 else dkvs[k][0, :, :]
+            grad = turn(grad.astype(F32), cosine, -sine) * gain[which : which + 1, lanes(head)]
+            scaled_out[:, lanes(head, which * cols)] = grad
+            total = total + grad * z[:, lanes(head, which * cols)]
+        part_out[:, which : which + 1] = jnp.sum(total, axis=1, keepdims=True)
 
 
 def unturn_heads(order, piece_at, dqs, dkvs, z, cs, gain):
     slots = len(dqs)
     rows = z.shape[0]
     cols = slots * HEAD_DIM
+    pieces = piece_at.shape[0]
+    size = rows // pieces
     return pl.pallas_call(
-        functools.partial(unturn_kernel, slots, piece_at.shape[0]),
+        functools.partial(unturn_kernel, slots),
         out_shape=[
             jax.ShapeDtypeStruct((rows, 2 * cols), F32),
             jax.ShapeDtypeStruct((rows, 2), F32),
         ],
         grid_spec=pltpu.PrefetchScalarGridSpec(
-            num_scalar_prefetch=2, in_specs=[WHOLE] * (2 * slots + 3), out_specs=[WHOLE] * 2
+            num_scalar_prefetch=2,
+            grid=(pieces,),
+            in_specs=[there(size)] * slots
+            + [there(size, 0)] * slots
+            + [here(size, 2 * cols), here(size, cs.shape[1]), all_of(gain)],
+            out_specs=[here(size, 2 * cols), here(size, 2)],
         ),
         compiler_params=BIG,
         name="unturn_heads",
     )(order, piece_at, *dqs, *dkvs, z, cs, gain)
 
 
-def norm_back_kernel(slots, pieces, order, piece_at, *refs):
-    dkvs, (scaled, z, coef, out) = refs[:slots], refs[slots:]
+def norm_back_kernel(slots, order, piece_at, *refs):
+    dkvs, (scaled, z, coef, second, pick, out, latent_out) = refs[:slots], refs[slots:]
     cols = slots * HEAD_DIM
-    size = z.shape[0] // pieces
-
-    def step(p, carry):
-        at, source = piece_rows(p, size), piece_rows(piece_at[p], size)
-        for which in range(2):
-            to = slice(which * cols, (which + 1) * cols)
-            out[at, to] = (
-                scaled[at, to] * coef[at, which : which + 1]
-                - z[at, to] * coef[at, 2 + which : 3 + which]
-            ).astype(BF16)
-        for k in range(slots):
-            out[at, lanes(order[k], 2 * cols)] = dkvs[k][1, source, :]
-        return carry
-
-    lax.fori_loop(0, pieces, step, 0)
-
-
-def norm_back_heads(order, piece_at, dkvs, scaled, z, coef):
+    low = second.shape[0]
+    for which in range(2):
+        to = slice(which * cols, (which + 1) * cols)
+        out[:, to] = (
+            scaled[:, to] * coef[:, which : which + 1] - z[:, to] * coef[:, 2 + which : 3 + which]
+        ).astype(BF16)
+    for k in range(slots):
+        out[:, lanes(order[k], 2 * cols)] = dkvs[k][0, :, :]
+    for which in range(3):
+        to = slice(which * cols, (which + 1) * cols)
+        at = slice(which * low, (which + 1) * low)
+        latent_out[:, at] = (mm_nt(out[:, to], second[:, to]) * pick[...]).astype(BF16)
+
+
+def norm_back_heads(order, piece_at, dkvs, scaled, z, coef, second, pick):
     slots = len(dkvs)
+    rows = z.shape[0]
+    cols = slots * HEAD_DIM
+    low = second.shape[0]
+    pieces = piece_at.shape[0]
+    size = rows // pieces
     return pl.pallas_call(
-        functools.partial(norm_back_kernel, slots, piece_at.shape[0]),
-        out_shape=jax.ShapeDtypeStruct(z.shape, BF16),
+        functools.partial(norm_back_kernel, slots),
+        out_shape=[
+            jax.ShapeDtypeStruct((rows, 3 * cols), BF16),
+            jax.ShapeDtypeStruct((rows, 3 * low), BF16),
+        ],
         grid_spec=pltpu.PrefetchScalarGridSpec(
-            num_scalar_prefetch=2, in_specs=[WHOLE] * (slots + 3), out_specs=WHOLE
+            num_scalar_prefetch=2,
+            grid=(pieces,),
+            in_specs=[there(size, 1)] * slots
+            + [
+                here(size, 2 * cols),
+                here(size, 2 * cols),
+                here(size, 4),
+                all_of(second),
+                here(size, low),
+            ],
+            out_specs=[here(size, 3 * cols), here(size, 3 * low)],
         ),
         compiler_params=BIG,
         name="norm_back_heads",
-    )(order, piece_at, *dkvs, scaled, z, coef)
+    )(order, piece_at, *dkvs, scaled, z, coef, second, pick)
 
 
 def fixed(*shape, at=None):
@@ -801,17 +832,6 @@
         ),
         name="ff_back",
     )(d_ff, b_down, pick, w_down, a_down, gate, up, w_gu, w_gu, b_gu, b_gu, a_gu)
-
-
-def blocked(parts):
-    zeros = lambda a, b: jnp.zeros((a.shape[0], b.shape[1]), a.dtype)
-    return jnp.concatenate(
-        [
-            jnp.concatenate([a if a is b else zeros(a, b) for b in parts], axis=1)
-            for a in parts
-        ],
-        axis=0,
-    )
 
 
 def local(
@@ -926,7 +946,6 @@
         a_qkv = lax.dynamic_update_slice(a_qkv, value[:, None], (0, tp_rank ^ mask, 0, 0))
     a_qkv = a_qkv.reshape(width, 3 * slots_a)
     b_qkv = first[:, k_rows : k_rows + rank_cols].reshape(slots_a, 3 * cols)
-    b_qkv = blocked([b_qkv[:, i * cols : (i + 1) * cols] for i in range(3)])
     owner = (
         ((head_rank - jnp.arange(heads)) % heads)[None, :] * group
         + ((group_rank + jnp.arange(group)) % group)[:, None]
@@ -975,7 +994,7 @@
     gain = lax.dynamic_slice_in_dim(norm_gain_table[:2], tp_rank * cols, cols, 1)
     latents = (mm(x, a_qkv) * pick3).astype(BF16)
     z, squares = qkv_product(
-        x, latents, first, first[:, k_rows : k_rows + rank_cols].reshape(slots_a, 3 * cols), k_rows, cols
+        x, latents, first, b_qkv, k_rows, cols
     )
     squares = sum_rows(squares[:2].reshape(2, rows), tp)
     inv = lax.rsqrt(squares / width + EPS)
@@ -1130,8 +1149,7 @@
     scaled, parts = unturn_heads(head_order, piece_at, dqs, dkvs, z, cs, gain)
     parts = sum_rows(parts.T, tp) / width
     coef = jnp.concatenate([inv, inv**3 * parts], axis=0)
-    dz = norm_back_heads(head_order, piece_at, dkvs, scaled, z, coef.T)
-    us = (mm_nt(dz, b_qkv) * pick3).astype(BF16)
+    dz, us = norm_back_heads(head_order, piece_at, dkvs, scaled, z, coef.T, b_qkv, select)
     grad_a_qkv = mm_tn(x, us)
     grad_b_qkv = mm_tn(latents, dz)
     lane3 = 3 * slots_a
@@ -1151,9 +1169,8 @@
     )
     dz, late = lax.optimization_barrier((dz, late))
     far_part = list(back_product(dz, 1, first, k_rows, us, a_qkv, 2))
-    far_part[0], dz = lax.optimization_barrier((far_part[0], dz))
+    far_part[0], dz, early, late_o = lax.optimization_barrier((far_part[0], dz, early, late_o))
     (near_part,) = back_product(dz, 0, first, k_rows, us, a_qkv, 1)
-    near_part, early, late_o = lax.optimization_barrier((near_part, early, late_o))
 
     down_size = rank_cols * width // lane
     o_size = rank_cols * width // cols
@@ -1164,9 +1181,11 @@
     late = lax.psum_scatter(late, "seq", scatter_dimension=0, tiled=False)
     summed = scatter_groups(near_part, far_part, tp)
     summed, late = lax.optimization_barrier((summed, late))
-    late = late.astype(F32)
     input_grad = jnp.concatenate([d_hidden[i] + summed[i] for i in groups], axis=0)
-    grad_a_qkv = sum_all(late[:k_rows].astype(BF16), "tp", tp).astype(F32)
+    grad_a_qkv = late[:k_rows].astype(F32)
+    for mask in range(1, tp):
+        got = lax.ppermute(late[:k_rows], "tp", [(i, i ^ mask) for i in range(tp)])
+        grad_a_qkv = grad_a_qkv + got.astype(F32)
     grad_a_gu = both[:k_rows]
     grad_b_down = both[k_rows : k_rows + down_size].reshape(rank_cols, width)
     grad_b_o = both[k_rows + down_size :].reshape(rank_cols, width)
@@ -1175,7 +1194,7 @@
     grad_a_down = rest[:a_size].reshape(rank_cols, hidden_cols).T
     grad_b_gu = rest[a_size:].reshape(2, rank_cols, hidden_cols)
     grad_a_o = late_o[o_size:].T
-    grad_b_qkv = late[k_rows:].reshape(rank_cols, 3, cols).transpose(1, 0, 2)
+    grad_b_qkv = late[k_rows:].astype(F32).reshape(rank_cols, 3, cols).transpose(1, 0, 2)
     grad_a_in = jnp.stack(
         [grad_a_qkv[:, i * slots_a : (i + 1) * slots_a] for i in range(3)]
         + [grad_a_gu[:, i * slots_a : (i + 1) * slots_a] for i in range(2)]

time: 826 us -> 829 us (level)
  waiting for transfers between devices: 273 us -> 284 us
    ppermute x37 -> x35, waiting for transfers between devices: 110 us -> 120 us  [flip(): return lax.ppermute(value, axis, [(i, i ^ 1 << bit) for i in range(count)])]
    ppermute x37 -> x35, starting transfers between devices: 39.6 us -> 36.6 us  [flip(): return lax.ppermute(value, axis, [(i, i ^ 1 << bit) for i in range(count)])]
  transfers between devices with their start and end apart: 78 -> 79, of which waited for: 47 -> 44; matrix products, arithmetic and copies ran while one was open for 21% -> 19% of each run, Pallas kernels for 17% -> 18%
where the time goes in v6:
time: 829 us; the launch traced here: 822 us
  waiting for transfers between devices  284 us (34%)
  Pallas kernels  207 us (25%)
  starting transfers between devices  123 us (15%)
  local copies, waits for them, and re-layouts  113 us (14%)
  other arithmetic  45.8 us (6%)
  matrix products  30.4 us (4%)
  between operations  19 us (2%)
    ppermute x35, waiting for transfers between devices, flip(): return lax.ppermute(value, axis, [(i, i ^ 1 << bit) for i in range(count)])  120 us
    ppermute x18, waiting for transfers between devices, head_shift(): lax.ppermute(value, 'seq', [(h * group + j, (h + by) % heads * group + j)...  94 us
    ppermute x18, starting transfers between devices, head_shift(): lax.ppermute(value, 'seq', [(h * group + j, (h + by) % heads * group + j)...  66.9 us
    pallas_call x2, Pallas kernels, ff_back(): pl.pallas_call(functools.partial(ff_back_kernel, parts, n), grid=(n,), ou...  45.9 us
    ppermute x35, starting transfers between devices, flip(): return lax.ppermute(value, axis, [(i, i ^ 1 << bit) for i in range(count)])  36.6 us
    unnamed x272, local copies, waits for them, and re-layouts  34.2 us
    pallas_call x1, Pallas kernels, attend_back(): pl.pallas_call(functools.partial(attend_back_kernel, slots, group, rows,...  30.8 us
    pallas_call x2, Pallas kernels, gate_up_product(): pl.pallas_call(gate_up_kernel, grid=(n,), out_shape=[jax.ShapeDtypeStruct...  29.6 us
  transfers between devices with their start and end apart: 79, of which 44 were waited for; matrix products, arithmetic and copies ran while one was open for 19% of the time, Pallas kernels for 18%

profile of v6, /device:TPU:0, one launch (start us, length us, event | category | flops | bytes accessed | tf_op | source)
XLA Modules:
  0.0 821.5 jit_solution(4129453574415142344)
XLA Ops:
  35.6 16.1 %collective-permute-done.1 = bf16[192,2048]{1,0:T(8,128)(2,1)} collective-permute-done((bf16[192,2048]{1,0:T(8,128)(2,1)S(1)}, bf16[192,2048]{1,0:T(8,128)(2,1)}, u32[]{:S(2)}, u32[]{:S(2)}) %collective-permute-start.1) | collective-permute-done | bytes 786464 | tf_op jit(solution)/shard_map/ppermute | solution.py:907
  60.6 24.9 %all-gather.11.cloned.1.call-done = bf16[2304,1536]{1,0:T(8,128)(2,1)} async-done(((bf16[288,1536]{1,0:T(8,128)(2,1)}), bf16[2304,1536]{1,0:T(8,128)(2,1)}) %all-gather.11.cloned.1.call-update) | async-done | bytes 7077904 | tf_op jit(solution)/shard_map/all_gather | solution.py:913
  106.2 10.1 %collective-permute-done.4 = bf16[8,64,384]{2,1,0:T(8,128)(2,1)} collective-permute-done((bf16[8,64,384]{2,1,0:T(8,128)(2,1)}, bf16[8,64,384]{2,1,0:T(8,128)(2,1)}, u32[]{:S(2)}, u32[]{:S(2)}) %collective-permute-start.4) | collective-permute-done | bytes 393248 | tf_op jit(solution)/shard_map/ppermute | solution.py:942
  123.6 10.4 %qkv_product.1 = (f32[768,1536]{1,0:T(8,128)}, f32[3,768,1]{2,1,0:T(8,128)}) custom-call(bf16[768,2048]{1,0:T(8,128)(2,1)} %slice_dynamic-update-slice_fusion.x, bf16[768,384]{1,0:T(8,128)(2,1)} %fusion.6.latent, bf16[8,288,1536]{2,1,0:T(8,128)(2,1)} %bitcast.260, bf16[128,1536]{1,0:T(8,128)(2,1)} %bitcast.304), custom_call_target="tpu_custom_call" | custom-call | flops 4831838208 | bytes 7077888 | tf_op jit(solution)/shard_map/qkv_product/pallas_call | solution.py:593
  150.6 9.7 %collective-permute-done.16 = bf16[8,64,512]{2,1,0:T(8,128)(2,1)S(1)} collective-permute-done((bf16[8,64,512]{2,1,0:T(8,128)(2,1)S(1)}, bf16[8,64,512]{2,1,0:T(8,128)(2,1)S(1)}, u32[]{:S(2)}, u32[]{:S(2)}) %collective-permute-start.16) | collective-permute-done | bytes 524320 | tf_op jit(solution)/shard_map/ppermute | solution.py:41
  165.0 8.2 %spread_heads.1 = (bf16[3,768,128]{2,1,0:T(8,128)(2,1)}, bf16[3,768,128]{2,1,0:T(8,128)(2,1)}, bf16[3,768,128]{2,1,0:T(8,128)(2,1)}, bf16[3,768,128]{2,1,0:T(8,128)(2,1)}) custom-call(s32[4]{0:T(128)} %get-tuple-element.397.order, s32[8]{0:T(128)} %copy-done.110, f32[768,1536]{1,0:T(8,128)} %get-tuple-element.127.z.refs_8_.refs_5_, f32[768,2]{1,0:T(8,128)} %bitcast.276, ...), custom_call_target="tpu_custom_call" | custom-call | tf_op jit(solution)/shard_map/spread_heads/pallas_call | solution.py:441
  195.3 8.8 %collective-permute-done.9.refs_1_ = bf16[3,768,128]{2,1,0:T(8,128)(2,1)} collective-permute-done((bf16[3,768,128]{2,1,0:T(8,128)(2,1)}, bf16[3,768,128]{2,1,0:T(8,128)(2,1)}, u32[]{:S(2)}, u32[]{:S(2)}) %collective-permute-start.9) | collective-permute-done | bytes 589856 | tf_op jit(solution)/shard_map/ppermute | solution.py:972
  205.9 37.7 %collective-permute-done.10.refs_2_ = bf16[3,768,128]{2,1,0:T(8,128)(2,1)} collective-permute-done((bf16[3,768,128]{2,1,0:T(8,128)(2,1)}, bf16[3,768,128]{2,1,0:T(8,128)(2,1)}, u32[]{:S(2)}, u32[]{:S(2)}) %collective-permute-start.10) | collective-permute-done | bytes 589856 | tf_op jit(solution)/shard_map/ppermute | solution.py:972
  258.7 18.6 %attend.1 = (bf16[768,128]{1,0:T(8,128)(2,1)}, bf16[768,128]{1,0:T(8,128)(2,1)}, bf16[768,128]{1,0:T(8,128)(2,1)}, bf16[768,128]{1,0:T(8,128)(2,1)}) custom-call(s32[24]{0:T(128)} %bitcast.333, s32[24]{0:T(128)} %bitcast.331, s32[24]{0:T(128)} %select_reduce_fusion.2.prompt_at, bf16[3,768,128]{2,1,0:T(8,128)(2,1)} %get-tuple-element.132.refs_0_, ...), custom_call_target="tpu_custom_call" | custom-call | flops 1811939328 | bytes 4718592 | tf_op jit(solution)/shard_map/attend/pallas_call | solution.py:332
  277.3 41.5 %collective-permute-start.18 = (bf16[768,128]{1,0:T(8,128)(2,1)}, bf16[768,128]{1,0:T(8,128)(2,1)S(1)}, u32[]{:S(2)}, u32[]{:S(2)}) collective-permute-start(bf16[768,128]{1,0:T(8,128)(2,1)} %get-tuple-element.142), channel_id=1, source_target_pairs={{0,24},{4,28},{8,0},{12,4},{16,8},{20,12},{24,16},{28,20},{1,25},{... | collective-permute-start | bytes 589832 | tf_op jit(solution)/shard_map/ppermute | solution.py:972
  326.7 17.6 %collective-permute-done.19.refs_2_ = bf16[768,128]{1,0:T(8,128)(2,1)S(1)} collective-permute-done((bf16[768,128]{1,0:T(8,128)(2,1)}, bf16[768,128]{1,0:T(8,128)(2,1)S(1)}, u32[]{:S(2)}, u32[]{:S(2)}) %collective-permute-start.19) | collective-permute-done | bytes 196640 | tf_op jit(solution)/shard_map/ppermute | solution.py:972
  361.4 10.9 %collective-permute-done.21 = bf16[192,2048]{1,0:T(8,128)(2,1)S(1)} collective-permute-done((bf16[192,2048]{1,0:T(8,128)(2,1)}, bf16[192,2048]{1,0:T(8,128)(2,1)S(1)}, u32[]{:S(2)}, u32[]{:S(2)}) %collective-permute-start.21) | collective-permute-done | bytes 786464 | tf_op jit(solution)/shard_map/ppermute | solution.py:41
  377.6 7.4 collective-permute-done.25
  398.8 13.7 %collective-permute-done.27 = bf16[192,2048]{1,0:T(8,128)(2,1)S(1)} collective-permute-done((bf16[192,2048]{1,0:T(8,128)(2,1)S(1)}, bf16[192,2048]{1,0:T(8,128)(2,1)S(1)}, u32[]{:S(2)}, u32[]{:S(2)}) %collective-permute-start.27) | collective-permute-done | bytes 786464 | tf_op jit(solution)/shard_map/ppermute | solution.py:41
  412.7 15.0 %gate_up_product.2 = (f32[384,2048]{1,0:T(8,128)}, f32[384,2048]{1,0:T(8,128)}, bf16[384,2048]{1,0:T(8,128)(2,1)}, bf16[384,256]{1,0:T(8,128)(2,1)}) custom-call(bf16[384,2048]{1,0:T(8,128)(2,1)} %pad_maximum_fusion.2.h, bf16[2048,256]{1,0:T(8,128)(2,1)} %bitcast.263, f32[384,128]{1,0:T(8,128)} %get-tuple-element.338.pick, ...), custom_call_target="tpu_custom_call" | custom-call | flops 6442450944 | bytes 16777216 | tf_op jit(solution)/shard_map/gate_up_product/pallas_call | solution.py:714
  427.7 14.6 %gate_up_product.3 = (f32[384,2048]{1,0:T(8,128)}, f32[384,2048]{1,0:T(8,128)}, bf16[384,2048]{1,0:T(8,128)(2,1)}, bf16[384,256]{1,0:T(8,128)(2,1)}) custom-call(bf16[384,2048]{1,0:T(8,128)(2,1)} %copy-done.7, bf16[2048,256]{1,0:T(8,128)(2,1)} %bitcast.264, f32[384,128]{1,0:T(8,128)} %get-tuple-element.339.pick, ...), custom_call_target="tpu_custom_call" | custom-call | flops 6442450944 | bytes 16777216 | tf_op jit(solution)/shard_map/gate_up_product/pallas_call | solution.py:714
  442.3 8.7 %add_product.7 = (bf16[192,2048]{1,0:T(8,128)(2,1)}, bf16[192,2048]{1,0:T(8,128)(2,1)}, bf16[384,128]{1,0:T(8,128)(2,1)}) custom-call(bf16[384,2048]{1,0:T(8,128)(2,1)} %get-tuple-element.163.a, bf16[2048,2048]{1,0:T(8,128)(2,1)} %all-gather.9.cloned.1.call-done.weight.w_down, bf16[2048,128]{1,0:T(8,128)(2,1)} %bitcast.282, ...), custom_call_target="tpu_custom_call" | custom-call | flops 3221225472 | bytes 8388608 | tf_op jit(solution)/shard_map/add_product/pallas_call | solution.py:636
  453.1 8.8 %add_product.6 = (bf16[384,2048]{1,0:T(8,128)(2,1)}, bf16[384,128]{1,0:T(8,128)(2,1)}) custom-call(bf16[384,2048]{1,0:T(8,128)(2,1)} %get-tuple-element.159.a, bf16[2048,2048]{1,0:T(8,128)(2,1)} %all-gather.9.cloned.1.call-done.weight.w_down, bf16[2048,128]{1,0:T(8,128)(2,1)} %bitcast.283, bf16[128,2048]{1,0:T(8,128)(2,1)} %get-tuple-element.318.second.b_down, ...), custom_call_target="tpu_custom_call" | custom-call | flops 3221225472 | bytes 8388608 | tf_op jit(solution)/shard_map/add_product/pallas_call | solution.py:636
  461.8 6.5 collective-permute-done.29
  472.5 6.9 collective-permute-done.32
  483.6 8.1 collective-permute-done.33
  497.5 9.4 %collective-permute-done.35 = bf16[192,2048]{1,0:T(8,128)(2,1)S(1)} collective-permute-done((bf16[192,2048]{1,0:T(8,128)(2,1)S(1)}, bf16[192,2048]{1,0:T(8,128)(2,1)S(1)}, u32[]{:S(2)}, u32[]{:S(2)}) %collective-permute-start.35) | collective-permute-done | bytes 786464 | tf_op jit(solution)/shard_map/ppermute | solution.py:41
  508.2 23.0 %ff_back.3 = (bf16[192,2048]{1,0:T(8,128)(2,1)}, bf16[192,2048]{1,0:T(8,128)(2,1)}, bf16[384,2048]{1,0:T(8,128)(2,1)}, bf16[384,2048]{1,0:T(8,128)(2,1)}, bf16[3...) custom-call(bf16[384,2048]{1,0:T(8,128)(2,1)} %copy-done.17, bf16[128,2048]{1,0:T(8,128)(2,1)} %get-tuple-element.318.second.b_down, ...), custom_call_target="tpu_custom_call" | custom-call | flops 9663676416 | bytes 25165824 | tf_op jit(solution)/shard_map/ff_back/pallas_call | solution.py:798
  533.8 22.9 %ff_back.2 = (bf16[384,2048]{1,0:T(8,128)(2,1)}, bf16[384,2048]{1,0:T(8,128)(2,1)}, bf16[384,2048]{1,0:T(8,128)(2,1)}, bf16[384,256]{1,0:T(8,128)(2,1)}, bf16[384,128]{1,0:T(8,128)(2,1)}) custom-call(bf16[384,2048]{1,0:T(8,128)(2,1)} %pad_maximum_fusion.4.d_ff, bf16[128,2048]{1,0:T(8,128)(2,1)} %get-tuple-element.318.second.b_down, ...), custom_call_target="tpu_custom_call" | custom-call | flops 9663676416 | bytes 25165824 | tf_op jit(solution)/shard_map/ff_back/pallas_call | solution.py:798
  561.7 6.3 collective-permute-done.38
  613.6 30.8 %attend_back.1 = (bf16[768,128]{1,0:T(8,128)(2,1)}, bf16[768,128]{1,0:T(8,128)(2,1)}, bf16[768,128]{1,0:T(8,128)(2,1)}, bf16[768,128]{1,0:T(8,128)(2,1)}, bf16[2...) custom-call(s32[24]{0:T(128)} %bitcast.334, s32[24]{0:T(128)} %bitcast.332, s32[24]{0:T(128)} %select_reduce_fusion.2.prompt_at, ...), custom_call_target="tpu_custom_call" | custom-call | flops 4529848320 | bytes 9437184 | tf_op jit(solution)/shard_map/attend_back/pallas_call | solution.py:364
  696.3 7.6 collective-permute-done.56.refs_6_.refs_2_
  705.2 8.3 %unturn_heads.1 = (f32[768,1024]{1,0:T(8,128)}, f32[768,2]{1,0:T(8,128)}) custom-call(s32[4]{0:T(128)} %get-tuple-element.397.order, s32[8]{0:T(128)} %copy-done.110, bf16[768,128]{1,0:T(8,128)(2,1)} %get-tuple-element.219.refs_0_, bf16[768,128]{1,0:T(8,128)(2,1)} %collective-permute-done.51.refs_1_, bf16[768,128]{1,0:T(8,128)(2,1)} %collective-permute-done.52.refs_2_, ...), custom_call_target="tpu_custom_call" | custom-call | tf_op jit(solution)/shard_map/unturn_heads/pallas_call | solution.py:506
  722.6 9.0 %norm_back_heads.1 = (bf16[768,1536]{1,0:T(8,128)(2,1)}, bf16[768,384]{1,0:T(8,128)(2,1)}) custom-call(s32[4]{0:T(128)} %get-tuple-element.397.order, s32[8]{0:T(128)} %copy-done.110, bf16[2,768,128]{2,1,0:T(8,128)(2,1)} %get-tuple-element.215.refs_4_.refs_0_, bf16[2,768,128]{2,1,0:T(8,128)(2,1)} %copy-done.55, ...), custom_call_target="tpu_custom_call" | custom-call | tf_op jit(solution)/shard_map/norm_back_heads/pallas_call | solution.py:549
  747.8 7.5 back_product.2
  769.3 7.6 back_product.3
  776.9 6.3 collective-permute-done.72
  (650 shorter events, 359.7 us)
Async XLA Ops:
  7.2 78.3 %all-gather.11.cloned.1.call-start = ((), (), s32[]{:S(2)}) async-start(), calls=%async_computation.6 | async-start | bytes 7962624 | tf_op jit(solution)/shard_map/all_gather | solution.py:913
  11.5 136.7 %all-gather.13.cloned.1.call-start = ((), (), s32[]{:S(2)}) async-start(), calls=%async_computation.7 | async-start | bytes 4866048 | tf_op jit(solution)/shard_map/all_gather | solution.py:934
  11.5 21.5 %collective-permute-start = (bf16[192,2048]{1,0:T(8,128)(2,1)S(1)}, bf16[192,2048]{1,0:T(8,128)(2,1)}, u32[]{:S(2)}, u32[]{:S(2)}) collective-permute-start(bf16[192,2048]{1,0:T(8,128)(2,1)S(1)} %copy-done.19), channel_id=1, source_target_pairs={{0,1},{1,0},{2,3},{3,2},{4,5},{5,4},{6,7},{7,6},{8,9},{9,8},{10,11... | collective-permute-start | bytes 2359304 | tf_op jit(solution)/shard_map/ppermute | solution.py:907
  14.5 40.7 %collective-permute-start.2 = (bf16[192,2048]{1,0:T(8,128)(2,1)S(1)}, bf16[192,2048]{1,0:T(8,128)(2,1)}, u32[]{:S(2)}, u32[]{:S(2)}) collective-permute-start(bf16[192,2048]{1,0:T(8,128)(2,1)S(1)} %copy-done.19), channel_id=1, source_target_pairs={{0,3},{1,2},{2,1},{3,0},{4,7},{5,6},{6,5},{7,4},{8,11},{9,10},{10,... | collective-permute-start | bytes 2359304 | tf_op jit(solution)/shard_map/ppermute | solution.py:907
  16.0 35.7 %collective-permute-start.1 = (bf16[192,2048]{1,0:T(8,128)(2,1)S(1)}, bf16[192,2048]{1,0:T(8,128)(2,1)}, u32[]{:S(2)}, u32[]{:S(2)}) collective-permute-start(bf16[192,2048]{1,0:T(8,128)(2,1)S(1)} %copy-done.19), channel_id=1, source_target_pairs={{0,2},{1,3},{2,0},{3,1},{4,6},{5,7},{6,4},{7,5},{8,10},{9,11},{10,... | collective-permute-start | bytes 2359304 | tf_op jit(solution)/shard_map/ppermute | solution.py:907
  85.6 327.0 %all-gather.7.cloned.1.call-start = ((), (), s32[]{:S(2)}) async-start(), calls=%async_computation.2 | async-start | bytes 18874368 | tf_op jit(solution)/shard_map/all_gather | solution.py:935
  86.4 355.9 %all-gather.9.cloned.1.call-start = ((), (), s32[]{:S(2)}) async-start(), calls=%async_computation.3 | async-start | bytes 9437184 | tf_op jit(solution)/shard_map/all_gather | solution.py:936
  87.0 668.5 %reduce-scatter.3.cloned.1.call-start = ((), (), s32[]{:S(2)}) async-start(), calls=%async_computation.4 | async-start | bytes 3538944 | tf_op jit(solution)/shard_map/reduce_scatter | solution.py:1146
  95.4 22.0 %collective-permute-start.5 = (bf16[8,64,384]{2,1,0:T(8,128)(2,1)}, bf16[8,64,384]{2,1,0:T(8,128)(2,1)}, u32[]{:S(2)}, u32[]{:S(2)}) collective-permute-start(bf16[8,64,384]{2,1,0:T(8,128)(2,1)} %reshape.563), channel_id=1, source_target_pairs={{0,3},{1,2},{2,1},{3,0},{4,7},{5,6},{6,5},{7,4},{8,11},{9,10},{10,... | collective-permute-start | bytes 1179656 | tf_op jit(solution)/shard_map/ppermute | solution.py:942
  96.8 19.4 %collective-permute-start.4 = (bf16[8,64,384]{2,1,0:T(8,128)(2,1)}, bf16[8,64,384]{2,1,0:T(8,128)(2,1)}, u32[]{:S(2)}, u32[]{:S(2)}) collective-permute-start(bf16[8,64,384]{2,1,0:T(8,128)(2,1)} %reshape.563), channel_id=1, source_target_pairs={{0,2},{1,3},{2,0},{3,1},{4,6},{5,7},{6,4},{7,5},{8,10},{9,11},{10,... | collective-permute-start | bytes 1179656 | tf_op jit(solution)/shard_map/ppermute | solution.py:942
  163.5 87.3 %collective-permute-start.17 = (bf16[2,8,64,512]{3,2,1,0:T(8,128)(2,1)}, bf16[2,8,64,512]{3,2,1,0:T(8,128)(2,1)}, u32[]{:S(2)}, u32[]{:S(2)}) collective-permute-start(bf16[2,8,64,512]{3,2,1,0:T(8,128)(2,1)} %pad_maximum_fusion.8), channel_id=1, source_target_pairs={{0,2},{1,3},{2,0},{3,1},{4,6},{5,7},{6,4},{7,5},{8,10},{9,11},{10,... | collective-permute-start | bytes 3145736 | tf_op jit(solution)/shard_map/ppermute | solution.py:41
  173.2 31.0 %collective-permute-start.9 = (bf16[3,768,128]{2,1,0:T(8,128)(2,1)}, bf16[3,768,128]{2,1,0:T(8,128)(2,1)}, u32[]{:S(2)}, u32[]{:S(2)}) collective-permute-start(bf16[3,768,128]{2,1,0:T(8,128)(2,1)} %get-tuple-element.133), channel_id=1, source_target_pairs={{0,8},{4,12},{8,16},{12,20},{16,24},{20,28},{24,0},{28,4},{1,9},{5... | collective-permute-start | bytes 1769480 | tf_op jit(solution)/shard_map/ppermute | solution.py:972
  173.2 70.4 %collective-permute-start.10 = (bf16[3,768,128]{2,1,0:T(8,128)(2,1)}, bf16[3,768,128]{2,1,0:T(8,128)(2,1)}, u32[]{:S(2)}, u32[]{:S(2)}) collective-permute-start(bf16[3,768,128]{2,1,0:T(8,128)(2,1)} %get-tuple-element.134), channel_id=1, source_target_pairs={{0,16},{4,20},{8,24},{12,28},{16,0},{20,4},{24,8},{28,12},{1,17},{... | collective-permute-start | bytes 1769480 | tf_op jit(solution)/shard_map/ppermute | solution.py:972
  174.5 74.5 %collective-permute-start.11 = (bf16[3,768,128]{2,1,0:T(8,128)(2,1)}, bf16[3,768,128]{2,1,0:T(8,128)(2,1)}, u32[]{:S(2)}, u32[]{:S(2)}) collective-permute-start(bf16[3,768,128]{2,1,0:T(8,128)(2,1)} %get-tuple-element.135), channel_id=1, source_target_pairs={{0,24},{4,28},{8,0},{12,4},{16,8},{20,12},{24,16},{28,20},{1,25},{... | collective-permute-start | bytes 1769480 | tf_op jit(solution)/shard_map/ppermute | solution.py:972
  192.9 65.7 %collective-permute-start.12 = (bf16[2,768,128]{2,1,0:T(8,128)(2,1)}, bf16[2,768,128]{2,1,0:T(8,128)(2,1)}, u32[]{:S(2)}, u32[]{:S(2)}) collective-permute-start(bf16[2,768,128]{2,1,0:T(8,128)(2,1)} %slice.489), channel_id=1, source_target_pairs={{0,4},{4,0},{8,12},{12,8},{16,20},{20,16},{24,28},{28,24},{1,5},{5... | collective-permute-start | bytes 1179656 | tf_op jit(solution)/shard_map/ppermute | solution.py:983
  205.9 52.7 %collective-permute-start.13 = (bf16[2,768,128]{2,1,0:T(8,128)(2,1)}, bf16[2,768,128]{2,1,0:T(8,128)(2,1)}, u32[]{:S(2)}, u32[]{:S(2)}) collective-permute-start(bf16[2,768,128]{2,1,0:T(8,128)(2,1)} %slice.622), channel_id=1, source_target_pairs={{0,4},{4,0},{8,12},{12,8},{16,20},{20,16},{24,28},{28,24},{1,5},{5... | collective-permute-start | bytes 1179656 | tf_op jit(solution)/shard_map/ppermute | solution.py:983
  277.3 49.4 %collective-permute-start.18 = (bf16[768,128]{1,0:T(8,128)(2,1)}, bf16[768,128]{1,0:T(8,128)(2,1)S(1)}, u32[]{:S(2)}, u32[]{:S(2)}) collective-permute-start(bf16[768,128]{1,0:T(8,128)(2,1)} %get-tuple-element.142), channel_id=1, source_target_pairs={{0,24},{4,28},{8,0},{12,4},{16,8},{20,12},{24,16},{28,20},{1,25},{... | collective-permute-start | bytes 589832 | tf_op jit(solution)/shard_map/ppermute | solution.py:972
  318.8 25.5 %collective-permute-start.19 = (bf16[768,128]{1,0:T(8,128)(2,1)}, bf16[768,128]{1,0:T(8,128)(2,1)S(1)}, u32[]{:S(2)}, u32[]{:S(2)}) collective-permute-start(bf16[768,128]{1,0:T(8,128)(2,1)} %get-tuple-element.143), channel_id=1, source_target_pairs={{0,16},{4,20},{8,24},{12,28},{16,0},{20,4},{24,8},{28,12},{1,17},{... | collective-permute-start | bytes 589832 | tf_op jit(solution)/shard_map/ppermute | solution.py:972
  318.8 25.5 %collective-permute-start.20 = (bf16[768,128]{1,0:T(8,128)(2,1)}, bf16[768,128]{1,0:T(8,128)(2,1)S(1)}, u32[]{:S(2)}, u32[]{:S(2)}) collective-permute-start(bf16[768,128]{1,0:T(8,128)(2,1)} %get-tuple-element.144), channel_id=1, source_target_pairs={{0,8},{4,12},{8,16},{12,20},{16,24},{20,28},{24,0},{28,4},{1,9},{5... | collective-permute-start | bytes 589832 | tf_op jit(solution)/shard_map/ppermute | solution.py:972
  353.2 19.1 %collective-permute-start.21 = (bf16[192,2048]{1,0:T(8,128)(2,1)}, bf16[192,2048]{1,0:T(8,128)(2,1)S(1)}, u32[]{:S(2)}, u32[]{:S(2)}) collective-permute-start(bf16[192,2048]{1,0:T(8,128)(2,1)} %get-tuple-element.151), channel_id=1, source_target_pairs={{0,2},{1,3},{2,0},{3,1},{4,6},{5,7},{6,4},{7,5},{8,10},{9,11},{10,... | collective-permute-start | bytes 2359304 | tf_op jit(solution)/shard_map/ppermute | solution.py:41
  354.9 18.7 %collective-permute-start.24 = (bf16[192,2048]{1,0:T(8,128)(2,1)}, bf16[192,2048]{1,0:T(8,128)(2,1)S(1)}, u32[]{:S(2)}, u32[]{:S(2)}) collective-permute-start(bf16[192,2048]{1,0:T(8,128)(2,1)} %get-tuple-element.152), channel_id=1, source_target_pairs={{0,1},{1,0},{2,3},{3,2},{4,5},{5,4},{6,7},{7,6},{8,9},{9,8},{10,11... | collective-permute-start | bytes 2359304 | tf_op jit(solution)/shard_map/ppermute | solution.py:41
  531.2 25.5 %collective-permute-start.37 = (bf16[192,2048]{1,0:T(8,128)(2,1)}, bf16[192,2048]{1,0:T(8,128)(2,1)S(1)}, u32[]{:S(2)}, u32[]{:S(2)}) collective-permute-start(bf16[192,2048]{1,0:T(8,128)(2,1)} %get-tuple-element.171), channel_id=1, source_target_pairs={{0,2},{1,3},{2,0},{3,1},{4,6},{5,7},{6,4},{7,5},{8,10},{9,11},{10,... | collective-permute-start | bytes 2359304 | tf_op jit(solution)/shard_map/ppermute | solution.py:41
  532.5 24.2 %collective-permute-start.40 = (bf16[192,2048]{1,0:T(8,128)(2,1)}, bf16[192,2048]{1,0:T(8,128)(2,1)S(1)}, u32[]{:S(2)}, u32[]{:S(2)}) collective-permute-start(bf16[192,2048]{1,0:T(8,128)(2,1)} %get-tuple-element.172), channel_id=1, source_target_pairs={{0,1},{1,0},{2,3},{3,2},{4,5},{5,4},{6,7},{7,6},{8,9},{9,8},{10,11... | collective-permute-start | bytes 2359304 | tf_op jit(solution)/shard_map/ppermute | solution.py:41
  651.9 41.2 %collective-permute-start.51 = (bf16[768,128]{1,0:T(8,128)(2,1)}, bf16[768,128]{1,0:T(8,128)(2,1)}, u32[]{:S(2)}, u32[]{:S(2)}) collective-permute-start(bf16[768,128]{1,0:T(8,128)(2,1)} %get-tuple-element.174), channel_id=1, source_target_pairs={{0,24},{4,28},{8,0},{12,4},{16,8},{20,12},{24,16},{28,20},{1,25},{... | collective-permute-start | bytes 589832 | tf_op jit(solution)/shard_map/ppermute | solution.py:972
  653.5 42.8 %collective-permute-start.52 = (bf16[768,128]{1,0:T(8,128)(2,1)}, bf16[768,128]{1,0:T(8,128)(2,1)}, u32[]{:S(2)}, u32[]{:S(2)}) collective-permute-start(bf16[768,128]{1,0:T(8,128)(2,1)} %get-tuple-element.175), channel_id=1, source_target_pairs={{0,16},{4,20},{8,24},{12,28},{16,0},{20,4},{24,8},{28,12},{1,17},{... | collective-permute-start | bytes 589832 | tf_op jit(solution)/shard_map/ppermute | solution.py:972
  654.3 42.0 %collective-permute-start.53 = (bf16[768,128]{1,0:T(8,128)(2,1)}, bf16[768,128]{1,0:T(8,128)(2,1)}, u32[]{:S(2)}, u32[]{:S(2)}) collective-permute-start(bf16[768,128]{1,0:T(8,128)(2,1)} %get-tuple-element.176), channel_id=1, source_target_pairs={{0,8},{4,12},{8,16},{12,20},{16,24},{20,28},{24,0},{28,4},{1,9},{5... | collective-permute-start | bytes 589832 | tf_op jit(solution)/shard_map/ppermute | solution.py:972
  654.5 41.7 %collective-permute-start.57 = (bf16[2,768,128]{2,1,0:T(8,128)(2,1)}, bf16[2,768,128]{2,1,0:T(8,128)(2,1)}, u32[]{:S(2)}, u32[]{:S(2)}) collective-permute-start(bf16[2,768,128]{2,1,0:T(8,128)(2,1)} %get-tuple-element.295), channel_id=1, source_target_pairs={{0,8},{4,12},{8,16},{12,20},{16,24},{20,28},{24,0},{28,4},{1,9},{5... | collective-permute-start | bytes 1179656 | tf_op jit(solution)/shard_map/ppermute | solution.py:972
  662.8 41.1 %collective-permute-start.56 = (bf16[2,768,128]{2,1,0:T(8,128)(2,1)}, bf16[2,768,128]{2,1,0:T(8,128)(2,1)}, u32[]{:S(2)}, u32[]{:S(2)}) collective-permute-start(bf16[2,768,128]{2,1,0:T(8,128)(2,1)} %get-tuple-element.296), channel_id=1, source_target_pairs={{0,16},{4,20},{8,24},{12,28},{16,0},{20,4},{24,8},{28,12},{1,17},{... | collective-permute-start | bytes 1179656 | tf_op jit(solution)/shard_map/ppermute | solution.py:972
  703.9 96.1 %reduce-scatter.5.cloned.1.call-start = ((), (), s32[]{:S(2)}) async-start(), calls=%async_computation.5 | async-start | bytes 2211840 | tf_op jit(solution)/shard_map/reduce_scatter | solution.py:1181
  719.0 20.3 %collective-permute-start.61 = (bf16[2,2,80,512]{3,2,1,0:T(8,128)(2,1)}, bf16[2,2,80,512]{3,2,1,0:T(8,128)(2,1)}, u32[]{:S(2)}, u32[]{:S(2)}) collective-permute-start(bf16[2,2,80,512]{3,2,1,0:T(8,128)(2,1)} %dynamic-slice_bitcast_fusion), channel_id=1, source_target_pairs={{0,4},{4,0},{8,12},{12,8},{16,20},{20,16},{24,28},{28,24},{1,5},{5... | collective-permute-start | bytes 983048 | tf_op jit(solution)/shard_map/ppermute | solution.py:41
  759.5 23.7 %collective-permute-start.66 = (bf16[192,2048]{1,0:T(8,128)(2,1)}, bf16[192,2048]{1,0:T(8,128)(2,1)S(1)}, u32[]{:S(2)}, u32[]{:S(2)}) collective-permute-start(bf16[192,2048]{1,0:T(8,128)(2,1)} %get-tuple-element.233), channel_id=1, source_target_pairs={{0,1},{1,0},{2,3},{3,2},{4,5},{5,4},{6,7},{7,6},{8,9},{9,8},{10,11... | collective-permute-start | bytes 2359304 | tf_op jit(solution)/shard_map/ppermute | solution.py:41
  760.1 24.0 %collective-permute-start.64 = (bf16[192,2048]{1,0:T(8,128)(2,1)}, bf16[192,2048]{1,0:T(8,128)(2,1)}, u32[]{:S(2)}, u32[]{:S(2)}) collective-permute-start(bf16[192,2048]{1,0:T(8,128)(2,1)} %get-tuple-element.232), channel_id=1, source_target_pairs={{0,2},{1,3},{2,0},{3,1},{4,6},{5,7},{6,4},{7,5},{8,10},{9,11},{10,... | collective-permute-start | bytes 2359304 | tf_op jit(solution)/shard_map/ppermute | solution.py:41
  (170 other events, 1286.3 us)
Sparse Core Ops, SparseCore 0:
  11.6 73.9 all-gather.10
  87.7 46.5 all-gather.12
  135.9 216.8 all-gather.6
  354.3 80.2 all-gather.8
  704.0 40.1 reduce-scatter.2
  746.4 35.7 reduce-scatter.4

commit v7 on v6

--- a/solution.py
+++ b/solution.py
@@ -39,37 +39,6 @@
 
 def flip(value, axis, count, bit):
     return lax.ppermute(value, axis, [(i, i ^ (1 << bit)) for i in range(count)])
-
-
-def gather_order(value, axis, count, order):
-    rank = lax.axis_index(axis)
-    have = []
-    current = value
-    for bit in order:
-        other = flip(current, axis, count, bit)
-        mine_low = ((rank >> bit) & 1) == 0
-        at = len([b for b in have if b > bit])
-        low = jnp.where(mine_low, current, other)
-        high = jnp.where(mine_low, other, current)
-        current = jnp.stack([low, high], axis=at)
-        have = sorted(have + [bit], reverse=True)
-    return current.reshape((count,) + value.shape)
-
-
-def scatter_order(value, axis, count, order):
-    n = bits_of(count)
-    rank = lax.axis_index(axis)
-    current = value.reshape((2,) * n + value.shape[1:])
-    have = list(range(n - 1, -1, -1))
-    for bit in order:
-        at = have.index(bit)
-        mine = (rank >> bit) & 1
-        keep = lax.dynamic_index_in_dim(current, mine, at, keepdims=False)
-        give = lax.dynamic_index_in_dim(current, 1 - mine, at, keepdims=False)
-        got = flip(give.astype(BF16), axis, count, bit)
-        current = keep.astype(F32) + got.astype(F32)
-        have.remove(bit)
-    return current
 
 
 def part_orders(count):
@@ -138,12 +107,6 @@
         order = [runs.index((other ^ mask, which)) for other, which in runs]
         total = total + jnp.concatenate([got[:, j : j + 1] for j in order], axis=1)
     return total.reshape(value.shape[0], -1)
-
-
-def sum_all(value, axis, count):
-    for bit in range(bits_of(count)):
-        value = value + flip(value, axis, count, bit)
-    return value
 
 
 def copy_all(pairs, sem):
@@ -935,7 +898,6 @@
     w_gu = lax.all_gather(w_gu, "seq", axis=0, tiled=True)
     w_down = lax.all_gather(w_down, "seq", axis=0, tiled=True)
 
-    tp_order, seq_order = list(range(bits_of(tp))), list(range(bits_of(seqs)))
     a_qkv = first[:, k_rows + rank_cols :].reshape(seqs, 3, a_part, slots_a)
     a_qkv = a_qkv.transpose(0, 2, 1, 3).reshape(seqs, a_part, 3 * slots_a)
     a_parts = [a_qkv] + [
@@ -1005,7 +967,11 @@
         at += piece.shape[0]
     w_o = split[0].reshape(width, cols)
     a_o = split[1].reshape(slots_a, cols).T
-    shared = gather_order(jnp.concatenate(split[2:4], axis=1), "tp", tp, tp_order)
+    mine = jnp.concatenate(split[2:4], axis=1)
+    shared = jnp.zeros((tp, *mine.shape), BF16)
+    for mask in range(tp):
+        got = lax.ppermute(mine, "tp", [(i, i ^ mask) for i in range(tp)]) if mask else mine
+        shared = lax.dynamic_update_slice(shared, got[None], (tp_rank ^ mask, 0, 0, 0))
     b_size = split[2].shape[1]
     b_od = (
         shared[:, :, :b_size]
@@ -1123,29 +1089,22 @@
     grad_b_up = both_groups(lambda g: mm_tn(gu_latents[g][:, slots_a:], d_ups[g]))
     lane = 2 * slots_a
     shards = lambda value: value.astype(BF16).reshape(seqs, -1, lane)
+    grad_a_o = both_groups(lambda g: mm_tn(u_os[g], heads_out[g]))
+    grad_b_o = both_groups(lambda g: mm_tn(o_latents[g], d_rows[g]))
     early = jnp.concatenate(
         [
             shards(grad_a_gu),
             shards(grad_b_down),
+            shards(grad_b_o),
             shards(grad_a_down),
             shards(grad_b_gate),
             shards(grad_b_up),
+            shards(grad_a_o),
         ],
         axis=1,
     )
-    grad_a_o = both_groups(lambda g: mm_tn(u_os[g], heads_out[g]))
-    grad_b_o = both_groups(lambda g: mm_tn(o_latents[g], d_rows[g]))
-    late_o = jnp.concatenate(
-        [
-            grad_b_o.astype(BF16).reshape(seqs, -1, cols),
-            grad_a_o.astype(BF16).reshape(seqs, -1, cols),
-        ],
-        axis=1,
-    )
-    dqs, dkvs, early, late_o = lax.optimization_barrier((dqs, dkvs, early, late_o))
+    dqs, dkvs, early = lax.optimization_barrier((dqs, dkvs, early))
     early = lax.psum_scatter(early, "seq", scatter_dimension=0, tiled=False)
-    dqs, dkvs, late_o = lax.optimization_barrier((dqs, dkvs, late_o))
-    late_o = scatter_order(late_o, "seq", seqs, seq_order)
     scaled, parts = unturn_heads(head_order, piece_at, dqs, dkvs, z, cs, gain)
     parts = sum_rows(parts.T, tp) / width
     coef = jnp.concatenate([inv, inv**3 * parts], axis=0)
@@ -1169,31 +1128,33 @@
     )
     dz, late = lax.optimization_barrier((dz, late))
     far_part = list(back_product(dz, 1, first, k_rows, us, a_qkv, 2))
-    far_part[0], dz, early, late_o = lax.optimization_barrier((far_part[0], dz, early, late_o))
+    far_part[0], dz = lax.optimization_barrier((far_part[0], dz))
     (near_part,) = back_product(dz, 0, first, k_rows, us, a_qkv, 1)
 
+    near_part, early = lax.optimization_barrier((near_part, early))
+
+    def sum_tp(value):
+        total = value.astype(F32)
+        for mask in range(1, tp):
+            got = lax.ppermute(value, "tp", [(i, i ^ mask) for i in range(tp)])
+            total = total + got.astype(F32)
+        return total
+
     down_size = rank_cols * width // lane
-    o_size = rank_cols * width // cols
-    both = jnp.concatenate(
-        [early[: k_rows + down_size], late_o[:o_size].astype(BF16).reshape(-1, lane)], axis=0
-    )
-    both = sum_all(both, "tp", tp).astype(F32)
+    both = sum_tp(early[: k_rows + 2 * down_size])
     late = lax.psum_scatter(late, "seq", scatter_dimension=0, tiled=False)
     summed = scatter_groups(near_part, far_part, tp)
     summed, late = lax.optimization_barrier((summed, late))
     input_grad = jnp.concatenate([d_hidden[i] + summed[i] for i in groups], axis=0)
-    grad_a_qkv = late[:k_rows].astype(F32)
-    for mask in range(1, tp):
-        got = lax.ppermute(late[:k_rows], "tp", [(i, i ^ mask) for i in range(tp)])
-        grad_a_qkv = grad_a_qkv + got.astype(F32)
+    grad_a_qkv = sum_tp(late[:k_rows])
     grad_a_gu = both[:k_rows]
     grad_b_down = both[k_rows : k_rows + down_size].reshape(rank_cols, width)
     grad_b_o = both[k_rows + down_size :].reshape(rank_cols, width)
     a_size = rank_cols * hidden_cols // lane
-    rest = early[k_rows + down_size :].astype(F32)
+    rest = early[k_rows + 2 * down_size :].astype(F32)
     grad_a_down = rest[:a_size].reshape(rank_cols, hidden_cols).T
-    grad_b_gu = rest[a_size:].reshape(2, rank_cols, hidden_cols)
-    grad_a_o = late_o[o_size:].T
+    grad_b_gu = rest[a_size : 3 * a_size].reshape(2, rank_cols, hidden_cols)
+    grad_a_o = rest[3 * a_size :].reshape(rank_cols, cols).T
     grad_b_qkv = late[k_rows:].astype(F32).reshape(rank_cols, 3, cols).transpose(1, 0, 2)
     grad_a_in = jnp.stack(
         [grad_a_qkv[:, i * slots_a : (i + 1) * slots_a] for i in range(3)]

time: 829 us -> 820 us (0.989)
  waiting for transfers between devices: 284 us -> 269 us
  local copies, waits for them, and re-layouts: 113 us -> 125 us
    ppermute x35 -> x28, waiting for transfers between devices: 120 us -> 105 us  [flip(): return lax.ppermute(value, axis, [(i, i ^ 1 << bit) for i in range(count)])]
    ppermute x35 -> x28, starting transfers between devices: 36.6 us -> 28.6 us  [flip(): return lax.ppermute(value, axis, [(i, i ^ 1 << bit) for i in range(count)])]
    unnamed x272 -> x276, local copies, waits for them, and re-layouts: 34.2 us -> 34.3 us
  transfers between devices with their start and end apart: 79 -> 78, of which waited for: 44 -> 42; matrix products, arithmetic and copies ran while one was open for 19% -> 20% of each run, Pallas kernels for 18% -> 18%
where the time goes in v7:
time: 820 us; the launch traced here: 812 us
  waiting for transfers between devices  269 us (33%)
  Pallas kernels  207 us (25%)
  local copies, waits for them, and re-layouts  125 us (15%)
  starting transfers between devices  122 us (15%)
  other arithmetic  40.9 us (5%)
  matrix products  29.2 us (4%)
  between operations  19 us (2%)
    ppermute x28, waiting for transfers between devices, flip(): return lax.ppermute(value, axis, [(i, i ^ 1 << bit) for i in range(count)])  105 us
    ppermute x18, waiting for transfers between devices, head_shift(): lax.ppermute(value, 'seq', [(h * group + j, (h + by) % heads * group + j)...  93.5 us
    ppermute x18, starting transfers between devices, head_shift(): lax.ppermute(value, 'seq', [(h * group + j, (h + by) % heads * group + j)...  67.2 us
    pallas_call x2, Pallas kernels, ff_back(): pl.pallas_call(functools.partial(ff_back_kernel, parts, n), grid=(n,), ou...  45.9 us
    unnamed x276, local copies, waits for them, and re-layouts  34.3 us
    pallas_call x1, Pallas kernels, attend_back(): pl.pallas_call(functools.partial(attend_back_kernel, slots, group, rows,...  30.8 us
    pallas_call x2, Pallas kernels, gate_up_product(): pl.pallas_call(gate_up_kernel, grid=(n,), out_shape=[jax.ShapeDtypeStruct...  29.7 us
    ppermute x28, starting transfers between devices, flip(): return lax.ppermute(value, axis, [(i, i ^ 1 << bit) for i in range(count)])  28.6 us
  transfers between devices with their start and end apart: 78, of which 42 were waited for; matrix products, arithmetic and copies ran while one was open for 20% of the time, Pallas kernels for 18%

profile of v7, /device:TPU:0, one launch (start us, length us, event | category | flops | bytes accessed | tf_op | source)
XLA Modules:
  0.0 812.2 jit_solution(16351894788300460350)
XLA Ops:
  35.6 16.1 %collective-permute-done.1 = bf16[192,2048]{1,0:T(8,128)(2,1)} collective-permute-done((bf16[192,2048]{1,0:T(8,128)(2,1)S(1)}, bf16[192,2048]{1,0:T(8,128)(2,1)}, u32[]{:S(2)}, u32[]{:S(2)}) %collective-permute-start.1) | collective-permute-done | bytes 786464 | tf_op jit(solution)/shard_map/ppermute | solution.py:870
  60.6 24.9 %all-gather.11.cloned.1.call-done = bf16[2304,1536]{1,0:T(8,128)(2,1)} async-done(((bf16[288,1536]{1,0:T(8,128)(2,1)}), bf16[2304,1536]{1,0:T(8,128)(2,1)}) %all-gather.11.cloned.1.call-update) | async-done | bytes 7077904 | tf_op jit(solution)/shard_map/all_gather | solution.py:876
  100.0 6.0 collective-permute-done.3
  107.1 10.1 %collective-permute-done.4 = bf16[8,64,384]{2,1,0:T(8,128)(2,1)} collective-permute-done((bf16[8,64,384]{2,1,0:T(8,128)(2,1)}, bf16[8,64,384]{2,1,0:T(8,128)(2,1)}, u32[]{:S(2)}, u32[]{:S(2)}) %collective-permute-start.4) | collective-permute-done | bytes 393248 | tf_op jit(solution)/shard_map/ppermute | solution.py:904
  124.4 10.4 %qkv_product.1 = (f32[768,1536]{1,0:T(8,128)}, f32[3,768,1]{2,1,0:T(8,128)}) custom-call(bf16[768,2048]{1,0:T(8,128)(2,1)} %slice_dynamic-update-slice_fusion.x, bf16[768,384]{1,0:T(8,128)(2,1)} %fusion.6.latent, bf16[8,288,1536]{2,1,0:T(8,128)(2,1)} %bitcast.243, bf16[128,1536]{1,0:T(8,128)(2,1)} %bitcast.286), custom_call_target="tpu_custom_call" | custom-call | flops 4831838208 | bytes 7077888 | tf_op jit(solution)/shard_map/qkv_product/pallas_call | solution.py:556
  134.9 5.8 copy.203
  158.4 8.8 %spread_heads.1 = (bf16[3,768,128]{2,1,0:T(8,128)(2,1)}, bf16[3,768,128]{2,1,0:T(8,128)(2,1)}, bf16[3,768,128]{2,1,0:T(8,128)(2,1)}, bf16[3,768,128]{2,1,0:T(8,128)(2,1)}) custom-call(s32[4]{0:T(128)} %get-tuple-element.372.order, s32[8]{0:T(128)} %copy-done.109, f32[768,1536]{1,0:T(8,128)} %get-tuple-element.117.z.refs_8_.refs_5_, f32[768,2]{1,0:T(8,128)} %bitcast.258, ...), custom_call_target="tpu_custom_call" | custom-call | tf_op jit(solution)/shard_map/spread_heads/pallas_call | solution.py:404
  188.9 9.2 %collective-permute-done.9.refs_1_ = bf16[3,768,128]{2,1,0:T(8,128)(2,1)} collective-permute-done((bf16[3,768,128]{2,1,0:T(8,128)(2,1)}, bf16[3,768,128]{2,1,0:T(8,128)(2,1)}, u32[]{:S(2)}, u32[]{:S(2)}) %collective-permute-start.9) | collective-permute-done | bytes 589856 | tf_op jit(solution)/shard_map/ppermute | solution.py:934
  200.0 38.3 %collective-permute-done.10.refs_2_ = bf16[3,768,128]{2,1,0:T(8,128)(2,1)} collective-permute-done((bf16[3,768,128]{2,1,0:T(8,128)(2,1)}, bf16[3,768,128]{2,1,0:T(8,128)(2,1)}, u32[]{:S(2)}, u32[]{:S(2)}) %collective-permute-start.10) | collective-permute-done | bytes 589856 | tf_op jit(solution)/shard_map/ppermute | solution.py:934
  253.5 18.6 %attend.1 = (bf16[768,128]{1,0:T(8,128)(2,1)}, bf16[768,128]{1,0:T(8,128)(2,1)}, bf16[768,128]{1,0:T(8,128)(2,1)}, bf16[768,128]{1,0:T(8,128)(2,1)}) custom-call(s32[24]{0:T(128)} %bitcast.317, s32[24]{0:T(128)} %bitcast.315, s32[24]{0:T(128)} %select_reduce_fusion.2.prompt_at, bf16[3,768,128]{2,1,0:T(8,128)(2,1)} %get-tuple-element.122.refs_0_, ...), custom_call_target="tpu_custom_call" | custom-call | flops 1811939328 | bytes 4718592 | tf_op jit(solution)/shard_map/attend/pallas_call | solution.py:295
  272.1 46.3 %collective-permute-start.19 = (bf16[768,128]{1,0:T(8,128)(2,1)}, bf16[768,128]{1,0:T(8,128)(2,1)S(1)}, u32[]{:S(2)}, u32[]{:S(2)}) collective-permute-start(bf16[768,128]{1,0:T(8,128)(2,1)} %get-tuple-element.132), channel_id=1, source_target_pairs={{0,24},{4,28},{8,0},{12,4},{16,8},{20,12},{24,16},{28,20},{1,25},{... | collective-permute-start | bytes 589832 | tf_op jit(solution)/shard_map/ppermute | solution.py:934
  320.6 5.8 collective-permute-done.19.refs_1_
  326.4 17.4 %collective-permute-done.20.refs_2_ = bf16[768,128]{1,0:T(8,128)(2,1)S(1)} collective-permute-done((bf16[768,128]{1,0:T(8,128)(2,1)}, bf16[768,128]{1,0:T(8,128)(2,1)S(1)}, u32[]{:S(2)}, u32[]{:S(2)}) %collective-permute-start.20) | collective-permute-done | bytes 196640 | tf_op jit(solution)/shard_map/ppermute | solution.py:934
  359.1 12.6 %collective-permute-done.22 = bf16[192,2048]{1,0:T(8,128)(2,1)S(1)} collective-permute-done((bf16[192,2048]{1,0:T(8,128)(2,1)}, bf16[192,2048]{1,0:T(8,128)(2,1)S(1)}, u32[]{:S(2)}, u32[]{:S(2)}) %collective-permute-start.22) | collective-permute-done | bytes 786464 | tf_op jit(solution)/shard_map/ppermute | solution.py:41
  376.1 7.5 collective-permute-done.26
  386.9 6.9 collective-permute-done.24
  398.3 12.9 %collective-permute-done.28 = bf16[192,2048]{1,0:T(8,128)(2,1)S(1)} collective-permute-done((bf16[192,2048]{1,0:T(8,128)(2,1)S(1)}, bf16[192,2048]{1,0:T(8,128)(2,1)S(1)}, u32[]{:S(2)}, u32[]{:S(2)}) %collective-permute-start.28) | collective-permute-done | bytes 786464 | tf_op jit(solution)/shard_map/ppermute | solution.py:41
  411.4 15.1 %gate_up_product.2 = (f32[384,2048]{1,0:T(8,128)}, f32[384,2048]{1,0:T(8,128)}, bf16[384,2048]{1,0:T(8,128)(2,1)}, bf16[384,256]{1,0:T(8,128)(2,1)}) custom-call(bf16[384,2048]{1,0:T(8,128)(2,1)} %pad_maximum_fusion.1.h, bf16[2048,256]{1,0:T(8,128)(2,1)} %bitcast.246, f32[384,128]{1,0:T(8,128)} %get-tuple-element.313.pick, ...), custom_call_target="tpu_custom_call" | custom-call | flops 6442450944 | bytes 16777216 | tf_op jit(solution)/shard_map/gate_up_product/pallas_call | solution.py:677
  426.5 14.7 %gate_up_product.3 = (f32[384,2048]{1,0:T(8,128)}, f32[384,2048]{1,0:T(8,128)}, bf16[384,2048]{1,0:T(8,128)(2,1)}, bf16[384,256]{1,0:T(8,128)(2,1)}) custom-call(bf16[384,2048]{1,0:T(8,128)(2,1)} %copy-done.7, bf16[2048,256]{1,0:T(8,128)(2,1)} %bitcast.247, f32[384,128]{1,0:T(8,128)} %get-tuple-element.314.pick, ...), custom_call_target="tpu_custom_call" | custom-call | flops 6442450944 | bytes 16777216 | tf_op jit(solution)/shard_map/gate_up_product/pallas_call | solution.py:677
  441.2 8.7 %add_product.7 = (bf16[192,2048]{1,0:T(8,128)(2,1)}, bf16[192,2048]{1,0:T(8,128)(2,1)}, bf16[384,128]{1,0:T(8,128)(2,1)}) custom-call(bf16[384,2048]{1,0:T(8,128)(2,1)} %get-tuple-element.153.a, bf16[2048,2048]{1,0:T(8,128)(2,1)} %all-gather.9.cloned.1.call-done.weight.w_down, bf16[2048,128]{1,0:T(8,128)(2,1)} %bitcast.266, ...), custom_call_target="tpu_custom_call" | custom-call | flops 3221225472 | bytes 8388608 | tf_op jit(solution)/shard_map/add_product/pallas_call | solution.py:599
  452.0 8.8 %add_product.6 = (bf16[384,2048]{1,0:T(8,128)(2,1)}, bf16[384,128]{1,0:T(8,128)(2,1)}) custom-call(bf16[384,2048]{1,0:T(8,128)(2,1)} %get-tuple-element.149.a, bf16[2048,2048]{1,0:T(8,128)(2,1)} %all-gather.9.cloned.1.call-done.weight.w_down, bf16[2048,128]{1,0:T(8,128)(2,1)} %bitcast.267, bf16[128,2048]{1,0:T(8,128)(2,1)} %get-tuple-element.295.second.b_down, ...), custom_call_target="tpu_custom_call" | custom-call | flops 3221225472 | bytes 8388608 | tf_op jit(solution)/shard_map/add_product/pallas_call | solution.py:599
  460.8 6.1 collective-permute-done.30
  483.1 8.6 %collective-permute-done.34 = bf16[96,2048]{1,0:T(8,128)(2,1)S(1)} collective-permute-done((bf16[96,2048]{1,0:T(8,128)(2,1)S(1)}, bf16[96,2048]{1,0:T(8,128)(2,1)S(1)}, u32[]{:S(2)}, u32[]{:S(2)}) %collective-permute-start.34) | collective-permute-done | bytes 393248 | tf_op jit(solution)/shard_map/ppermute | solution.py:41
  496.2 10.2 %collective-permute-done.36 = bf16[192,2048]{1,0:T(8,128)(2,1)S(1)} collective-permute-done((bf16[192,2048]{1,0:T(8,128)(2,1)S(1)}, bf16[192,2048]{1,0:T(8,128)(2,1)S(1)}, u32[]{:S(2)}, u32[]{:S(2)}) %collective-permute-start.36) | collective-permute-done | bytes 786464 | tf_op jit(solution)/shard_map/ppermute | solution.py:41
  507.7 22.9 %ff_back.3 = (bf16[192,2048]{1,0:T(8,128)(2,1)}, bf16[192,2048]{1,0:T(8,128)(2,1)}, bf16[384,2048]{1,0:T(8,128)(2,1)}, bf16[384,2048]{1,0:T(8,128)(2,1)}, bf16[3...) custom-call(bf16[384,2048]{1,0:T(8,128)(2,1)} %copy-done.17, bf16[128,2048]{1,0:T(8,128)(2,1)} %get-tuple-element.295.second.b_down, ...), custom_call_target="tpu_custom_call" | custom-call | flops 9663676416 | bytes 25165824 | tf_op jit(solution)/shard_map/ff_back/pallas_call | solution.py:761
  532.5 22.9 %ff_back.2 = (bf16[384,2048]{1,0:T(8,128)(2,1)}, bf16[384,2048]{1,0:T(8,128)(2,1)}, bf16[384,2048]{1,0:T(8,128)(2,1)}, bf16[384,256]{1,0:T(8,128)(2,1)}, bf16[384,128]{1,0:T(8,128)(2,1)}) custom-call(bf16[384,2048]{1,0:T(8,128)(2,1)} %pad_maximum_fusion.3.d_ff, bf16[128,2048]{1,0:T(8,128)(2,1)} %get-tuple-element.295.second.b_down, ...), custom_call_target="tpu_custom_call" | custom-call | flops 9663676416 | bytes 25165824 | tf_op jit(solution)/shard_map/ff_back/pallas_call | solution.py:761
  611.0 30.8 %attend_back.1 = (bf16[768,128]{1,0:T(8,128)(2,1)}, bf16[768,128]{1,0:T(8,128)(2,1)}, bf16[768,128]{1,0:T(8,128)(2,1)}, bf16[768,128]{1,0:T(8,128)(2,1)}, bf16[2...) custom-call(s32[24]{0:T(128)} %bitcast.318, s32[24]{0:T(128)} %bitcast.316, s32[24]{0:T(128)} %select_reduce_fusion.2.prompt_at, ...), custom_call_target="tpu_custom_call" | custom-call | flops 4529848320 | bytes 9437184 | tf_op jit(solution)/shard_map/attend_back/pallas_call | solution.py:327
  693.7 7.6 collective-permute-done.57.refs_6_.refs_2_
  701.7 8.3 %unturn_heads.1 = (f32[768,1024]{1,0:T(8,128)}, f32[768,2]{1,0:T(8,128)}) custom-call(s32[4]{0:T(128)} %get-tuple-element.372.order, s32[8]{0:T(128)} %copy-done.109, bf16[768,128]{1,0:T(8,128)(2,1)} %get-tuple-element.200.refs_0_, bf16[768,128]{1,0:T(8,128)(2,1)} %collective-permute-done.52.refs_1_, bf16[768,128]{1,0:T(8,128)(2,1)} %collective-permute-done.53.refs_2_, ...), custom_call_target="tpu_custom_call" | custom-call | tf_op jit(solution)/shard_map/unturn_heads/pallas_call | solution.py:469
  719.5 9.0 %norm_back_heads.1 = (bf16[768,1536]{1,0:T(8,128)(2,1)}, bf16[768,384]{1,0:T(8,128)(2,1)}) custom-call(s32[4]{0:T(128)} %get-tuple-element.372.order, s32[8]{0:T(128)} %copy-done.109, bf16[2,768,128]{2,1,0:T(8,128)(2,1)} %get-tuple-element.196.refs_4_.refs_0_, bf16[2,768,128]{2,1,0:T(8,128)(2,1)} %copy-done.55, ...), custom_call_target="tpu_custom_call" | custom-call | tf_op jit(solution)/shard_map/norm_back_heads/pallas_call | solution.py:512
  737.7 7.6 back_product.2
  748.8 7.6 back_product.3
  (646 shorter events, 346.6 us)
Async XLA Ops:
  7.2 78.3 %all-gather.11.cloned.1.call-start = ((), (), s32[]{:S(2)}) async-start(), calls=%async_computation.6 | async-start | bytes 7962624 | tf_op jit(solution)/shard_map/all_gather | solution.py:876
  11.5 139.2 %all-gather.13.cloned.1.call-start = ((), (), s32[]{:S(2)}) async-start(), calls=%async_computation.7 | async-start | bytes 4866048 | tf_op jit(solution)/shard_map/all_gather | solution.py:897
  11.5 21.5 %collective-permute-start = (bf16[192,2048]{1,0:T(8,128)(2,1)S(1)}, bf16[192,2048]{1,0:T(8,128)(2,1)}, u32[]{:S(2)}, u32[]{:S(2)}) collective-permute-start(bf16[192,2048]{1,0:T(8,128)(2,1)S(1)} %copy-done.19), channel_id=1, source_target_pairs={{0,1},{1,0},{2,3},{3,2},{4,5},{5,4},{6,7},{7,6},{8,9},{9,8},{10,11... | collective-permute-start | bytes 2359304 | tf_op jit(solution)/shard_map/ppermute | solution.py:870
  14.5 40.7 %collective-permute-start.2 = (bf16[192,2048]{1,0:T(8,128)(2,1)S(1)}, bf16[192,2048]{1,0:T(8,128)(2,1)}, u32[]{:S(2)}, u32[]{:S(2)}) collective-permute-start(bf16[192,2048]{1,0:T(8,128)(2,1)S(1)} %copy-done.19), channel_id=1, source_target_pairs={{0,3},{1,2},{2,1},{3,0},{4,7},{5,6},{6,5},{7,4},{8,11},{9,10},{10,... | collective-permute-start | bytes 2359304 | tf_op jit(solution)/shard_map/ppermute | solution.py:870
  16.0 35.7 %collective-permute-start.1 = (bf16[192,2048]{1,0:T(8,128)(2,1)S(1)}, bf16[192,2048]{1,0:T(8,128)(2,1)}, u32[]{:S(2)}, u32[]{:S(2)}) collective-permute-start(bf16[192,2048]{1,0:T(8,128)(2,1)S(1)} %copy-done.19), channel_id=1, source_target_pairs={{0,2},{1,3},{2,0},{3,1},{4,6},{5,7},{6,4},{7,5},{8,10},{9,11},{10,... | collective-permute-start | bytes 2359304 | tf_op jit(solution)/shard_map/ppermute | solution.py:870
  85.6 325.8 %all-gather.7.cloned.1.call-start = ((), (), s32[]{:S(2)}) async-start(), calls=%async_computation.2 | async-start | bytes 18874368 | tf_op jit(solution)/shard_map/all_gather | solution.py:898
  86.4 354.8 %all-gather.9.cloned.1.call-start = ((), (), s32[]{:S(2)}) async-start(), calls=%async_computation.3 | async-start | bytes 9437184 | tf_op jit(solution)/shard_map/all_gather | solution.py:899
  87.0 669.5 %reduce-scatter.3.cloned.1.call-start = ((), (), s32[]{:S(2)}) async-start(), calls=%async_computation.4 | async-start | bytes 4276224 | tf_op jit(solution)/shard_map/reduce_scatter | solution.py:1107
  96.3 22.0 %collective-permute-start.5 = (bf16[8,64,384]{2,1,0:T(8,128)(2,1)}, bf16[8,64,384]{2,1,0:T(8,128)(2,1)}, u32[]{:S(2)}, u32[]{:S(2)}) collective-permute-start(bf16[8,64,384]{2,1,0:T(8,128)(2,1)} %reshape.553), channel_id=1, source_target_pairs={{0,3},{1,2},{2,1},{3,0},{4,7},{5,6},{6,5},{7,4},{8,11},{9,10},{10,... | collective-permute-start | bytes 1179656 | tf_op jit(solution)/shard_map/ppermute | solution.py:904
  154.9 32.9 %collective-permute-start.17 = (bf16[8,64,512]{2,1,0:T(8,128)(2,1)}, bf16[8,64,512]{2,1,0:T(8,128)(2,1)}, u32[]{:S(2)}, u32[]{:S(2)}) collective-permute-start(bf16[8,64,512]{2,1,0:T(8,128)(2,1)} %get-tuple-element.273), channel_id=1, source_target_pairs={{0,2},{1,3},{2,0},{3,1},{4,6},{5,7},{6,4},{7,5},{8,10},{9,11},{10,... | collective-permute-start | bytes 1572872 | tf_op jit(solution)/shard_map/ppermute | solution.py:973
  156.1 88.8 %collective-permute-start.18 = (bf16[8,64,512]{2,1,0:T(8,128)(2,1)}, bf16[8,64,512]{2,1,0:T(8,128)(2,1)}, u32[]{:S(2)}, u32[]{:S(2)}) collective-permute-start(bf16[8,64,512]{2,1,0:T(8,128)(2,1)} %get-tuple-element.273), channel_id=1, source_target_pairs={{0,3},{1,2},{2,1},{3,0},{4,7},{5,6},{6,5},{7,4},{8,11},{9,10},{10,... | collective-permute-start | bytes 1572872 | tf_op jit(solution)/shard_map/ppermute | solution.py:973
  167.2 31.0 %collective-permute-start.9 = (bf16[3,768,128]{2,1,0:T(8,128)(2,1)}, bf16[3,768,128]{2,1,0:T(8,128)(2,1)}, u32[]{:S(2)}, u32[]{:S(2)}) collective-permute-start(bf16[3,768,128]{2,1,0:T(8,128)(2,1)} %get-tuple-element.123), channel_id=1, source_target_pairs={{0,8},{4,12},{8,16},{12,20},{16,24},{20,28},{24,0},{28,4},{1,9},{5... | collective-permute-start | bytes 1769480 | tf_op jit(solution)/shard_map/ppermute | solution.py:934
  167.2 71.0 %collective-permute-start.10 = (bf16[3,768,128]{2,1,0:T(8,128)(2,1)}, bf16[3,768,128]{2,1,0:T(8,128)(2,1)}, u32[]{:S(2)}, u32[]{:S(2)}) collective-permute-start(bf16[3,768,128]{2,1,0:T(8,128)(2,1)} %get-tuple-element.124), channel_id=1, source_target_pairs={{0,16},{4,20},{8,24},{12,28},{16,0},{20,4},{24,8},{28,12},{1,17},{... | collective-permute-start | bytes 1769480 | tf_op jit(solution)/shard_map/ppermute | solution.py:934
  169.5 73.5 %collective-permute-start.11 = (bf16[3,768,128]{2,1,0:T(8,128)(2,1)}, bf16[3,768,128]{2,1,0:T(8,128)(2,1)}, u32[]{:S(2)}, u32[]{:S(2)}) collective-permute-start(bf16[3,768,128]{2,1,0:T(8,128)(2,1)} %get-tuple-element.125), channel_id=1, source_target_pairs={{0,24},{4,28},{8,0},{12,4},{16,8},{20,12},{24,16},{28,20},{1,25},{... | collective-permute-start | bytes 1769480 | tf_op jit(solution)/shard_map/ppermute | solution.py:934
  187.8 65.7 %collective-permute-start.12 = (bf16[2,768,128]{2,1,0:T(8,128)(2,1)}, bf16[2,768,128]{2,1,0:T(8,128)(2,1)}, u32[]{:S(2)}, u32[]{:S(2)}) collective-permute-start(bf16[2,768,128]{2,1,0:T(8,128)(2,1)} %slice.482), channel_id=1, source_target_pairs={{0,4},{4,0},{8,12},{12,8},{16,20},{20,16},{24,28},{28,24},{1,5},{5... | collective-permute-start | bytes 1179656 | tf_op jit(solution)/shard_map/ppermute | solution.py:945
  199.9 53.6 %collective-permute-start.13 = (bf16[2,768,128]{2,1,0:T(8,128)(2,1)}, bf16[2,768,128]{2,1,0:T(8,128)(2,1)}, u32[]{:S(2)}, u32[]{:S(2)}) collective-permute-start(bf16[2,768,128]{2,1,0:T(8,128)(2,1)} %slice.614), channel_id=1, source_target_pairs={{0,4},{4,0},{8,12},{12,8},{16,20},{20,16},{24,28},{28,24},{1,5},{5... | collective-permute-start | bytes 1179656 | tf_op jit(solution)/shard_map/ppermute | solution.py:945
  272.1 54.3 %collective-permute-start.19 = (bf16[768,128]{1,0:T(8,128)(2,1)}, bf16[768,128]{1,0:T(8,128)(2,1)S(1)}, u32[]{:S(2)}, u32[]{:S(2)}) collective-permute-start(bf16[768,128]{1,0:T(8,128)(2,1)} %get-tuple-element.132), channel_id=1, source_target_pairs={{0,24},{4,28},{8,0},{12,4},{16,8},{20,12},{24,16},{28,20},{1,25},{... | collective-permute-start | bytes 589832 | tf_op jit(solution)/shard_map/ppermute | solution.py:934
  318.5 25.4 %collective-permute-start.20 = (bf16[768,128]{1,0:T(8,128)(2,1)}, bf16[768,128]{1,0:T(8,128)(2,1)S(1)}, u32[]{:S(2)}, u32[]{:S(2)}) collective-permute-start(bf16[768,128]{1,0:T(8,128)(2,1)} %get-tuple-element.133), channel_id=1, source_target_pairs={{0,16},{4,20},{8,24},{12,28},{16,0},{20,4},{24,8},{28,12},{1,17},{... | collective-permute-start | bytes 589832 | tf_op jit(solution)/shard_map/ppermute | solution.py:934
  318.5 25.4 %collective-permute-start.21 = (bf16[768,128]{1,0:T(8,128)(2,1)}, bf16[768,128]{1,0:T(8,128)(2,1)S(1)}, u32[]{:S(2)}, u32[]{:S(2)}) collective-permute-start(bf16[768,128]{1,0:T(8,128)(2,1)} %get-tuple-element.134), channel_id=1, source_target_pairs={{0,8},{4,12},{8,16},{12,20},{16,24},{20,28},{24,0},{28,4},{1,9},{5... | collective-permute-start | bytes 589832 | tf_op jit(solution)/shard_map/ppermute | solution.py:934
  530.7 24.8 %collective-permute-start.38 = (bf16[192,2048]{1,0:T(8,128)(2,1)}, bf16[192,2048]{1,0:T(8,128)(2,1)S(1)}, u32[]{:S(2)}, u32[]{:S(2)}) collective-permute-start(bf16[192,2048]{1,0:T(8,128)(2,1)} %get-tuple-element.161), channel_id=1, source_target_pairs={{0,2},{1,3},{2,0},{3,1},{4,6},{5,7},{6,4},{7,5},{8,10},{9,11},{10,... | collective-permute-start | bytes 2359304 | tf_op jit(solution)/shard_map/ppermute | solution.py:41
  531.5 24.0 %collective-permute-start.41 = (bf16[192,2048]{1,0:T(8,128)(2,1)}, bf16[192,2048]{1,0:T(8,128)(2,1)S(1)}, u32[]{:S(2)}, u32[]{:S(2)}) collective-permute-start(bf16[192,2048]{1,0:T(8,128)(2,1)} %get-tuple-element.162), channel_id=1, source_target_pairs={{0,1},{1,0},{2,3},{3,2},{4,5},{5,4},{6,7},{7,6},{8,9},{9,8},{10,11... | collective-permute-start | bytes 2359304 | tf_op jit(solution)/shard_map/ppermute | solution.py:41
  649.9 41.6 %collective-permute-start.52 = (bf16[768,128]{1,0:T(8,128)(2,1)}, bf16[768,128]{1,0:T(8,128)(2,1)}, u32[]{:S(2)}, u32[]{:S(2)}) collective-permute-start(bf16[768,128]{1,0:T(8,128)(2,1)} %get-tuple-element.164), channel_id=1, source_target_pairs={{0,24},{4,28},{8,0},{12,4},{16,8},{20,12},{24,16},{28,20},{1,25},{... | collective-permute-start | bytes 589832 | tf_op jit(solution)/shard_map/ppermute | solution.py:934
  651.0 42.7 %collective-permute-start.53 = (bf16[768,128]{1,0:T(8,128)(2,1)}, bf16[768,128]{1,0:T(8,128)(2,1)}, u32[]{:S(2)}, u32[]{:S(2)}) collective-permute-start(bf16[768,128]{1,0:T(8,128)(2,1)} %get-tuple-element.165), channel_id=1, source_target_pairs={{0,16},{4,20},{8,24},{12,28},{16,0},{20,4},{24,8},{28,12},{1,17},{... | collective-permute-start | bytes 589832 | tf_op jit(solution)/shard_map/ppermute | solution.py:934
  651.8 42.0 %collective-permute-start.54 = (bf16[768,128]{1,0:T(8,128)(2,1)}, bf16[768,128]{1,0:T(8,128)(2,1)}, u32[]{:S(2)}, u32[]{:S(2)}) collective-permute-start(bf16[768,128]{1,0:T(8,128)(2,1)} %get-tuple-element.166), channel_id=1, source_target_pairs={{0,8},{4,12},{8,16},{12,20},{16,24},{20,28},{24,0},{28,4},{1,9},{5... | collective-permute-start | bytes 589832 | tf_op jit(solution)/shard_map/ppermute | solution.py:934
  652.0 41.7 %collective-permute-start.58 = (bf16[2,768,128]{2,1,0:T(8,128)(2,1)}, bf16[2,768,128]{2,1,0:T(8,128)(2,1)}, u32[]{:S(2)}, u32[]{:S(2)}) collective-permute-start(bf16[2,768,128]{2,1,0:T(8,128)(2,1)} %get-tuple-element.274), channel_id=1, source_target_pairs={{0,8},{4,12},{8,16},{12,20},{16,24},{20,28},{24,0},{28,4},{1,9},{5... | collective-permute-start | bytes 1179656 | tf_op jit(solution)/shard_map/ppermute | solution.py:934
  660.3 41.1 %collective-permute-start.57 = (bf16[2,768,128]{2,1,0:T(8,128)(2,1)}, bf16[2,768,128]{2,1,0:T(8,128)(2,1)}, u32[]{:S(2)}, u32[]{:S(2)}) collective-permute-start(bf16[2,768,128]{2,1,0:T(8,128)(2,1)} %get-tuple-element.275), channel_id=1, source_target_pairs={{0,16},{4,20},{8,24},{12,28},{16,0},{20,4},{24,8},{28,12},{1,17},{... | collective-permute-start | bytes 1179656 | tf_op jit(solution)/shard_map/ppermute | solution.py:934
  701.4 89.3 %reduce-scatter.5.cloned.1.call-start = ((), (), s32[]{:S(2)}) async-start(), calls=%async_computation.5 | async-start | bytes 2211840 | tf_op jit(solution)/shard_map/reduce_scatter | solution.py:1145
  745.3 20.3 %collective-permute-start.62 = (bf16[192,2048]{1,0:T(8,128)(2,1)}, bf16[192,2048]{1,0:T(8,128)(2,1)S(1)}, u32[]{:S(2)}, u32[]{:S(2)}) collective-permute-start(bf16[192,2048]{1,0:T(8,128)(2,1)} %get-tuple-element.213), channel_id=1, source_target_pairs={{0,2},{1,3},{2,0},{3,1},{4,6},{5,7},{6,4},{7,5},{8,10},{9,11},{10,... | collective-permute-start | bytes 2359304 | tf_op jit(solution)/shard_map/ppermute | solution.py:41
  745.7 20.8 %collective-permute-start.64 = (bf16[192,2048]{1,0:T(8,128)(2,1)}, bf16[192,2048]{1,0:T(8,128)(2,1)}, u32[]{:S(2)}, u32[]{:S(2)}) collective-permute-start(bf16[192,2048]{1,0:T(8,128)(2,1)} %get-tuple-element.214), channel_id=1, source_target_pairs={{0,1},{1,0},{2,3},{3,2},{4,5},{5,4},{6,7},{7,6},{8,9},{9,8},{10,11... | collective-permute-start | bytes 2359304 | tf_op jit(solution)/shard_map/ppermute | solution.py:41
  758.1 22.8 %collective-permute-start.70 = (bf16[512,256]{1,0:T(8,128)(2,1)}, bf16[512,256]{1,0:T(8,128)(2,1)}, u32[]{:S(2)}, u32[]{:S(2)}) collective-permute-start(bf16[512,256]{1,0:T(8,128)(2,1)} %slice.567), channel_id=1, source_target_pairs={{0,2},{1,3},{2,0},{3,1},{4,6},{5,7},{6,4},{7,5},{8,10},{9,11},{10,... | collective-permute-start | bytes 786440 | tf_op jit(solution)/shard_map/ppermute | solution.py:1139
  759.0 22.0 %collective-permute-start.69 = (bf16[512,256]{1,0:T(8,128)(2,1)}, bf16[512,256]{1,0:T(8,128)(2,1)}, u32[]{:S(2)}, u32[]{:S(2)}) collective-permute-start(bf16[512,256]{1,0:T(8,128)(2,1)} %slice.567), channel_id=1, source_target_pairs={{0,1},{1,0},{2,3},{3,2},{4,5},{5,4},{6,7},{7,6},{8,9},{9,8},{10,11... | collective-permute-start | bytes 786440 | tf_op jit(solution)/shard_map/ppermute | solution.py:1139
  759.9 21.1 %collective-permute-start.71 = (bf16[512,256]{1,0:T(8,128)(2,1)}, bf16[512,256]{1,0:T(8,128)(2,1)}, u32[]{:S(2)}, u32[]{:S(2)}) collective-permute-start(bf16[512,256]{1,0:T(8,128)(2,1)} %slice.567), channel_id=1, source_target_pairs={{0,3},{1,2},{2,1},{3,0},{4,7},{5,6},{6,5},{7,4},{8,11},{9,10},{10,... | collective-permute-start | bytes 786440 | tf_op jit(solution)/shard_map/ppermute | solution.py:1139
  (170 other events, 1360.4 us)
Sparse Core Ops, SparseCore 0:
  11.6 73.9 all-gather.10
  87.7 46.5 all-gather.12
  135.9 216.8 all-gather.6
  354.3 80.2 all-gather.8
  701.5 46.3 reduce-scatter.2
  750.1 33.9 reduce-scatter.4

commit v8 on v7

--- a/solution.py
+++ b/solution.py
@@ -1144,7 +1144,7 @@
     both = sum_tp(early[: k_rows + 2 * down_size])
     late = lax.psum_scatter(late, "seq", scatter_dimension=0, tiled=False)
     summed = scatter_groups(near_part, far_part, tp)
-    summed, late = lax.optimization_barrier((summed, late))
+    summed, late, early, both = lax.optimization_barrier((summed, late, early, both))
     input_grad = jnp.concatenate([d_hidden[i] + summed[i] for i in groups], axis=0)
     grad_a_qkv = sum_tp(late[:k_rows])
     grad_a_gu = both[:k_rows]

time: 820 us -> 825 us (level)
    unnamed x276 -> x274, local copies, waits for them, and re-layouts: 34.3 us -> 33.1 us
  transfers between devices with their start and end apart: 78 -> 78, of which waited for: 42 -> 41; matrix products, arithmetic and copies ran while one was open for 20% -> 20% of each run, Pallas kernels for 18% -> 18%
where the time goes in v8:
time: 825 us; the launch traced here: 817 us
  waiting for transfers between devices  273 us (33%)
  Pallas kernels  207 us (25%)
  starting transfers between devices  127 us (15%)
  local copies, waits for them, and re-layouts  123 us (15%)
  other arithmetic  37.2 us (5%)
  matrix products  30.1 us (4%)
  between operations  19.1 us (2%)
    ppermute x28, waiting for transfers between devices, flip(): return lax.ppermute(value, axis, [(i, i ^ 1 << bit) for i in range(count)])  102 us
    ppermute x18, waiting for transfers between devices, head_shift(): lax.ppermute(value, 'seq', [(h * group + j, (h + by) % heads * group + j)...  93.9 us
    ppermute x18, starting transfers between devices, head_shift(): lax.ppermute(value, 'seq', [(h * group + j, (h + by) % heads * group + j)...  66.5 us
    pallas_call x2, Pallas kernels, ff_back(): pl.pallas_call(functools.partial(ff_back_kernel, parts, n), grid=(n,), ou...  45.8 us
    ppermute x28, starting transfers between devices, flip(): return lax.ppermute(value, axis, [(i, i ^ 1 << bit) for i in range(count)])  34.1 us
    unnamed x274, local copies, waits for them, and re-layouts  33.1 us
    pallas_call x1, Pallas kernels, attend_back(): pl.pallas_call(functools.partial(attend_back_kernel, slots, group, rows,...  30.8 us
    pallas_call x2, Pallas kernels, gate_up_product(): pl.pallas_call(gate_up_kernel, grid=(n,), out_shape=[jax.ShapeDtypeStruct...  29.6 us
  transfers between devices with their start and end apart: 78, of which 41 were waited for; matrix products, arithmetic and copies ran while one was open for 20% of the time, Pallas kernels for 18%

profile of v8, /device:TPU:0, one launch (start us, length us, event | category | flops | bytes accessed | tf_op | source)
XLA Modules:
  0.0 816.9 jit_solution(5815386404171874334)
XLA Ops:
  35.6 16.1 %collective-permute-done.1 = bf16[192,2048]{1,0:T(8,128)(2,1)} collective-permute-done((bf16[192,2048]{1,0:T(8,128)(2,1)S(1)}, bf16[192,2048]{1,0:T(8,128)(2,1)}, u32[]{:S(2)}, u32[]{:S(2)}) %collective-permute-start.1) | collective-permute-done | bytes 786464 | tf_op jit(solution)/shard_map/ppermute | solution.py:870
  60.6 24.9 %all-gather.11.cloned.1.call-done = bf16[2304,1536]{1,0:T(8,128)(2,1)} async-done(((bf16[288,1536]{1,0:T(8,128)(2,1)}), bf16[2304,1536]{1,0:T(8,128)(2,1)}) %all-gather.11.cloned.1.call-update) | async-done | bytes 7077904 | tf_op jit(solution)/shard_map/all_gather | solution.py:876
  107.1 10.1 %collective-permute-done.4 = bf16[8,64,384]{2,1,0:T(8,128)(2,1)} collective-permute-done((bf16[8,64,384]{2,1,0:T(8,128)(2,1)}, bf16[8,64,384]{2,1,0:T(8,128)(2,1)}, u32[]{:S(2)}, u32[]{:S(2)}) %collective-permute-start.4) | collective-permute-done | bytes 393248 | tf_op jit(solution)/shard_map/ppermute | solution.py:904
  123.5 10.4 %qkv_product.1 = (f32[768,1536]{1,0:T(8,128)}, f32[3,768,1]{2,1,0:T(8,128)}) custom-call(bf16[768,2048]{1,0:T(8,128)(2,1)} %slice_dynamic-update-slice_fusion.x, bf16[768,384]{1,0:T(8,128)(2,1)} %fusion.6.latent, bf16[8,288,1536]{2,1,0:T(8,128)(2,1)} %bitcast.239, bf16[128,1536]{1,0:T(8,128)(2,1)} %bitcast.282), custom_call_target="tpu_custom_call" | custom-call | flops 4831838208 | bytes 7077888 | tf_op jit(solution)/shard_map/qkv_product/pallas_call | solution.py:556
  157.5 8.7 %spread_heads.1 = (bf16[3,768,128]{2,1,0:T(8,128)(2,1)}, bf16[3,768,128]{2,1,0:T(8,128)(2,1)}, bf16[3,768,128]{2,1,0:T(8,128)(2,1)}, bf16[3,768,128]{2,1,0:T(8,128)(2,1)}) custom-call(s32[4]{0:T(128)} %get-tuple-element.376.order, s32[8]{0:T(128)} %copy-done.108, f32[768,1536]{1,0:T(8,128)} %get-tuple-element.119.z.refs_8_.refs_5_, f32[768,2]{1,0:T(8,128)} %bitcast.254, ...), custom_call_target="tpu_custom_call" | custom-call | tf_op jit(solution)/shard_map/spread_heads/pallas_call | solution.py:404
  188.1 9.2 %collective-permute-done.9.refs_1_ = bf16[3,768,128]{2,1,0:T(8,128)(2,1)} collective-permute-done((bf16[3,768,128]{2,1,0:T(8,128)(2,1)}, bf16[3,768,128]{2,1,0:T(8,128)(2,1)}, u32[]{:S(2)}, u32[]{:S(2)}) %collective-permute-start.9) | collective-permute-done | bytes 589856 | tf_op jit(solution)/shard_map/ppermute | solution.py:934
  199.0 38.3 %collective-permute-done.10.refs_2_ = bf16[3,768,128]{2,1,0:T(8,128)(2,1)} collective-permute-done((bf16[3,768,128]{2,1,0:T(8,128)(2,1)}, bf16[3,768,128]{2,1,0:T(8,128)(2,1)}, u32[]{:S(2)}, u32[]{:S(2)}) %collective-permute-start.10) | collective-permute-done | bytes 589856 | tf_op jit(solution)/shard_map/ppermute | solution.py:934
  252.6 18.6 %attend.1 = (bf16[768,128]{1,0:T(8,128)(2,1)}, bf16[768,128]{1,0:T(8,128)(2,1)}, bf16[768,128]{1,0:T(8,128)(2,1)}, bf16[768,128]{1,0:T(8,128)(2,1)}) custom-call(s32[24]{0:T(128)} %bitcast.313, s32[24]{0:T(128)} %bitcast.311, s32[24]{0:T(128)} %select_reduce_fusion.2.prompt_at, bf16[3,768,128]{2,1,0:T(8,128)(2,1)} %get-tuple-element.124.refs_0_, ...), custom_call_target="tpu_custom_call" | custom-call | flops 1811939328 | bytes 4718592 | tf_op jit(solution)/shard_map/attend/pallas_call | solution.py:295
  271.3 46.3 %collective-permute-start.19 = (bf16[768,128]{1,0:T(8,128)(2,1)}, bf16[768,128]{1,0:T(8,128)(2,1)S(1)}, u32[]{:S(2)}, u32[]{:S(2)}) collective-permute-start(bf16[768,128]{1,0:T(8,128)(2,1)} %get-tuple-element.134), channel_id=1, source_target_pairs={{0,24},{4,28},{8,0},{12,4},{16,8},{20,12},{24,16},{28,20},{1,25},{... | collective-permute-start | bytes 589832 | tf_op jit(solution)/shard_map/ppermute | solution.py:934
  324.5 18.3 %collective-permute-done.20.refs_2_ = bf16[768,128]{1,0:T(8,128)(2,1)S(1)} collective-permute-done((bf16[768,128]{1,0:T(8,128)(2,1)}, bf16[768,128]{1,0:T(8,128)(2,1)S(1)}, u32[]{:S(2)}, u32[]{:S(2)}) %collective-permute-start.20) | collective-permute-done | bytes 196640 | tf_op jit(solution)/shard_map/ppermute | solution.py:934
  358.5 12.2 %collective-permute-done.22 = bf16[192,2048]{1,0:T(8,128)(2,1)S(1)} collective-permute-done((bf16[192,2048]{1,0:T(8,128)(2,1)}, bf16[192,2048]{1,0:T(8,128)(2,1)S(1)}, u32[]{:S(2)}, u32[]{:S(2)}) %collective-permute-start.22) | collective-permute-done | bytes 786464 | tf_op jit(solution)/shard_map/ppermute | solution.py:41
  375.5 7.4 collective-permute-done.26
  388.0 6.2 collective-permute-done.24
  398.7 13.8 %collective-permute-done.28 = bf16[192,2048]{1,0:T(8,128)(2,1)S(1)} collective-permute-done((bf16[192,2048]{1,0:T(8,128)(2,1)S(1)}, bf16[192,2048]{1,0:T(8,128)(2,1)S(1)}, u32[]{:S(2)}, u32[]{:S(2)}) %collective-permute-start.28) | collective-permute-done | bytes 786464 | tf_op jit(solution)/shard_map/ppermute | solution.py:41
  412.7 15.0 %gate_up_product.2 = (f32[384,2048]{1,0:T(8,128)}, f32[384,2048]{1,0:T(8,128)}, bf16[384,2048]{1,0:T(8,128)(2,1)}, bf16[384,256]{1,0:T(8,128)(2,1)}) custom-call(bf16[384,2048]{1,0:T(8,128)(2,1)} %pad_maximum_fusion.1.h, bf16[2048,256]{1,0:T(8,128)(2,1)} %bitcast.242, f32[384,128]{1,0:T(8,128)} %get-tuple-element.317.pick, ...), custom_call_target="tpu_custom_call" | custom-call | flops 6442450944 | bytes 16777216 | tf_op jit(solution)/shard_map/gate_up_product/pallas_call | solution.py:677
  427.7 14.6 %gate_up_product.3 = (f32[384,2048]{1,0:T(8,128)}, f32[384,2048]{1,0:T(8,128)}, bf16[384,2048]{1,0:T(8,128)(2,1)}, bf16[384,256]{1,0:T(8,128)(2,1)}) custom-call(bf16[384,2048]{1,0:T(8,128)(2,1)} %copy-done.7, bf16[2048,256]{1,0:T(8,128)(2,1)} %bitcast.243, f32[384,128]{1,0:T(8,128)} %get-tuple-element.318.pick, ...), custom_call_target="tpu_custom_call" | custom-call | flops 6442450944 | bytes 16777216 | tf_op jit(solution)/shard_map/gate_up_product/pallas_call | solution.py:677
  442.3 8.7 %add_product.7 = (bf16[192,2048]{1,0:T(8,128)(2,1)}, bf16[192,2048]{1,0:T(8,128)(2,1)}, bf16[384,128]{1,0:T(8,128)(2,1)}) custom-call(bf16[384,2048]{1,0:T(8,128)(2,1)} %get-tuple-element.155.a, bf16[2048,2048]{1,0:T(8,128)(2,1)} %all-gather.9.cloned.1.call-done.weight.w_down, bf16[2048,128]{1,0:T(8,128)(2,1)} %bitcast.262, ...), custom_call_target="tpu_custom_call" | custom-call | flops 3221225472 | bytes 8388608 | tf_op jit(solution)/shard_map/add_product/pallas_call | solution.py:599
  453.5 8.8 %add_product.6 = (bf16[384,2048]{1,0:T(8,128)(2,1)}, bf16[384,128]{1,0:T(8,128)(2,1)}) custom-call(bf16[384,2048]{1,0:T(8,128)(2,1)} %get-tuple-element.151.a, bf16[2048,2048]{1,0:T(8,128)(2,1)} %all-gather.9.cloned.1.call-done.weight.w_down, bf16[2048,128]{1,0:T(8,128)(2,1)} %bitcast.263, bf16[128,2048]{1,0:T(8,128)(2,1)} %get-tuple-element.299.second.b_down, ...), custom_call_target="tpu_custom_call" | custom-call | flops 3221225472 | bytes 8388608 | tf_op jit(solution)/shard_map/add_product/pallas_call | solution.py:599
  462.3 6.6 collective-permute-done.30
  473.0 6.8 collective-permute-done.33
  483.6 7.8 collective-permute-done.34
  497.5 9.4 %collective-permute-done.36 = bf16[192,2048]{1,0:T(8,128)(2,1)S(1)} collective-permute-done((bf16[192,2048]{1,0:T(8,128)(2,1)S(1)}, bf16[192,2048]{1,0:T(8,128)(2,1)S(1)}, u32[]{:S(2)}, u32[]{:S(2)}) %collective-permute-start.36) | collective-permute-done | bytes 786464 | tf_op jit(solution)/shard_map/ppermute | solution.py:41
  508.3 22.9 %ff_back.3 = (bf16[192,2048]{1,0:T(8,128)(2,1)}, bf16[192,2048]{1,0:T(8,128)(2,1)}, bf16[384,2048]{1,0:T(8,128)(2,1)}, bf16[384,2048]{1,0:T(8,128)(2,1)}, bf16[3...) custom-call(bf16[384,2048]{1,0:T(8,128)(2,1)} %copy-done.17, bf16[128,2048]{1,0:T(8,128)(2,1)} %get-tuple-element.299.second.b_down, ...), custom_call_target="tpu_custom_call" | custom-call | flops 9663676416 | bytes 25165824 | tf_op jit(solution)/shard_map/ff_back/pallas_call | solution.py:761
  534.1 22.9 %ff_back.2 = (bf16[384,2048]{1,0:T(8,128)(2,1)}, bf16[384,2048]{1,0:T(8,128)(2,1)}, bf16[384,2048]{1,0:T(8,128)(2,1)}, bf16[384,256]{1,0:T(8,128)(2,1)}, bf16[384,128]{1,0:T(8,128)(2,1)}) custom-call(bf16[384,2048]{1,0:T(8,128)(2,1)} %pad_maximum_fusion.3.d_ff, bf16[128,2048]{1,0:T(8,128)(2,1)} %get-tuple-element.299.second.b_down, ...), custom_call_target="tpu_custom_call" | custom-call | flops 9663676416 | bytes 25165824 | tf_op jit(solution)/shard_map/ff_back/pallas_call | solution.py:761
  561.6 6.5 collective-permute-done.39
  611.2 30.8 %attend_back.1 = (bf16[768,128]{1,0:T(8,128)(2,1)}, bf16[768,128]{1,0:T(8,128)(2,1)}, bf16[768,128]{1,0:T(8,128)(2,1)}, bf16[768,128]{1,0:T(8,128)(2,1)}, bf16[2...) custom-call(s32[24]{0:T(128)} %bitcast.314, s32[24]{0:T(128)} %bitcast.312, s32[24]{0:T(128)} %select_reduce_fusion.2.prompt_at, ...), custom_call_target="tpu_custom_call" | custom-call | flops 4529848320 | bytes 9437184 | tf_op jit(solution)/shard_map/attend_back/pallas_call | solution.py:327
  693.4 7.9 collective-permute-done.57.refs_6_.refs_2_
  701.7 8.3 %unturn_heads.1 = (f32[768,1024]{1,0:T(8,128)}, f32[768,2]{1,0:T(8,128)}) custom-call(s32[4]{0:T(128)} %get-tuple-element.376.order, s32[8]{0:T(128)} %copy-done.108, bf16[768,128]{1,0:T(8,128)(2,1)} %get-tuple-element.202.refs_0_, bf16[768,128]{1,0:T(8,128)(2,1)} %collective-permute-done.52.refs_1_, bf16[768,128]{1,0:T(8,128)(2,1)} %collective-permute-done.53.refs_2_, ...), custom_call_target="tpu_custom_call" | custom-call | tf_op jit(solution)/shard_map/unturn_heads/pallas_call | solution.py:469
  719.3 9.0 %norm_back_heads.1 = (bf16[768,1536]{1,0:T(8,128)(2,1)}, bf16[768,384]{1,0:T(8,128)(2,1)}) custom-call(s32[4]{0:T(128)} %get-tuple-element.376.order, s32[8]{0:T(128)} %copy-done.108, bf16[2,768,128]{2,1,0:T(8,128)(2,1)} %get-tuple-element.198.refs_4_.refs_0_, bf16[2,768,128]{2,1,0:T(8,128)(2,1)} %copy-done.52, ...), custom_call_target="tpu_custom_call" | custom-call | tf_op jit(solution)/shard_map/norm_back_heads/pallas_call | solution.py:512
  737.4 7.5 back_product.2
  746.8 7.6 back_product.3
  758.9 6.5 collective-permute-done.62
  (644 shorter events, 349.8 us)
Async XLA Ops:
  7.2 78.3 %all-gather.11.cloned.1.call-start = ((), (), s32[]{:S(2)}) async-start(), calls=%async_computation.6 | async-start | bytes 7962624 | tf_op jit(solution)/shard_map/all_gather | solution.py:876
  11.5 138.2 %all-gather.13.cloned.1.call-start = ((), (), s32[]{:S(2)}) async-start(), calls=%async_computation.7 | async-start | bytes 4866048 | tf_op jit(solution)/shard_map/all_gather | solution.py:897
  11.5 21.5 %collective-permute-start = (bf16[192,2048]{1,0:T(8,128)(2,1)S(1)}, bf16[192,2048]{1,0:T(8,128)(2,1)}, u32[]{:S(2)}, u32[]{:S(2)}) collective-permute-start(bf16[192,2048]{1,0:T(8,128)(2,1)S(1)} %copy-done.19), channel_id=1, source_target_pairs={{0,1},{1,0},{2,3},{3,2},{4,5},{5,4},{6,7},{7,6},{8,9},{9,8},{10,11... | collective-permute-start | bytes 2359304 | tf_op jit(solution)/shard_map/ppermute | solution.py:870
  14.5 40.7 %collective-permute-start.2 = (bf16[192,2048]{1,0:T(8,128)(2,1)S(1)}, bf16[192,2048]{1,0:T(8,128)(2,1)}, u32[]{:S(2)}, u32[]{:S(2)}) collective-permute-start(bf16[192,2048]{1,0:T(8,128)(2,1)S(1)} %copy-done.19), channel_id=1, source_target_pairs={{0,3},{1,2},{2,1},{3,0},{4,7},{5,6},{6,5},{7,4},{8,11},{9,10},{10,... | collective-permute-start | bytes 2359304 | tf_op jit(solution)/shard_map/ppermute | solution.py:870
  16.0 35.7 %collective-permute-start.1 = (bf16[192,2048]{1,0:T(8,128)(2,1)S(1)}, bf16[192,2048]{1,0:T(8,128)(2,1)}, u32[]{:S(2)}, u32[]{:S(2)}) collective-permute-start(bf16[192,2048]{1,0:T(8,128)(2,1)S(1)} %copy-done.19), channel_id=1, source_target_pairs={{0,2},{1,3},{2,0},{3,1},{4,6},{5,7},{6,4},{7,5},{8,10},{9,11},{10,... | collective-permute-start | bytes 2359304 | tf_op jit(solution)/shard_map/ppermute | solution.py:870
  85.6 327.0 %all-gather.7.cloned.1.call-start = ((), (), s32[]{:S(2)}) async-start(), calls=%async_computation.2 | async-start | bytes 18874368 | tf_op jit(solution)/shard_map/all_gather | solution.py:898
  86.4 355.9 %all-gather.9.cloned.1.call-start = ((), (), s32[]{:S(2)}) async-start(), calls=%async_computation.3 | async-start | bytes 9437184 | tf_op jit(solution)/shard_map/all_gather | solution.py:899
  87.0 667.4 %reduce-scatter.3.cloned.1.call-start = ((), (), s32[]{:S(2)}) async-start(), calls=%async_computation.4 | async-start | bytes 4276224 | tf_op jit(solution)/shard_map/reduce_scatter | solution.py:1107
  96.3 22.0 %collective-permute-start.5 = (bf16[8,64,384]{2,1,0:T(8,128)(2,1)}, bf16[8,64,384]{2,1,0:T(8,128)(2,1)S(1)}, u32[]{:S(2)}, u32[]{:S(2)}) collective-permute-start(bf16[8,64,384]{2,1,0:T(8,128)(2,1)} %reshape.553), channel_id=1, source_target_pairs={{0,3},{1,2},{2,1},{3,0},{4,7},{5,6},{6,5},{7,4},{8,11},{9,10},{10,... | collective-permute-start | bytes 1179656 | tf_op jit(solution)/shard_map/ppermute | solution.py:904
  97.7 19.4 %collective-permute-start.4 = (bf16[8,64,384]{2,1,0:T(8,128)(2,1)}, bf16[8,64,384]{2,1,0:T(8,128)(2,1)}, u32[]{:S(2)}, u32[]{:S(2)}) collective-permute-start(bf16[8,64,384]{2,1,0:T(8,128)(2,1)} %reshape.553), channel_id=1, source_target_pairs={{0,2},{1,3},{2,0},{3,1},{4,6},{5,7},{6,4},{7,5},{8,10},{9,11},{10,... | collective-permute-start | bytes 1179656 | tf_op jit(solution)/shard_map/ppermute | solution.py:904
  154.0 32.9 %collective-permute-start.17 = (bf16[8,64,512]{2,1,0:T(8,128)(2,1)}, bf16[8,64,512]{2,1,0:T(8,128)(2,1)}, u32[]{:S(2)}, u32[]{:S(2)}) collective-permute-start(bf16[8,64,512]{2,1,0:T(8,128)(2,1)} %get-tuple-element.277), channel_id=1, source_target_pairs={{0,2},{1,3},{2,0},{3,1},{4,6},{5,7},{6,4},{7,5},{8,10},{9,11},{10,... | collective-permute-start | bytes 1572872 | tf_op jit(solution)/shard_map/ppermute | solution.py:973
  155.3 88.7 %collective-permute-start.18 = (bf16[8,64,512]{2,1,0:T(8,128)(2,1)}, bf16[8,64,512]{2,1,0:T(8,128)(2,1)}, u32[]{:S(2)}, u32[]{:S(2)}) collective-permute-start(bf16[8,64,512]{2,1,0:T(8,128)(2,1)} %get-tuple-element.277), channel_id=1, source_target_pairs={{0,3},{1,2},{2,1},{3,0},{4,7},{5,6},{6,5},{7,4},{8,11},{9,10},{10,... | collective-permute-start | bytes 1572872 | tf_op jit(solution)/shard_map/ppermute | solution.py:973
  166.3 31.0 %collective-permute-start.9 = (bf16[3,768,128]{2,1,0:T(8,128)(2,1)}, bf16[3,768,128]{2,1,0:T(8,128)(2,1)}, u32[]{:S(2)}, u32[]{:S(2)}) collective-permute-start(bf16[3,768,128]{2,1,0:T(8,128)(2,1)} %get-tuple-element.125), channel_id=1, source_target_pairs={{0,8},{4,12},{8,16},{12,20},{16,24},{20,28},{24,0},{28,4},{1,9},{5... | collective-permute-start | bytes 1769480 | tf_op jit(solution)/shard_map/ppermute | solution.py:934
  166.3 71.0 %collective-permute-start.10 = (bf16[3,768,128]{2,1,0:T(8,128)(2,1)}, bf16[3,768,128]{2,1,0:T(8,128)(2,1)}, u32[]{:S(2)}, u32[]{:S(2)}) collective-permute-start(bf16[3,768,128]{2,1,0:T(8,128)(2,1)} %get-tuple-element.126), channel_id=1, source_target_pairs={{0,16},{4,20},{8,24},{12,28},{16,0},{20,4},{24,8},{28,12},{1,17},{... | collective-permute-start | bytes 1769480 | tf_op jit(solution)/shard_map/ppermute | solution.py:934
  168.9 73.3 %collective-permute-start.11 = (bf16[3,768,128]{2,1,0:T(8,128)(2,1)}, bf16[3,768,128]{2,1,0:T(8,128)(2,1)}, u32[]{:S(2)}, u32[]{:S(2)}) collective-permute-start(bf16[3,768,128]{2,1,0:T(8,128)(2,1)} %get-tuple-element.127), channel_id=1, source_target_pairs={{0,24},{4,28},{8,0},{12,4},{16,8},{20,12},{24,16},{28,20},{1,25},{... | collective-permute-start | bytes 1769480 | tf_op jit(solution)/shard_map/ppermute | solution.py:934
  186.9 65.7 %collective-permute-start.12 = (bf16[2,768,128]{2,1,0:T(8,128)(2,1)}, bf16[2,768,128]{2,1,0:T(8,128)(2,1)}, u32[]{:S(2)}, u32[]{:S(2)}) collective-permute-start(bf16[2,768,128]{2,1,0:T(8,128)(2,1)} %slice.482), channel_id=1, source_target_pairs={{0,4},{4,0},{8,12},{12,8},{16,20},{20,16},{24,28},{28,24},{1,5},{5... | collective-permute-start | bytes 1179656 | tf_op jit(solution)/shard_map/ppermute | solution.py:945
  199.0 53.6 %collective-permute-start.13 = (bf16[2,768,128]{2,1,0:T(8,128)(2,1)}, bf16[2,768,128]{2,1,0:T(8,128)(2,1)}, u32[]{:S(2)}, u32[]{:S(2)}) collective-permute-start(bf16[2,768,128]{2,1,0:T(8,128)(2,1)} %slice.614), channel_id=1, source_target_pairs={{0,4},{4,0},{8,12},{12,8},{16,20},{20,16},{24,28},{28,24},{1,5},{5... | collective-permute-start | bytes 1179656 | tf_op jit(solution)/shard_map/ppermute | solution.py:945
  271.3 53.3 %collective-permute-start.19 = (bf16[768,128]{1,0:T(8,128)(2,1)}, bf16[768,128]{1,0:T(8,128)(2,1)S(1)}, u32[]{:S(2)}, u32[]{:S(2)}) collective-permute-start(bf16[768,128]{1,0:T(8,128)(2,1)} %get-tuple-element.134), channel_id=1, source_target_pairs={{0,24},{4,28},{8,0},{12,4},{16,8},{20,12},{24,16},{28,20},{1,25},{... | collective-permute-start | bytes 589832 | tf_op jit(solution)/shard_map/ppermute | solution.py:934
  317.5 25.3 %collective-permute-start.20 = (bf16[768,128]{1,0:T(8,128)(2,1)}, bf16[768,128]{1,0:T(8,128)(2,1)S(1)}, u32[]{:S(2)}, u32[]{:S(2)}) collective-permute-start(bf16[768,128]{1,0:T(8,128)(2,1)} %get-tuple-element.135), channel_id=1, source_target_pairs={{0,16},{4,20},{8,24},{12,28},{16,0},{20,4},{24,8},{28,12},{1,17},{... | collective-permute-start | bytes 589832 | tf_op jit(solution)/shard_map/ppermute | solution.py:934
  317.5 25.3 %collective-permute-start.21 = (bf16[768,128]{1,0:T(8,128)(2,1)}, bf16[768,128]{1,0:T(8,128)(2,1)S(1)}, u32[]{:S(2)}, u32[]{:S(2)}) collective-permute-start(bf16[768,128]{1,0:T(8,128)(2,1)} %get-tuple-element.136), channel_id=1, source_target_pairs={{0,8},{4,12},{8,16},{12,20},{16,24},{20,28},{24,0},{28,4},{1,9},{5... | collective-permute-start | bytes 589832 | tf_op jit(solution)/shard_map/ppermute | solution.py:934
  531.2 25.8 %collective-permute-start.38 = (bf16[192,2048]{1,0:T(8,128)(2,1)}, bf16[192,2048]{1,0:T(8,128)(2,1)S(1)}, u32[]{:S(2)}, u32[]{:S(2)}) collective-permute-start(bf16[192,2048]{1,0:T(8,128)(2,1)} %get-tuple-element.163), channel_id=1, source_target_pairs={{0,2},{1,3},{2,0},{3,1},{4,6},{5,7},{6,4},{7,5},{8,10},{9,11},{10,... | collective-permute-start | bytes 2359304 | tf_op jit(solution)/shard_map/ppermute | solution.py:41
  532.5 24.5 %collective-permute-start.41 = (bf16[192,2048]{1,0:T(8,128)(2,1)}, bf16[192,2048]{1,0:T(8,128)(2,1)S(1)}, u32[]{:S(2)}, u32[]{:S(2)}) collective-permute-start(bf16[192,2048]{1,0:T(8,128)(2,1)} %get-tuple-element.164), channel_id=1, source_target_pairs={{0,1},{1,0},{2,3},{3,2},{4,5},{5,4},{6,7},{7,6},{8,9},{9,8},{10,11... | collective-permute-start | bytes 2359304 | tf_op jit(solution)/shard_map/ppermute | solution.py:41
  649.7 41.9 %collective-permute-start.52 = (bf16[768,128]{1,0:T(8,128)(2,1)}, bf16[768,128]{1,0:T(8,128)(2,1)}, u32[]{:S(2)}, u32[]{:S(2)}) collective-permute-start(bf16[768,128]{1,0:T(8,128)(2,1)} %get-tuple-element.166), channel_id=1, source_target_pairs={{0,24},{4,28},{8,0},{12,4},{16,8},{20,12},{24,16},{28,20},{1,25},{... | collective-permute-start | bytes 589832 | tf_op jit(solution)/shard_map/ppermute | solution.py:934
  651.1 42.3 %collective-permute-start.53 = (bf16[768,128]{1,0:T(8,128)(2,1)}, bf16[768,128]{1,0:T(8,128)(2,1)}, u32[]{:S(2)}, u32[]{:S(2)}) collective-permute-start(bf16[768,128]{1,0:T(8,128)(2,1)} %get-tuple-element.167), channel_id=1, source_target_pairs={{0,16},{4,20},{8,24},{12,28},{16,0},{20,4},{24,8},{28,12},{1,17},{... | collective-permute-start | bytes 589832 | tf_op jit(solution)/shard_map/ppermute | solution.py:934
  651.9 41.5 %collective-permute-start.54 = (bf16[768,128]{1,0:T(8,128)(2,1)}, bf16[768,128]{1,0:T(8,128)(2,1)}, u32[]{:S(2)}, u32[]{:S(2)}) collective-permute-start(bf16[768,128]{1,0:T(8,128)(2,1)} %get-tuple-element.168), channel_id=1, source_target_pairs={{0,8},{4,12},{8,16},{12,20},{16,24},{20,28},{24,0},{28,4},{1,9},{5... | collective-permute-start | bytes 589832 | tf_op jit(solution)/shard_map/ppermute | solution.py:934
  651.9 41.5 %collective-permute-start.58 = (bf16[2,768,128]{2,1,0:T(8,128)(2,1)}, bf16[2,768,128]{2,1,0:T(8,128)(2,1)}, u32[]{:S(2)}, u32[]{:S(2)}) collective-permute-start(bf16[2,768,128]{2,1,0:T(8,128)(2,1)} %get-tuple-element.278), channel_id=1, source_target_pairs={{0,8},{4,12},{8,16},{12,20},{16,24},{20,28},{24,0},{28,4},{1,9},{5... | collective-permute-start | bytes 1179656 | tf_op jit(solution)/shard_map/ppermute | solution.py:934
  660.4 40.9 %collective-permute-start.57 = (bf16[2,768,128]{2,1,0:T(8,128)(2,1)}, bf16[2,768,128]{2,1,0:T(8,128)(2,1)}, u32[]{:S(2)}, u32[]{:S(2)}) collective-permute-start(bf16[2,768,128]{2,1,0:T(8,128)(2,1)} %get-tuple-element.279), channel_id=1, source_target_pairs={{0,16},{4,20},{8,24},{12,28},{16,0},{20,4},{24,8},{28,12},{1,17},{... | collective-permute-start | bytes 1179656 | tf_op jit(solution)/shard_map/ppermute | solution.py:934
  701.3 83.7 %reduce-scatter.5.cloned.1.call-start = ((), (), s32[]{:S(2)}) async-start(), calls=%async_computation.5 | async-start | bytes 2211840 | tf_op jit(solution)/shard_map/reduce_scatter | solution.py:1145
  744.9 20.5 %collective-permute-start.62 = (bf16[192,2048]{1,0:T(8,128)(2,1)}, bf16[192,2048]{1,0:T(8,128)(2,1)S(1)}, u32[]{:S(2)}, u32[]{:S(2)}) collective-permute-start(bf16[192,2048]{1,0:T(8,128)(2,1)} %get-tuple-element.215), channel_id=1, source_target_pairs={{0,2},{1,3},{2,0},{3,1},{4,6},{5,7},{6,4},{7,5},{8,10},{9,11},{10,... | collective-permute-start | bytes 2359304 | tf_op jit(solution)/shard_map/ppermute | solution.py:41
  746.0 20.6 %collective-permute-start.64 = (bf16[192,2048]{1,0:T(8,128)(2,1)}, bf16[192,2048]{1,0:T(8,128)(2,1)S(1)}, u32[]{:S(2)}, u32[]{:S(2)}) collective-permute-start(bf16[192,2048]{1,0:T(8,128)(2,1)} %get-tuple-element.216), channel_id=1, source_target_pairs={{0,1},{1,0},{2,3},{3,2},{4,5},{5,4},{6,7},{7,6},{8,9},{9,8},{10,11... | collective-permute-start | bytes 2359304 | tf_op jit(solution)/shard_map/ppermute | solution.py:41
  757.6 20.6 %collective-permute-start.68 = (bf16[512,256]{1,0:T(8,128)(2,1)S(1)}, bf16[512,256]{1,0:T(8,128)(2,1)S(1)}, u32[]{:S(2)}, u32[]{:S(2)}) collective-permute-start(bf16[512,256]{1,0:T(8,128)(2,1)S(1)} %slice.563), channel_id=1, source_target_pairs={{0,3},{1,2},{2,1},{3,0},{4,7},{5,6},{6,5},{7,4},{8,11},{9,10},{10,... | collective-permute-start | bytes 786440 | tf_op jit(solution)/shard_map/ppermute | solution.py:1139
  788.1 19.3 %collective-permute-start.70 = (bf16[256,384]{1,0:T(8,128)(2,1)}, bf16[256,384]{1,0:T(8,128)(2,1)}, u32[]{:S(2)}, u32[]{:S(2)}) collective-permute-start(bf16[256,384]{1,0:T(8,128)(2,1)} %slice.564), channel_id=1, source_target_pairs={{0,2},{1,3},{2,0},{3,1},{4,6},{5,7},{6,4},{7,5},{8,10},{9,11},{10,... | collective-permute-start | bytes 589832 | tf_op jit(solution)/shard_map/ppermute | solution.py:1139
  (169 other events, 1387.0 us)
Sparse Core Ops, SparseCore 0:
  11.6 73.9 all-gather.10
  87.7 46.5 all-gather.12
  135.9 216.8 all-gather.6
  354.3 80.2 all-gather.8
  701.4 47.0 reduce-scatter.2
  750.7 34.1 reduce-scatter.4
